TPU v7x, 32 devices: a whole 2x2x4 slice. The times are simulated.
32 devices in a mesh: seq: 8 (over z, x), head: 4 (over y, core).
Axes of the slice: x: 2, y: 2, z: 4, core: 2. Of those that a mesh axis runs over, the one named last changes fastest.
Arguments:
- layer_in: bfloat16 [2, 4096, 2048], P(None, 'seq'), may hold values from -6 to 6
- seg_starts: int32 [2, 4096], P(None, 'seq'), may hold values from 0 to 1, as said below
- attn_gain: bfloat16 [2048], P('seq'), may hold values from 0.5 to 1.5
- query_weight: bfloat16 [2048, 1024], P('seq', 'head'), may hold values from -0.125 to 0.125
- key_weight: bfloat16 [2048, 1024], P('seq', 'head'), may hold values from -0.125 to 0.125
- value_weight: bfloat16 [2048, 2048], P('seq', 'head'), may hold values from -0.125 to 0.125
- gate_weight: bfloat16 [2048, 2048], P('seq', 'head'), may hold values from -0.125 to 0.125
- decay_down: bfloat16 [2048, 16], P('seq'), may hold values from -0.125 to 0.125
- decay_up: bfloat16 [16, 1024], P(None, ('head', 'seq')), may hold values from -1.5 to 1.5
- decay_bias: bfloat16 [1024], P(('head', 'seq')), may hold values from -1 to 9
- head_gain: bfloat16 [512], P('seq'), may hold values from 0.5 to 1.5
- out_weight: bfloat16 [2048, 2048], P('head', 'seq'), may hold values from -0.25 to 0.25
- ffn_gain: bfloat16 [2048], P('seq'), may hold values from 0.5 to 1.5
- ffn_gate: bfloat16 [2048, 5632], P('seq', 'head'), may hold values from -0.125 to 0.125
- ffn_up: bfloat16 [2048, 5632], P('seq', 'head'), may hold values from -0.125 to 0.125
- ffn_down: bfloat16 [5632, 2048], P('head', 'seq'), may hold values from -0.15625 to 0.15625
- out_grad: bfloat16 [2, 4096, 2048], P(None, 'seq'), may hold values from -6 to 6
Outputs:
- layer_out: bfloat16 [2, 4096, 2048], P(None, 'seq')
- input_grad: bfloat16 [2, 4096, 2048], P(None, 'seq')
- grad_attn_gain: float32 [2048], P('seq')
- grad_query: float32 [2048, 1024], P('seq', 'head')
- grad_key: float32 [2048, 1024], P('seq', 'head')
- grad_value: float32 [2048, 2048], P('seq', 'head')
- grad_gate: float32 [2048, 2048], P('seq', 'head')
- grad_decay_down: float32 [2048, 16], P('seq')
- grad_decay_up: float32 [16, 1024], P(None, ('head', 'seq'))
- grad_decay_bias: float32 [1024], P(('head', 'seq'))
- grad_head_gain: float32 [512], P('seq')
- grad_out_weight: float32 [2048, 2048], P('head', 'seq')
- grad_ffn_gain: float32 [2048], P('seq')
- grad_ffn_gate: float32 [2048, 5632], P('seq', 'head')
- grad_ffn_up: float32 [2048, 5632], P('seq', 'head')
- grad_ffn_down: float32 [5632, 2048], P('head', 'seq')
Inputs may be any that keep to these rules, and one draw needn't show every extreme that they name: `seg_starts`: the first token of each sequence begins a segment; every segment holds 1024 tokens or more; in one micro-batch, drawn from the seed, the whole sequence is one segment.
All inputs are finite; a program needn't handle non-finite values.
Results may differ from a plain program's by a relative error of at most 0.039.
Values may be sent and summed in bfloat16 or wider, within the bound.
A program may use at most 256 MiB of HBM per device.

v0:
```python
import jax
import jax.numpy as jnp
from jax import lax
from jax.sharding import PartitionSpec as P

DK = 256
DV = 512
GROUP = 64


EPS = 1e-06
HIGH = lax.Precision.HIGHEST


def prefix_2(value, axis, join, neutral):
    count, mine = (lax.axis_size(axis), lax.axis_index(axis))
    pieces = jax.tree.map(lambda part: lax.all_gather(part, axis), value)
    total = jax.tree.map(
        lambda part, zero: jnp.full_like(part, 0) + jnp.asarray(zero, part.dtype), value, neutral
    )

    def turn(position, total):
        longer = join(total, jax.tree.map(lambda part: part[position], pieces))
        return jax.tree.map(lambda new, old: jnp.where(position < mine, new, old), longer, total)

    return lax.fori_loop(0, count - 1, turn, total)


def entering(array, axis, join, neutral):
    count = lax.axis_size(axis)
    place = lax.axis_index(axis)
    ahead = count - 1 - place
    gathered = jax.tree.map(
        lambda a, kind: lax.all_gather(a.astype(kind), axis),
        array,
        jax.tree.map(lambda a: jnp.bfloat16 if a.dtype == jnp.float32 else a.dtype, array),
    )
    state = jax.tree.map(lambda a, e: jnp.zeros_like(a) + jnp.asarray(e, a.dtype), array, neutral)

    def one(turn, state):
        source = count - 1 - turn
        return join(
            state,
            jax.tree.map(
                lambda a, own: lax.dynamic_index_in_dim(a, source, 0, False).astype(own.dtype),
                gathered,
                array,
            ),
        )

    return lax.fori_loop(0, ahead, one, state)


def root_scale(field):
    return lax.rsqrt(jnp.mean(field * field, axis=-1, keepdims=True) + EPS)


def norm_back(upstream, unit, scale):
    return scale * (upstream - unit * jnp.mean(upstream * unit, axis=-1, keepdims=True))


def matmul(left, right):
    return jnp.dot(left, right, preferred_element_type=jnp.float32)


def matmul_nt(left, right):
    return lax.dot_general(
        left, right, (((1,), (1,)), ((), ())), preferred_element_type=jnp.float32
    )


def matmul_tn(left, right):
    return lax.dot_general(
        left, right, (((0,), (0,)), ((), ())), preferred_element_type=jnp.float32
    )


def combine_states(earlier, later):
    return (earlier[0] * later[0], later[0][..., None] * earlier[1] + later[1])


def mixer_scan(queries, keys, values, decays, starts, state):
    batch, length, heads, key_size = queries.shape
    value_size = values.shape[-1]
    number = length // GROUP

    def blocks(field):
        return jnp.moveaxis(field.reshape((batch, number, GROUP) + field.shape[2:]), 1, 0)

    def advance(carry, piece):
        query_block, key_block, value_block, decay_block, start_block = piece
        cumulative = jnp.cumsum(decay_block, axis=1)
        segment = jnp.cumsum(start_block, axis=1, dtype=jnp.int32)
        untouched = (segment == 0).astype(jnp.float32)
        query_scaled = query_block * key_size ** (-0.5) * jnp.exp(cumulative)
        key_scaled = key_block * jnp.exp(-cumulative)
        scores = jnp.einsum("bthk,bshk->bhts", query_scaled, key_scaled, precision=HIGH)
        places = jnp.arange(GROUP)
        allowed = (segment[:, :, None] == segment[:, None, :]) & (
            places[:, None] >= places[None, :]
        )[None]
        scores = jnp.where(allowed[:, None], scores, 0.0)
        within = jnp.einsum("bhts,bshv->bthv", scores, value_block, precision=HIGH)
        carried = jnp.einsum(
            "bthk,bhkv->bthv", query_scaled * untouched[:, :, None, None], carry, precision=HIGH
        )
        final_decay = cumulative[:, -1]
        trailing = (segment == segment[:, -1:]).astype(jnp.float32)
        key_trailing = (
            key_block * jnp.exp(final_decay[:, None] - cumulative) * trailing[:, :, None, None]
        )
        kept_state = carry * (jnp.exp(final_decay) * untouched[:, -1, None, None])[..., None]
        carry = kept_state + jnp.einsum(
            "bshk,bshv->bhkv", key_trailing, value_block, precision=HIGH
        )
        return (carry, within + carried)

    pieces = (blocks(queries), blocks(keys), blocks(values), blocks(decays), blocks(starts))
    final_state, outputs = lax.scan(jax.checkpoint(advance), state, pieces)
    return (jnp.moveaxis(outputs, 0, 1).reshape(batch, length, heads, value_size), final_state)


def shards(
    layer_in,
    seg_starts,
    attn_gain,
    query_weight,
    key_weight,
    value_weight,
    gate_weight,
    decay_down,
    decay_up,
    decay_bias,
    head_gain,
    out_weight,
    ffn_gain,
    ffn_gate,
    ffn_up,
    ffn_down,
    out_grad,
):
    gathered = (
        lax.all_gather(attn_gain, "seq", axis=0, tiled=True),
        lax.all_gather(query_weight, "seq", axis=0, tiled=True),
        lax.all_gather(key_weight, "seq", axis=0, tiled=True),
        lax.all_gather(value_weight, "seq", axis=0, tiled=True),
        lax.all_gather(gate_weight, "seq", axis=0, tiled=True),
        lax.all_gather(decay_down, "seq", axis=0, tiled=True),
        lax.all_gather(decay_up, "seq", axis=1, tiled=True),
        lax.all_gather(decay_bias, "seq", axis=0, tiled=True),
        lax.all_gather(head_gain, "seq", axis=0, tiled=True),
        lax.all_gather(out_weight, "seq", axis=1, tiled=True),
        lax.all_gather(ffn_gain, "seq", axis=0, tiled=True),
        lax.all_gather(ffn_gate, "seq", axis=0, tiled=True),
        lax.all_gather(ffn_up, "seq", axis=0, tiled=True),
        lax.all_gather(ffn_down, "seq", axis=1, tiled=True),
    )
    (
        gain_one_all,
        query_all,
        key_all,
        value_all,
        gate_all,
        down_all,
        up_all,
        bias_all,
        head_gain_all,
        out_all,
        gain_two_all,
        fgate_all,
        fup_all,
        fdown_all,
    ) = gathered
    batch, block, width = layer_in.shape
    rows = batch * block
    inputs = layer_in.reshape(rows, width).astype(jnp.float32)
    scale_one = root_scale(inputs)
    unit_one = inputs * scale_one
    gain_one = gain_one_all.astype(jnp.float32)
    normed = (unit_one * gain_one).astype(jnp.bfloat16)
    queries = matmul(normed, query_all).astype(jnp.bfloat16)
    keys = matmul(normed, key_all).astype(jnp.bfloat16)
    values = matmul(normed, value_all).astype(jnp.bfloat16)
    lowrank = matmul(normed, down_all)
    raw = jnp.dot(lowrank, up_all.astype(jnp.float32), precision=HIGH) + bias_all.astype(
        jnp.float32
    )
    decays = jax.nn.log_sigmoid(raw) / 16.0
    gates = matmul(normed, gate_all)
    heads = values.shape[1] // DV
    query_heads = queries.astype(jnp.float32).reshape(batch, block, heads, DK)
    key_heads = keys.astype(jnp.float32).reshape(batch, block, heads, DK)
    value_heads = values.astype(jnp.float32).reshape(batch, block, heads, DV)
    decay_heads = decays.reshape(batch, block, heads, DK)
    zero_state = jnp.zeros((batch, heads, DK, DV), jnp.float32)
    local_out, local_state = mixer_scan(
        query_heads, key_heads, value_heads, decay_heads, seg_starts, zero_state
    )
    block_segment = jnp.cumsum(seg_starts, axis=1, dtype=jnp.int32)
    untouched = (block_segment == 0).astype(jnp.float32)
    cumulative = jnp.cumsum(decay_heads, axis=1)
    carry_query = query_heads * DK ** (-0.5) * jnp.exp(cumulative) * untouched[:, :, None, None]
    block_decay = jnp.exp(cumulative[:, -1]) * untouched[:, -1, None, None]
    identity = (jnp.ones_like(block_decay), jnp.zeros_like(local_state))
    prefix = prefix_2((block_decay, local_state), "seq", combine_states, identity)
    state_in = prefix[1]
    mixed = local_out + jnp.einsum("bthk,bhkv->bthv", carry_query, state_in, precision=HIGH)
    head_scale = root_scale(mixed)
    head_unit = mixed * head_scale
    head_gain_f = head_gain_all.astype(jnp.float32)
    sigma_gate = jax.nn.sigmoid(gates)
    gate_act = (gates * sigma_gate).reshape(batch, block, heads, DV)
    normed_heads = (
        (head_unit * head_gain_f * gate_act).reshape(rows, heads * DV).astype(jnp.bfloat16)
    )
    attn_part = matmul(normed_heads, out_all)
    gain_two = gain_two_all.astype(jnp.float32)
    attn = lax.psum(attn_part.astype(jnp.bfloat16), "head").astype(jnp.float32)
    resid = inputs + attn
    scale_two = root_scale(resid)
    unit_two = resid * scale_two
    normed_two = (unit_two * gain_two).astype(jnp.bfloat16)
    pre_gate = matmul(normed_two, fgate_all)
    pre_up = matmul(normed_two, fup_all)
    sigma_pre = jax.nn.sigmoid(pre_gate)
    silu_pre = pre_gate * sigma_pre
    act = (silu_pre * pre_up).astype(jnp.bfloat16)
    ffn_part = matmul(act, fdown_all)
    ffn = lax.psum(ffn_part.astype(jnp.bfloat16), "head").astype(jnp.float32)
    layer_out = (resid + ffn).astype(jnp.bfloat16).reshape(batch, block, width)
    again = (
        lax.all_gather(query_weight, "seq", axis=0, tiled=True),
        lax.all_gather(key_weight, "seq", axis=0, tiled=True),
        lax.all_gather(value_weight, "seq", axis=0, tiled=True),
        lax.all_gather(gate_weight, "seq", axis=0, tiled=True),
        lax.all_gather(decay_down, "seq", axis=0, tiled=True),
        lax.all_gather(decay_up, "seq", axis=1, tiled=True),
        lax.all_gather(out_weight, "seq", axis=1, tiled=True),
        lax.all_gather(ffn_gate, "seq", axis=0, tiled=True),
        lax.all_gather(ffn_up, "seq", axis=0, tiled=True),
        lax.all_gather(ffn_down, "seq", axis=1, tiled=True),
    )
    (
        query_back,
        key_back,
        value_back,
        gate_back,
        down_back,
        up_back,
        out_back,
        fgate_back,
        fup_back,
        fdown_back,
    ) = again
    grad_rows = out_grad.reshape(rows, width)
    grad_float = grad_rows.astype(jnp.float32)
    d_act = matmul_nt(grad_rows, fdown_back)
    grad_fdown = matmul_tn(act, grad_rows)
    d_pre_gate = (d_act * pre_up * sigma_pre * (1.0 + pre_gate * (1.0 - sigma_pre))).astype(
        jnp.bfloat16
    )
    d_pre_up = (d_act * silu_pre).astype(jnp.bfloat16)
    grad_fgate = matmul_tn(normed_two, d_pre_gate)
    grad_fup = matmul_tn(normed_two, d_pre_up)
    d_normed_two_part = matmul_nt(d_pre_gate, fgate_back) + matmul_nt(d_pre_up, fup_back)
    d_normed_two = lax.psum(d_normed_two_part.astype(jnp.bfloat16), "head").astype(jnp.float32)
    grad_gain_two = jnp.sum(d_normed_two * unit_two, axis=0)
    d_resid = grad_float + norm_back(d_normed_two * gain_two, unit_two, scale_two)
    d_attn = d_resid.astype(jnp.bfloat16)
    grad_out = matmul_tn(normed_heads, d_attn)
    d_heads = matmul_nt(d_attn, out_back).reshape(batch, block, heads, DV)
    d_gate_act = (d_heads * head_unit * head_gain_f).reshape(rows, heads * DV)
    d_gates = (d_gate_act * sigma_gate * (1.0 + gates * (1.0 - sigma_gate))).astype(jnp.bfloat16)
    grad_head_part = jnp.sum(d_heads * gate_act * head_unit, axis=(0, 1, 2))
    d_mixed = norm_back(d_heads * gate_act * head_gain_f, head_unit, head_scale)
    local_grad = jnp.einsum("bthk,bthv->bhkv", carry_query, d_mixed, precision=HIGH)
    suffix = entering((block_decay, local_grad), "seq", combine_states, identity)

    def recurrence(query_in, key_in, value_in, decay_in):
        return mixer_scan(query_in, key_in, value_in, decay_in, seg_starts, state_in)

    unused, pullback = jax.vjp(recurrence, query_heads, key_heads, value_heads, decay_heads)
    d_query_heads, d_key_heads, d_value_heads, d_decay_heads = pullback((d_mixed, suffix[1]))
    d_raw = d_decay_heads.reshape(rows, heads * DK) / 16.0 * jax.nn.sigmoid(-raw)
    grad_up = jnp.dot(lowrank.T, d_raw, precision=HIGH)
    grad_bias = jnp.sum(d_raw, axis=0)
    d_lowrank = jnp.dot(d_raw, up_back.astype(jnp.float32).T, precision=HIGH).astype(jnp.bfloat16)
    d_queries = d_query_heads.reshape(rows, heads * DK).astype(jnp.bfloat16)
    d_keys = d_key_heads.reshape(rows, heads * DK).astype(jnp.bfloat16)
    d_values = d_value_heads.reshape(rows, heads * DV).astype(jnp.bfloat16)
    grad_query = matmul_tn(normed, d_queries)
    grad_key = matmul_tn(normed, d_keys)
    grad_value = matmul_tn(normed, d_values)
    grad_gate = matmul_tn(normed, d_gates)
    grad_down_part = matmul_tn(normed, d_lowrank)
    d_normed_part = (
        matmul_nt(d_queries, query_back)
        + matmul_nt(d_keys, key_back)
        + matmul_nt(d_values, value_back)
        + matmul_nt(d_gates, gate_back)
        + matmul_nt(d_lowrank, down_back)
    )
    d_normed, grad_down, grad_head_gain = (
        lax.psum(d_normed_part.astype(jnp.bfloat16), "head").astype(jnp.float32),
        lax.psum(grad_down_part.astype(jnp.bfloat16), "head").astype(jnp.float32),
        lax.psum(grad_head_part.astype(jnp.bfloat16), "head").astype(jnp.float32),
    )
    grad_gain_one = jnp.sum(d_normed * unit_one, axis=0)
    input_grad = (d_resid + norm_back(d_normed * gain_one, unit_one, scale_one)).astype(
        jnp.bfloat16
    )
    input_grad = input_grad.reshape(batch, block, width)
    summed = (
        lax.psum_scatter(
            grad_gain_one.astype(jnp.bfloat16), "seq", scatter_dimension=0, tiled=True
        ).astype(jnp.float32),
        lax.psum_scatter(
            grad_query.astype(jnp.bfloat16), "seq", scatter_dimension=0, tiled=True
        ).astype(jnp.float32),
        lax.psum_scatter(
            grad_key.astype(jnp.bfloat16), "seq", scatter_dimension=0, tiled=True
        ).astype(jnp.float32),
        lax.psum_scatter(
            grad_value.astype(jnp.bfloat16), "seq", scatter_dimension=0, tiled=True
        ).astype(jnp.float32),
        lax.psum_scatter(
            grad_gate.astype(jnp.bfloat16), "seq", scatter_dimension=0, tiled=True
        ).astype(jnp.float32),
        lax.psum_scatter(
            grad_down.astype(jnp.bfloat16), "seq", scatter_dimension=0, tiled=True
        ).astype(jnp.float32),
        lax.psum_scatter(
            grad_up.astype(jnp.bfloat16), "seq", scatter_dimension=1, tiled=True
        ).astype(jnp.float32),
        lax.psum_scatter(
            grad_bias.astype(jnp.bfloat16), "seq", scatter_dimension=0, tiled=True
        ).astype(jnp.float32),
        lax.psum_scatter(
            grad_head_gain.astype(jnp.bfloat16), "seq", scatter_dimension=0, tiled=True
        ).astype(jnp.float32),
        lax.psum_scatter(
            grad_out.astype(jnp.bfloat16), "seq", scatter_dimension=1, tiled=True
        ).astype(jnp.float32),
        lax.psum_scatter(
            grad_gain_two.astype(jnp.bfloat16), "seq", scatter_dimension=0, tiled=True
        ).astype(jnp.float32),
        lax.psum_scatter(
            grad_fgate.astype(jnp.bfloat16), "seq", scatter_dimension=0, tiled=True
        ).astype(jnp.float32),
        lax.psum_scatter(
            grad_fup.astype(jnp.bfloat16), "seq", scatter_dimension=0, tiled=True
        ).astype(jnp.float32),
        lax.psum_scatter(
            grad_fdown.astype(jnp.bfloat16), "seq", scatter_dimension=1, tiled=True
        ).astype(jnp.float32),
    )
    return (
        layer_out,
        input_grad,
        summed[0],
        summed[1],
        summed[2],
        summed[3],
        summed[4],
        summed[5],
        summed[6],
        summed[7],
        summed[8],
        summed[9],
        summed[10],
        summed[11],
        summed[12],
        summed[13],
    )


def solution(mesh):
    return jax.shard_map(
        shards,
        mesh=mesh,
        in_specs=(
            P(None, "seq", None),
            P(None, "seq"),
            P("seq"),
            P("seq", "head"),
            P("seq", "head"),
            P("seq", "head"),
            P("seq", "head"),
            P("seq", None),
            P(None, ("head", "seq")),
            P(("head", "seq")),
            P("seq"),
            P("head", "seq"),
            P("seq"),
            P("seq", "head"),
            P("seq", "head"),
            P("head", "seq"),
            P(None, "seq", None),
        ),
        out_specs=(
            P(None, "seq", None),
            P(None, "seq", None),
            P("seq"),
            P("seq", "head"),
            P("seq", "head"),
            P("seq", "head"),
            P("seq", "head"),
            P("seq", None),
            P(None, ("head", "seq")),
            P(("head", "seq")),
            P("seq"),
            P("head", "seq"),
            P("seq"),
            P("seq", "head"),
            P("seq", "head"),
            P("head", "seq"),
        ),
        check_vma=False,
    )
```

profile of v0, /device:TPU:0, one launch (start us, length us, event | category | flops | bytes accessed | tf_op | source)
XLA Modules:
  0.0 2032.2 jit_solution(7846979979835801152)
XLA Ops:
  10.2 22.2 %all-gather.2 = bf16[8,1,256]{2,1,0:T(2,128)(2,1)S(1)} all-gather(bf16[1,1,256]{2,1,0:T(2,128)(2,1)S(1)} %reshape.1011), channel_id=1, replica_groups=mesh['seq'=8,'head'=4] {'seq'}, dimensions={0}, use_global_device_ids=true | all-gather | bytes 4608 | tf_op jit(solution)/shard_map/all_gather | solution.py:143
  38.6 17.2 all-reduce.8
  55.8 30.5 %all-gather.3 = bf16[8,32,16]{1,2,0:T(8,128)(2,1)S(1)} all-gather(bf16[1,32,16]{1,2,0:T(8,128)(2,1)S(1)} %bitcast.663), channel_id=1, replica_groups=mesh['seq'=8,'head'=4] {'seq'}, dimensions={0}, use_global_device_ids=true | all-gather | bytes 9216 | tf_op jit(solution)/shard_map/all_gather | solution.py:149
  86.5 30.9 %all_gather.73 = bf16[2048,16]{0,1:T(8,128)(2,1)S(1)} all-gather(bf16[256,16]{0,1:T(8,128)(2,1)S(1)} %copy-done.45), channel_id=1, replica_groups=mesh['seq'=8,'head'=4] {'seq'}, dimensions={0}, use_global_device_ids=true | all-gather | bytes 73728 | tf_op jit(solution)/shard_map/all_gather | solution.py:148
  117.4 3.2 fusion.127
  127.1 4.7 broadcast_multiply_fusion
  131.8 3.7 convolution_convert_fusion.13
  137.1 8.1 all-gather.18.cloned.1.call-done
  145.2 5.2 convolution_convert_fusion.11
  150.7 65.1 %while.78 = (s32[]{:T(128)}, f32[2,1,256,512]{3,2,0,1:T(8,128)S(1)}, f32[8,2,64,1,512]{4,2,1,3,0:T(8,128)}, f32[8,2,64,1,256]{4,3,2,1,0:T(1,128)}, s32[8,2,64]{2...) while((s32[]{:T(128)}, ...), condition=%wide.region_4.5_spmd.clone, body=%wide.region_1.4_spmd.clone.sunk | while | flops 481694592 | bytes 5905576 | solution.py:119
  225.1 26.4 %all_gather.79 = f32[8,2,1,256]{3,1,2,0:T(2,128)S(1)} all-gather(f32[1,2,1,256]{3,1,2,0:T(2,128)S(1)} %copy.116), channel_id=1, replica_groups=mesh['seq'=8,'head'=4] {'seq'}, dimensions={0}, use_global_device_ids=true | all-gather | bytes 18432 | tf_op jit(solution)/shard_map/all_gather | solution.py:17
  251.6 3.2 copy.112
  254.8 85.8 %all-gather.32.cloned.1.call-done = f32[16,1,256,512]{3,2,1,0:T(8,128)} async-done(((f32[2,1,256,512]{3,2,1,0:T(8,128)}), f32[16,1,256,512]{3,2,1,0:T(8,128)}) %all-gather.32.cloned.1.call-update) | async-done | bytes 8388624 | tf_op jit(solution)/shard_map/all_gather | solution.py:17
  340.6 10.9 while.79
  351.5 5.1 multiply_reduce_fusion.4
  356.6 33.5 %all-gather.22.cloned.1.call-done = bf16[2048,512]{1,0:T(8,128)(2,1)} async-done(((bf16[256,512]{1,0:T(8,128)(2,1)}), bf16[2048,512]{1,0:T(8,128)(2,1)}) %all-gather.22.cloned.1.call-update) | async-done | bytes 2097168 | tf_op jit(solution)/shard_map/all_gather | solution.py:147
  390.1 7.1 multiply_convert_fusion.4
  397.2 44.4 %all-gather.24.cloned.1.call-done = bf16[512,2048]{1,0:T(8,128)(2,1)} async-done(((bf16[512,256]{1,0:T(8,128)(2,1)}), bf16[512,2048]{1,0:T(8,128)(2,1)}) %all-gather.24.cloned.1.call-update) | async-done | bytes 2097168 | tf_op jit(solution)/shard_map/all_gather | solution.py:152
  441.6 6.3 convolution_convert_fusion.4
  450.0 17.7 all-gather.4
  467.7 64.0 %all-reduce.15.cloned.1.call-done = bf16[1024,2048]{1,0:T(8,128)(2,1)} async-done(((bf16[1024,2048]{1,0:T(8,128)(2,1)}), bf16[1024,2048]{1,0:T(8,128)(2,1)}) %all-reduce.15.cloned.1.call-update) | async-done | bytes 4194320 | tf_op jit(solution)/shard_map/psum | solution.py:218
  531.7 5.0 multiply_reduce_fusion.1
  537.6 4.4 multiply_convert_fusion
  542.0 84.9 %all-gather.26.cloned.1.call-done = bf16[2048,1408]{1,0:T(8,128)(2,1)} async-done(((bf16[256,1408]{1,0:T(8,128)(2,1)}), bf16[2048,1408]{1,0:T(8,128)(2,1)}) %all-gather.26.cloned.1.call-update) | async-done | bytes 5767184 | tf_op jit(solution)/shard_map/all_gather | solution.py:154
  626.9 11.7 fusion.163
  638.6 81.6 %all-gather.28.cloned.1.call-done = bf16[2048,1408]{1,0:T(8,128)(2,1)} async-done(((bf16[256,1408]{1,0:T(8,128)(2,1)}), bf16[2048,1408]{1,0:T(8,128)(2,1)}) %all-gather.28.cloned.1.call-update) | async-done | bytes 5767184 | tf_op jit(solution)/shard_map/all_gather | solution.py:155
  720.2 11.7 fusion.164
  731.9 82.2 %all-gather.30.cloned.1.call-done = bf16[1408,2048]{1,0:T(8,128)(2,1)} async-done(((bf16[1408,256]{1,0:T(8,128)(2,1)}), bf16[1408,2048]{1,0:T(8,128)(2,1)}) %all-gather.30.cloned.1.call-update) | async-done | bytes 5767184 | tf_op jit(solution)/shard_map/all_gather | solution.py:156
  814.1 15.6 multiply_convert_fusion.1
  829.7 10.9 fusion.165
  840.6 8.5 add_convert_fusion.1
  851.1 81.8 %all-reduce.17.cloned.1.call-done = bf16[1024,2048]{1,0:T(8,128)(2,1)} async-done(((bf16[1024,2048]{1,0:T(8,128)(2,1)}), bf16[1024,2048]{1,0:T(8,128)(2,1)}) %all-reduce.17.cloned.1.call-update) | async-done | bytes 4194320 | tf_op jit(solution)/shard_map/psum | solution.py:266
  932.9 8.2 fusion.123
  941.2 6.8 fusion.122
  961.0 20.9 %all_gather.89 = bf16[8,2,1,256]{3,1,2,0:T(2,128)(2,1)S(1)} all-gather(bf16[1,2,1,256]{3,1,2,0:T(2,128)(2,1)S(1)} %copy.119), channel_id=1, replica_groups=mesh['seq'=8,'head'=4] {'seq'}, dimensions={0}, use_global_device_ids=true | all-gather | bytes 9216 | tf_op jit(solution)/shard_map/all_gather | solution.py:34
  981.9 7.5 convolution_convert_fusion.5
  989.4 42.6 %while.76 = (s32[]{:T(128)}, f32[2,1,256,512]{3,2,0,1:T(8,128)S(1)}, f32[8,2,1,256,512]{4,3,1,2,0:T(8,128)}, f32[8,2,64,1,256]{4,3,2,1,0:T(1,128)}, s32[8,2,64]{...) while((s32[]{:T(128)}, ...), condition=%wide.region_23.24_spmd, body=%wide.region_20.23_spmd.sunk | while | flops 204022528 | bytes 5003023 | solution.py:119
  1032.1 3.2 copy.237
  1037.1 3.8 convolution_convert_fusion.6
  1041.1 9.8 while.75
  1055.8 136.4 %while.77 = (s32[]{:T(128)}, f32[2,1,256,512]{2,3,0,1:T(8,128)S(1)}, bf16[8,2,64,1,256]{4,2,0,1,3:T(8,128)(2,1)}, bf16[8,2,64,1,256]{4,2,0,1,3:T(8,128)(2,1)}, b...) while((s32[]{:T(128)}, ...), condition=%wide.region_30.31_spmd, body=%wide.region_24.30_spmd.sunk | while | flops 988149120 | bytes 20699900 | solution.py:119
  1196.6 11.0 convolution_convert_fusion.2
  1207.6 11.0 convolution_convert_fusion.1
  1218.7 10.5 convolution_convert_fusion
  1230.0 3.3 fusion.130
  1237.9 11.0 convolution_convert_fusion.3
  1248.9 5.6 fusion.169
  1259.8 4.6 fusion.167
  1265.0 5.6 fusion.168
  1270.6 11.8 add_convert_fusion
  1282.6 3.6 convolution_convert_fusion.10
  1286.5 6.0 convolution_convert_fusion.7
  1299.5 67.4 %reduce-scatter.23.cloned.1.call-done = bf16[256,1408]{1,0:T(8,128)(2,1)} async-done(((bf16[2048,1408]{1,0:T(8,128)(2,1)}), bf16[256,1408]{1,0:T(8,128)(2,1)}) %reduce-scatter.23.cloned.1.call-update) | async-done | bytes 720912 | tf_op jit(solution)/shard_map/reduce_scatter | solution.py:347
  1369.2 110.9 %reduce-scatter.25.cloned.1.call-done = bf16[256,1408]{1,0:T(8,128)(2,1)} async-done(((bf16[2048,1408]{1,0:T(8,128)(2,1)}), bf16[256,1408]{1,0:T(8,128)(2,1)}) %reduce-scatter.25.cloned.1.call-update) | async-done | bytes 720912 | tf_op jit(solution)/shard_map/reduce_scatter | solution.py:350
  1482.4 111.4 %reduce-scatter.27.cloned.1.call-done = bf16[1408,256]{1,0:T(8,128)(2,1)} async-done(((bf16[1408,2048]{1,0:T(8,128)(2,1)}), bf16[1408,256]{1,0:T(8,128)(2,1)}) %reduce-scatter.27.cloned.1.call-update) | async-done | bytes 720912 | tf_op jit(solution)/shard_map/reduce_scatter | solution.py:353
  1596.2 64.3 %reduce-scatter.13.cloned.1.call-done = bf16[256,256]{1,0:T(8,128)(2,1)} async-done(((bf16[2048,256]{1,0:T(8,128)(2,1)}), bf16[256,256]{1,0:T(8,128)(2,1)}) %reduce-scatter.13.cloned.1.call-update) | async-done | bytes 131088 | tf_op jit(solution)/shard_map/reduce_scatter | solution.py:317
  1662.1 64.5 %reduce-scatter.15.cloned.1.call-done = bf16[256,256]{1,0:T(8,128)(2,1)} async-done(((bf16[2048,256]{1,0:T(8,128)(2,1)}), bf16[256,256]{1,0:T(8,128)(2,1)}) %reduce-scatter.15.cloned.1.call-update) | async-done | bytes 131088 | tf_op jit(solution)/shard_map/reduce_scatter | solution.py:320
  1728.2 153.8 %all-reduce.19.cloned.1.call-done = (bf16[1024,2048]{1,0:T(8,128)(2,1)}, bf16[1024,2048]{1,0:T(8,128)(2,1)}) async-done(((bf16[1024,2048]{1,0:T(8,128)(2,1)}, bf16[1024,2048]{1,0:T(8,128)(2,1)}), (bf16[1024,2048]{1,0:T(8,128)(2,1)}, bf16[1024,2048]{1,0:T(8,128)(2,1)})) %all-reduce.19.cloned.1.call-update) | async-done | bytes 8388624 | tf_op jit(solution)/shard_map/psum | solution.py:229
  1882.1 5.0 fusion.124
  1887.1 21.9 %all-reduce.7 = (bf16[2048]{0:T(1024)(128)(2,1)S(1)}, bf16[256]{0:T(256)(128)(2,1)S(1)}, bf16[512]{0:T(512)(128)(2,1)S(1)}, bf16[2048]{0:T(1024)(128)(2,1)S(1)}) all-reduce(bf16[2048]{0:T(1024)(128)(2,1)S(1)} %get-tuple-element.697, bf16[256]{0:T(256)(128)(2,1)S(1)} %get-tuple-element.787, ...), channel_id=4, replica_groups=mesh['seq'=8,'head'=4] {'seq'}, use_global_device_ids=true, to_apply=%region_34.35.clone | all-reduce | flops 4864 | bytes 19456
  1909.1 30.5 %reduce-scatter.29.cloned.1.call-done = bf16[256,16]{0,1:T(8,128)(2,1)} async-done(((bf16[2048,16]{0,1:T(8,128)(2,1)}), bf16[256,16]{0,1:T(8,128)(2,1)}) %reduce-scatter.29.cloned.1.call-update) | async-done | bytes 8208 | tf_op jit(solution)/shard_map/reduce_scatter | solution.py:329
  1939.6 6.0 all-reduce.9
  1948.6 61.8 %reduce-scatter.17.cloned.1.call-done = bf16[256,512]{1,0:T(8,128)(2,1)} async-done(((bf16[2048,512]{1,0:T(8,128)(2,1)}), bf16[256,512]{1,0:T(8,128)(2,1)}) %reduce-scatter.17.cloned.1.call-update) | async-done | bytes 262160 | tf_op jit(solution)/shard_map/reduce_scatter | solution.py:323
  2012.2 13.3 fusion.119
  (710 shorter events, 348.5 us)
Async XLA Ops:
  7.2 29.0 %copy-start.47 = (u32[32]{0:T(128)S(1)}, u32[32]{0:T(128)}, u32[]{:S(2)}) copy-start(u32[32]{0:T(128)} %constant.222) | copy-start | bytes 388
  7.2 30.9 %copy-start.51 = (bf16[64]{0:T(256)(128)(2,1)S(1)}, bf16[64]{0:T(256)(128)(2,1)}, u32[]{:S(2)}) copy-start(bf16[64]{0:T(256)(128)(2,1)} %param.37) | copy-start | bytes 388
  7.2 31.1 %copy-start.52 = (bf16[32]{0:T(256)(128)(2,1)S(1)}, bf16[32]{0:T(256)(128)(2,1)}, u32[]{:S(2)}) copy-start(bf16[32]{0:T(256)(128)(2,1)} %param.36) | copy-start | bytes 196
  7.2 48.6 %copy-start.46 = (bf16[16,32]{1,0:T(8,128)(2,1)S(1)}, bf16[16,32]{1,0:T(8,128)(2,1)}, u32[]{:S(2)}) copy-start(bf16[16,32]{1,0:T(8,128)(2,1)} %param.35) | copy-start | bytes 3076
  7.2 79.2 %copy-start.45 = (bf16[256,16]{0,1:T(8,128)(2,1)S(1)}, bf16[256,16]{0,1:T(8,128)(2,1)}, u32[]{:S(2)}) copy-start(bf16[256,16]{0,1:T(8,128)(2,1)} %param.34) | copy-start | bytes 24580
  7.2 119.9 %all-gather.20.cloned.1.call-start = ((), (), s32[]{:S(2)}) async-start(), calls=%async_computation.12 | async-start | bytes 1179648 | tf_op jit(solution)/shard_map/all_gather | solution.py:144
  8.0 123.9 %all-gather.16.cloned.1.call-start = ((), (), s32[]{:S(2)}) async-start(), calls=%async_computation.10 | async-start | bytes 1179648 | tf_op jit(solution)/shard_map/all_gather | solution.py:145
  8.7 136.5 %all-gather.18.cloned.1.call-start = ((), (), s32[]{:S(2)}) async-start(), calls=%async_computation.11 | async-start | bytes 2359296 | tf_op jit(solution)/shard_map/all_gather | solution.py:146
  9.5 331.1 %all-gather.32.cloned.1.call-start = ((), (), s32[]{:S(2)}) async-start(), calls=%async_computation.28 | async-start | bytes 9437184 | tf_op jit(solution)/shard_map/all_gather | solution.py:17
  32.4 88.2 %copy-start.36 = (f32[8,1,256]{2,1,0:T(1,128)}, f32[8,1,256]{2,1,0:T(1,128)S(1)}, u32[]{:S(2)}) copy-start(f32[8,1,256]{2,1,0:T(1,128)S(1)} %convert_element_type.421) | copy-start | bytes 24580
  36.1 84.5 %copy-start.38 = (f32[1,4,2,128]{3,1,2,0:T(4,128)}, f32[1,4,2,128]{3,1,2,0:T(4,128)S(1)}, u32[]{:S(2)}) copy-start(f32[1,4,2,128]{3,1,2,0:T(4,128)S(1)} %copy.166) | copy-start | bytes 12292
  86.5 35.4 %copy-start.40 = (bf16[256,16]{0,1:T(8,128)(2,1)}, bf16[256,16]{0,1:T(8,128)(2,1)S(1)}, u32[]{:S(2)}) copy-start(bf16[256,16]{0,1:T(8,128)(2,1)S(1)} %reshape.1014) | copy-start | bytes 24580
  120.6 3.3 copy-start.5
  120.6 6.4 copy-start.44
  215.8 39.0 %copy-start.9 = (f32[8,2,64,1,512]{4,2,1,3,0:T(8,128)}, f32[8,2,64,1,512]{4,2,1,3,0:T(8,128)S(1)}, u32[]{:S(2)}) copy-start(f32[8,2,64,1,512]{4,2,1,3,0:T(8,128)S(1)} %get-tuple-element.1289) | copy-start | bytes 6291460
  216.8 173.3 %all-gather.22.cloned.1.call-start = ((), (), s32[]{:S(2)}) async-start(), calls=%async_computation.13 | async-start | bytes 2359296 | tf_op jit(solution)/shard_map/all_gather | solution.py:147
  217.4 224.2 %all-gather.24.cloned.1.call-start = ((), (), s32[]{:S(2)}) async-start(), calls=%async_computation.14 | async-start | bytes 2359296 | tf_op jit(solution)/shard_map/all_gather | solution.py:152
  218.0 313.7 %all-reduce.15.cloned.1.call-start = ((), (), s32[]{:S(2)}) async-start(), calls=%async_computation.15 | async-start | bytes 8388608 | tf_op jit(solution)/shard_map/psum | solution.py:218
  340.6 10.9 copy-start.13
  340.6 10.9 copy-start.20
  447.9 179.1 %all-gather.26.cloned.1.call-start = ((), (), s32[]{:S(2)}) async-start(), calls=%async_computation.16 | async-start | bytes 6488064 | tf_op jit(solution)/shard_map/all_gather | solution.py:154
  448.6 271.6 %all-gather.28.cloned.1.call-start = ((), (), s32[]{:S(2)}) async-start(), calls=%async_computation.17 | async-start | bytes 6488064 | tf_op jit(solution)/shard_map/all_gather | solution.py:155
  449.3 364.7 %all-gather.30.cloned.1.call-start = ((), (), s32[]{:S(2)}) async-start(), calls=%async_computation.18 | async-start | bytes 6488064 | tf_op jit(solution)/shard_map/all_gather | solution.py:156
  449.9 483.0 %all-reduce.17.cloned.1.call-start = ((), (), s32[]{:S(2)}) async-start(), calls=%async_computation.19 | async-start | bytes 8388608 | tf_op jit(solution)/shard_map/psum | solution.py:266
  531.7 5.0 copy-start
  531.7 5.9 copy-start.3
  829.7 10.9 copy-start.54
  829.7 10.9 copy-start.55
  829.7 10.9 copy-start.48
  849.1 191.9 %all-gather.34.cloned.1.call-start = ((), (), s32[]{:S(2)}) async-start(), calls=%async_computation.29 | async-start | bytes 4718592 | tf_op jit(solution)/shard_map/all_gather | solution.py:34
  932.9 8.2 copy-start.1
  932.9 8.2 copy-start.4
  932.9 8.3 copy-start.11
  941.2 6.8 copy-start.50
  948.0 4.3 copy-start.7
  948.0 4.2 copy-start.8
  948.0 5.2 copy-start.16
  954.5 3.4 copy-start.14
  954.5 3.4 copy-start.21
  960.9 333.6 %reduce-scatter.21.cloned.1.call-start = ((), (), s32[]{:S(2)}) async-start(), calls=%async_computation.24 | async-start | bytes 2359296 | tf_op jit(solution)/shard_map/reduce_scatter | solution.py:341
  989.4 306.9 %reduce-scatter.19.cloned.1.call-start = ((), (), s32[]{:S(2)}) async-start(), calls=%async_computation.23 | async-start | bytes 2359296 | tf_op jit(solution)/shard_map/reduce_scatter | solution.py:326
  1032.0 3.3 copy-start.15
  1032.1 5.0 copy-start.6
  1040.9 257.2 %reduce-scatter.31.cloned.1.call-start = ((), (), s32[]{:S(2)}) async-start(), calls=%async_computation.31 | async-start | bytes 73728
  1196.4 170.5 %reduce-scatter.23.cloned.1.call-start = ((), (), s32[]{:S(2)}) async-start(), calls=%async_computation.25 | async-start | bytes 6488064 | tf_op jit(solution)/shard_map/reduce_scatter | solution.py:347
  1207.6 272.5 %reduce-scatter.25.cloned.1.call-start = ((), (), s32[]{:S(2)}) async-start(), calls=%async_computation.26 | async-start | bytes 6488064 | tf_op jit(solution)/shard_map/reduce_scatter | solution.py:350
  1218.7 375.2 %reduce-scatter.27.cloned.1.call-start = ((), (), s32[]{:S(2)}) async-start(), calls=%async_computation.27 | async-start | bytes 6488064 | tf_op jit(solution)/shard_map/reduce_scatter | solution.py:353
  1229.3 431.2 %reduce-scatter.13.cloned.1.call-start = ((), (), s32[]{:S(2)}) async-start(), calls=%async_computation.20 | async-start | bytes 1179648 | tf_op jit(solution)/shard_map/reduce_scatter | solution.py:317
  1230.0 5.3 copy-start.22
  1237.6 11.3 copy-start.28
  1237.6 489.0 %reduce-scatter.15.cloned.1.call-start = ((), (), s32[]{:S(2)}) async-start(), calls=%async_computation.21 | async-start | bytes 1179648 | tf_op jit(solution)/shard_map/reduce_scatter | solution.py:320
  1237.9 11.0 copy-start.25
  1248.9 5.6 copy-start.18
  1248.9 5.6 copy-start.23
  1256.9 625.2 %all-reduce.19.cloned.1.call-start = ((), (), s32[]{:S(2)}) async-start(), calls=%async_computation.32 | async-start | bytes 16777216 | tf_op jit(solution)/shard_map/psum | solution.py:229
  1259.8 4.6 copy-start.41
  1259.8 5.2 copy-start.30
  1259.8 5.2 copy-start.49
  1265.0 5.6 copy-start.33
  1282.5 4.0 copy-start.31
  1282.5 657.1 %reduce-scatter.29.cloned.1.call-start = ((), (), s32[]{:S(2)}) async-start(), calls=%async_computation.30 | async-start | bytes 73728 | tf_op jit(solution)/shard_map/reduce_scatter | solution.py:329
  1286.2 724.2 %reduce-scatter.17.cloned.1.call-start = ((), (), s32[]{:S(2)}) async-start(), calls=%async_computation.22 | async-start | bytes 2359296 | tf_op jit(solution)/shard_map/reduce_scatter | solution.py:323
  1296.3 585.8 %copy-start.39 = (f32[1,4,2,128]{3,1,2,0:T(4,128)S(1)}, f32[1,4,2,128]{3,1,2,0:T(4,128)}, u32[]{:S(2)}) copy-start(f32[1,4,2,128]{3,1,2,0:T(4,128)} %copy-done.38) | copy-start | bytes 12292
  1882.1 5.0 copy-start.43
  (15 other events, 27.2 us)
Sparse Core Ops, SparseCore 0:
  10.2 43.0 all-gather.19
  55.5 39.2 all-gather.15
  96.9 48.2 all-gather.17
  216.9 123.6 all-gather.31
  342.6 47.4 all-gather.21
  392.0 49.5 all-gather.23
  448.0 83.6 all-reduce.14
  534.1 92.7 all-gather.25
  629.3 90.8 all-gather.27
  722.3 91.7 all-gather.29
  849.2 83.6 all-reduce.16
  961.1 73.5 all-gather.33
  1038.2 66.6 reduce-scatter.20
  1108.3 66.6 reduce-scatter.18
  1196.5 57.6 reduce-scatter.30
  1257.7 109.0 reduce-scatter.22
  1370.4 109.7 reduce-scatter.24
  1483.7 110.1 reduce-scatter.26
  1597.3 63.1 reduce-scatter.12
  1664.1 62.4 reduce-scatter.14
  1729.8 152.2 all-reduce.18
  1885.8 53.7 reduce-scatter.28
  1943.7 66.6 reduce-scatter.16
where the time goes:
time: 2040 us; the launch traced here: 2030 us
  waiting for transfers between devices  1240 us (61%)
  matrix products  327 us (16%)
  blocking collectives  194 us (10%)
  other arithmetic  151 us (7%)
  local copies, waits for them, and re-layouts  102 us (5%)
    psum x1, waiting for transfers between devices, shards(): ffn = lax.psum(ffn_part.astype(jnp.bfloat16), 'head').astype(jnp.float32)  154 us
    reduce_scatter x1, waiting for transfers between devices, shards(): lax.psum_scatter(grad_fdown.astype(jnp.bfloat16), 'seq', scatter_dimensio...  111 us
    reduce_scatter x1, waiting for transfers between devices, shards(): lax.psum_scatter(grad_fup.astype(jnp.bfloat16), 'seq', scatter_dimension=...  111 us
    all_gather x1, waiting for transfers between devices, prefix_2(): pieces = jax.tree.map(lambda part: lax.all_gather(part, axis), value)  85.8 us
    all_gather x1, waiting for transfers between devices, shards(): lax.all_gather(ffn_gate, 'seq', axis=0, tiled=True)  84.9 us
    all_gather x1, waiting for transfers between devices, shards(): lax.all_gather(ffn_down, 'seq', axis=1, tiled=True)  82.2 us
    psum x1, waiting for transfers between devices, shards(): lax.psum(d_normed_two_part.astype(jnp.bfloat16), 'head').astype(jnp.float32)  81.8 us
    all_gather x1, waiting for transfers between devices, shards(): lax.all_gather(ffn_up, 'seq', axis=0, tiled=True)  81.6 us
  transfers between devices with their start and end apart: 23, of which 17 were waited for; matrix products, arithmetic and copies ran while one was open for 21% of the time, Pallas kernels for 0%

commit v1 on v0

v1 whole, which is shorter than its diff:
```python
import jax
import jax.numpy as jnp
from jax import lax
from jax.sharding import PartitionSpec as P

DK = 256
DV = 512
GROUP = 64


EPS = 1e-06
HIGH = lax.Precision.HIGHEST


def prefix_states(value, axis, join, neutral, later):
    count, mine = (lax.axis_size(axis), lax.axis_index(axis))
    pieces = (
        lax.all_gather(value[0], axis),
        lax.all_gather(value[1].astype(jnp.bfloat16), axis),
    )
    total = neutral
    for position in range(count - 1):
        source = count - 1 - position if later else position
        longer = join(total, (pieces[0][source], pieces[1][source].astype(jnp.float32)))
        use = source > mine if later else source < mine
        total = jax.tree.map(lambda new, old: jnp.where(use, new, old), longer, total)
    return total


def root_scale(field):
    return lax.rsqrt(jnp.mean(field * field, axis=-1, keepdims=True) + EPS)


def norm_back(upstream, unit, scale):
    return scale * (upstream - unit * jnp.mean(upstream * unit, axis=-1, keepdims=True))


def matmul(left, right):
    return jnp.dot(left, right, preferred_element_type=jnp.float32)


def matmul_nt(left, right):
    return lax.dot_general(
        left, right, (((1,), (1,)), ((), ())), preferred_element_type=jnp.float32
    )


def matmul_tn(left, right):
    return lax.dot_general(
        left, right, (((0,), (0,)), ((), ())), preferred_element_type=jnp.float32
    )


def running(field, axis=1):
    length = field.shape[axis]
    places = jnp.arange(length)
    lower = (places[:, None] >= places[None, :]).astype(jnp.float32)
    return jnp.einsum("ts,bs...->bt...", lower, field.astype(jnp.float32), precision=HIGH)


def ring_order(count):
    return list(range(0, count, 2)) + list(range(count - 1 - count % 2, 0, -2))


class Ring:
    def __init__(self, axis):
        self.axis = axis
        self.count = count = lax.axis_size(axis)
        order = ring_order(count)
        place = [order.index(i) for i in range(count)]
        self.right = [(order[i], order[(i + 1) % count]) for i in range(count)]
        self.left = [(order[i], order[(i - 1) % count]) for i in range(count)]
        owners = [[order[(place[i] + r) % count] for r in range(count)] for i in range(count)]
        slots = [[(place[i] - place[me]) % count for i in range(count)] for me in range(count)]
        mine = lax.axis_index(axis)
        self.owners = jnp.asarray(owners, jnp.int32)[mine]
        self.slots = jnp.asarray(slots, jnp.int32)[mine]

    def arrange(self, field, dim, table):
        width = field.shape[dim] // self.count
        return jnp.concatenate(
            [
                lax.dynamic_slice_in_dim(field, table[r] * width, width, dim)
                for r in range(self.count)
            ],
            axis=dim,
        )

    def near(self, field, dim):
        return self.arrange(field, dim, self.owners)

    def home(self, field, dim):
        return self.arrange(field, dim, self.slots)

    def gather(self, block, after=None):
        count, half = self.count, block.shape[0] // 2
        up, down = block[:half], block[half:]
        if after is not None:
            up, down, _ = lax.optimization_barrier((up, down, after))
        pieces = [None] * (2 * count)
        pieces[0], pieces[1] = up, down
        for step in range(1, count):
            up = lax.ppermute(up, self.axis, self.right)
            down = lax.ppermute(down, self.axis, self.left)
            pieces[2 * (count - step)] = up
            pieces[2 * step + 1] = down
            if step == count - 2:
                late = up[:8, :128]
        return jnp.concatenate(pieces, axis=0), late

    def scatter(self, total):
        count = self.count
        rows = total.shape[0] // count
        half = rows // 2

        def piece(slot, part):
            start = slot * rows + part * half
            return total[start : start + half]

        up, down = piece(count - 1, 0), piece(1, 1)
        for step in range(count - 1):
            up = lax.ppermute(up, self.axis, self.right)
            down = lax.ppermute(down, self.axis, self.left)
            up = up.astype(jnp.float32) + piece(count - 2 - step, 0).astype(jnp.float32)
            down = down.astype(jnp.float32) + piece((step + 2) % count, 1).astype(jnp.float32)
            if step < count - 2:
                up, down = up.astype(jnp.bfloat16), down.astype(jnp.bfloat16)
        return jnp.concatenate([up, down], axis=0)


def combine_states(earlier, later):
    return (earlier[0] * later[0], later[0][..., None] * earlier[1] + later[1])


def mixer_scan(queries, keys, values, decays, starts, state):
    batch, length, heads, key_size = queries.shape
    value_size = values.shape[-1]
    number = length // GROUP

    def blocks(field):
        return jnp.moveaxis(field.reshape((batch, number, GROUP) + field.shape[2:]), 1, 0)

    def advance(carry, piece):
        query_block, key_block, value_block, decay_block, start_block = piece
        cumulative = running(decay_block)
        segment = running(start_block)
        untouched = (segment == 0).astype(jnp.float32)
        query_scaled = query_block * key_size ** (-0.5) * jnp.exp(cumulative)
        key_scaled = key_block * jnp.exp(-cumulative)
        scores = jnp.einsum("bthk,bshk->bhts", query_scaled, key_scaled, precision=HIGH)
        places = jnp.arange(GROUP)
        allowed = (segment[:, :, None] == segment[:, None, :]) & (
            places[:, None] >= places[None, :]
        )[None]
        scores = jnp.where(allowed[:, None], scores, 0.0)
        within = jnp.einsum("bhts,bshv->bthv", scores, value_block, precision=HIGH)
        carried = jnp.einsum(
            "bthk,bhkv->bthv", query_scaled * untouched[:, :, None, None], carry, precision=HIGH
        )
        final_decay = cumulative[:, -1]
        trailing = (segment == segment[:, -1:]).astype(jnp.float32)
        key_trailing = (
            key_block * jnp.exp(final_decay[:, None] - cumulative) * trailing[:, :, None, None]
        )
        kept_state = carry * (jnp.exp(final_decay) * untouched[:, -1, None, None])[..., None]
        carry = kept_state + jnp.einsum(
            "bshk,bshv->bhkv", key_trailing, value_block, precision=HIGH
        )
        return (carry, within + carried)

    pieces = (blocks(queries), blocks(keys), blocks(values), blocks(decays), blocks(starts))
    final_state, outputs = lax.scan(jax.checkpoint(advance), state, pieces)
    return (jnp.moveaxis(outputs, 0, 1).reshape(batch, length, heads, value_size), final_state)


def shards(
    layer_in,
    seg_starts,
    attn_gain,
    query_weight,
    key_weight,
    value_weight,
    gate_weight,
    decay_down,
    decay_up,
    decay_bias,
    head_gain,
    out_weight,
    ffn_gain,
    ffn_gate,
    ffn_up,
    ffn_down,
    out_grad,
):
    ring = Ring("seq")
    batch, block, width = layer_in.shape
    key_cols, value_cols = key_weight.shape[1], value_weight.shape[1]
    rank = decay_down.shape[1]
    first, mark = ring.gather(jnp.concatenate([key_weight, value_weight, decay_down], axis=1))
    second, mark = ring.gather(jnp.concatenate([query_weight, gate_weight], axis=1), mark)
    out_t, mark = ring.gather(out_weight.T, mark)
    fgate_all, mark_gate = ring.gather(ffn_gate, mark)
    fup_all, mark_up = ring.gather(ffn_up, mark)
    fdown_t, mark = ring.gather(ffn_down.T, mark_up)
    small = jnp.concatenate([attn_gain, ffn_gain, head_gain, decay_bias, decay_up.reshape(-1)])
    small = lax.all_gather(small, "seq")
    cuts = [attn_gain.size, ffn_gain.size, head_gain.size, decay_bias.size]
    cuts = [sum(cuts[: i + 1]) for i in range(4)]
    gain_one_all = ring.near(small[:, : cuts[0]].reshape(-1), 0)
    gain_two_all = ring.near(small[:, cuts[0] : cuts[1]].reshape(-1), 0)
    head_gain_all = small[:, cuts[1] : cuts[2]].reshape(-1)
    bias_all = small[:, cuts[2] : cuts[3]].reshape(-1)
    up_all = jnp.moveaxis(small[:, cuts[3] :].reshape(ring.count, rank, -1), 0, 1)
    up_all = up_all.reshape(rank, -1)
    rows = batch * block
    inputs = ring.near(layer_in.reshape(rows, width), 1).astype(jnp.float32)
    scale_one = root_scale(inputs)
    unit_one = inputs * scale_one
    gain_one = gain_one_all.astype(jnp.float32)
    normed = (unit_one * gain_one).astype(jnp.bfloat16)
    firsts = matmul(normed, first)
    keys = firsts[:, :key_cols].astype(jnp.bfloat16)
    values = firsts[:, key_cols : key_cols + value_cols].astype(jnp.bfloat16)
    lowrank = firsts[:, key_cols + value_cols :]
    raw = jnp.dot(lowrank, up_all.astype(jnp.float32), precision=HIGH) + bias_all.astype(
        jnp.float32
    )
    decays = jax.nn.log_sigmoid(raw) / 16.0
    seconds = matmul(normed, second)
    queries = seconds[:, :key_cols].astype(jnp.bfloat16)
    gates = seconds[:, key_cols:]
    heads = values.shape[1] // DV
    query_heads = queries.astype(jnp.float32).reshape(batch, block, heads, DK)
    key_heads = keys.astype(jnp.float32).reshape(batch, block, heads, DK)
    value_heads = values.astype(jnp.float32).reshape(batch, block, heads, DV)
    decay_heads = decays.reshape(batch, block, heads, DK)
    zero_state = jnp.zeros((batch, heads, DK, DV), jnp.float32)
    local_out, local_state = mixer_scan(
        query_heads, key_heads, value_heads, decay_heads, seg_starts, zero_state
    )
    block_segment = running(seg_starts)
    untouched = (block_segment == 0).astype(jnp.float32)
    cumulative = running(decay_heads)
    carry_query = query_heads * DK ** (-0.5) * jnp.exp(cumulative) * untouched[:, :, None, None]
    block_decay = jnp.exp(cumulative[:, -1]) * untouched[:, -1, None, None]
    identity = (jnp.ones_like(block_decay), jnp.zeros_like(local_state))
    prefix = prefix_states((block_decay, local_state), "seq", combine_states, identity, False)
    state_in = prefix[1]
    mixed = local_out + jnp.einsum("bthk,bhkv->bthv", carry_query, state_in, precision=HIGH)
    head_scale = root_scale(mixed)
    head_unit = mixed * head_scale
    head_gain_f = head_gain_all.astype(jnp.float32)
    sigma_gate = jax.nn.sigmoid(gates)
    gate_act = (gates * sigma_gate).reshape(batch, block, heads, DV)
    normed_heads = (
        (head_unit * head_gain_f * gate_act).reshape(rows, heads * DV).astype(jnp.bfloat16)
    )
    attn_part = matmul_nt(normed_heads, out_t)
    gain_two = gain_two_all.astype(jnp.float32)
    attn = lax.psum(attn_part.astype(jnp.bfloat16), "head").astype(jnp.float32)
    resid = inputs + attn
    scale_two = root_scale(resid)
    unit_two = resid * scale_two
    normed_two = (unit_two * gain_two).astype(jnp.bfloat16)
    pre_gate = matmul(normed_two, fgate_all)
    pre_up = matmul(normed_two, fup_all)
    sigma_pre = jax.nn.sigmoid(pre_gate)
    silu_pre = pre_gate * sigma_pre
    act = (silu_pre * pre_up).astype(jnp.bfloat16)
    ffn_part = matmul_nt(act, fdown_t)
    ffn = lax.psum(ffn_part.astype(jnp.bfloat16), "head").astype(jnp.float32)
    layer_out = ring.home((resid + ffn).astype(jnp.bfloat16), 1).reshape(batch, block, width)
    grad_rows = ring.near(out_grad.reshape(rows, width), 1)
    grad_float = grad_rows.astype(jnp.float32)
    d_act = matmul(grad_rows, fdown_t)
    grad_fdown_t = matmul_tn(grad_rows, act).astype(jnp.bfloat16)
    d_pre_gate = (d_act * pre_up * sigma_pre * (1.0 + pre_gate * (1.0 - sigma_pre))).astype(
        jnp.bfloat16
    )
    d_pre_up = (d_act * silu_pre).astype(jnp.bfloat16)
    grad_fgate = matmul_tn(normed_two, d_pre_gate).astype(jnp.bfloat16)
    grad_fup = matmul_tn(normed_two, d_pre_up).astype(jnp.bfloat16)
    d_normed_two_part = matmul_nt(d_pre_gate, fgate_all) + matmul_nt(d_pre_up, fup_all)
    d_normed_two = lax.psum(d_normed_two_part.astype(jnp.bfloat16), "head").astype(jnp.float32)
    grad_gain_two = jnp.sum(d_normed_two * unit_two, axis=0)
    d_resid = grad_float + norm_back(d_normed_two * gain_two, unit_two, scale_two)
    d_attn = d_resid.astype(jnp.bfloat16)
    grad_out_t = matmul_tn(d_attn, normed_heads).astype(jnp.bfloat16)
    d_heads = matmul(d_attn, out_t).reshape(batch, block, heads, DV)
    d_gate_act = (d_heads * head_unit * head_gain_f).reshape(rows, heads * DV)
    d_gates = (d_gate_act * sigma_gate * (1.0 + gates * (1.0 - sigma_gate))).astype(jnp.bfloat16)
    grad_head_part = jnp.sum(d_heads * gate_act * head_unit, axis=(0, 1, 2))
    d_mixed = norm_back(d_heads * gate_act * head_gain_f, head_unit, head_scale)
    local_grad = jnp.einsum("bthk,bthv->bhkv", carry_query, d_mixed, precision=HIGH)
    suffix = prefix_states((block_decay, local_grad), "seq", combine_states, identity, True)

    def recurrence(query_in, key_in, value_in, decay_in):
        return mixer_scan(query_in, key_in, value_in, decay_in, seg_starts, state_in)

    unused, pullback = jax.vjp(recurrence, query_heads, key_heads, value_heads, decay_heads)
    d_query_heads, d_key_heads, d_value_heads, d_decay_heads = pullback((d_mixed, suffix[1]))
    d_raw = d_decay_heads.reshape(rows, heads * DK) / 16.0 * jax.nn.sigmoid(-raw)
    grad_up = jnp.dot(lowrank.T, d_raw, precision=HIGH)
    grad_bias = jnp.sum(d_raw, axis=0)
    d_lowrank = jnp.dot(d_raw, up_all.astype(jnp.float32).T, precision=HIGH).astype(jnp.bfloat16)
    d_queries = d_query_heads.reshape(rows, heads * DK).astype(jnp.bfloat16)
    d_keys = d_key_heads.reshape(rows, heads * DK).astype(jnp.bfloat16)
    d_values = d_value_heads.reshape(rows, heads * DV).astype(jnp.bfloat16)
    d_first = jnp.concatenate([d_keys, d_values, d_lowrank], axis=1)
    d_second = jnp.concatenate([d_queries, d_gates], axis=1)
    grad_first = matmul_tn(normed, d_first).astype(jnp.bfloat16)
    grad_second = matmul_tn(normed, d_second).astype(jnp.bfloat16)
    d_normed_part = matmul_nt(d_first, first) + matmul_nt(d_second, second)
    d_normed = lax.psum(d_normed_part.astype(jnp.bfloat16), "head").astype(jnp.float32)
    grad_gain_one = jnp.sum(d_normed * unit_one, axis=0)
    input_grad = (d_resid + norm_back(d_normed * gain_one, unit_one, scale_one)).astype(
        jnp.bfloat16
    )
    input_grad = ring.home(input_grad, 1).reshape(batch, block, width)
    grad_fdown = ring.scatter(grad_fdown_t).T
    grad_fgate = ring.scatter(grad_fgate)
    grad_fup = ring.scatter(grad_fup)
    grad_out = ring.scatter(grad_out_t).T
    grad_second = ring.scatter(grad_second)
    grad_first = ring.scatter(grad_first)
    share = lax.axis_index("seq")
    heads_sum = lax.psum((grad_first[:, key_cols + value_cols :], grad_head_part), "head")
    sums = (
        ring.home(grad_gain_one, 0),
        ring.home(grad_gain_two, 0),
        heads_sum[1],
        grad_bias,
        jnp.moveaxis(grad_up.reshape(rank, ring.count, -1), 1, 0).reshape(-1),
    )
    sizes = [part.size for part in sums]
    sums = lax.psum(jnp.concatenate(sums), "seq")
    ends = [sum(sizes[: i + 1]) for i in range(5)]
    mine = [
        lax.dynamic_slice_in_dim(
            sums[end - size : end], share * (size // ring.count), size // ring.count
        )
        for end, size in zip(ends, sizes)
    ]
    return (
        layer_out,
        input_grad,
        mine[0],
        grad_second[:, :key_cols],
        grad_first[:, :key_cols],
        grad_first[:, key_cols : key_cols + value_cols],
        grad_second[:, key_cols:],
        heads_sum[0],
        mine[4].reshape(rank, -1),
        mine[3],
        mine[2],
        grad_out,
        mine[1],
        grad_fgate,
        grad_fup,
        grad_fdown,
    )


def solution(mesh):
    return jax.shard_map(
        shards,
        mesh=mesh,
        in_specs=(
            P(None, "seq", None),
            P(None, "seq"),
            P("seq"),
            P("seq", "head"),
            P("seq", "head"),
            P("seq", "head"),
            P("seq", "head"),
            P("seq", None),
            P(None, ("head", "seq")),
            P(("head", "seq")),
            P("seq"),
            P("head", "seq"),
            P("seq"),
            P("seq", "head"),
            P("seq", "head"),
            P("head", "seq"),
            P(None, "seq", None),
        ),
        out_specs=(
            P(None, "seq", None),
            P(None, "seq", None),
            P("seq"),
            P("seq", "head"),
            P("seq", "head"),
            P("seq", "head"),
            P("seq", "head"),
            P("seq", None),
            P(None, ("head", "seq")),
            P(("head", "seq")),
            P("seq"),
            P("head", "seq"),
            P("seq"),
            P("seq", "head"),
            P("seq", "head"),
            P("head", "seq"),
        ),
        check_vma=False,
    )
```

time: 2040 us -> 1390 us (0.68)
  waiting for transfers between devices: 1240 us -> 301 us
  starting transfers between devices: 1.77 us -> 194 us
  local copies, waits for them, and re-layouts: 102 us -> 270 us
  blocking collectives: 194 us -> 146 us
  other arithmetic: 151 us -> 115 us
    reduce_scatter x9 -> x0, waiting for transfers between devices: 511 us -> none  [the longest x1 111 us: shards(): lax.psum_scatter(grad_fdown.astype(jnp.bfloat16), 'seq', scatter_dimensio...]
    all_gather x10 -> x2, waiting for transfers between devices: 420 us -> 0.01 us  [prefix_states(): lax.all_gather(value[1].astype(jnp.bfloat16), axis)]
    ppermute x0 -> x168, starting transfers between devices: none -> 194 us  [the longest x42 56.8 us: scatter(): down = lax.ppermute(down, self.axis, self.left)]
    ppermute x0 -> x168, waiting for transfers between devices: none -> 185 us  [the longest x42 81.3 us: scatter(): down = lax.ppermute(down, self.axis, self.left)]
    unnamed x127 -> x381, local copies, waits for them, and re-layouts: 15.5 us -> 149 us
    all_gather x6 -> x1, blocking collectives: 149 us -> 59.7 us  [prefix_states(): lax.all_gather(value[0], axis)]
    psum x1, waiting for transfers between devices: 81.8 us -> 0.01 us  [shards(): lax.psum(d_normed_two_part.astype(jnp.bfloat16), 'head').astype(jnp.float32)]
    psum x1, waiting for transfers between devices: 154 us -> 76.5 us  [shards(): ffn = lax.psum(ffn_part.astype(jnp.bfloat16), 'head').astype(jnp.float32)]
  transfers between devices with their start and end apart: 23 -> 173, of which waited for: 17 -> 69; matrix products, arithmetic and copies ran while one was open for 21% -> 31% of each run, Pallas kernels for 0% -> 0%
where the time goes in v1:
time: 1390 us; the launch traced here: 1370 us
  matrix products  318 us (23%)
  waiting for transfers between devices  301 us (22%)
  local copies, waits for them, and re-layouts  270 us (19%)
  starting transfers between devices  194 us (14%)
  blocking collectives  146 us (11%)
  other arithmetic  115 us (8%)
  between operations  27.2 us (2%)
    unnamed x381, local copies, waits for them, and re-layouts  149 us
    ppermute x42, waiting for transfers between devices, scatter(): down = lax.ppermute(down, self.axis, self.left)  81.3 us
    psum x1, waiting for transfers between devices, shards(): ffn = lax.psum(ffn_part.astype(jnp.bfloat16), 'head').astype(jnp.float32)  76.5 us
    all_gather x1, blocking collectives, prefix_states(): lax.all_gather(value[0], axis)  59.7 us
    ppermute x42, starting transfers between devices, scatter(): down = lax.ppermute(down, self.axis, self.left)  56.8 us
    dot_general x32, matrix products, advance(): jnp.einsum('bshk,bshv->bhkv', key_trailing, value_block, precision=HIGH)  52.3 us
    ppermute x42, waiting for transfers between devices, scatter(): up = lax.ppermute(up, self.axis, self.right)  51.7 us
    ppermute x42, starting transfers between devices, scatter(): up = lax.ppermute(up, self.axis, self.right)  48.8 us
  transfers between devices with their start and end apart: 173, of which 69 were waited for; matrix products, arithmetic and copies ran while one was open for 31% of the time, Pallas kernels for 0%

profile of v1, /device:TPU:0, one launch (start us, length us, event | category | flops | bytes accessed | tf_op | source)
XLA Modules:
  0.0 1373.5 jit_solution(608376796155186153)
XLA Ops:
  30.7 36.2 %all-reduce.1 = bf16[8960]{0:T(1024)(128)(2,1)S(1)} all-reduce(bf16[8960]{0:T(1024)(128)(2,1)S(1)} %dynamic-update-slice), channel_id=2, replica_groups=mesh['seq'=8,'head'=4] {'seq'}, use_global_device_ids=true, to_apply=%add.1 | all-reduce | flops 8960 | bytes 35840
  85.3 3.1 fusion.140
  98.8 3.6 collective-permute-done.29
  103.4 4.7 collective-permute-done.30
  109.1 4.0 collective-permute-done.31
  194.1 9.2 collective-permute-done.41
  216.7 4.0 collective-permute-done.11
  220.7 3.3 collective-permute-start.56
  224.9 3.3 collective-permute-start.6
  228.2 3.5 fusion.244
  257.9 5.7 fusion.266
  290.8 65.1 %while.52 = (s32[]{:T(128)}, f32[2,1,256,512]{3,2,0,1:T(8,128)S(1)}, f32[8,2,64,1,512]{4,2,1,3,0:T(8,128)}, f32[8,2,64,1,256]{4,2,1,3,0:T(8,128)}, s32[8,2,64]{2...) while((s32[]{:T(128)}, ...), condition=%wide.region_2.3_spmd.clone, body=%wide.region_1.2_spmd.clone.sunk | while | flops 504894592 | bytes 5905060 | solution.py:172
  362.3 3.2 copy.154
  373.8 59.7 %all_gather.26 = f32[8,2,1,256]{3,1,2,0:T(2,128)S(1)} all-gather(f32[1,2,1,256]{3,1,2,0:T(2,128)S(1)} %bitcast_multiply_fusion.9), channel_id=1, replica_groups=mesh['seq'=8,'head'=4] {'seq'}, dimensions={0}, use_global_device_ids=true | all-gather | bytes 18432 | tf_op jit(solution)/shard_map/all_gather | solution.py:18
  463.4 4.4 collective-permute-done.67
  473.8 11.7 fusion.268
  520.2 6.5 multiply_reduce_fusion.4
  529.1 4.4 convolution_convert_fusion.4
  533.9 4.2 fusion.177
  538.1 42.4 %while.51 = (s32[]{:T(128)}, f32[2,1,256,512]{3,2,0,1:T(8,128)S(1)}, f32[8,2,1,256,512]{4,3,1,2,0:T(8,128)}, f32[8,2,64,1,256]{4,2,1,3,0:T(8,128)}, s32[8,2,64]{...) while((s32[]{:T(128)}, ...), condition=%wide.region_11.12_spmd.clone.clone, body=%wide.region_10.11_spmd.clone.clone.sunk | while | flops 227230720 | bytes 5003011 | solution.py:172
  580.5 39.0 %all-reduce.8.cloned.1.call-done = bf16[1024,2048]{1,0:T(8,128)(2,1)} async-done(((bf16[1024,2048]{1,0:T(8,128)(2,1)}), bf16[1024,2048]{1,0:T(8,128)(2,1)}) %all-reduce.8.cloned.1.call-update) | async-done | bytes 4194320 | tf_op jit(solution)/shard_map/psum | solution.py:260
  619.6 5.0 multiply_reduce_fusion.1
  628.2 8.4 fusion.267
  636.6 13.9 %multiply_convert_fusion.2 = (bf16[1024,1408]{1,0:T(8,128)(2,1)}, bf16[1024,1408]{1,0:T(8,128)(2,1)}, bf16[1024,1408]{1,0:T(8,128)(2,1)S(1)}) fusion(f32[1024,1408]{1,0:T(8,128)S(1)} %bitcast.732, f32[1024,1408]{1,0:T(8,128)} %fusion.267, bf16[1024,2048]{1,0:T(8,128)(2,1)S(1)} %multiply_convert_fusion, ...), kind=kOutput, calls=%fused_computation.212 | convolution fusion | flops 5927206912 | bytes 30146560 | tf_op jit(solution)/shard_map/dot_general | solution.py:39
  650.6 9.5 convolution_convert_fusion.1
  660.1 8.9 fusion.269
  669.1 9.4 convolution_convert_fusion
  678.5 8.2 convolution_convert_fusion.3
  691.7 7.2 convolution_convert_fusion.2
  703.1 10.9 add_convert_fusion.1
  721.7 3.8 collective-permute-done.133
  728.9 4.3 collective-permute-done.162
  736.6 4.3 collective-permute-done.148
  744.4 4.3 collective-permute-done.134
  752.1 4.3 collective-permute-done.163
  759.8 4.3 collective-permute-done.149
  767.5 4.3 collective-permute-done.135
  775.3 4.3 collective-permute-done.164
  783.0 4.3 collective-permute-done.150
  790.7 4.3 collective-permute-done.136
  799.2 3.5 collective-permute-done.165
  806.9 3.6 collective-permute-done.151
  814.1 8.5 fusion.136
  822.6 6.8 fusion.135
  847.6 6.5 convolution_convert_fusion.7
  862.0 3.2 collective-permute-done.112
  865.2 4.8 collective-permute-start.138
  875.8 7.0 collective-permute-done.113
  888.7 19.5 %collective-permute-done.114 = bf16[128,512]{1,0:T(8,128)(2,1)S(1)} collective-permute-done((bf16[128,512]{1,0:T(8,128)(2,1)S(1)}, bf16[128,512]{1,0:T(8,128)(2,1)S(1)}, u32[]{:S(2)}, u32[]{:S(2)}) %collective-permute-start.114) | collective-permute-done | bytes 131104 | tf_op jit(solution)/shard_map/ppermute | solution.py:122
  908.2 13.0 collective-permute-start.153
  926.7 9.7 collective-permute-done.153
  937.6 6.5 collective-permute-done.139
  954.4 3.2 collective-permute-start.117
  970.3 4.4 fusion.183
  978.0 140.6 %while.50 = (s32[]{:T(128)}, f32[2,1,256,512]{2,3,0,1:T(8,128)S(1)}, bf16[8,2,64,1,256]{4,2,1,3,0:T(8,128)(2,1)}, bf16[8,2,64,1,256]{4,2,0,1,3:T(8,128)(2,1)}, b...) while((s32[]{:T(128)}, ...), condition=%wide.region_15.16_spmd, body=%wide.region_12.15_spmd.sunk | while | flops 1034454656 | bytes 20216564 | solution.py:172
  1123.9 4.4 convolution_convert_fusion.6
  1128.3 5.9 fusion.205
  1137.2 6.7 convolution_convert_fusion.5
  1144.0 9.5 add_convert_fusion
  1215.9 12.5 all-reduce.2
  1228.4 76.5 %all-reduce.12.cloned.1.call-done = (bf16[1024,2048]{1,0:T(8,128)(2,1)}, bf16[1024,2048]{1,0:T(8,128)(2,1)}) async-done(((bf16[1024,2048]{1,0:T(8,128)(2,1)}, bf16[1024,2048]{1,0:T(8,128)(2,1)}), (bf16[1024,2048]{1,0:T(8,128)(2,1)}, bf16[1024,2048]{1,0:T(8,128)(2,1)})) %all-reduce.12.cloned.1.call-update) | async-done | bytes 8388624 | tf_op jit(solution)/shard_map/psum | solution.py:271
  1305.0 5.1 fusion.139
  1311.3 37.4 %psum.54 = f32[8960]{0:T(1024)S(1)} all-reduce(f32[8960]{0:T(1024)S(1)} %constant_dynamic-update-slice_fusion.105), channel_id=1, replica_groups=mesh['seq'=8,'head'=4] {'seq'}, use_global_device_ids=true, to_apply=%region_23.24 | all-reduce | flops 8960 | bytes 71680 | tf_op jit(solution)/shard_map/psum | solution.py:336
  1350.8 11.0 fusion.132
  (1275 shorter events, 737.6 us)
Async XLA Ops:
  7.2 513.1 %all-gather.6.cloned.1.call-start = ((), (), s32[]{:S(2)}) async-start(), calls=%async_computation.2 | async-start | bytes 4718592 | tf_op jit(solution)/shard_map/all_gather | solution.py:19
  9.2 127.1 %collective-permute-start.14 = (bf16[128,768]{1,0:T(8,128)(2,1)S(1)}, bf16[128,768]{1,0:T(8,128)(2,1)}, u32[]{:S(2)}, u32[]{:S(2)}) collective-permute-start(bf16[128,768]{1,0:T(8,128)(2,1)S(1)} %get-tuple-element.402), channel_id=1, source_target_pairs={{0,8},{8,16},{16,24},{24,28},{28,20},{20,12},{12,4},{4,0},{1,9},{9... | collective-permute-start | bytes 589832 | tf_op jit(solution)/shard_map/ppermute | solution.py:103
  12.2 131.1 %collective-permute-start.21 = (bf16[128,768]{1,0:T(8,128)(2,1)S(1)}, bf16[128,768]{1,0:T(8,128)(2,1)}, u32[]{:S(2)}, u32[]{:S(2)}) collective-permute-start(bf16[128,768]{1,0:T(8,128)(2,1)S(1)} %get-tuple-element.403), channel_id=1, source_target_pairs={{0,4},{8,0},{16,8},{24,16},{28,24},{20,28},{12,20},{4,12},{1,5},{9... | collective-permute-start | bytes 589832 | tf_op jit(solution)/shard_map/ppermute | solution.py:104
  13.2 84.0 %collective-permute-start.28 = (bf16[128,512]{0,1:T(8,128)(2,1)S(1)}, bf16[128,512]{0,1:T(8,128)(2,1)}, u32[]{:S(2)}, u32[]{:S(2)}) collective-permute-start(bf16[128,512]{0,1:T(8,128)(2,1)S(1)} %get-tuple-element.406), channel_id=1, source_target_pairs={{0,8},{8,16},{16,24},{24,28},{28,20},{20,12},{12,4},{4,0},{1,9},{9... | collective-permute-start | bytes 393224 | tf_op jit(solution)/shard_map/ppermute | solution.py:103
  15.3 118.9 %collective-permute-start.35 = (bf16[128,512]{0,1:T(8,128)(2,1)S(1)}, bf16[128,512]{0,1:T(8,128)(2,1)}, u32[]{:S(2)}, u32[]{:S(2)}) collective-permute-start(bf16[128,512]{0,1:T(8,128)(2,1)S(1)} %get-tuple-element.407), channel_id=1, source_target_pairs={{0,4},{8,0},{16,8},{24,16},{28,24},{20,28},{12,20},{4,12},{1,5},{9... | collective-permute-start | bytes 393224 | tf_op jit(solution)/shard_map/ppermute | solution.py:104
  16.4 138.2 %collective-permute-start.70 = (bf16[128,1408]{0,1:T(8,128)(2,1)S(1)}, bf16[128,1408]{0,1:T(8,128)(2,1)}, u32[]{:S(2)}, u32[]{:S(2)}) collective-permute-start(bf16[128,1408]{0,1:T(8,128)(2,1)S(1)} %get-tuple-element.412), channel_id=1, source_target_pairs={{0,8},{8,16},{16,24},{24,28},{28,20},{20,12},{12,4},{4,0},{1,9},{9... | collective-permute-start | bytes 1081352 | tf_op jit(solution)/shard_map/ppermute | solution.py:103
  134.2 20.7 %collective-permute-start.77 = (bf16[128,1408]{0,1:T(8,128)(2,1)S(1)}, bf16[128,1408]{0,1:T(8,128)(2,1)S(1)}, u32[]{:S(2)}, u32[]{:S(2)}) collective-permute-start(bf16[128,1408]{0,1:T(8,128)(2,1)S(1)} %get-tuple-element.413), channel_id=1, source_target_pairs={{0,4},{8,0},{16,8},{24,16},{28,24},{20,28},{12,20},{4,12},{1,5},{9... | collective-permute-start | bytes 1081352 | tf_op jit(solution)/shard_map/ppermute | solution.py:104
  161.6 21.4 %collective-permute-start.71 = (bf16[128,1408]{0,1:T(8,128)(2,1)}, bf16[128,1408]{0,1:T(8,128)(2,1)}, u32[]{:S(2)}, u32[]{:S(2)}) collective-permute-start(bf16[128,1408]{0,1:T(8,128)(2,1)} %collective-permute-done.70), channel_id=1, source_target_pairs={{0,8},{8,16},{16,24},{24,28},{28,20},{20,12},{12,4},{4,0},{1,9},{9... | collective-permute-start | bytes 1081352 | tf_op jit(solution)/shard_map/ppermute | solution.py:103
  181.5 26.5 %collective-permute-start.78 = (bf16[128,1408]{0,1:T(8,128)(2,1)S(1)}, bf16[128,1408]{0,1:T(8,128)(2,1)}, u32[]{:S(2)}, u32[]{:S(2)}) collective-permute-start(bf16[128,1408]{0,1:T(8,128)(2,1)S(1)} %collective-permute-done.77), channel_id=1, source_target_pairs={{0,4},{8,0},{16,8},{24,16},{28,24},{20,28},{12,20},{4,12},{1,5},{9... | collective-permute-start | bytes 1081352 | tf_op jit(solution)/shard_map/ppermute | solution.py:104
  208.0 57.1 %collective-permute-start.72 = (bf16[128,1408]{0,1:T(8,128)(2,1)}, bf16[128,1408]{0,1:T(8,128)(2,1)}, u32[]{:S(2)}, u32[]{:S(2)}) collective-permute-start(bf16[128,1408]{0,1:T(8,128)(2,1)} %collective-permute-done.71), channel_id=1, source_target_pairs={{0,8},{8,16},{16,24},{24,28},{28,20},{20,12},{12,4},{4,0},{1,9},{9... | collective-permute-start | bytes 1081352 | tf_op jit(solution)/shard_map/ppermute | solution.py:103
  208.7 57.8 %collective-permute-start.79 = (bf16[128,1408]{0,1:T(8,128)(2,1)}, bf16[128,1408]{0,1:T(8,128)(2,1)}, u32[]{:S(2)}, u32[]{:S(2)}) collective-permute-start(bf16[128,1408]{0,1:T(8,128)(2,1)} %collective-permute-done.78), channel_id=1, source_target_pairs={{0,4},{8,0},{16,8},{24,16},{28,24},{20,28},{12,20},{4,12},{1,5},{9... | collective-permute-start | bytes 1081352 | tf_op jit(solution)/shard_map/ppermute | solution.py:104
  220.7 46.5 %collective-permute-start.56 = (bf16[128,1408]{1,0:T(8,128)(2,1)}, bf16[128,1408]{1,0:T(8,128)(2,1)}, u32[]{:S(2)}, u32[]{:S(2)}) collective-permute-start(bf16[128,1408]{1,0:T(8,128)(2,1)} %get-tuple-element.410), channel_id=1, source_target_pairs={{0,8},{8,16},{16,24},{24,28},{28,20},{20,12},{12,4},{4,0},{1,9},{9... | collective-permute-start | bytes 1081352 | tf_op jit(solution)/shard_map/ppermute | solution.py:103
  236.6 32.0 %collective-permute-start.63 = (bf16[128,1408]{1,0:T(8,128)(2,1)}, bf16[128,1408]{1,0:T(8,128)(2,1)}, u32[]{:S(2)}, u32[]{:S(2)}) collective-permute-start(bf16[128,1408]{1,0:T(8,128)(2,1)} %get-tuple-element.411), channel_id=1, source_target_pairs={{0,4},{8,0},{16,8},{24,16},{28,24},{20,28},{12,20},{4,12},{1,5},{9... | collective-permute-start | bytes 1081352 | tf_op jit(solution)/shard_map/ppermute | solution.py:104
  265.1 21.0 %collective-permute-start.49 = (bf16[128,1408]{1,0:T(8,128)(2,1)}, bf16[128,1408]{1,0:T(8,128)(2,1)}, u32[]{:S(2)}, u32[]{:S(2)}) collective-permute-start(bf16[128,1408]{1,0:T(8,128)(2,1)} %get-tuple-element.409), channel_id=1, source_target_pairs={{0,4},{8,0},{16,8},{24,16},{28,24},{20,28},{12,20},{4,12},{1,5},{9... | collective-permute-start | bytes 1081352 | tf_op jit(solution)/shard_map/ppermute | solution.py:104
  267.2 20.9 %collective-permute-start.80 = (bf16[128,1408]{0,1:T(8,128)(2,1)}, bf16[128,1408]{0,1:T(8,128)(2,1)}, u32[]{:S(2)}, u32[]{:S(2)}) collective-permute-start(bf16[128,1408]{0,1:T(8,128)(2,1)} %collective-permute-done.79), channel_id=1, source_target_pairs={{0,4},{8,0},{16,8},{24,16},{28,24},{20,28},{12,20},{4,12},{1,5},{9... | collective-permute-start | bytes 1081352 | tf_op jit(solution)/shard_map/ppermute | solution.py:104
  286.1 69.9 %collective-permute-start.43 = (bf16[128,1408]{1,0:T(8,128)(2,1)}, bf16[128,1408]{1,0:T(8,128)(2,1)}, u32[]{:S(2)}, u32[]{:S(2)}) collective-permute-start(bf16[128,1408]{1,0:T(8,128)(2,1)} %copy-done.41), channel_id=1, source_target_pairs={{0,8},{8,16},{16,24},{24,28},{28,20},{20,12},{12,4},{4,0},{1,9},{9... | collective-permute-start | bytes 1081352 | tf_op jit(solution)/shard_map/ppermute | solution.py:103
  286.7 70.7 %collective-permute-start.50 = (bf16[128,1408]{1,0:T(8,128)(2,1)}, bf16[128,1408]{1,0:T(8,128)(2,1)}, u32[]{:S(2)}, u32[]{:S(2)}) collective-permute-start(bf16[128,1408]{1,0:T(8,128)(2,1)} %collective-permute-done.49), channel_id=1, source_target_pairs={{0,4},{8,0},{16,8},{24,16},{28,24},{20,28},{12,20},{4,12},{1,5},{9... | collective-permute-start | bytes 1081352 | tf_op jit(solution)/shard_map/ppermute | solution.py:104
  288.1 69.9 %collective-permute-start.74 = (bf16[128,1408]{0,1:T(8,128)(2,1)}, bf16[128,1408]{0,1:T(8,128)(2,1)}, u32[]{:S(2)}, u32[]{:S(2)}) collective-permute-start(bf16[128,1408]{0,1:T(8,128)(2,1)} %collective-permute-done.73), channel_id=1, source_target_pairs={{0,8},{8,16},{16,24},{24,28},{28,20},{20,12},{12,4},{4,0},{1,9},{9... | collective-permute-start | bytes 1081352 | tf_op jit(solution)/shard_map/ppermute | solution.py:103
  288.8 70.7 %collective-permute-start.81 = (bf16[128,1408]{0,1:T(8,128)(2,1)}, bf16[128,1408]{0,1:T(8,128)(2,1)}, u32[]{:S(2)}, u32[]{:S(2)}) collective-permute-start(bf16[128,1408]{0,1:T(8,128)(2,1)} %collective-permute-done.80), channel_id=1, source_target_pairs={{0,4},{8,0},{16,8},{24,16},{28,24},{20,28},{12,20},{4,12},{1,5},{9... | collective-permute-start | bytes 1081352 | tf_op jit(solution)/shard_map/ppermute | solution.py:104
  290.1 69.9 %collective-permute-start.58 = (bf16[128,1408]{1,0:T(8,128)(2,1)}, bf16[128,1408]{1,0:T(8,128)(2,1)}, u32[]{:S(2)}, u32[]{:S(2)}) collective-permute-start(bf16[128,1408]{1,0:T(8,128)(2,1)} %collective-permute-done.57), channel_id=1, source_target_pairs={{0,8},{8,16},{16,24},{24,28},{28,20},{20,12},{12,4},{4,0},{1,9},{9... | collective-permute-start | bytes 1081352 | tf_op jit(solution)/shard_map/ppermute | solution.py:103
  365.5 254.1 %all-reduce.8.cloned.1.call-start = ((), (), s32[]{:S(2)}) async-start(), calls=%async_computation | async-start | bytes 8388608 | tf_op jit(solution)/shard_map/psum | solution.py:260
  369.0 65.1 %collective-permute-start.59 = (bf16[128,1408]{1,0:T(8,128)(2,1)}, bf16[128,1408]{1,0:T(8,128)(2,1)S(1)}, u32[]{:S(2)}, u32[]{:S(2)}) collective-permute-start(bf16[128,1408]{1,0:T(8,128)(2,1)} %collective-permute-done.58), channel_id=1, source_target_pairs={{0,8},{8,16},{16,24},{24,28},{28,20},{20,12},{12,4},{4,0},{1,9},{9... | collective-permute-start | bytes 1081352 | tf_op jit(solution)/shard_map/ppermute | solution.py:103
  369.7 64.5 %collective-permute-start.66 = (bf16[128,1408]{1,0:T(8,128)(2,1)}, bf16[128,1408]{1,0:T(8,128)(2,1)S(1)}, u32[]{:S(2)}, u32[]{:S(2)}) collective-permute-start(bf16[128,1408]{1,0:T(8,128)(2,1)} %collective-permute-done.65), channel_id=1, source_target_pairs={{0,4},{8,0},{16,8},{24,16},{28,24},{20,28},{12,20},{4,12},{1,5},{9... | collective-permute-start | bytes 1081352 | tf_op jit(solution)/shard_map/ppermute | solution.py:104
  371.0 65.1 %collective-permute-start.45 = (bf16[128,1408]{1,0:T(8,128)(2,1)}, bf16[128,1408]{1,0:T(8,128)(2,1)S(1)}, u32[]{:S(2)}, u32[]{:S(2)}) collective-permute-start(bf16[128,1408]{1,0:T(8,128)(2,1)} %collective-permute-done.44), channel_id=1, source_target_pairs={{0,8},{8,16},{16,24},{24,28},{28,20},{20,12},{12,4},{4,0},{1,9},{9... | collective-permute-start | bytes 1081352 | tf_op jit(solution)/shard_map/ppermute | solution.py:103
  371.7 64.5 %collective-permute-start.52 = (bf16[128,1408]{1,0:T(8,128)(2,1)}, bf16[128,1408]{1,0:T(8,128)(2,1)S(1)}, u32[]{:S(2)}, u32[]{:S(2)}) collective-permute-start(bf16[128,1408]{1,0:T(8,128)(2,1)} %collective-permute-done.51), channel_id=1, source_target_pairs={{0,4},{8,0},{16,8},{24,16},{28,24},{20,28},{12,20},{4,12},{1,5},{9... | collective-permute-start | bytes 1081352 | tf_op jit(solution)/shard_map/ppermute | solution.py:104
  373.1 65.1 %collective-permute-start.76 = (bf16[128,1408]{0,1:T(8,128)(2,1)}, bf16[128,1408]{0,1:T(8,128)(2,1)S(1)}, u32[]{:S(2)}, u32[]{:S(2)}) collective-permute-start(bf16[128,1408]{0,1:T(8,128)(2,1)} %collective-permute-done.75), channel_id=1, source_target_pairs={{0,8},{8,16},{16,24},{24,28},{28,20},{20,12},{12,4},{4,0},{1,9},{9... | collective-permute-start | bytes 1081352 | tf_op jit(solution)/shard_map/ppermute | solution.py:103
  434.1 28.4 %collective-permute-start.83 = (bf16[128,1408]{0,1:T(8,128)(2,1)}, bf16[128,1408]{0,1:T(8,128)(2,1)S(1)}, u32[]{:S(2)}, u32[]{:S(2)}) collective-permute-start(bf16[128,1408]{0,1:T(8,128)(2,1)} %collective-permute-done.82), channel_id=1, source_target_pairs={{0,4},{8,0},{16,8},{24,16},{28,24},{20,28},{12,20},{4,12},{1,5},{9... | collective-permute-start | bytes 1081352 | tf_op jit(solution)/shard_map/ppermute | solution.py:104
  434.1 24.6 %collective-permute-start.60 = (bf16[128,1408]{1,0:T(8,128)(2,1)S(1)}, bf16[128,1408]{1,0:T(8,128)(2,1)S(1)}, u32[]{:S(2)}, u32[]{:S(2)}) collective-permute-start(bf16[128,1408]{1,0:T(8,128)(2,1)S(1)} %collective-permute-done.59), channel_id=1, source_target_pairs={{0,8},{8,16},{16,24},{24,28},{28,20},{20,12},{12,4},{4,0},{1,9},{9... | collective-permute-start | bytes 1081352 | tf_op jit(solution)/shard_map/ppermute | solution.py:103
  436.2 31.6 %collective-permute-start.67 = (bf16[128,1408]{1,0:T(8,128)(2,1)S(1)}, bf16[128,1408]{1,0:T(8,128)(2,1)S(1)}, u32[]{:S(2)}, u32[]{:S(2)}) collective-permute-start(bf16[128,1408]{1,0:T(8,128)(2,1)S(1)} %collective-permute-done.66), channel_id=1, source_target_pairs={{0,4},{8,0},{16,8},{24,16},{28,24},{20,28},{12,20},{4,12},{1,5},{9... | collective-permute-start | bytes 1081352 | tf_op jit(solution)/shard_map/ppermute | solution.py:104
  436.2 31.5 %collective-permute-start.46 = (bf16[128,1408]{1,0:T(8,128)(2,1)S(1)}, bf16[128,1408]{1,0:T(8,128)(2,1)S(1)}, u32[]{:S(2)}, u32[]{:S(2)}) collective-permute-start(bf16[128,1408]{1,0:T(8,128)(2,1)S(1)} %collective-permute-done.45), channel_id=1, source_target_pairs={{0,8},{8,16},{16,24},{24,28},{28,20},{20,12},{12,4},{4,0},{1,9},{9... | collective-permute-start | bytes 1081352 | tf_op jit(solution)/shard_map/ppermute | solution.py:103
  438.2 33.4 %collective-permute-start.53 = (bf16[128,1408]{1,0:T(8,128)(2,1)S(1)}, bf16[128,1408]{1,0:T(8,128)(2,1)S(1)}, u32[]{:S(2)}, u32[]{:S(2)}) collective-permute-start(bf16[128,1408]{1,0:T(8,128)(2,1)S(1)} %collective-permute-done.52), channel_id=1, source_target_pairs={{0,4},{8,0},{16,8},{24,16},{28,24},{20,28},{12,20},{4,12},{1,5},{9... | collective-permute-start | bytes 1081352 | tf_op jit(solution)/shard_map/ppermute | solution.py:104
  485.5 33.2 %collective-permute-start.69 = (bf16[128,1408]{1,0:T(8,128)(2,1)S(1)}, bf16[128,1408]{1,0:T(8,128)(2,1)S(1)}, u32[]{:S(2)}, u32[]{:S(2)}) collective-permute-start(bf16[128,1408]{1,0:T(8,128)(2,1)S(1)} %collective-permute-done.68), channel_id=1, source_target_pairs={{0,4},{8,0},{16,8},{24,16},{28,24},{20,28},{12,20},{4,12},{1,5},{9... | collective-permute-start | bytes 1081352 | tf_op jit(solution)/shard_map/ppermute | solution.py:104
  487.6 31.9 %collective-permute-start.55 = (bf16[128,1408]{1,0:T(8,128)(2,1)S(1)}, bf16[128,1408]{1,0:T(8,128)(2,1)S(1)}, u32[]{:S(2)}, u32[]{:S(2)}) collective-permute-start(bf16[128,1408]{1,0:T(8,128)(2,1)S(1)} %collective-permute-done.54), channel_id=1, source_target_pairs={{0,4},{8,0},{16,8},{24,16},{28,24},{20,28},{12,20},{4,12},{1,5},{9... | collective-permute-start | bytes 1081352 | tf_op jit(solution)/shard_map/ppermute | solution.py:104
  533.6 280.5 %all-reduce.10.cloned.1.call-start = ((), (), s32[]{:S(2)}) async-start(), calls=%async_computation.1 | async-start | bytes 8388608 | tf_op jit(solution)/shard_map/psum | solution.py:284
  687.5 26.5 %collective-permute-start.154 = (bf16[128,1408]{1,0:T(8,128)(2,1)}, bf16[128,1408]{1,0:T(8,128)(2,1)S(1)}, u32[]{:S(2)}, u32[]{:S(2)}) collective-permute-start(bf16[128,1408]{1,0:T(8,128)(2,1)} %get-tuple-element.744), channel_id=1, source_target_pairs={{0,8},{8,16},{16,24},{24,28},{28,20},{20,12},{12,4},{4,0},{1,9},{9... | collective-permute-start | bytes 1081352 | tf_op jit(solution)/shard_map/ppermute | solution.py:122
  689.0 25.6 %collective-permute-start.161 = (bf16[128,1408]{1,0:T(8,128)(2,1)S(1)}, bf16[128,1408]{1,0:T(8,128)(2,1)}, u32[]{:S(2)}, u32[]{:S(2)}) collective-permute-start(bf16[128,1408]{1,0:T(8,128)(2,1)S(1)} %get-tuple-element.745), channel_id=1, source_target_pairs={{0,4},{8,0},{16,8},{24,16},{28,24},{20,28},{12,20},{4,12},{1,5},{9... | collective-permute-start | bytes 1081352 | tf_op jit(solution)/shard_map/ppermute | solution.py:123
  689.6 27.9 %collective-permute-start.140 = (bf16[128,1408]{1,0:T(8,128)(2,1)S(1)}, bf16[128,1408]{1,0:T(8,128)(2,1)S(1)}, u32[]{:S(2)}, u32[]{:S(2)}) collective-permute-start(bf16[128,1408]{1,0:T(8,128)(2,1)S(1)} %get-tuple-element.760), channel_id=1, source_target_pairs={{0,8},{8,16},{16,24},{24,28},{28,20},{20,12},{12,4},{4,0},{1,9},{9... | collective-permute-start | bytes 1081352 | tf_op jit(solution)/shard_map/ppermute | solution.py:122
  691.2 27.0 %collective-permute-start.147 = (bf16[128,1408]{1,0:T(8,128)(2,1)S(1)}, bf16[128,1408]{1,0:T(8,128)(2,1)S(1)}, u32[]{:S(2)}, u32[]{:S(2)}) collective-permute-start(bf16[128,1408]{1,0:T(8,128)(2,1)S(1)} %get-tuple-element.761), channel_id=1, source_target_pairs={{0,4},{8,0},{16,8},{24,16},{28,24},{20,28},{12,20},{4,12},{1,5},{9... | collective-permute-start | bytes 1081352 | tf_op jit(solution)/shard_map/ppermute | solution.py:123
  714.0 256.2 %all-gather.8.cloned.1.call-start = ((), (), s32[]{:S(2)}) async-start(), calls=%async_computation.3 | async-start | bytes 4718592 | tf_op jit(solution)/shard_map/all_gather | solution.py:19
  728.3 20.4 %collective-permute-start.134 = (bf16[128,1408]{1,0:T(8,128)(2,1)S(1)}, bf16[128,1408]{1,0:T(8,128)(2,1)S(1)}, u32[]{:S(2)}, u32[]{:S(2)}) collective-permute-start(bf16[128,1408]{1,0:T(8,128)(2,1)S(1)} %get-tuple-element.775), channel_id=1, source_target_pairs={{0,4},{8,0},{16,8},{24,16},{28,24},{20,28},{12,20},{4,12},{1,5},{9... | collective-permute-start | bytes 1081352 | tf_op jit(solution)/shard_map/ppermute | solution.py:123
  743.7 20.4 %collective-permute-start.149 = (bf16[128,1408]{1,0:T(8,128)(2,1)S(1)}, bf16[128,1408]{1,0:T(8,128)(2,1)S(1)}, u32[]{:S(2)}, u32[]{:S(2)}) collective-permute-start(bf16[128,1408]{1,0:T(8,128)(2,1)S(1)} %get-tuple-element.757), channel_id=1, source_target_pairs={{0,4},{8,0},{16,8},{24,16},{28,24},{20,28},{12,20},{4,12},{1,5},{9... | collective-permute-start | bytes 1081352 | tf_op jit(solution)/shard_map/ppermute | solution.py:123
  751.4 20.4 %collective-permute-start.135 = (bf16[128,1408]{1,0:T(8,128)(2,1)S(1)}, bf16[128,1408]{1,0:T(8,128)(2,1)S(1)}, u32[]{:S(2)}, u32[]{:S(2)}) collective-permute-start(bf16[128,1408]{1,0:T(8,128)(2,1)S(1)} %get-tuple-element.773), channel_id=1, source_target_pairs={{0,4},{8,0},{16,8},{24,16},{28,24},{20,28},{12,20},{4,12},{1,5},{9... | collective-permute-start | bytes 1081352 | tf_op jit(solution)/shard_map/ppermute | solution.py:123
  759.2 20.4 %collective-permute-start.164 = (bf16[128,1408]{1,0:T(8,128)(2,1)S(1)}, bf16[128,1408]{1,0:T(8,128)(2,1)S(1)}, u32[]{:S(2)}, u32[]{:S(2)}) collective-permute-start(bf16[128,1408]{1,0:T(8,128)(2,1)S(1)} %get-tuple-element.739), channel_id=1, source_target_pairs={{0,4},{8,0},{16,8},{24,16},{28,24},{20,28},{12,20},{4,12},{1,5},{9... | collective-permute-start | bytes 1081352 | tf_op jit(solution)/shard_map/ppermute | solution.py:123
  790.1 20.4 %collective-permute-start.151 = (bf16[128,1408]{1,0:T(8,128)(2,1)S(1)}, bf16[128,1408]{1,0:T(8,128)(2,1)S(1)}, u32[]{:S(2)}, u32[]{:S(2)}) collective-permute-start(bf16[128,1408]{1,0:T(8,128)(2,1)S(1)} %get-tuple-element.753), channel_id=1, source_target_pairs={{0,4},{8,0},{16,8},{24,16},{28,24},{20,28},{12,20},{4,12},{1,5},{9... | collective-permute-start | bytes 1081352 | tf_op jit(solution)/shard_map/ppermute | solution.py:123
  797.2 46.4 %collective-permute-start.130 = (bf16[128,1408]{1,0:T(8,128)(2,1)}, bf16[128,1408]{1,0:T(8,128)(2,1)}, u32[]{:S(2)}, u32[]{:S(2)}) collective-permute-start(bf16[128,1408]{1,0:T(8,128)(2,1)} %get-tuple-element.768), channel_id=1, source_target_pairs={{0,8},{8,16},{16,24},{24,28},{28,20},{20,12},{12,4},{4,0},{1,9},{9... | collective-permute-start | bytes 1081352 | tf_op jit(solution)/shard_map/ppermute | solution.py:122
  798.6 45.6 %collective-permute-start.137 = (bf16[128,1408]{1,0:T(8,128)(2,1)}, bf16[128,1408]{1,0:T(8,128)(2,1)}, u32[]{:S(2)}, u32[]{:S(2)}) collective-permute-start(bf16[128,1408]{1,0:T(8,128)(2,1)} %get-tuple-element.769), channel_id=1, source_target_pairs={{0,4},{8,0},{16,8},{24,16},{28,24},{20,28},{12,20},{4,12},{1,5},{9... | collective-permute-start | bytes 1081352 | tf_op jit(solution)/shard_map/ppermute | solution.py:123
  804.8 53.6 %collective-permute-start.159 = (bf16[128,1408]{1,0:T(8,128)(2,1)}, bf16[128,1408]{1,0:T(8,128)(2,1)}, u32[]{:S(2)}, u32[]{:S(2)}) collective-permute-start(bf16[128,1408]{1,0:T(8,128)(2,1)} %get-tuple-element.734), channel_id=1, source_target_pairs={{0,8},{8,16},{16,24},{24,28},{28,20},{20,12},{12,4},{4,0},{1,9},{9... | collective-permute-start | bytes 1081352 | tf_op jit(solution)/shard_map/ppermute | solution.py:122
  806.3 53.5 %collective-permute-start.166 = (bf16[128,1408]{1,0:T(8,128)(2,1)}, bf16[128,1408]{1,0:T(8,128)(2,1)}, u32[]{:S(2)}, u32[]{:S(2)}) collective-permute-start(bf16[128,1408]{1,0:T(8,128)(2,1)} %get-tuple-element.735), channel_id=1, source_target_pairs={{0,4},{8,0},{16,8},{24,16},{28,24},{20,28},{12,20},{4,12},{1,5},{9... | collective-permute-start | bytes 1081352 | tf_op jit(solution)/shard_map/ppermute | solution.py:123
  812.6 59.8 %collective-permute-start.145 = (bf16[128,1408]{1,0:T(8,128)(2,1)}, bf16[128,1408]{1,0:T(8,128)(2,1)S(1)}, u32[]{:S(2)}, u32[]{:S(2)}) collective-permute-start(bf16[128,1408]{1,0:T(8,128)(2,1)} %get-tuple-element.750), channel_id=1, source_target_pairs={{0,8},{8,16},{16,24},{24,28},{28,20},{20,12},{12,4},{4,0},{1,9},{9... | collective-permute-start | bytes 1081352 | tf_op jit(solution)/shard_map/ppermute | solution.py:122
  843.5 461.4 %all-reduce.12.cloned.1.call-start = ((), (), s32[]{:S(2)}) async-start(), calls=%async_computation.4 | async-start | bytes 16777216 | tf_op jit(solution)/shard_map/psum | solution.py:271
  843.6 29.2 %collective-permute-start.152 = (bf16[128,1408]{1,0:T(8,128)(2,1)}, bf16[128,1408]{1,0:T(8,128)(2,1)S(1)}, u32[]{:S(2)}, u32[]{:S(2)}) collective-permute-start(bf16[128,1408]{1,0:T(8,128)(2,1)} %get-tuple-element.751), channel_id=1, source_target_pairs={{0,4},{8,0},{16,8},{24,16},{28,24},{20,28},{12,20},{4,12},{1,5},{9... | collective-permute-start | bytes 1081352 | tf_op jit(solution)/shard_map/ppermute | solution.py:123
  845.7 39.6 %collective-permute-start.131 = (bf16[128,1408]{1,0:T(8,128)(2,1)S(1)}, bf16[128,1408]{1,0:T(8,128)(2,1)S(1)}, u32[]{:S(2)}, u32[]{:S(2)}) collective-permute-start(bf16[128,1408]{1,0:T(8,128)(2,1)S(1)} %get-tuple-element.766), channel_id=1, source_target_pairs={{0,8},{8,16},{16,24},{24,28},{28,20},{20,12},{12,4},{4,0},{1,9},{9... | collective-permute-start | bytes 1081352 | tf_op jit(solution)/shard_map/ppermute | solution.py:122
  865.2 22.2 %collective-permute-start.138 = (bf16[128,1408]{1,0:T(8,128)(2,1)S(1)}, bf16[128,1408]{1,0:T(8,128)(2,1)S(1)}, u32[]{:S(2)}, u32[]{:S(2)}) collective-permute-start(bf16[128,1408]{1,0:T(8,128)(2,1)S(1)} %get-tuple-element.767), channel_id=1, source_target_pairs={{0,4},{8,0},{16,8},{24,16},{28,24},{20,28},{12,20},{4,12},{1,5},{9... | collective-permute-start | bytes 1081352 | tf_op jit(solution)/shard_map/ppermute | solution.py:123
  872.3 49.0 %collective-permute-start.160 = (bf16[128,1408]{1,0:T(8,128)(2,1)S(1)}, bf16[128,1408]{1,0:T(8,128)(2,1)S(1)}, u32[]{:S(2)}, u32[]{:S(2)}) collective-permute-start(bf16[128,1408]{1,0:T(8,128)(2,1)S(1)} %get-tuple-element.732), channel_id=1, source_target_pairs={{0,8},{8,16},{16,24},{24,28},{28,20},{20,12},{12,4},{4,0},{1,9},{9... | collective-permute-start | bytes 1081352 | tf_op jit(solution)/shard_map/ppermute | solution.py:122
  882.8 40.6 %collective-permute-start.167 = (bf16[128,1408]{1,0:T(8,128)(2,1)S(1)}, bf16[128,1408]{1,0:T(8,128)(2,1)S(1)}, u32[]{:S(2)}, u32[]{:S(2)}) collective-permute-start(bf16[128,1408]{1,0:T(8,128)(2,1)S(1)} %get-tuple-element.733), channel_id=1, source_target_pairs={{0,4},{8,0},{16,8},{24,16},{28,24},{20,28},{12,20},{4,12},{1,5},{9... | collective-permute-start | bytes 1081352 | tf_op jit(solution)/shard_map/ppermute | solution.py:123
  884.7 39.9 %collective-permute-start.146 = (bf16[128,1408]{1,0:T(8,128)(2,1)S(1)}, bf16[128,1408]{1,0:T(8,128)(2,1)S(1)}, u32[]{:S(2)}, u32[]{:S(2)}) collective-permute-start(bf16[128,1408]{1,0:T(8,128)(2,1)S(1)} %get-tuple-element.748), channel_id=1, source_target_pairs={{0,8},{8,16},{16,24},{24,28},{28,20},{20,12},{12,4},{4,0},{1,9},{9... | collective-permute-start | bytes 1081352 | tf_op jit(solution)/shard_map/ppermute | solution.py:122
  885.3 22.9 %collective-permute-start.114 = (bf16[128,512]{1,0:T(8,128)(2,1)S(1)}, bf16[128,512]{1,0:T(8,128)(2,1)S(1)}, u32[]{:S(2)}, u32[]{:S(2)}) collective-permute-start(bf16[128,512]{1,0:T(8,128)(2,1)S(1)} %get-tuple-element.824), channel_id=1, source_target_pairs={{0,8},{8,16},{16,24},{24,28},{28,20},{20,12},{12,4},{4,0},{1,9},{9... | collective-permute-start | bytes 393224 | tf_op jit(solution)/shard_map/ppermute | solution.py:122
  887.4 33.8 %collective-permute-start.121 = (bf16[128,512]{1,0:T(8,128)(2,1)S(1)}, bf16[128,512]{1,0:T(8,128)(2,1)S(1)}, u32[]{:S(2)}, u32[]{:S(2)}) collective-permute-start(bf16[128,512]{1,0:T(8,128)(2,1)S(1)} %get-tuple-element.825), channel_id=1, source_target_pairs={{0,4},{8,0},{16,8},{24,16},{28,24},{20,28},{12,20},{4,12},{1,5},{9... | collective-permute-start | bytes 393224 | tf_op jit(solution)/shard_map/ppermute | solution.py:123
  908.2 28.2 %collective-permute-start.153 = (bf16[128,1408]{1,0:T(8,128)(2,1)S(1)}, bf16[128,1408]{1,0:T(8,128)(2,1)S(1)}, u32[]{:S(2)}, u32[]{:S(2)}) collective-permute-start(bf16[128,1408]{1,0:T(8,128)(2,1)S(1)} %get-tuple-element.749), channel_id=1, source_target_pairs={{0,4},{8,0},{16,8},{24,16},{28,24},{20,28},{12,20},{4,12},{1,5},{9... | collective-permute-start | bytes 1081352 | tf_op jit(solution)/shard_map/ppermute | solution.py:123
  921.3 22.8 %collective-permute-start.139 = (bf16[128,1408]{1,0:T(8,128)(2,1)S(1)}, bf16[128,1408]{1,0:T(8,128)(2,1)S(1)}, u32[]{:S(2)}, u32[]{:S(2)}) collective-permute-start(bf16[128,1408]{1,0:T(8,128)(2,1)S(1)} %get-tuple-element.765), channel_id=1, source_target_pairs={{0,4},{8,0},{16,8},{24,16},{28,24},{20,28},{12,20},{4,12},{1,5},{9... | collective-permute-start | bytes 1081352 | tf_op jit(solution)/shard_map/ppermute | solution.py:123
  923.4 22.0 %collective-permute-start.115 = (bf16[128,512]{1,0:T(8,128)(2,1)S(1)}, bf16[128,512]{1,0:T(8,128)(2,1)S(1)}, u32[]{:S(2)}, u32[]{:S(2)}) collective-permute-start(bf16[128,512]{1,0:T(8,128)(2,1)S(1)} %get-tuple-element.822), channel_id=1, source_target_pairs={{0,8},{8,16},{16,24},{24,28},{28,20},{20,12},{12,4},{4,0},{1,9},{9... | collective-permute-start | bytes 393224 | tf_op jit(solution)/shard_map/ppermute | solution.py:122
  924.6 21.6 %collective-permute-start.122 = (bf16[128,512]{1,0:T(8,128)(2,1)S(1)}, bf16[128,512]{1,0:T(8,128)(2,1)S(1)}, u32[]{:S(2)}, u32[]{:S(2)}) collective-permute-start(bf16[128,512]{1,0:T(8,128)(2,1)S(1)} %get-tuple-element.823), channel_id=1, source_target_pairs={{0,4},{8,0},{16,8},{24,16},{28,24},{20,28},{12,20},{4,12},{1,5},{9... | collective-permute-start | bytes 393224 | tf_op jit(solution)/shard_map/ppermute | solution.py:123
  1135.0 21.5 %collective-permute-start.84 = (bf16[128,768]{1,0:T(8,128)(2,1)}, bf16[128,768]{1,0:T(8,128)(2,1)}, u32[]{:S(2)}, u32[]{:S(2)}) collective-permute-start(bf16[128,768]{1,0:T(8,128)(2,1)} %get-tuple-element.812), channel_id=1, source_target_pairs={{0,8},{8,16},{16,24},{24,28},{28,20},{20,12},{12,4},{4,0},{1,9},{9... | collective-permute-start | bytes 589832 | tf_op jit(solution)/shard_map/ppermute | solution.py:122
  1135.3 21.2 %collective-permute-start.91 = (bf16[128,768]{1,0:T(8,128)(2,1)}, bf16[128,768]{1,0:T(8,128)(2,1)}, u32[]{:S(2)}, u32[]{:S(2)}) collective-permute-start(bf16[128,768]{1,0:T(8,128)(2,1)} %get-tuple-element.813), channel_id=1, source_target_pairs={{0,4},{8,0},{16,8},{24,16},{28,24},{20,28},{12,20},{4,12},{1,5},{9... | collective-permute-start | bytes 589832 | tf_op jit(solution)/shard_map/ppermute | solution.py:123
  (219 other events, 4009.4 us)
Sparse Core Ops, SparseCore 0:
  365.7 99.7 all-gather.5
  533.7 85.8 all-reduce.7
  714.1 84.6 all-reduce.9
  843.7 94.5 all-gather.7
  1153.6 151.3 all-reduce.11

commit v2 on v1

v2 whole, which is shorter than its diff:
```python
import functools

import jax
import jax.numpy as jnp
from jax import lax
from jax.experimental import pallas as pl
from jax.experimental.pallas import tpu as pltpu
from jax.sharding import PartitionSpec as P

DK = 256
DV = 512
CHUNK = 128
EPS = 1e-06
HIGH = lax.Precision.HIGHEST
NN = (((1,), (0,)), ((), ()))
NT = (((1,), (1,)), ((), ()))
TN = (((0,), (0,)), ((), ()))
VMEM_BYTES = 48 * 1024 * 1024


def product(left, right, dims, precision=None):
    return lax.dot_general(
        left, right, dims, precision=precision, preferred_element_type=jnp.float32
    )


def narrow(field):
    return field.astype(jnp.bfloat16)


def wide(field):
    return field.astype(jnp.float32)


def root_scale(field):
    return lax.rsqrt(jnp.mean(field * field, axis=-1, keepdims=True) + EPS)


def norm_back(upstream, unit, scale):
    return scale * (upstream - unit * jnp.mean(upstream * unit, axis=-1, keepdims=True))


def triangle(lower):
    rows = lax.broadcasted_iota(jnp.int32, (CHUNK, CHUNK), 0)
    columns = lax.broadcasted_iota(jnp.int32, (CHUNK, CHUNK), 1)
    return (rows >= columns if lower else rows <= columns).astype(jnp.float32)


def permitted(mark_column, mark_row):
    rows = lax.broadcasted_iota(jnp.int32, (CHUNK, CHUNK), 0)
    columns = lax.broadcasted_iota(jnp.int32, (CHUNK, CHUNK), 1)
    return (rows >= columns) & (mark_column == mark_row)


def state_kernel(
    value_ref, key_ref, low_ref, up_ref, bias_ref, mark_ref,
    run_ref, slope_ref, state_ref, total_ref, state, total,
):
    step = pl.program_id(0)

    @pl.when(step == 0)
    def _():
        state[...] = jnp.zeros_like(state)
        total[...] = jnp.ones_like(total)

    lower = triangle(True)
    for b in range(value_ref.shape[0]):
        raw = product(low_ref[b], up_ref[...], NN, HIGH) + bias_ref[...]
        soft = jnp.log1p(jnp.exp(-jnp.abs(raw)))
        decay = (jnp.minimum(raw, 0.0) - soft) / 16.0
        slope_ref[b] = jnp.exp(jnp.minimum(-raw, 0.0) - soft) / 16.0
        run = product(lower, decay, NN, HIGH)
        run_ref[b] = run
        mark = mark_ref[b]
        last = run[CHUNK - 1 :]
        trailing = mark == mark[CHUNK - 1 :]
        kept = jnp.where(trailing, jnp.exp(last - run), 0.0)
        keep = jnp.where(mark[CHUNK - 1 :] == 0.0, jnp.exp(last), 0.0)
        tail = narrow(wide(key_ref[b]) * kept)
        state[b] = state[b] * keep + product(value_ref[b], tail, TN)
        total[b] = total[b] * keep

    @pl.when(step == pl.num_programs(0) - 1)
    def _():
        state_ref[...] = narrow(state[...])
        total_ref[...] = total[...]


def mixer_kernel(
    query_ref, value_ref, key_ref, run_ref, mark_ref, row_ref, first_ref, gate_ref, gain_ref,
    heads_ref, mixed_ref, states_ref, state,
):
    step = pl.program_id(0)

    @pl.when(step == 0)
    def _():
        state[...] = wide(first_ref[...])

    for b in range(value_ref.shape[0]):
        run, mark = run_ref[b], mark_ref[b]
        middle, last = run[CHUNK // 2 - 1 : CHUNK // 2], run[CHUNK - 1 :]
        query = wide(query_ref[b]) * DK ** (-0.5)
        key = wide(key_ref[b])
        start = narrow(state[b])
        states_ref[0, b] = start
        scores = product(
            narrow(query * jnp.exp(run - middle)), narrow(key * jnp.exp(middle - run)), NT
        )
        scores = jnp.where(permitted(mark, row_ref[0, b]), scores, 0.0)
        opened = narrow(query * jnp.where(mark == 0.0, jnp.exp(run), 0.0))
        mixed = product(narrow(scores), value_ref[b], NN) + product(opened, start, NT)
        kept = jnp.where(mark == mark[CHUNK - 1 :], jnp.exp(last - run), 0.0)
        keep = jnp.where(mark[CHUNK - 1 :] == 0.0, jnp.exp(last), 0.0)
        state[b] = state[b] * keep + product(value_ref[b], narrow(key * kept), TN)
        states_ref[1, b] = narrow(state[b])
        mixed_ref[b] = mixed
        gate = gate_ref[b]
        active = gate * jax.nn.sigmoid(gate)
        heads_ref[b] = narrow(mixed * root_scale(mixed) * gain_ref[...] * active)


def head_back_kernel(
    grad_ref, gate_ref, mixed_ref, gain_ref, query_ref, run_ref, mark_ref,
    gate_grad_ref, mixed_grad_ref, gain_grad_ref, state_ref, state,
):
    step = pl.program_id(0)

    @pl.when(step == 0)
    def _():
        state[...] = jnp.zeros_like(state)
        gain_grad_ref[...] = jnp.zeros_like(gain_grad_ref)

    gain = gain_ref[...]
    for b in range(grad_ref.shape[0]):
        mixed, gate, grad = mixed_ref[b], gate_ref[b], wide(grad_ref[b])
        scale = root_scale(mixed)
        unit = mixed * scale
        sigma = jax.nn.sigmoid(gate)
        active = gate * sigma
        gate_grad_ref[b] = narrow(grad * unit * gain * sigma * (1.0 + gate * (1.0 - sigma)))
        weighted = grad * active
        gain_grad_ref[...] += jnp.sum(weighted * unit, axis=0, keepdims=True)
        mixed_grad = narrow(norm_back(weighted * gain, unit, scale))
        mixed_grad_ref[b] = mixed_grad
        run, mark = run_ref[b], mark_ref[b]
        last = run[CHUNK - 1 :]
        query = wide(query_ref[b]) * DK ** (-0.5)
        opened = narrow(query * jnp.where(mark == 0.0, jnp.exp(run), 0.0))
        keep = jnp.where(mark[CHUNK - 1 :] == 0.0, jnp.exp(last), 0.0)
        state[b] = state[b] * keep + product(mixed_grad, opened, TN)

    @pl.when(step == pl.num_programs(0) - 1)
    def _():
        state_ref[...] = narrow(state[...])


def mixer_back_kernel(
    query_ref, value_ref, key_ref, run_ref, slope_ref, mark_ref, row_ref, grad_ref,
    start_ref, end_ref, last_ref, low_ref, up_ref,
    query_grad_ref, value_grad_ref, key_grad_ref, low_grad_ref, up_grad_ref, bias_grad_ref, state,
):
    step = pl.program_id(0)

    @pl.when(step == 0)
    def _():
        state[...] = wide(last_ref[...])
        up_grad_ref[...] = jnp.zeros_like(up_grad_ref)
        bias_grad_ref[...] = jnp.zeros_like(bias_grad_ref)

    upper = triangle(False)
    for b in range(value_ref.shape[0]):
        run, mark = run_ref[b], mark_ref[b]
        middle, last = run[CHUNK // 2 - 1 : CHUNK // 2], run[CHUNK - 1 :]
        query = wide(query_ref[b]) * DK ** (-0.5)
        key, value, grad = wide(key_ref[b]), value_ref[b], grad_ref[b]
        start, later = start_ref[0, b], narrow(state[b])
        rise, fall = jnp.exp(run - middle), jnp.exp(middle - run)
        opens = jnp.where(mark == 0.0, jnp.exp(run), 0.0)
        kept = jnp.where(mark == mark[CHUNK - 1 :], jnp.exp(last - run), 0.0)
        keep = jnp.where(mark[CHUNK - 1 :] == 0.0, jnp.exp(last), 0.0)
        allowed = permitted(mark, row_ref[0, b])
        risen, fallen = narrow(query * rise), narrow(key * fall)
        scores = narrow(jnp.where(allowed, product(risen, fallen, NT), 0.0))
        scores_grad = narrow(jnp.where(allowed, product(grad, value, NT), 0.0))
        query_grad = rise * product(scores_grad, fallen, NN) + opens * product(grad, start, NN)
        key_grad = fall * product(scores_grad, risen, TN) + kept * product(value, later, NN)
        value_grad = product(scores, grad, TN) + product(narrow(key * kept), later, NT)
        ends = jnp.sum(state[b] * wide(end_ref[0, b]), axis=0, keepdims=True)
        state[b] = state[b] * keep + product(grad, narrow(query * opens), TN)
        turn = query * query_grad - key * key_grad
        raw_grad = (product(upper, turn, NN, HIGH) + ends) * slope_ref[b]
        query_grad_ref[b] = narrow(query_grad * DK ** (-0.5))
        key_grad_ref[b] = narrow(key_grad)
        value_grad_ref[b] = narrow(value_grad)
        low_grad_ref[b] = product(raw_grad, up_ref[...], NT, HIGH)
        up_grad_ref[...] += product(low_ref[b], raw_grad, TN, HIGH)
        bias_grad_ref[...] += jnp.sum(raw_grad, axis=0, keepdims=True)


def along(batch, width, last=0, reverse=0):
    if reverse:
        return pl.BlockSpec((batch, CHUNK, width), lambda i: (0, reverse - 1 - i, last))
    return pl.BlockSpec((batch, CHUNK, width), lambda i: (0, i, last))


def still(*shape):
    return pl.BlockSpec(shape, lambda i: (0,) * len(shape))


def shape_of(dtype, *shape):
    return jax.ShapeDtypeStruct(shape, dtype)


def call(kernel, steps, in_specs, out_specs, out_shape, scratch, operands, flops):
    moved = sum(a.size * a.dtype.itemsize for a in operands)
    moved += sum(s.size * s.dtype.itemsize for s in out_shape)
    return pl.pallas_call(
        kernel,
        grid=(steps,),
        in_specs=in_specs,
        out_specs=out_specs,
        out_shape=out_shape,
        scratch_shapes=scratch,
        cost_estimate=pl.CostEstimate(flops=flops, bytes_accessed=moved, transcendentals=0),
        compiler_params=pltpu.CompilerParams(
            dimension_semantics=("arbitrary",), vmem_limit_bytes=VMEM_BYTES
        ),
    )(*operands)


F32, BF16 = jnp.float32, jnp.bfloat16


def local_states(value_key, low, up, bias, mark):
    batch, block, rank = low.shape
    steps = block // CHUNK
    return call(
        state_kernel,
        steps,
        [along(batch, DV), along(batch, DK, DV // DK), along(batch, rank), still(rank, DK),
         still(1, DK), along(batch, 1)],
        [along(batch, DK), along(batch, DK), still(batch, DV, DK), still(batch, 1, DK)],
        [shape_of(F32, batch, block, DK), shape_of(F32, batch, block, DK),
         shape_of(BF16, batch, DV, DK), shape_of(F32, batch, 1, DK)],
        [pltpu.VMEM((batch, DV, DK), F32), pltpu.VMEM((batch, 1, DK), F32)],
        (value_key, value_key, low, up, bias, mark),
        2 * batch * block * DK * (DV + 6 * CHUNK),
    )


def mix(query, value_key, run, mark, row, first, gates, gain):
    batch, block, _ = run.shape
    steps = block // CHUNK
    heads, mixed, states = call(
        mixer_kernel,
        steps,
        [along(batch, DK), along(batch, DV), along(batch, DK, DV // DK), along(batch, DK),
         along(batch, 1), pl.BlockSpec((1, batch, 1, CHUNK), lambda i: (i, 0, 0, 0)),
         still(batch, DV, DK), along(batch, DV), still(1, DV)],
        [along(batch, DV), along(batch, DV),
         pl.BlockSpec((2, batch, DV, DK), lambda i: (i, 0, 0, 0))],
        [shape_of(BF16, batch, block, DV), shape_of(F32, batch, block, DV),
         shape_of(BF16, 2 * steps, batch, DV, DK)],
        [pltpu.VMEM((batch, DV, DK), F32)],
        (query, value_key, value_key, run, mark, row, first, gates, gain),
        2 * batch * block * DK * (2 * DV + 3 * CHUNK),
    )
    return heads, mixed, states


def head_back(grad, gates, mixed, gain, query, run, mark):
    batch, block, _ = run.shape
    steps = block // CHUNK
    return call(
        head_back_kernel,
        steps,
        [along(batch, DV, 0, steps), along(batch, DV, 0, steps), along(batch, DV, 0, steps),
         still(1, DV), along(batch, DK, 0, steps), along(batch, DK, 0, steps),
         along(batch, 1, 0, steps)],
        [along(batch, DV, 0, steps), along(batch, DV, 0, steps), still(1, DV),
         still(batch, DV, DK)],
        [shape_of(BF16, batch, block, DV), shape_of(BF16, batch, block, DV),
         shape_of(F32, 1, DV), shape_of(BF16, batch, DV, DK)],
        [pltpu.VMEM((batch, DV, DK), F32)],
        (grad, gates, mixed, gain, query, run, mark),
        2 * batch * block * DK * DV,
    )


def mix_back(query, value_key, run, slope, mark, row, grad, states, later, low, up):
    batch, block, rank = low.shape
    steps = block // CHUNK
    return call(
        mixer_back_kernel,
        steps,
        [along(batch, DK, 0, steps), along(batch, DV, 0, steps),
         along(batch, DK, DV // DK, steps), along(batch, DK, 0, steps),
         along(batch, DK, 0, steps), along(batch, 1, 0, steps),
         pl.BlockSpec((1, batch, 1, CHUNK), lambda i: (steps - 1 - i, 0, 0, 0)),
         along(batch, DV, 0, steps),
         pl.BlockSpec((1, batch, DV, DK), lambda i: (2 * (steps - 1 - i), 0, 0, 0)),
         pl.BlockSpec((1, batch, DV, DK), lambda i: (2 * (steps - 1 - i) + 1, 0, 0, 0)),
         still(batch, DV, DK), along(batch, rank, 0, steps), still(rank, DK)],
        [along(batch, DK, 0, steps), along(batch, DV, 0, steps), along(batch, DK, 0, steps),
         along(batch, rank, 0, steps), still(rank, DK), still(1, DK)],
        [shape_of(BF16, batch, block, DK), shape_of(BF16, batch, block, DV),
         shape_of(BF16, batch, block, DK), shape_of(F32, batch, block, rank),
         shape_of(F32, rank, DK), shape_of(F32, 1, DK)],
        [pltpu.VMEM((batch, DV, DK), F32)],
        (query, value_key, value_key, run, slope, mark, row, grad, states, states, later, low, up),
        2 * batch * block * DK * (5 * DV + 6 * CHUNK),
    )


def matmul(left, right):
    return product(left, right, NN)


def matmul_nt(left, right):
    return product(left, right, NT)


def matmul_tn(left, right):
    return product(left, right, TN)


def ring_order(count):
    return list(range(0, count, 2)) + list(range(count - 1 - count % 2, 0, -2))


class Ring:
    def __init__(self, axis):
        self.axis = axis
        self.count = count = lax.axis_size(axis)
        order = ring_order(count)
        place = [order.index(i) for i in range(count)]
        self.right = [(order[i], order[(i + 1) % count]) for i in range(count)]
        self.left = [(order[i], order[(i - 1) % count]) for i in range(count)]
        owners = [[order[(place[i] + r) % count] for r in range(count)] for i in range(count)]
        slots = [[(place[i] - place[me]) % count for i in range(count)] for me in range(count)]
        mine = lax.axis_index(axis)
        self.owners = jnp.asarray(owners, jnp.int32)[mine]
        self.slots = jnp.asarray(slots, jnp.int32)[mine]

    def arrange(self, field, dim, table):
        width = field.shape[dim] // self.count
        return jnp.concatenate(
            [
                lax.dynamic_slice_in_dim(field, table[r] * width, width, dim)
                for r in range(self.count)
            ],
            axis=dim,
        )

    def near(self, field, dim):
        return self.arrange(field, dim, self.owners)

    def home(self, field, dim):
        return self.arrange(field, dim, self.slots)

    def gather(self, block, after=None):
        count, half = self.count, block.shape[0] // 2
        up, down = block[:half], block[half:]
        if after is not None:
            up, down, _ = lax.optimization_barrier((up, down, after))
        pieces = [None] * (2 * count)
        pieces[0], pieces[1] = up, down
        for step in range(1, count):
            up = lax.ppermute(up, self.axis, self.right)
            down = lax.ppermute(down, self.axis, self.left)
            pieces[2 * (count - step)] = up
            pieces[2 * step + 1] = down
            if step == count - 2:
                late = up[:8, :128]
        return jnp.concatenate(pieces, axis=0), late

    def scatter(self, total):
        count = self.count
        rows = total.shape[0] // count
        half = rows // 2

        def piece(slot, part):
            start = slot * rows + part * half
            return total[start : start + half]

        up, down = piece(count - 1, 0), piece(1, 1)
        for step in range(count - 1):
            up = lax.ppermute(up, self.axis, self.right)
            down = lax.ppermute(down, self.axis, self.left)
            up = wide(up) + wide(piece(count - 2 - step, 0))
            down = wide(down) + wide(piece((step + 2) % count, 1))
            if step < count - 2:
                up, down = narrow(up), narrow(down)
        return jnp.concatenate([up, down], axis=0)


def swap(axis, distance):
    return [(i, i ^ distance) for i in range(lax.axis_size(axis))]


def head_scatter(part):
    count, mine = lax.axis_size("head"), lax.axis_index("head")
    rows = part.shape[0] // count
    held = part.reshape((count, rows) + part.shape[1:])
    distance = 1
    while distance < count:
        bit = (mine // distance) % 2
        split = held.reshape((held.shape[0] // 2, 2) + held.shape[1:])
        sent = lax.dynamic_index_in_dim(split, 1 - bit, 1, False)
        kept = lax.dynamic_index_in_dim(split, bit, 1, False)
        got = lax.ppermute(narrow(sent), "head", swap("head", distance))
        held = wide(kept) + wide(got)
        distance *= 2
    return held[0]


def head_gather(share):
    count, mine = lax.axis_size("head"), lax.axis_index("head")
    held = share[None]
    distance = count // 2
    while distance:
        bit = (mine // distance) % 2
        got = lax.ppermute(held, "head", swap("head", distance))
        lower = jnp.where(bit == 0, held, got)
        upper = jnp.where(bit == 0, got, held)
        held = jnp.stack([lower, upper], axis=1).reshape((-1,) + share.shape)
        distance //= 2
    return held.reshape((-1,) + share.shape[1:])


def with_decay(state, decay):
    high = narrow(decay)
    low = narrow(decay - wide(high))
    return jnp.concatenate([narrow(state), high, low], axis=1)


def split_decay(message):
    rows = message.shape[1] - 2
    decay = wide(message[:, rows : rows + 1]) + wide(message[:, rows + 1 :])
    return wide(message[:, :rows]), decay


def entering(state, decay, later):
    count, mine = lax.axis_size("seq"), lax.axis_index("seq")
    inner = mine % 2
    ahead = (inner == 0) != later
    half = state.shape[1] // 2
    kept = wide(lax.dynamic_slice_in_dim(state, inner * half, half, 1))
    sent = lax.dynamic_slice_in_dim(state, (1 - inner) * half, half, 1)
    pair = swap("seq", 1)
    other, other_decay = split_decay(lax.ppermute(with_decay(sent, decay), "seq", pair))
    earliest = jnp.where(ahead, kept, other)
    joined = jnp.where(ahead, other_decay, decay) * earliest + jnp.where(ahead, other, kept)
    message = with_decay(joined, decay * other_decay)
    if later:
        chain = [(i, i - 2) for i in range(2, count)]
    else:
        chain = [(i, i + 2) for i in range(count - 2)]
    before, reach = jnp.zeros_like(kept), jnp.ones_like(decay)
    for _ in range(count // 2 - 1):
        message = lax.ppermute(message, "seq", chain)
        far, far_decay = split_decay(message)
        before = before + reach * far
        reach = reach * far_decay
    second = jnp.where(ahead, decay, other_decay) * before + earliest
    got = lax.ppermute(narrow(jnp.where(ahead, second, before)), "seq", pair)
    own = narrow(jnp.where(ahead, before, second))
    return jnp.concatenate(
        [jnp.where(inner == 0, own, got), jnp.where(inner == 0, got, own)], axis=1
    )


def columns_of(vector, rows):
    width = -(-vector.shape[-1] // rows)
    pad = [(0, 0)] * (vector.ndim - 1) + [(0, width * rows - vector.shape[-1])]
    shaped = jnp.pad(vector, pad).reshape(vector.shape[:-1] + (width, rows))
    return jnp.swapaxes(shaped, -1, -2)


def shards(
    layer_in,
    seg_starts,
    attn_gain,
    query_weight,
    key_weight,
    value_weight,
    gate_weight,
    decay_down,
    decay_up,
    decay_bias,
    head_gain,
    out_weight,
    ffn_gain,
    ffn_gate,
    ffn_up,
    ffn_down,
    out_grad,
):
    ring = Ring("seq")
    count = ring.count
    batch, block, width = layer_in.shape
    rows = batch * block
    chunks = block // CHUNK
    rank, share = decay_down.shape[1], attn_gain.shape[0]
    hidden = ffn_gate.shape[1]
    mixed_cols, rank_end = DV + DK, DV + DK + rank

    sizes = [head_gain.size, decay_bias.size, decay_up.size]
    small = jnp.concatenate([head_gain, decay_bias, decay_up.reshape(-1)])
    extra = columns_of(small, share)
    block_one = jnp.concatenate(
        [value_weight, key_weight, decay_down, attn_gain[:, None], ffn_gain[:, None], extra], axis=1
    )
    block_two = jnp.concatenate([query_weight, gate_weight, out_weight.T], axis=1)
    first, mark = ring.gather(block_one)
    second, mark = ring.gather(block_two, mark)
    third, mark = ring.gather(jnp.concatenate([ffn_gate, ffn_up], axis=1), mark)
    fdown_t, mark = ring.gather(ffn_down.T, mark)
    vk_all, down_all = first[:, :mixed_cols], first[:, mixed_cols:rank_end]
    gain_one, gain_two = wide(first[:, rank_end]), wide(first[:, rank_end + 1])
    small = first[:, rank_end + 2 :].reshape(count, share, -1)
    small = ring.home(jnp.swapaxes(small, 1, 2).reshape(count, -1), 0)
    gain_head = wide(small[:, : sizes[0]]).reshape(1, DV)
    bias_all = wide(small[:, sizes[0] : sizes[0] + sizes[1]]).reshape(1, DK)
    up_all = small[:, sizes[0] + sizes[1] : sum(sizes)].reshape(count, rank, -1)
    up_all = wide(jnp.swapaxes(up_all, 0, 1).reshape(rank, DK))
    query_all, gate_all, out_t = second[:, :DK], second[:, DK:mixed_cols], second[:, mixed_cols:]

    starts = seg_starts.reshape(batch, chunks, CHUNK).astype(jnp.float32)
    places = jnp.arange(CHUNK)
    lower = (places[:, None] >= places[None, :]).astype(jnp.float32)
    marks = jnp.einsum("bcs,ts->bct", starts, lower, precision=HIGH)
    column, row = marks.reshape(batch, block, 1), jnp.swapaxes(marks, 0, 1)[:, :, None, :]

    inputs = ring.near(layer_in.reshape(rows, width), 1)
    grad_rows = ring.near(out_grad.reshape(rows, width), 1)
    head = lax.axis_index("head")
    quarter = rows // lax.axis_size("head")
    inputs_own = wide(lax.dynamic_slice_in_dim(inputs, head * quarter, quarter, 0))
    grad_own = wide(lax.dynamic_slice_in_dim(grad_rows, head * quarter, quarter, 0))
    scale_one = root_scale(wide(inputs))
    normed = narrow(wide(inputs) * scale_one * gain_one)

    def tokens(field):
        return field.reshape(batch, block, field.shape[-1])

    value_key = tokens(narrow(matmul(normed, vk_all)))
    low = tokens(matmul(normed, down_all))
    run, slope, state, total = local_states(value_key, low, up_all, bias_all, column)
    query = tokens(narrow(matmul(normed, query_all)))
    gates = tokens(matmul(normed, gate_all))
    state_in = entering(state, total, False)
    heads, mixed, states = mix(query, value_key, run, column, row, state_in, gates, gain_head)
    heads = heads.reshape(rows, DV)
    resid = inputs_own + head_scatter(narrow(matmul_nt(heads, out_t)))
    scale_two = root_scale(resid)
    unit_two = resid * scale_two
    normed_two = head_gather(narrow(unit_two * gain_two))
    pre_gate = matmul(normed_two, third[:, :hidden])
    pre_up = matmul(normed_two, third[:, hidden:])
    sigma = jax.nn.sigmoid(pre_gate)
    act = narrow(pre_gate * sigma * pre_up)
    layer_out = narrow(resid + head_scatter(narrow(matmul_nt(act, fdown_t))))
    layer_out = ring.home(head_gather(layer_out), 1)

    d_act = matmul(grad_rows, fdown_t)
    grad_fdown = ring.scatter(narrow(matmul_tn(grad_rows, act)))
    d_gate = narrow(d_act * pre_up * sigma * (1.0 + pre_gate * (1.0 - sigma)))
    d_up = narrow(d_act * pre_gate * sigma)
    d_third = jnp.concatenate([d_gate, d_up], axis=1)
    grad_third = ring.scatter(narrow(matmul_tn(normed_two, d_third)))
    d_normed_two = head_scatter(narrow(matmul_nt(d_third, third)))
    grad_gain_two = jnp.sum(d_normed_two * unit_two, axis=0)
    d_resid = grad_own + norm_back(d_normed_two * gain_two, unit_two, scale_two)
    d_attn = head_gather(narrow(d_resid))
    d_heads = tokens(matmul(d_attn, out_t))
    d_gates, d_mixed, grad_gain_head, state_grad = head_back(
        d_heads, gates, mixed, gain_head, query, run, column
    )
    state_back = entering(state_grad, total, True)
    d_query, d_value, d_key, d_low, grad_up, grad_bias = mix_back(
        query, value_key, run, slope, column, row, d_mixed, states, state_back, low, up_all
    )
    d_gates = d_gates.reshape(rows, DV)
    grad_out = matmul_tn(d_attn, heads)
    grad_gate = matmul_tn(normed, d_gates)
    grad_fourth = ring.scatter(narrow(jnp.concatenate([grad_gate, grad_out], axis=1)))
    d_first = jnp.concatenate(
        [d_value.reshape(rows, DV), d_key.reshape(rows, DK), narrow(d_low.reshape(rows, rank))],
        axis=1,
    )
    d_query = d_query.reshape(rows, DK)
    d_normed_part = (
        matmul_nt(d_first, first[:, :rank_end])
        + matmul_nt(d_query, query_all)
        + matmul_nt(d_gates, gate_all)
    )
    d_normed = head_scatter(narrow(d_normed_part))
    unit_own = inputs_own * root_scale(inputs_own)
    grad_gain_one = jnp.sum(d_normed * unit_own, axis=0)
    d_unit = norm_back(d_normed * gain_one, unit_own, root_scale(inputs_own))
    input_grad = ring.home(head_gather(narrow(d_resid + d_unit)), 1)

    small = jnp.concatenate(
        [
            grad_gain_head.reshape(count, -1),
            grad_bias.reshape(count, -1),
            jnp.swapaxes(grad_up.reshape(rank, count, -1), 0, 1).reshape(count, -1),
        ],
        axis=1,
    )
    small = columns_of(ring.near(small, 0), share).reshape(width, -1)
    grad_last = jnp.concatenate(
        [
            matmul_tn(normed, d_first),
            matmul_tn(normed, d_query),
            small,
            grad_gain_two[:, None],
        ],
        axis=1,
    )
    grad_last = ring.scatter(narrow(grad_last))
    gain_one_sum = lax.psum(ring.home(grad_gain_one, 0), ("seq", "head"))
    gain_one_sum = lax.dynamic_slice_in_dim(gain_one_sum, lax.axis_index("seq") * share, share)
    small = jnp.swapaxes(grad_last[:, rank_end + DK : -1], 0, 1).reshape(-1)
    shared = lax.psum(
        (
            grad_last[:, mixed_cols:rank_end],
            grad_last[:, -1],
            small[: sizes[0]],
        ),
        "head",
    )
    return (
        layer_out.reshape(batch, block, width),
        input_grad.reshape(batch, block, width),
        gain_one_sum,
        grad_last[:, rank_end : rank_end + DK],
        grad_last[:, DV:mixed_cols],
        grad_last[:, :DV],
        grad_fourth[:, :DV],
        shared[0],
        small[sizes[0] + sizes[1] : sum(sizes)].reshape(rank, -1),
        small[sizes[0] : sizes[0] + sizes[1]],
        shared[2],
        grad_fourth[:, DV:].T,
        shared[1],
        grad_third[:, :hidden],
        grad_third[:, hidden:],
        grad_fdown.T,
    )


def solution(mesh):
    return jax.shard_map(
        shards,
        mesh=mesh,
        in_specs=(
            P(None, "seq", None),
            P(None, "seq"),
            P("seq"),
            P("seq", "head"),
            P("seq", "head"),
            P("seq", "head"),
            P("seq", "head"),
            P("seq", None),
            P(None, ("head", "seq")),
            P(("head", "seq")),
            P("seq"),
            P("head", "seq"),
            P("seq"),
            P("seq", "head"),
            P("seq", "head"),
            P("head", "seq"),
            P(None, "seq", None),
        ),
        out_specs=(
            P(None, "seq", None),
            P(None, "seq", None),
            P("seq"),
            P("seq", "head"),
            P("seq", "head"),
            P("seq", "head"),
            P("seq", "head"),
            P("seq", None),
            P(None, ("head", "seq")),
            P(("head", "seq")),
            P("seq"),
            P("head", "seq"),
            P("seq"),
            P("seq", "head"),
            P("seq", "head"),
            P("head", "seq"),
        ),
        check_vma=False,
    )
```

time: 1390 us -> 958 us (0.69)
  matrix products: 318 us -> 142 us
  local copies, waits for them, and re-layouts: 270 us -> 167 us
  blocking collectives: 146 us -> 51.6 us
  starting transfers between devices: 194 us -> 148 us
  other arithmetic: 115 us -> 69.5 us
  Pallas kernels: 0 us -> 29.5 us
  between operations: 27.2 us -> 42.3 us
    dot_general x193 -> x21, matrix products: 318 us -> 142 us  [the longest x20 142 us: product(): lax.dot_general(left, right, dims, precision=precision, preferred_element...]
    psum x3 -> x0, waiting for transfers between devices: 116 us -> none  [the longest x1 76.5 us: shards(): ffn = lax.psum(ffn_part.astype(jnp.bfloat16), 'head').astype(jnp.float32)]
    ppermute x0 -> x26, waiting for transfers between devices: none -> 65.7 us  [the longest x8 42 us: head_gather(): got = lax.ppermute(held, 'head', swap('head', distance))]
    all_gather x1 -> x0, blocking collectives: 59.7 us -> none  [prefix_states(): lax.all_gather(value[0], axis)]
    unnamed x1 -> x0, blocking collectives: 36.2 us -> none
    dynamic_slice x21 -> x3, local copies, waits for them, and re-layouts: 33.8 us -> 0.68 us  [the longest x1 0.63 us: shards(): lax.dynamic_slice_in_dim(gain_one_sum, lax.axis_index('seq') * share, share)]
    ppermute x42 -> x28, starting transfers between devices: 56.8 us -> 26.2 us  [scatter(): down = lax.ppermute(down, self.axis, self.left)]
    ppermute x0 -> x26, starting transfers between devices: none -> 30.3 us  [the longest x6 15.4 us: entering(): message = lax.ppermute(message, 'seq', chain)]
  transfers between devices with their start and end apart: 173 -> 138, of which waited for: 69 -> 68; matrix products, arithmetic and copies ran while one was open for 31% -> 34% of each run, Pallas kernels for 0% -> 3%
where the time goes in v2:
time: 958 us; the launch traced here: 945 us
  waiting for transfers between devices  296 us (31%)
  local copies, waits for them, and re-layouts  167 us (17%)
  starting transfers between devices  148 us (15%)
  matrix products  142 us (15%)
  other arithmetic  69.5 us (7%)
  blocking collectives  51.6 us (5%)
  between operations  42.3 us (4%)
  Pallas kernels  29.5 us (3%)
    dot_general x20, matrix products, product(): lax.dot_general(left, right, dims, precision=precision, preferred_element...  142 us
    unnamed x269, local copies, waits for them, and re-layouts  124 us
    ppermute x28, waiting for transfers between devices, scatter(): down = lax.ppermute(down, self.axis, self.left)  74.6 us
    ppermute x28, waiting for transfers between devices, scatter(): up = lax.ppermute(up, self.axis, self.right)  60.3 us
    ppermute x28, waiting for transfers between devices, gather(): up = lax.ppermute(up, self.axis, self.right)  49.3 us
    ppermute x28, waiting for transfers between devices, gather(): down = lax.ppermute(down, self.axis, self.left)  45.6 us
    ppermute x8, waiting for transfers between devices, head_gather(): got = lax.ppermute(held, 'head', swap('head', distance))  42 us
    psum x1, blocking collectives, shards(): gain_one_sum = lax.psum(ring.home(grad_gain_one, 0), ('seq', 'head'))  39.1 us
  transfers between devices with their start and end apart: 138, of which 68 were waited for; matrix products, arithmetic and copies ran while one was open for 34% of the time, Pallas kernels for 3%

profile of v2, /device:TPU:0, one launch (start us, length us, event | category | flops | bytes accessed | tf_op | source)
XLA Modules:
  0.0 945.3 jit_solution(7972991424832616957)
XLA Ops:
  6.8 3.0 collective-permute-start
  49.9 3.1 fusion
  85.9 3.2 collective-permute-done.10
  98.8 5.9 collective-permute-done.12
  109.0 4.0 collective-permute-done.13
  115.3 3.4 fusion.33
  126.1 7.1 shard_map.306
  137.5 7.6 collective-permute-done.22
  160.3 3.3 collective-permute-done.28
  163.7 5.9 collective-permute-done.53
  174.9 11.2 %collective-permute-done.17 = bf16[128,1280]{1,0:T(8,128)(2,1)S(1)} collective-permute-done((bf16[128,1280]{1,0:T(8,128)(2,1)}, bf16[128,1280]{1,0:T(8,128)(2,1)S(1)}, u32[]{:S(2)}, u32[]{:S(2)}) %collective-permute-start.17) | collective-permute-done | bytes 327712 | tf_op jit(solution)/shard_map/ppermute | solution.py:369
  186.2 12.4 %collective-permute-done.24 = bf16[128,1280]{1,0:T(8,128)(2,1)S(1)} collective-permute-done((bf16[128,1280]{1,0:T(8,128)(2,1)}, bf16[128,1280]{1,0:T(8,128)(2,1)S(1)}, u32[]{:S(2)}, u32[]{:S(2)}) %collective-permute-start.24) | collective-permute-done | bytes 327712 | tf_op jit(solution)/shard_map/ppermute | solution.py:370
  203.1 4.0 collective-permute-start.29
  212.8 4.5 collective-permute-done.55
  220.3 5.2 collective-permute-start.30
  289.0 5.4 fusion.29
  319.9 6.2 shard_map.307
  331.1 9.6 %collective-permute-done.41 = bf16[128,2816]{1,0:T(8,128)(2,1)S(1)} collective-permute-done((bf16[128,2816]{1,0:T(8,128)(2,1)S(1)}, bf16[128,2816]{1,0:T(8,128)(2,1)S(1)}, u32[]{:S(2)}, u32[]{:S(2)}) %collective-permute-start.41) | collective-permute-done | bytes 720928 | tf_op jit(solution)/shard_map/ppermute | solution.py:369
  343.3 11.8 %fusion.114 = f32[1024,1408]{1,0:T(8,128)} fusion(bf16[1024,2048]{1,0:T(8,128)(2,1)} %dynamic-slice_dynamic-update-slice_fusion.8, bf16[2048,1408]{0,1:T(8,128)(2,1)} %constant_dynamic-update-slice_fusion.49), kind=kOutput, calls=%fused_computation.472 | convolution fusion | flops 5905580032 | bytes 15728640 | tf_op jit(solution)/shard_map/dot_general | solution.py:22
  362.1 6.3 collective-permute-done.43
  385.8 12.1 %collective-permute-done.35 = bf16[1,256,2048]{2,1,0:T(8,128)(2,1)S(1)} collective-permute-done((bf16[1,256,2048]{2,1,0:T(8,128)(2,1)S(1)}, bf16[1,256,2048]{2,1,0:T(8,128)(2,1)S(1)}, u32[]{:S(2)}, u32[]{:S(2)}) %collective-permute-start.35) | collective-permute-done | bytes 1048608 | tf_op jit(solution)/shard_map/ppermute | solution.py:423
  408.8 5.1 copy-done.66
  413.9 6.7 fusion.3
  420.6 15.0 %multiply_convert_fusion.1 = (bf16[1024,1408]{1,0:T(8,128)(2,1)}, bf16[1024,1408]{1,0:T(8,128)(2,1)}, bf16[1024,1408]{1,0:T(8,128)(2,1)}) fusion(f32[1024,1408]{1,0:T(8,128)} %fusion.114, f32[1024,1408]{1,0:T(8,128)S(1)} %fusion.3, bf16[1024,2048]{1,0:T(8,128)(2,1)S(1)} %bitcast.296, bf16[2048,2816]{1,0:T(8,128)(2,1)} %constant_dynamic-update-slice_fusion.33), kind=kOutput, calls=%fused_computation.44 | convolution fusion | flops 5928648704 | bytes 30146560 | tf_op jit(solution)/shard_map/dot_general | solution.py:22
  435.6 9.4 convolution_convert_fusion.1
  447.2 18.4 %convolution_convert_fusion.2 = bf16[1024,2048]{1,0:T(8,128)(2,1)} fusion(bf16[2048,2816]{1,0:T(8,128)(2,1)} %constant_dynamic-update-slice_fusion.33, bf16[1024,1408]{1,0:T(8,128)(2,1)} %get-tuple-element.137, bf16[1024,1408]{1,0:T(8,128)(2,1)} %get-tuple-element.135), kind=kOutput, calls=%fused_computation.55 | convolution fusion | flops 11824791552 | bytes 21495808 | tf_op jit(solution)/shard_map/dot_general | solution.py:22
  465.6 18.3 %convolution_convert_fusion = bf16[2048,2816]{1,0:T(8,128)(2,1)} fusion(bf16[1024,2048]{1,0:T(8,128)(2,1)} %bitcast.297, bf16[1024,1408]{1,0:T(8,128)(2,1)} %get-tuple-element.137, bf16[1024,1408]{1,0:T(8,128)(2,1)} %get-tuple-element.135), kind=kOutput, calls=%fused_computation.30 | convolution fusion | flops 11828461568 | bytes 21495808 | tf_op jit(solution)/shard_map/dot_general | solution.py:22
  486.3 10.1 %convolution_convert_fusion.3 = bf16[1024,2048]{1,0:T(8,128)(2,1)S(1)} fusion(bf16[1024,1408]{1,0:T(8,128)(2,1)} %get-tuple-element.136, bf16[2048,1408]{0,1:T(8,128)(2,1)} %constant_dynamic-update-slice_fusion.49), kind=kOutput, calls=%fused_computation.56 | convolution fusion | flops 5907677184 | bytes 12845056 | tf_op jit(solution)/shard_map/dot_general | solution.py:22
  501.1 6.9 collective-permute-done.126
  512.1 13.2 %collective-permute-done.117 = bf16[128,2816]{1,0:T(8,128)(2,1)S(1)} collective-permute-done((bf16[128,2816]{1,0:T(8,128)(2,1)S(1)}, bf16[128,2816]{1,0:T(8,128)(2,1)S(1)}, u32[]{:S(2)}, u32[]{:S(2)}) %collective-permute-start.117) | collective-permute-done | bytes 720928 | tf_op jit(solution)/shard_map/ppermute | solution.py:389
  528.0 3.2 collective-permute-done.127
  535.2 11.5 %collective-permute-done.118 = bf16[128,2816]{1,0:T(8,128)(2,1)S(1)} collective-permute-done((bf16[128,2816]{1,0:T(8,128)(2,1)S(1)}, bf16[128,2816]{1,0:T(8,128)(2,1)S(1)}, u32[]{:S(2)}, u32[]{:S(2)}) %collective-permute-start.118) | collective-permute-done | bytes 720928 | tf_op jit(solution)/shard_map/ppermute | solution.py:389
  548.7 3.7 collective-permute-done.128
  554.2 3.9 collective-permute-done.135
  566.5 10.2 %collective-permute-done.129 = bf16[128,1408]{1,0:T(8,128)(2,1)S(1)} collective-permute-done((bf16[128,1408]{1,0:T(8,128)(2,1)S(1)}, bf16[128,1408]{1,0:T(8,128)(2,1)S(1)}, u32[]{:S(2)}, u32[]{:S(2)}) %collective-permute-start.129) | collective-permute-done | bytes 360480 | tf_op jit(solution)/shard_map/ppermute | solution.py:388
  585.9 5.4 collective-permute-done.130
  594.1 10.0 %collective-permute-done.120 = bf16[128,2816]{1,0:T(8,128)(2,1)S(1)} collective-permute-done((bf16[128,2816]{1,0:T(8,128)(2,1)S(1)}, bf16[128,2816]{1,0:T(8,128)(2,1)S(1)}, u32[]{:S(2)}, u32[]{:S(2)}) %collective-permute-start.120) | collective-permute-done | bytes 720928 | tf_op jit(solution)/shard_map/ppermute | solution.py:389
  609.4 4.6 convert_bitcast_fusion
  625.0 15.4 %collective-permute-done.71 = bf16[1,256,2048]{2,1,0:T(8,128)(2,1)} collective-permute-done((bf16[1,256,2048]{2,1,0:T(8,128)(2,1)}, bf16[1,256,2048]{2,1,0:T(8,128)(2,1)}, u32[]{:S(2)}, u32[]{:S(2)}) %collective-permute-start.71) | collective-permute-done | bytes 1048608 | tf_op jit(solution)/shard_map/ppermute | solution.py:423
  646.4 9.9 %collective-permute-done.67 = bf16[1,256,2048]{2,1,0:T(8,128)(2,1)S(1)} collective-permute-done((bf16[1,256,2048]{2,1,0:T(8,128)(2,1)}, bf16[1,256,2048]{2,1,0:T(8,128)(2,1)S(1)}, u32[]{:S(2)}, u32[]{:S(2)}) %collective-permute-start.67) | collective-permute-done | bytes 1048608 | tf_op jit(solution)/shard_map/ppermute | solution.py:423
  658.0 4.8 collective-permute-done.123
  667.9 5.3 fusion.21.grad_ref
  673.2 5.8 shard_map.308
  688.8 4.2 collective-permute-done.103
  695.9 6.6 collective-permute-done.104
  709.5 4.3 collective-permute-done.105
  714.1 5.5 collective-permute-done.75
  721.4 3.9 collective-permute-done.106
  726.1 5.0 collective-permute-done.76
  739.8 10.4 %shard_map.309 = (bf16[2,512,256]{2,1,0:T(8,128)(2,1)S(1)}, bf16[2,512,512]{2,1,0:T(8,128)(2,1)S(1)}, bf16[2,512,256]{2,1,0:T(8,128)(2,1)S(1)}, f32[2,512,16]{2,...) custom-call(bf16[2,512,256]{2,1,0:T(8,128)(2,1)S(1)} %bitcast.256, bf16[2,512,768]{2,1,0:T(8,128)(2,1)} %bitcast.252, ...), custom_call_target="tpu_custom_call" | custom-call | flops 1744830464 | bytes 17998848 | tf_op jit(solution)/shard_map/pallas_call | solution.py:217
  750.3 6.7 fusion.7
  757.0 5.0 convolution_convert_fusion.5
  762.0 5.7 fusion.40
  770.1 17.6 %concatenate.118 = bf16[2048,1044]{0,1:T(8,128)(2,1)} concatenate(bf16[2048,784]{0,1:T(8,128)(2,1)} %convolution_convert_fusion.5, bf16[2048,256]{0,1:T(8,128)(2,1)S(1)} %convolution_convert_fusion.8, bf16[2048,3]{0,1:T(4,128)(2,1)S(1)} %bitcast.330, bf16[2048,1]{0,1:T(2,128)(2,1)S(1)} %broadcast_in_dim.44), dimensions={1} | concatenate | bytes 8552448 | tf_op jit(solution)/shard_map/concatenate | solution.py:613
  791.2 8.7 add_convert_fusion
  808.5 4.4 collective-permute-done.109
  818.9 5.0 collective-permute-done.97
  825.1 4.6 collective-permute-done.84
  831.9 3.4 collective-permute-done.98
  847.8 4.5 collective-permute-done.86
  866.0 5.3 collective-permute-done.101
  872.0 4.6 collective-permute-done.80
  882.6 12.5 %all-reduce.2 = (f32[256,16]{0,1:T(8,128)}, f32[64]{0:T(128)}, f32[256]{0:T(256)}) all-reduce(f32[256,16]{0,1:T(8,128)S(1)} %fusion.72, f32[64]{0:T(128)S(1)} %slice.567, f32[256]{0:T(256)S(1)} %bitcast.350), channel_id=1, replica_groups=mesh['seq'=8,'head'=4] {'head'}, use_global_device_ids=true, to_apply=%region_8.9 | all-reduce | flops 4416 | bytes 35328 | tf_op jit(solution)/shard_map/psum | solution.py:626
  899.7 39.1 %psum.28 = f32[2048]{0:T(1024)S(1)} all-reduce(f32[2048]{0:T(1024)S(1)} %constant_dynamic-update-slice_fusion.66), channel_id=1, replica_groups=mesh['seq'=8,'head'=4] {'seq','head'}, use_global_device_ids=true, to_apply=%region_6.7 | all-reduce | flops 2048 | bytes 16384 | tf_op jit(solution)/shard_map/psum | solution.py:623
  (687 shorter events, 404.0 us)
Async XLA Ops:
  6.8 54.5 %collective-permute-start = (bf16[128,789]{1,0:T(8,128)(2,1)}, bf16[128,789]{1,0:T(8,128)(2,1)}, u32[]{:S(2)}, u32[]{:S(2)}) collective-permute-start(bf16[128,789]{1,0:T(8,128)(2,1)} %get-tuple-element.205), channel_id=1, source_target_pairs={{0,8},{8,16},{16,24},{24,28},{28,20},{20,12},{12,4},{4,0},{1,9},{9... | collective-permute-start | bytes 605960 | tf_op jit(solution)/shard_map/ppermute | solution.py:369
  9.8 55.1 %collective-permute-start.7 = (bf16[128,789]{1,0:T(8,128)(2,1)}, bf16[128,789]{1,0:T(8,128)(2,1)}, u32[]{:S(2)}, u32[]{:S(2)}) collective-permute-start(bf16[128,789]{1,0:T(8,128)(2,1)} %get-tuple-element.204), channel_id=1, source_target_pairs={{0,4},{8,0},{16,8},{24,16},{28,24},{20,28},{12,20},{4,12},{1,5},{9... | collective-permute-start | bytes 605960 | tf_op jit(solution)/shard_map/ppermute | solution.py:370
  12.7 108.7 %collective-permute-start.14 = (bf16[128,1280]{1,0:T(8,128)(2,1)}, bf16[128,1280]{1,0:T(8,128)(2,1)}, u32[]{:S(2)}, u32[]{:S(2)}) collective-permute-start(bf16[128,1280]{1,0:T(8,128)(2,1)} %get-tuple-element.39), channel_id=1, source_target_pairs={{0,8},{8,16},{16,24},{24,28},{28,20},{20,12},{12,4},{4,0},{1,9},{9... | collective-permute-start | bytes 983048 | tf_op jit(solution)/shard_map/ppermute | solution.py:369
  16.1 130.4 %collective-permute-start.37 = (bf16[128,2816]{1,0:T(8,128)(2,1)}, bf16[128,2816]{1,0:T(8,128)(2,1)}, u32[]{:S(2)}, u32[]{:S(2)}) collective-permute-start(bf16[128,2816]{1,0:T(8,128)(2,1)} %get-tuple-element.45), channel_id=1, source_target_pairs={{0,8},{8,16},{16,24},{24,28},{28,20},{20,12},{12,4},{4,0},{1,9},{9... | collective-permute-start | bytes 2162696 | tf_op jit(solution)/shard_map/ppermute | solution.py:369
  17.7 129.5 %collective-permute-start.44 = (bf16[128,2816]{1,0:T(8,128)(2,1)}, bf16[128,2816]{1,0:T(8,128)(2,1)}, u32[]{:S(2)}, u32[]{:S(2)}) collective-permute-start(bf16[128,2816]{1,0:T(8,128)(2,1)} %get-tuple-element.46), channel_id=1, source_target_pairs={{0,4},{8,0},{16,8},{24,16},{28,24},{20,28},{12,20},{4,12},{1,5},{9... | collective-permute-start | bytes 2162696 | tf_op jit(solution)/shard_map/ppermute | solution.py:370
  104.7 29.5 %collective-permute-start.51 = (bf16[128,1408]{0,1:T(8,128)(2,1)}, bf16[128,1408]{0,1:T(8,128)(2,1)}, u32[]{:S(2)}, u32[]{:S(2)}) collective-permute-start(bf16[128,1408]{0,1:T(8,128)(2,1)} %get-tuple-element.47), channel_id=1, source_target_pairs={{0,8},{8,16},{16,24},{24,28},{28,20},{20,12},{12,4},{4,0},{1,9},{9... | collective-permute-start | bytes 1081352 | tf_op jit(solution)/shard_map/ppermute | solution.py:369
  136.3 16.5 %collective-permute-start.59 = (bf16[128,1408]{0,1:T(8,128)(2,1)}, bf16[128,1408]{0,1:T(8,128)(2,1)}, u32[]{:S(2)}, u32[]{:S(2)}) collective-permute-start(bf16[128,1408]{0,1:T(8,128)(2,1)} %collective-permute-done.58), channel_id=1, source_target_pairs={{0,4},{8,0},{16,8},{24,16},{28,24},{20,28},{12,20},{4,12},{1,5},{9... | collective-permute-start | bytes 1081352 | tf_op jit(solution)/shard_map/ppermute | solution.py:370
  149.5 20.0 %collective-permute-start.53 = (bf16[128,1408]{0,1:T(8,128)(2,1)}, bf16[128,1408]{0,1:T(8,128)(2,1)}, u32[]{:S(2)}, u32[]{:S(2)}) collective-permute-start(bf16[128,1408]{0,1:T(8,128)(2,1)} %collective-permute-done.52), channel_id=1, source_target_pairs={{0,8},{8,16},{16,24},{24,28},{28,20},{20,12},{12,4},{4,0},{1,9},{9... | collective-permute-start | bytes 1081352 | tf_op jit(solution)/shard_map/ppermute | solution.py:369
  152.8 18.5 %collective-permute-start.60 = (bf16[128,1408]{0,1:T(8,128)(2,1)}, bf16[128,1408]{0,1:T(8,128)(2,1)}, u32[]{:S(2)}, u32[]{:S(2)}) collective-permute-start(bf16[128,1408]{0,1:T(8,128)(2,1)} %collective-permute-done.59), channel_id=1, source_target_pairs={{0,4},{8,0},{16,8},{24,16},{28,24},{20,28},{12,20},{4,12},{1,5},{9... | collective-permute-start | bytes 1081352 | tf_op jit(solution)/shard_map/ppermute | solution.py:370
  157.0 41.6 %collective-permute-start.38 = (bf16[128,2816]{1,0:T(8,128)(2,1)}, bf16[128,2816]{1,0:T(8,128)(2,1)}, u32[]{:S(2)}, u32[]{:S(2)}) collective-permute-start(bf16[128,2816]{1,0:T(8,128)(2,1)} %collective-permute-done.37), channel_id=1, source_target_pairs={{0,8},{8,16},{16,24},{24,28},{28,20},{20,12},{12,4},{4,0},{1,9},{9... | collective-permute-start | bytes 2162696 | tf_op jit(solution)/shard_map/ppermute | solution.py:369
  159.8 43.3 %collective-permute-start.45 = (bf16[128,2816]{1,0:T(8,128)(2,1)}, bf16[128,2816]{1,0:T(8,128)(2,1)}, u32[]{:S(2)}, u32[]{:S(2)}) collective-permute-start(bf16[128,2816]{1,0:T(8,128)(2,1)} %collective-permute-done.44), channel_id=1, source_target_pairs={{0,4},{8,0},{16,8},{24,16},{28,24},{20,28},{12,20},{4,12},{1,5},{9... | collective-permute-start | bytes 2162696 | tf_op jit(solution)/shard_map/ppermute | solution.py:370
  163.6 22.5 %collective-permute-start.17 = (bf16[128,1280]{1,0:T(8,128)(2,1)}, bf16[128,1280]{1,0:T(8,128)(2,1)S(1)}, u32[]{:S(2)}, u32[]{:S(2)}) collective-permute-start(bf16[128,1280]{1,0:T(8,128)(2,1)} %collective-permute-done.16), channel_id=1, source_target_pairs={{0,8},{8,16},{16,24},{24,28},{28,20},{20,12},{12,4},{4,0},{1,9},{9... | collective-permute-start | bytes 983048 | tf_op jit(solution)/shard_map/ppermute | solution.py:369
  169.6 31.5 %collective-permute-start.54 = (bf16[128,1408]{0,1:T(8,128)(2,1)}, bf16[128,1408]{0,1:T(8,128)(2,1)S(1)}, u32[]{:S(2)}, u32[]{:S(2)}) collective-permute-start(bf16[128,1408]{0,1:T(8,128)(2,1)} %collective-permute-done.53), channel_id=1, source_target_pairs={{0,8},{8,16},{16,24},{24,28},{28,20},{20,12},{12,4},{4,0},{1,9},{9... | collective-permute-start | bytes 1081352 | tf_op jit(solution)/shard_map/ppermute | solution.py:369
  171.4 29.7 %collective-permute-start.61 = (bf16[128,1408]{0,1:T(8,128)(2,1)}, bf16[128,1408]{0,1:T(8,128)(2,1)S(1)}, u32[]{:S(2)}, u32[]{:S(2)}) collective-permute-start(bf16[128,1408]{0,1:T(8,128)(2,1)} %collective-permute-done.60), channel_id=1, source_target_pairs={{0,4},{8,0},{16,8},{24,16},{28,24},{20,28},{12,20},{4,12},{1,5},{9... | collective-permute-start | bytes 1081352 | tf_op jit(solution)/shard_map/ppermute | solution.py:370
  203.1 17.2 %collective-permute-start.29 = (bf16[2,258,256]{2,1,0:T(8,128)(2,1)S(1)}, bf16[2,258,256]{2,1,0:T(8,128)(2,1)}, u32[]{:S(2)}, u32[]{:S(2)}) collective-permute-start(bf16[2,258,256]{2,1,0:T(8,128)(2,1)S(1)} %pad_maximum_fusion.19), channel_id=1, source_target_pairs={{0,8},{4,12},{8,16},{12,20},{16,24},{20,28},{1,9},{5,13},{9,17},{1... | collective-permute-start | bytes 792584 | tf_op jit(solution)/shard_map/ppermute | solution.py:461
  210.8 43.7 %collective-permute-start.39 = (bf16[128,2816]{1,0:T(8,128)(2,1)}, bf16[128,2816]{1,0:T(8,128)(2,1)}, u32[]{:S(2)}, u32[]{:S(2)}) collective-permute-start(bf16[128,2816]{1,0:T(8,128)(2,1)} %collective-permute-done.38), channel_id=1, source_target_pairs={{0,8},{8,16},{16,24},{24,28},{28,20},{20,12},{12,4},{4,0},{1,9},{9... | collective-permute-start | bytes 2162696 | tf_op jit(solution)/shard_map/ppermute | solution.py:369
  212.1 44.5 %collective-permute-start.46 = (bf16[128,2816]{1,0:T(8,128)(2,1)}, bf16[128,2816]{1,0:T(8,128)(2,1)}, u32[]{:S(2)}, u32[]{:S(2)}) collective-permute-start(bf16[128,2816]{1,0:T(8,128)(2,1)} %collective-permute-done.45), channel_id=1, source_target_pairs={{0,4},{8,0},{16,8},{24,16},{28,24},{20,28},{12,20},{4,12},{1,5},{9... | collective-permute-start | bytes 2162696 | tf_op jit(solution)/shard_map/ppermute | solution.py:370
  217.3 31.8 %collective-permute-start.19 = (bf16[128,1280]{1,0:T(8,128)(2,1)}, bf16[128,1280]{1,0:T(8,128)(2,1)}, u32[]{:S(2)}, u32[]{:S(2)}) collective-permute-start(bf16[128,1280]{1,0:T(8,128)(2,1)} %collective-permute-done.18), channel_id=1, source_target_pairs={{0,8},{8,16},{16,24},{24,28},{28,20},{20,12},{12,4},{4,0},{1,9},{9... | collective-permute-start | bytes 983048 | tf_op jit(solution)/shard_map/ppermute | solution.py:369
  217.3 33.4 %collective-permute-start.26 = (bf16[128,1280]{1,0:T(8,128)(2,1)}, bf16[128,1280]{1,0:T(8,128)(2,1)}, u32[]{:S(2)}, u32[]{:S(2)}) collective-permute-start(bf16[128,1280]{1,0:T(8,128)(2,1)} %collective-permute-done.25), channel_id=1, source_target_pairs={{0,4},{8,0},{16,8},{24,16},{28,24},{20,28},{12,20},{4,12},{1,5},{9... | collective-permute-start | bytes 983048 | tf_op jit(solution)/shard_map/ppermute | solution.py:370
  220.3 33.3 %collective-permute-start.30 = (bf16[2,258,256]{2,1,0:T(8,128)(2,1)}, bf16[2,258,256]{2,1,0:T(8,128)(2,1)}, u32[]{:S(2)}, u32[]{:S(2)}) collective-permute-start(bf16[2,258,256]{2,1,0:T(8,128)(2,1)} %collective-permute-done.29), channel_id=1, source_target_pairs={{0,8},{4,12},{8,16},{12,20},{16,24},{20,28},{1,9},{5,13},{9,17},{1... | collective-permute-start | bytes 792584 | tf_op jit(solution)/shard_map/ppermute | solution.py:461
  254.5 31.8 %collective-permute-start.27 = (bf16[128,1280]{1,0:T(8,128)(2,1)}, bf16[128,1280]{1,0:T(8,128)(2,1)S(1)}, u32[]{:S(2)}, u32[]{:S(2)}) collective-permute-start(bf16[128,1280]{1,0:T(8,128)(2,1)} %collective-permute-done.26), channel_id=1, source_target_pairs={{0,4},{8,0},{16,8},{24,16},{28,24},{20,28},{12,20},{4,12},{1,5},{9... | collective-permute-start | bytes 983048 | tf_op jit(solution)/shard_map/ppermute | solution.py:370
  256.6 69.6 %collective-permute-start.40 = (bf16[128,2816]{1,0:T(8,128)(2,1)}, bf16[128,2816]{1,0:T(8,128)(2,1)S(1)}, u32[]{:S(2)}, u32[]{:S(2)}) collective-permute-start(bf16[128,2816]{1,0:T(8,128)(2,1)} %collective-permute-done.39), channel_id=1, source_target_pairs={{0,8},{8,16},{16,24},{24,28},{28,20},{20,12},{12,4},{4,0},{1,9},{9... | collective-permute-start | bytes 2162696 | tf_op jit(solution)/shard_map/ppermute | solution.py:369
  259.2 67.8 %collective-permute-start.47 = (bf16[128,2816]{1,0:T(8,128)(2,1)}, bf16[128,2816]{1,0:T(8,128)(2,1)S(1)}, u32[]{:S(2)}, u32[]{:S(2)}) collective-permute-start(bf16[128,2816]{1,0:T(8,128)(2,1)} %collective-permute-done.46), channel_id=1, source_target_pairs={{0,4},{8,0},{16,8},{24,16},{28,24},{20,28},{12,20},{4,12},{1,5},{9... | collective-permute-start | bytes 2162696 | tf_op jit(solution)/shard_map/ppermute | solution.py:370
  261.3 38.1 %collective-permute-start.57 = (bf16[128,1408]{0,1:T(8,128)(2,1)}, bf16[128,1408]{0,1:T(8,128)(2,1)S(1)}, u32[]{:S(2)}, u32[]{:S(2)}) collective-permute-start(bf16[128,1408]{0,1:T(8,128)(2,1)} %collective-permute-done.56), channel_id=1, source_target_pairs={{0,8},{8,16},{16,24},{24,28},{28,20},{20,12},{12,4},{4,0},{1,9},{9... | collective-permute-start | bytes 1081352 | tf_op jit(solution)/shard_map/ppermute | solution.py:369
  262.7 55.0 %collective-permute-start.64 = (bf16[128,1408]{0,1:T(8,128)(2,1)}, bf16[128,1408]{0,1:T(8,128)(2,1)S(1)}, u32[]{:S(2)}, u32[]{:S(2)}) collective-permute-start(bf16[128,1408]{0,1:T(8,128)(2,1)} %collective-permute-done.63), channel_id=1, source_target_pairs={{0,4},{8,0},{16,8},{24,16},{28,24},{20,28},{12,20},{4,12},{1,5},{9... | collective-permute-start | bytes 1081352 | tf_op jit(solution)/shard_map/ppermute | solution.py:370
  297.3 21.3 %collective-permute-start.32 = (bf16[2,256,256]{2,1,0:T(8,128)(2,1)S(1)}, bf16[2,256,256]{2,1,0:T(8,128)(2,1)S(1)}, u32[]{:S(2)}, u32[]{:S(2)}) collective-permute-start(bf16[2,256,256]{2,1,0:T(8,128)(2,1)S(1)} %select_convert_fusion.2), channel_id=1, source_target_pairs={{0,4},{4,0},{8,12},{12,8},{16,20},{20,16},{24,28},{28,24},{1,5},{5... | collective-permute-start | bytes 786440 | tf_op jit(solution)/shard_map/ppermute | solution.py:466
  331.0 28.6 %collective-permute-start.33 = (bf16[2,256,2048]{2,1,0:T(8,128)(2,1)S(1)}, bf16[2,256,2048]{2,1,0:T(8,128)(2,1)S(1)}, u32[]{:S(2)}, u32[]{:S(2)}) collective-permute-start(bf16[2,256,2048]{2,1,0:T(8,128)(2,1)S(1)} %dynamic-slice_bitcast_fusion.3), channel_id=1, source_target_pairs={{0,1},{1,0},{2,3},{3,2},{4,5},{5,4},{6,7},{7,6},{8,9},{9,8},{10,11... | collective-permute-start | bytes 6291464 | tf_op jit(solution)/shard_map/ppermute | solution.py:411
  358.7 47.9 %collective-permute-start.50 = (bf16[128,2816]{1,0:T(8,128)(2,1)S(1)}, bf16[128,2816]{1,0:T(8,128)(2,1)S(1)}, u32[]{:S(2)}, u32[]{:S(2)}) collective-permute-start(bf16[128,2816]{1,0:T(8,128)(2,1)S(1)} %collective-permute-done.49), channel_id=1, source_target_pairs={{0,4},{8,0},{16,8},{24,16},{28,24},{20,28},{12,20},{4,12},{1,5},{9... | collective-permute-start | bytes 2162696 | tf_op jit(solution)/shard_map/ppermute | solution.py:370
  360.5 17.6 %collective-permute-start.34 = (bf16[1,256,2048]{2,1,0:T(8,128)(2,1)S(1)}, bf16[1,256,2048]{2,1,0:T(8,128)(2,1)S(1)}, u32[]{:S(2)}, u32[]{:S(2)}) collective-permute-start(bf16[1,256,2048]{2,1,0:T(8,128)(2,1)S(1)} %dynamic-slice_convert_fusion.3), channel_id=1, source_target_pairs={{0,2},{1,3},{2,0},{3,1},{4,6},{5,7},{6,4},{7,5},{8,10},{9,11},{10,... | collective-permute-start | bytes 3145736 | tf_op jit(solution)/shard_map/ppermute | solution.py:411
  380.3 17.6 %collective-permute-start.35 = (bf16[1,256,2048]{2,1,0:T(8,128)(2,1)S(1)}, bf16[1,256,2048]{2,1,0:T(8,128)(2,1)S(1)}, u32[]{:S(2)}, u32[]{:S(2)}) collective-permute-start(bf16[1,256,2048]{2,1,0:T(8,128)(2,1)S(1)} %fusion.37), channel_id=1, source_target_pairs={{0,2},{1,3},{2,0},{3,1},{4,6},{5,7},{6,4},{7,5},{8,10},{9,11},{10,... | collective-permute-start | bytes 3145736 | tf_op jit(solution)/shard_map/ppermute | solution.py:423
  445.1 38.9 %collective-permute-start.124 = (bf16[128,1408]{1,0:T(8,128)(2,1)S(1)}, bf16[128,1408]{1,0:T(8,128)(2,1)S(1)}, u32[]{:S(2)}, u32[]{:S(2)}) collective-permute-start(bf16[128,1408]{1,0:T(8,128)(2,1)S(1)} %get-tuple-element.152), channel_id=1, source_target_pairs={{0,8},{8,16},{16,24},{24,28},{28,20},{20,12},{12,4},{4,0},{1,9},{9... | collective-permute-start | bytes 1081352 | tf_op jit(solution)/shard_map/ppermute | solution.py:388
  446.6 37.4 %collective-permute-start.131 = (bf16[128,1408]{1,0:T(8,128)(2,1)S(1)}, bf16[128,1408]{1,0:T(8,128)(2,1)S(1)}, u32[]{:S(2)}, u32[]{:S(2)}) collective-permute-start(bf16[128,1408]{1,0:T(8,128)(2,1)S(1)} %get-tuple-element.153), channel_id=1, source_target_pairs={{0,4},{8,0},{16,8},{24,16},{28,24},{20,28},{12,20},{4,12},{1,5},{9... | collective-permute-start | bytes 1081352 | tf_op jit(solution)/shard_map/ppermute | solution.py:389
  498.8 26.5 %collective-permute-start.117 = (bf16[128,2816]{1,0:T(8,128)(2,1)S(1)}, bf16[128,2816]{1,0:T(8,128)(2,1)S(1)}, u32[]{:S(2)}, u32[]{:S(2)}) collective-permute-start(bf16[128,2816]{1,0:T(8,128)(2,1)S(1)} %get-tuple-element.133), channel_id=1, source_target_pairs={{0,4},{8,0},{16,8},{24,16},{28,24},{20,28},{12,20},{4,12},{1,5},{9... | collective-permute-start | bytes 2162696 | tf_op jit(solution)/shard_map/ppermute | solution.py:389
  499.2 26.0 %collective-permute-start.110 = (bf16[128,2816]{1,0:T(8,128)(2,1)S(1)}, bf16[128,2816]{1,0:T(8,128)(2,1)S(1)}, u32[]{:S(2)}, u32[]{:S(2)}) collective-permute-start(bf16[128,2816]{1,0:T(8,128)(2,1)S(1)} %get-tuple-element.134), channel_id=1, source_target_pairs={{0,8},{8,16},{16,24},{24,28},{28,20},{20,12},{12,4},{4,0},{1,9},{9... | collective-permute-start | bytes 2162696 | tf_op jit(solution)/shard_map/ppermute | solution.py:388
  501.0 59.0 %collective-permute-start.69 = (bf16[2,256,2048]{2,1,0:T(8,128)(2,1)S(1)}, bf16[2,256,2048]{2,1,0:T(8,128)(2,1)S(1)}, u32[]{:S(2)}, u32[]{:S(2)}) collective-permute-start(bf16[2,256,2048]{2,1,0:T(8,128)(2,1)S(1)} %dynamic-slice_bitcast_fusion.1), channel_id=1, source_target_pairs={{0,1},{1,0},{2,3},{3,2},{4,5},{5,4},{6,7},{7,6},{8,9},{9,8},{10,11... | collective-permute-start | bytes 6291464 | tf_op jit(solution)/shard_map/ppermute | solution.py:411
  510.0 21.2 %collective-permute-start.127 = (bf16[128,1408]{1,0:T(8,128)(2,1)S(1)}, bf16[128,1408]{1,0:T(8,128)(2,1)S(1)}, u32[]{:S(2)}, u32[]{:S(2)}) collective-permute-start(bf16[128,1408]{1,0:T(8,128)(2,1)S(1)} %get-tuple-element.146), channel_id=1, source_target_pairs={{0,8},{8,16},{16,24},{24,28},{28,20},{20,12},{12,4},{4,0},{1,9},{9... | collective-permute-start | bytes 1081352 | tf_op jit(solution)/shard_map/ppermute | solution.py:388
  512.1 20.9 %collective-permute-start.134 = (bf16[128,1408]{1,0:T(8,128)(2,1)S(1)}, bf16[128,1408]{1,0:T(8,128)(2,1)S(1)}, u32[]{:S(2)}, u32[]{:S(2)}) collective-permute-start(bf16[128,1408]{1,0:T(8,128)(2,1)S(1)} %get-tuple-element.147), channel_id=1, source_target_pairs={{0,4},{8,0},{16,8},{24,16},{28,24},{20,28},{12,20},{4,12},{1,5},{9... | collective-permute-start | bytes 1081352 | tf_op jit(solution)/shard_map/ppermute | solution.py:389
  525.6 21.1 %collective-permute-start.118 = (bf16[128,2816]{1,0:T(8,128)(2,1)S(1)}, bf16[128,2816]{1,0:T(8,128)(2,1)S(1)}, u32[]{:S(2)}, u32[]{:S(2)}) collective-permute-start(bf16[128,2816]{1,0:T(8,128)(2,1)S(1)} %get-tuple-element.131), channel_id=1, source_target_pairs={{0,4},{8,0},{16,8},{24,16},{28,24},{20,28},{12,20},{4,12},{1,5},{9... | collective-permute-start | bytes 2162696 | tf_op jit(solution)/shard_map/ppermute | solution.py:389
  525.9 20.8 %collective-permute-start.111 = (bf16[128,2816]{1,0:T(8,128)(2,1)S(1)}, bf16[128,2816]{1,0:T(8,128)(2,1)S(1)}, u32[]{:S(2)}, u32[]{:S(2)}) collective-permute-start(bf16[128,2816]{1,0:T(8,128)(2,1)S(1)} %get-tuple-element.132), channel_id=1, source_target_pairs={{0,8},{8,16},{16,24},{24,28},{28,20},{20,12},{12,4},{4,0},{1,9},{9... | collective-permute-start | bytes 2162696 | tf_op jit(solution)/shard_map/ppermute | solution.py:388
  531.2 30.1 %collective-permute-start.65 = (bf16[2,256,2048]{2,1,0:T(8,128)(2,1)S(1)}, bf16[2,256,2048]{2,1,0:T(8,128)(2,1)S(1)}, u32[]{:S(2)}, u32[]{:S(2)}) collective-permute-start(bf16[2,256,2048]{2,1,0:T(8,128)(2,1)S(1)} %dynamic-slice_bitcast_fusion.2), channel_id=1, source_target_pairs={{0,1},{1,0},{2,3},{3,2},{4,5},{5,4},{6,7},{7,6},{8,9},{9,8},{10,11... | collective-permute-start | bytes 6291464 | tf_op jit(solution)/shard_map/ppermute | solution.py:411
  533.2 19.3 %collective-permute-start.128 = (bf16[128,1408]{1,0:T(8,128)(2,1)S(1)}, bf16[128,1408]{1,0:T(8,128)(2,1)S(1)}, u32[]{:S(2)}, u32[]{:S(2)}) collective-permute-start(bf16[128,1408]{1,0:T(8,128)(2,1)S(1)} %get-tuple-element.144), channel_id=1, source_target_pairs={{0,8},{8,16},{16,24},{24,28},{28,20},{20,12},{12,4},{4,0},{1,9},{9... | collective-permute-start | bytes 1081352 | tf_op jit(solution)/shard_map/ppermute | solution.py:388
  548.1 33.8 %collective-permute-start.119 = (bf16[128,2816]{1,0:T(8,128)(2,1)}, bf16[128,2816]{1,0:T(8,128)(2,1)}, u32[]{:S(2)}, u32[]{:S(2)}) collective-permute-start(bf16[128,2816]{1,0:T(8,128)(2,1)} %get-tuple-element.129), channel_id=1, source_target_pairs={{0,4},{8,0},{16,8},{24,16},{28,24},{20,28},{12,20},{4,12},{1,5},{9... | collective-permute-start | bytes 2162696 | tf_op jit(solution)/shard_map/ppermute | solution.py:389
  552.4 29.5 %collective-permute-start.112 = (bf16[128,2816]{1,0:T(8,128)(2,1)}, bf16[128,2816]{1,0:T(8,128)(2,1)}, u32[]{:S(2)}, u32[]{:S(2)}) collective-permute-start(bf16[128,2816]{1,0:T(8,128)(2,1)} %get-tuple-element.130), channel_id=1, source_target_pairs={{0,8},{8,16},{16,24},{24,28},{28,20},{20,12},{12,4},{4,0},{1,9},{9... | collective-permute-start | bytes 2162696 | tf_op jit(solution)/shard_map/ppermute | solution.py:388
  558.2 18.4 %collective-permute-start.129 = (bf16[128,1408]{1,0:T(8,128)(2,1)S(1)}, bf16[128,1408]{1,0:T(8,128)(2,1)S(1)}, u32[]{:S(2)}, u32[]{:S(2)}) collective-permute-start(bf16[128,1408]{1,0:T(8,128)(2,1)S(1)} %get-tuple-element.142), channel_id=1, source_target_pairs={{0,8},{8,16},{16,24},{24,28},{28,20},{20,12},{12,4},{4,0},{1,9},{9... | collective-permute-start | bytes 1081352 | tf_op jit(solution)/shard_map/ppermute | solution.py:388
  560.0 18.5 %collective-permute-start.136 = (bf16[128,1408]{1,0:T(8,128)(2,1)S(1)}, bf16[128,1408]{1,0:T(8,128)(2,1)S(1)}, u32[]{:S(2)}, u32[]{:S(2)}) collective-permute-start(bf16[128,1408]{1,0:T(8,128)(2,1)S(1)} %get-tuple-element.143), channel_id=1, source_target_pairs={{0,4},{8,0},{16,8},{24,16},{28,24},{20,28},{12,20},{4,12},{1,5},{9... | collective-permute-start | bytes 1081352 | tf_op jit(solution)/shard_map/ppermute | solution.py:389
  562.6 45.0 %collective-permute-start.70 = (bf16[1,256,2048]{2,1,0:T(8,128)(2,1)S(1)}, bf16[1,256,2048]{2,1,0:T(8,128)(2,1)S(1)}, u32[]{:S(2)}, u32[]{:S(2)}) collective-permute-start(bf16[1,256,2048]{2,1,0:T(8,128)(2,1)S(1)} %dynamic-slice_convert_fusion.1), channel_id=1, source_target_pairs={{0,2},{1,3},{2,0},{3,1},{4,6},{5,7},{6,4},{7,5},{8,10},{9,11},{10,... | collective-permute-start | bytes 3145736 | tf_op jit(solution)/shard_map/ppermute | solution.py:411
  583.7 20.4 %collective-permute-start.120 = (bf16[128,2816]{1,0:T(8,128)(2,1)S(1)}, bf16[128,2816]{1,0:T(8,128)(2,1)S(1)}, u32[]{:S(2)}, u32[]{:S(2)}) collective-permute-start(bf16[128,2816]{1,0:T(8,128)(2,1)S(1)} %get-tuple-element.127), channel_id=1, source_target_pairs={{0,4},{8,0},{16,8},{24,16},{28,24},{20,28},{12,20},{4,12},{1,5},{9... | collective-permute-start | bytes 2162696 | tf_op jit(solution)/shard_map/ppermute | solution.py:389
  584.0 20.1 %collective-permute-start.113 = (bf16[128,2816]{1,0:T(8,128)(2,1)S(1)}, bf16[128,2816]{1,0:T(8,128)(2,1)S(1)}, u32[]{:S(2)}, u32[]{:S(2)}) collective-permute-start(bf16[128,2816]{1,0:T(8,128)(2,1)S(1)} %get-tuple-element.128), channel_id=1, source_target_pairs={{0,8},{8,16},{16,24},{24,28},{28,20},{20,12},{12,4},{4,0},{1,9},{9... | collective-permute-start | bytes 2162696 | tf_op jit(solution)/shard_map/ppermute | solution.py:388
  591.3 18.2 %collective-permute-start.66 = (bf16[1,256,2048]{2,1,0:T(8,128)(2,1)S(1)}, bf16[1,256,2048]{2,1,0:T(8,128)(2,1)}, u32[]{:S(2)}, u32[]{:S(2)}) collective-permute-start(bf16[1,256,2048]{2,1,0:T(8,128)(2,1)S(1)} %dynamic-slice_convert_fusion.2), channel_id=1, source_target_pairs={{0,2},{1,3},{2,0},{3,1},{4,6},{5,7},{6,4},{7,5},{8,10},{9,11},{10,... | collective-permute-start | bytes 3145736 | tf_op jit(solution)/shard_map/ppermute | solution.py:411
  614.0 26.4 %collective-permute-start.71 = (bf16[1,256,2048]{2,1,0:T(8,128)(2,1)}, bf16[1,256,2048]{2,1,0:T(8,128)(2,1)}, u32[]{:S(2)}, u32[]{:S(2)}) collective-permute-start(bf16[1,256,2048]{2,1,0:T(8,128)(2,1)} %get-tuple-element.109), channel_id=1, source_target_pairs={{0,2},{1,3},{2,0},{3,1},{4,6},{5,7},{6,4},{7,5},{8,10},{9,11},{10,... | collective-permute-start | bytes 3145736 | tf_op jit(solution)/shard_map/ppermute | solution.py:423
  617.2 39.1 %collective-permute-start.67 = (bf16[1,256,2048]{2,1,0:T(8,128)(2,1)}, bf16[1,256,2048]{2,1,0:T(8,128)(2,1)S(1)}, u32[]{:S(2)}, u32[]{:S(2)}) collective-permute-start(bf16[1,256,2048]{2,1,0:T(8,128)(2,1)} %get-tuple-element.189), channel_id=1, source_target_pairs={{0,2},{1,3},{2,0},{3,1},{4,6},{5,7},{6,4},{7,5},{8,10},{9,11},{10,... | collective-permute-start | bytes 3145736 | tf_op jit(solution)/shard_map/ppermute | solution.py:423
  622.9 19.5 %collective-permute-start.122 = (bf16[128,2816]{1,0:T(8,128)(2,1)S(1)}, bf16[128,2816]{1,0:T(8,128)(2,1)S(1)}, u32[]{:S(2)}, u32[]{:S(2)}) collective-permute-start(bf16[128,2816]{1,0:T(8,128)(2,1)S(1)} %get-tuple-element.123), channel_id=1, source_target_pairs={{0,4},{8,0},{16,8},{24,16},{28,24},{20,28},{12,20},{4,12},{1,5},{9... | collective-permute-start | bytes 2162696 | tf_op jit(solution)/shard_map/ppermute | solution.py:389
  623.8 18.6 %collective-permute-start.115 = (bf16[128,2816]{1,0:T(8,128)(2,1)S(1)}, bf16[128,2816]{1,0:T(8,128)(2,1)S(1)}, u32[]{:S(2)}, u32[]{:S(2)}) collective-permute-start(bf16[128,2816]{1,0:T(8,128)(2,1)S(1)} %get-tuple-element.124), channel_id=1, source_target_pairs={{0,8},{8,16},{16,24},{24,28},{28,20},{20,12},{12,4},{4,0},{1,9},{9... | collective-permute-start | bytes 2162696 | tf_op jit(solution)/shard_map/ppermute | solution.py:388
  642.3 24.5 %collective-permute-start.72 = (bf16[2,256,2048]{2,1,0:T(8,128)(2,1)S(1)}, bf16[2,256,2048]{2,1,0:T(8,128)(2,1)S(1)}, u32[]{:S(2)}, u32[]{:S(2)}) collective-permute-start(bf16[2,256,2048]{2,1,0:T(8,128)(2,1)S(1)} %maximum_bitcast_fusion.2), channel_id=1, source_target_pairs={{0,1},{1,0},{2,3},{3,2},{4,5},{5,4},{6,7},{7,6},{8,9},{9,8},{10,11... | collective-permute-start | bytes 6291464 | tf_op jit(solution)/shard_map/ppermute | solution.py:423
  644.2 18.5 %collective-permute-start.123 = (bf16[128,2816]{1,0:T(8,128)(2,1)S(1)}, bf16[128,2816]{1,0:T(8,128)(2,1)S(1)}, u32[]{:S(2)}, u32[]{:S(2)}) collective-permute-start(bf16[128,2816]{1,0:T(8,128)(2,1)S(1)} %get-tuple-element.121), channel_id=1, source_target_pairs={{0,4},{8,0},{16,8},{24,16},{28,24},{20,28},{12,20},{4,12},{1,5},{9... | collective-permute-start | bytes 2162696 | tf_op jit(solution)/shard_map/ppermute | solution.py:389
  645.1 18.4 %collective-permute-start.116 = (bf16[128,2816]{1,0:T(8,128)(2,1)S(1)}, bf16[128,2816]{1,0:T(8,128)(2,1)S(1)}, u32[]{:S(2)}, u32[]{:S(2)}) collective-permute-start(bf16[128,2816]{1,0:T(8,128)(2,1)S(1)} %get-tuple-element.122), channel_id=1, source_target_pairs={{0,8},{8,16},{16,24},{24,28},{28,20},{20,12},{12,4},{4,0},{1,9},{9... | collective-permute-start | bytes 2162696 | tf_op jit(solution)/shard_map/ppermute | solution.py:388
  658.0 29.0 %collective-permute-start.68 = (bf16[2,256,2048]{2,1,0:T(8,128)(2,1)}, bf16[2,256,2048]{2,1,0:T(8,128)(2,1)}, u32[]{:S(2)}, u32[]{:S(2)}) collective-permute-start(bf16[2,256,2048]{2,1,0:T(8,128)(2,1)} %maximum_bitcast_fusion.1), channel_id=1, source_target_pairs={{0,1},{1,0},{2,3},{3,2},{4,5},{5,4},{6,7},{7,6},{8,9},{9,8},{10,11... | collective-permute-start | bytes 6291464 | tf_op jit(solution)/shard_map/ppermute | solution.py:423
  703.6 104.9 %collective-permute-start.96 = (bf16[128,1024]{0,1:T(8,128)(2,1)}, bf16[128,1024]{0,1:T(8,128)(2,1)}, u32[]{:S(2)}, u32[]{:S(2)}) collective-permute-start(bf16[128,1024]{0,1:T(8,128)(2,1)} %get-tuple-element.173), channel_id=1, source_target_pairs={{0,8},{8,16},{16,24},{24,28},{28,20},{20,12},{12,4},{4,0},{1,9},{9... | collective-permute-start | bytes 786440 | tf_op jit(solution)/shard_map/ppermute | solution.py:388
  737.3 62.9 %collective-permute-start.108 = (bf16[128,1024]{0,1:T(8,128)(2,1)}, bf16[128,1024]{0,1:T(8,128)(2,1)}, u32[]{:S(2)}, u32[]{:S(2)}) collective-permute-start(bf16[128,1024]{0,1:T(8,128)(2,1)} %add_convert_fusion.38), channel_id=1, source_target_pairs={{0,4},{8,0},{16,8},{24,16},{28,24},{20,28},{12,20},{4,12},{1,5},{9... | collective-permute-start | bytes 786440 | tf_op jit(solution)/shard_map/ppermute | solution.py:389
  800.1 36.3 %collective-permute-start.78 = (bf16[2,256,2048]{2,1,0:T(8,128)(2,1)S(1)}, bf16[2,256,2048]{2,1,0:T(8,128)(2,1)S(1)}, u32[]{:S(2)}, u32[]{:S(2)}) collective-permute-start(bf16[2,256,2048]{2,1,0:T(8,128)(2,1)S(1)} %dynamic-slice_bitcast_fusion), channel_id=1, source_target_pairs={{0,1},{1,0},{2,3},{3,2},{4,5},{5,4},{6,7},{7,6},{8,9},{9,8},{10,11... | collective-permute-start | bytes 6291464 | tf_op jit(solution)/shard_map/ppermute | solution.py:411
  837.4 19.9 %collective-permute-start.79 = (bf16[1,256,2048]{2,1,0:T(8,128)(2,1)S(1)}, bf16[1,256,2048]{2,1,0:T(8,128)(2,1)S(1)}, u32[]{:S(2)}, u32[]{:S(2)}) collective-permute-start(bf16[1,256,2048]{2,1,0:T(8,128)(2,1)S(1)} %dynamic-slice_convert_fusion), channel_id=1, source_target_pairs={{0,2},{1,3},{2,0},{3,1},{4,6},{5,7},{6,4},{7,5},{8,10},{9,11},{10,... | collective-permute-start | bytes 3145736 | tf_op jit(solution)/shard_map/ppermute | solution.py:411
  858.8 17.7 %collective-permute-start.80 = (bf16[1,256,2048]{2,1,0:T(8,128)(2,1)S(1)}, bf16[1,256,2048]{2,1,0:T(8,128)(2,1)S(1)}, u32[]{:S(2)}, u32[]{:S(2)}) collective-permute-start(bf16[1,256,2048]{2,1,0:T(8,128)(2,1)S(1)} %fusion.39), channel_id=1, source_target_pairs={{0,2},{1,3},{2,0},{3,1},{4,6},{5,7},{6,4},{7,5},{8,10},{9,11},{10,... | collective-permute-start | bytes 3145736 | tf_op jit(solution)/shard_map/ppermute | solution.py:423
  872.0 23.1 %collective-permute-start.102 = (bf16[128,1024]{0,1:T(8,128)(2,1)}, bf16[128,1024]{0,1:T(8,128)(2,1)}, u32[]{:S(2)}, u32[]{:S(2)}) collective-permute-start(bf16[128,1024]{0,1:T(8,128)(2,1)} %add_convert_fusion.43), channel_id=1, source_target_pairs={{0,8},{8,16},{16,24},{24,28},{28,20},{20,12},{12,4},{4,0},{1,9},{9... | collective-permute-start | bytes 786440 | tf_op jit(solution)/shard_map/ppermute | solution.py:388
  878.4 61.1 %collective-permute-start.81 = (bf16[2,256,2048]{2,1,0:T(8,128)(2,1)}, bf16[2,256,2048]{2,1,0:T(8,128)(2,1)}, u32[]{:S(2)}, u32[]{:S(2)}) collective-permute-start(bf16[2,256,2048]{2,1,0:T(8,128)(2,1)} %maximum_bitcast_fusion.3), channel_id=1, source_target_pairs={{0,1},{1,0},{2,3},{3,2},{4,5},{5,4},{6,7},{7,6},{8,9},{9,8},{10,11... | collective-permute-start | bytes 6291464 | tf_op jit(solution)/shard_map/ppermute | solution.py:423
  (153 other events, 2299.8 us)

commit v3 on v2

--- a/solution.py
+++ b/solution.py
@@ -16,6 +16,7 @@
 NT = (((1,), (1,)), ((), ()))
 TN = (((0,), (0,)), ((), ()))
 VMEM_BYTES = 48 * 1024 * 1024
+MESH = pl.DeviceIdType.MESH
 
 
 def product(left, right, dims, precision=None):
@@ -312,6 +313,166 @@
     )
 
 
+def place_of(table, index):
+    found = jnp.int32(table[0])
+    for i, entry in enumerate(table[1:], 1):
+        found = jnp.where(index == i, jnp.int32(entry), found)
+    return found
+
+
+def block_at(order, distance):
+    count = len(order)
+    place = place_of([order.index(i) for i in range(count)], lax.axis_index("seq"))
+    return place_of(order, lax.rem(place + distance + count, count))
+
+
+def greet(axis, count):
+    barrier, mine = pltpu.get_barrier_semaphore(), lax.axis_index(axis)
+    for d in range(1, count):
+        pl.semaphore_signal(
+            barrier, inc=1, device_id={axis: lax.rem(mine + d, count)}, device_id_type=MESH
+        )
+    pl.semaphore_wait(barrier, count - 1)
+
+
+def enter_kernel(
+    order, input_ref, block_ref, small_ref,
+    normed_ref, weight_ref, vk_ref, query_ref, gate_ref, low_ref, smalls_ref,
+    total, low_total, send, receive, small_send, small_receive,
+):
+    count = len(order)
+    share, half = block_ref.shape[0], block_ref.shape[0] // 2
+    rows, tile = input_ref.shape[0], 256
+    wide_cols = total.shape[1]
+    low_start = block_ref.shape[1] - low_ref.shape[1]
+    mine = lax.axis_index("seq")
+    right, left = block_at(order, 1), block_at(order, -1)
+    greet("seq", count)
+
+    def hop(step, side):
+        part = pl.ds(side * half, half)
+        if step == 1:
+            source = block_ref.at[part]
+        else:
+            source = weight_ref.at[(count - step + 1) if side == 0 else step - 1, part]
+        return pltpu.make_async_remote_copy(
+            src_ref=source,
+            dst_ref=weight_ref.at[(count - step) if side == 0 else step, part],
+            send_sem=send.at[step - 1, side],
+            recv_sem=receive.at[step - 1, side],
+            device_id={"seq": right if side == 0 else left},
+            device_id_type=MESH,
+        )
+
+    def small_hop(d):
+        return pltpu.make_async_remote_copy(
+            src_ref=small_ref,
+            dst_ref=smalls_ref.at[mine],
+            send_sem=small_send.at[d - 1],
+            recv_sem=small_receive.at[d - 1],
+            device_id={"seq": lax.rem(mine + d, count)},
+            device_id_type=MESH,
+        )
+
+    smalls = [small_hop(d) for d in range(1, count)]
+    for copy in smalls:
+        copy.start()
+    hops = {(step, side): hop(step, side) for step in range(1, count) for side in range(2)}
+    hops[1, 0].start()
+    hops[1, 1].start()
+    smalls_ref[mine] = small_ref[...]
+    weight_ref[0] = block_ref[...]
+
+    scales = []
+    for t in range(rows // tile):
+        field = wide(input_ref[t * tile : (t + 1) * tile])
+        scales.append(root_scale(field))
+
+    def gain_of(slot):
+        owner = block_at(order, slot)
+        return owner, wide(smalls_ref[owner])[:, :share]
+
+    def multiply(first, second, begin):
+        sides = []
+        for slot, side in (first, second):
+            owner, gain = gain_of(slot)
+            sides.append((slot, side, owner, gain[:, side * half : (side + 1) * half]))
+        for t in range(rows // tile):
+            here = slice(t * tile, (t + 1) * tile)
+            parts, blocks = [], []
+            for slot, side, owner, gain in sides:
+                start = pl.multiple_of(owner * share + side * half, half)
+                field = wide(input_ref[here, pl.ds(start, half)])
+                part = narrow(field * scales[t] * gain)
+                column = slot * share + side * half
+                normed_ref[here, column : column + half] = part
+                parts.append(part)
+                blocks.append(weight_ref[slot, side * half : (side + 1) * half, :])
+            left_side = jnp.concatenate(parts, axis=1)
+            right_side = jnp.concatenate(blocks, axis=0)
+            added = product(left_side, right_side[:, :wide_cols], NN)
+            low_added = product(left_side, right_side[:, low_start:], NN)
+            if begin:
+                total[here] = added
+                low_total[here] = low_added
+            else:
+                total[here] += added
+                low_total[here] += low_added
+
+    for copy in smalls:
+        copy.wait_recv()
+    multiply((0, 0), (0, 1), True)
+    for step in range(1, count):
+        for side in range(2):
+            hops[step, side].wait_recv()
+            if step + 1 < count:
+                hops[step + 1, side].start()
+        multiply((count - step, 0), (step, 1), False)
+    vk_cols, query_cols = vk_ref.shape[1], query_ref.shape[1]
+    vk_ref[...] = narrow(total[:, :vk_cols])
+    query_ref[...] = narrow(total[:, vk_cols : vk_cols + query_cols])
+    gate_ref[...] = total[:, vk_cols + query_cols :]
+    low_ref[...] = low_total[...]
+    for copy in smalls + list(hops.values()):
+        copy.wait_send()
+
+
+def enter(inputs, block, small, rank):
+    count = lax.axis_size("seq")
+    rows, width = inputs.shape
+    cols = DV + DK + DK + DV
+    out_shape = [
+        shape_of(BF16, rows, width),
+        shape_of(BF16, count, *block.shape),
+        shape_of(BF16, rows, DV + DK),
+        shape_of(BF16, rows, DK),
+        shape_of(F32, rows, DV),
+        shape_of(F32, rows, rank),
+        shape_of(BF16, count, *small.shape),
+    ]
+    steps = count - 1
+    return pl.pallas_call(
+        functools.partial(enter_kernel, ring_order(count)),
+        in_specs=[pl.BlockSpec(memory_space=pltpu.VMEM)] * 3,
+        out_specs=[pl.BlockSpec(memory_space=pltpu.VMEM)] * 7,
+        out_shape=out_shape,
+        scratch_shapes=[
+            pltpu.VMEM((rows, cols), F32),
+            pltpu.VMEM((rows, rank), F32),
+            pltpu.SemaphoreType.DMA((steps, 2)),
+            pltpu.SemaphoreType.DMA((steps, 2)),
+            pltpu.SemaphoreType.DMA((steps,)),
+            pltpu.SemaphoreType.DMA((steps,)),
+        ],
+        cost_estimate=pl.CostEstimate(
+            flops=2 * rows * width * cols, bytes_accessed=400_000_000, transcendentals=0
+        ),
+        compiler_params=pltpu.CompilerParams(
+            collective_id=0, has_side_effects=True, vmem_limit_bytes=VMEM_BYTES
+        ),
+    )(inputs, block, small)
+
+
 def matmul(left, right):
     return product(left, right, NN)
 
@@ -503,28 +664,37 @@
     chunks = block // CHUNK
     rank, share = decay_down.shape[1], attn_gain.shape[0]
     hidden = ffn_gate.shape[1]
-    mixed_cols, rank_end = DV + DK, DV + DK + rank
-
-    sizes = [head_gain.size, decay_bias.size, decay_up.size]
-    small = jnp.concatenate([head_gain, decay_bias, decay_up.reshape(-1)])
-    extra = columns_of(small, share)
-    block_one = jnp.concatenate(
-        [value_weight, key_weight, decay_down, attn_gain[:, None], ffn_gain[:, None], extra], axis=1
-    )
-    block_two = jnp.concatenate([query_weight, gate_weight, out_weight.T], axis=1)
-    first, mark = ring.gather(block_one)
-    second, mark = ring.gather(block_two, mark)
+
+    smalls = [attn_gain, ffn_gain, head_gain, decay_bias, decay_up.reshape(-1)]
+    ends = [sum(part.size for part in smalls[: i + 1]) for i in range(len(smalls))]
+    small = jnp.pad(jnp.concatenate(smalls), (0, -ends[-1] % 128))[None]
+    shard = jnp.concatenate(
+        [value_weight, key_weight, query_weight, gate_weight, out_weight.T, decay_down], axis=1
+    )
+    inputs = layer_in.reshape(rows, width)
+    if share % 256 == 0:
+        normed, weights, value_key, query, gates, low, small = enter(inputs, shard, small, rank)
+        weights = weights.reshape(width, -1)
+        mark = low[:8]
+    else:
+        weights, mark = ring.gather(shard)
+        small = lax.all_gather(small, "seq")
+        gain = wide(small[:, 0, :share]).reshape(width)
+        normed = ring.near(narrow(wide(inputs) * root_scale(wide(inputs)) * gain), 1)
+        projected = matmul(normed, weights)
+        value_key, query = narrow(projected[:, : DV + DK]), narrow(projected[:, DV + DK : DV + 2 * DK])
+        gates, low = projected[:, DV + 2 * DK : 2 * DV + 2 * DK], projected[:, -rank:]
     third, mark = ring.gather(jnp.concatenate([ffn_gate, ffn_up], axis=1), mark)
     fdown_t, mark = ring.gather(ffn_down.T, mark)
-    vk_all, down_all = first[:, :mixed_cols], first[:, mixed_cols:rank_end]
-    gain_one, gain_two = wide(first[:, rank_end]), wide(first[:, rank_end + 1])
-    small = first[:, rank_end + 2 :].reshape(count, share, -1)
-    small = ring.home(jnp.swapaxes(small, 1, 2).reshape(count, -1), 0)
-    gain_head = wide(small[:, : sizes[0]]).reshape(1, DV)
-    bias_all = wide(small[:, sizes[0] : sizes[0] + sizes[1]]).reshape(1, DK)
-    up_all = small[:, sizes[0] + sizes[1] : sum(sizes)].reshape(count, rank, -1)
+    projections = weights[:, : 2 * DV + 2 * DK]
+    out_t, down_all = weights[:, 2 * DV + 2 * DK : -rank], weights[:, -rank:]
+    small = small[:, 0]
+    gain_one = wide(ring.near(small[:, : ends[0]], 0)).reshape(width)
+    gain_two = wide(ring.near(small[:, ends[0] : ends[1]], 0)).reshape(width)
+    gain_head = wide(small[:, ends[1] : ends[2]]).reshape(1, DV)
+    bias_all = wide(small[:, ends[2] : ends[3]]).reshape(1, DK)
+    up_all = small[:, ends[3] : ends[4]].reshape(count, rank, -1)
     up_all = wide(jnp.swapaxes(up_all, 0, 1).reshape(rank, DK))
-    query_all, gate_all, out_t = second[:, :DK], second[:, DK:mixed_cols], second[:, mixed_cols:]
 
     starts = seg_starts.reshape(batch, chunks, CHUNK).astype(jnp.float32)
     places = jnp.arange(CHUNK)
@@ -532,23 +702,18 @@
     marks = jnp.einsum("bcs,ts->bct", starts, lower, precision=HIGH)
     column, row = marks.reshape(batch, block, 1), jnp.swapaxes(marks, 0, 1)[:, :, None, :]
 
-    inputs = ring.near(layer_in.reshape(rows, width), 1)
     grad_rows = ring.near(out_grad.reshape(rows, width), 1)
     head = lax.axis_index("head")
     quarter = rows // lax.axis_size("head")
-    inputs_own = wide(lax.dynamic_slice_in_dim(inputs, head * quarter, quarter, 0))
+    inputs_own = lax.dynamic_slice_in_dim(inputs, head * quarter, quarter, 0)
+    inputs_own = wide(ring.near(inputs_own, 1))
     grad_own = wide(lax.dynamic_slice_in_dim(grad_rows, head * quarter, quarter, 0))
-    scale_one = root_scale(wide(inputs))
-    normed = narrow(wide(inputs) * scale_one * gain_one)
 
     def tokens(field):
         return field.reshape(batch, block, field.shape[-1])
 
-    value_key = tokens(narrow(matmul(normed, vk_all)))
-    low = tokens(matmul(normed, down_all))
+    value_key, query, gates, low = map(tokens, (value_key, query, gates, low))
     run, slope, state, total = local_states(value_key, low, up_all, bias_all, column)
-    query = tokens(narrow(matmul(normed, query_all)))
-    gates = tokens(matmul(normed, gate_all))
     state_in = entering(state, total, False)
     heads, mixed, states = mix(query, value_key, run, column, row, state_in, gates, gain_head)
     heads = heads.reshape(rows, DV)
@@ -585,21 +750,21 @@
     grad_out = matmul_tn(d_attn, heads)
     grad_gate = matmul_tn(normed, d_gates)
     grad_fourth = ring.scatter(narrow(jnp.concatenate([grad_gate, grad_out], axis=1)))
-    d_first = jnp.concatenate(
-        [d_value.reshape(rows, DV), d_key.reshape(rows, DK), narrow(d_low.reshape(rows, rank))],
-        axis=1,
-    )
-    d_query = d_query.reshape(rows, DK)
+    d_low = narrow(d_low.reshape(rows, rank))
+    d_last = jnp.concatenate(
+        [d_value.reshape(rows, DV), d_key.reshape(rows, DK), d_query.reshape(rows, DK)], axis=1
+    )
     d_normed_part = (
-        matmul_nt(d_first, first[:, :rank_end])
-        + matmul_nt(d_query, query_all)
-        + matmul_nt(d_gates, gate_all)
+        matmul_nt(jnp.concatenate([d_last, d_gates], axis=1), projections)
+        + matmul_nt(d_low, down_all)
     )
     d_normed = head_scatter(narrow(d_normed_part))
-    unit_own = inputs_own * root_scale(inputs_own)
-    grad_gain_one = jnp.sum(d_normed * unit_own, axis=0)
-    d_unit = norm_back(d_normed * gain_one, unit_own, root_scale(inputs_own))
+    scale_own = root_scale(inputs_own)
+    unit_own = inputs_own * scale_own
+    d_unit = norm_back(d_normed * gain_one, unit_own, scale_own)
     input_grad = ring.home(head_gather(narrow(d_resid + d_unit)), 1)
+    unit_all = ring.near(wide(inputs) * root_scale(wide(inputs)), 1)
+    grad_gain_one = jnp.sum(d_normed_part * unit_all, axis=0)
 
     small = jnp.concatenate(
         [
@@ -610,41 +775,40 @@
         axis=1,
     )
     small = columns_of(ring.near(small, 0), share).reshape(width, -1)
-    grad_last = jnp.concatenate(
-        [
-            matmul_tn(normed, d_first),
-            matmul_tn(normed, d_query),
-            small,
-            grad_gain_two[:, None],
-        ],
-        axis=1,
-    )
+    small = jnp.concatenate([grad_gain_one[:, None], grad_gain_two[:, None], small], axis=1)
+    used = d_last.shape[1] + rank
+    spare = -(used + small.shape[1]) % 128
+    d_last = jnp.concatenate(
+        [d_last, d_low, jnp.zeros((rows, small.shape[1] + spare), BF16)], axis=1
+    )
+    grad_last = matmul_tn(normed, d_last) + jnp.pad(small, ((0, 0), (used, spare)))
     grad_last = ring.scatter(narrow(grad_last))
-    gain_one_sum = lax.psum(ring.home(grad_gain_one, 0), ("seq", "head"))
-    gain_one_sum = lax.dynamic_slice_in_dim(gain_one_sum, lax.axis_index("seq") * share, share)
-    small = jnp.swapaxes(grad_last[:, rank_end + DK : -1], 0, 1).reshape(-1)
-    shared = lax.psum(
-        (
-            grad_last[:, mixed_cols:rank_end],
-            grad_last[:, -1],
-            small[: sizes[0]],
-        ),
-        "head",
-    )
+    shared = grad_last[:, used - rank :]
+    distance = 1
+    while distance < lax.axis_size("head"):
+        shared = shared + lax.ppermute(shared, "head", swap("head", distance))
+        distance *= 2
+
+    def lone(field):
+        return jnp.swapaxes(field[:, rank + 2 : rank + small.shape[1]], 0, 1).reshape(-1)
+
+    own = lone(grad_last[:, used - rank :])
+    bounds = [0, head_gain.size, head_gain.size + decay_bias.size]
+    bounds.append(bounds[2] + decay_up.size)
     return (
         layer_out.reshape(batch, block, width),
         input_grad.reshape(batch, block, width),
-        gain_one_sum,
-        grad_last[:, rank_end : rank_end + DK],
-        grad_last[:, DV:mixed_cols],
+        shared[:, rank],
+        grad_last[:, DV + DK : DV + 2 * DK],
+        grad_last[:, DV : DV + DK],
         grad_last[:, :DV],
         grad_fourth[:, :DV],
-        shared[0],
-        small[sizes[0] + sizes[1] : sum(sizes)].reshape(rank, -1),
-        small[sizes[0] : sizes[0] + sizes[1]],
-        shared[2],
+        shared[:, :rank],
+        own[bounds[2] : bounds[3]].reshape(rank, -1),
+        own[bounds[1] : bounds[2]],
+        lone(shared)[: bounds[1]],
         grad_fourth[:, DV:].T,
-        shared[1],
+        shared[:, rank + 1],
         grad_third[:, :hidden],
         grad_third[:, hidden:],
         grad_fdown.T,

time: 958 us -> 889 us (0.928)
  Pallas kernels: 29.5 us -> 131 us
  blocking collectives: 51.6 us -> 0 us
  local copies, waits for them, and re-layouts: 167 us -> 133 us
  waiting for transfers between devices: 296 us -> 263 us
  starting transfers between devices: 148 us -> 116 us
  between operations: 42.3 us -> 28.7 us
    pallas_call x0 -> x1, Pallas kernels: none -> 101 us  [enter(): pl.pallas_call(functools.partial(enter_kernel, ring_order(count)), in_spe...]
    psum x2 -> x0, blocking collectives: 51.6 us -> none  [the longest x1 39.1 us: shards(): gain_one_sum = lax.psum(ring.home(grad_gain_one, 0), ('seq', 'head'))]
    ppermute x28, waiting for transfers between devices: 74.6 us -> 30.7 us  [scatter(): down = lax.ppermute(down, self.axis, self.left)]
    ppermute x28, waiting for transfers between devices: 60.3 us -> 98.4 us  [scatter(): up = lax.ppermute(up, self.axis, self.right)]
    unnamed x269 -> x250, local copies, waits for them, and re-layouts: 124 us -> 98.9 us
    ppermute x28 -> x14, waiting for transfers between devices: 45.6 us -> 26.7 us  [gather(): down = lax.ppermute(down, self.axis, self.left)]
    ppermute x28 -> x14, starting transfers between devices: 31.1 us -> 14.3 us  [gather(): up = lax.ppermute(up, self.axis, self.right)]
    concatenate x2 -> x4, local copies, waits for them, and re-layouts: 18.8 us -> 6.34 us  [the longest x1 3.21 us: shards(): jnp.concatenate([d_last, d_low, jnp.zeros((rows, small.shape[1] + spare),...]
  transfers between devices with their start and end apart: 138 -> 112, of which waited for: 68 -> 52; matrix products, arithmetic and copies ran while one was open for 34% -> 30% of each run, Pallas kernels for 3% -> 3%
where the time goes in v3:
time: 889 us; the launch traced here: 877 us
  waiting for transfers between devices  263 us (30%)
  matrix products  135 us (15%)
  local copies, waits for them, and re-layouts  133 us (15%)
  Pallas kernels  131 us (15%)
  starting transfers between devices  116 us (13%)
  other arithmetic  70.1 us (8%)
  between operations  28.7 us (3%)
    dot_general x14, matrix products, product(): lax.dot_general(left, right, dims, precision=precision, preferred_element...  135 us
    pallas_call x1, Pallas kernels, enter(): pl.pallas_call(functools.partial(enter_kernel, ring_order(count)), in_spe...  101 us
    unnamed x250, local copies, waits for them, and re-layouts  98.9 us
    ppermute x28, waiting for transfers between devices, scatter(): up = lax.ppermute(up, self.axis, self.right)  98.4 us
    ppermute x14, waiting for transfers between devices, gather(): up = lax.ppermute(up, self.axis, self.right)  39 us
    ppermute x8, waiting for transfers between devices, head_gather(): got = lax.ppermute(held, 'head', swap('head', distance))  36.6 us
    ppermute x28, starting transfers between devices, scatter(): down = lax.ppermute(down, self.axis, self.left)  34.1 us
    ppermute x28, waiting for transfers between devices, scatter(): down = lax.ppermute(down, self.axis, self.left)  30.7 us
  transfers between devices with their start and end apart: 112, of which 52 were waited for; matrix products, arithmetic and copies ran while one was open for 30% of the time, Pallas kernels for 3%

profile of v3, /device:TPU:0, one launch (start us, length us, event | category | flops | bytes accessed | tf_op | source)
XLA Modules:
  0.0 877.4 jit_solution(8611552969103586060)
XLA Ops:
  4.3 2.8 concatenate.127
  10.0 101.2 %shard_map.306 = (bf16[1024,2048]{1,0:T(8,128)(2,1)}, bf16[8,256,2064]{2,1,0:T(8,128)(2,1)}, bf16[1024,768]{1,0:T(8,128)(2,1)S(1)}, bf16[1024,256]{1,0:T(8,128)(...) custom-call(bf16[1024,2048]{1,0:T(8,128)(2,1)} %bitcast.278, ...), custom_call_target="tpu_custom_call" | custom-call | flops 6442450944 | bytes 400000000 | tf_op jit(solution)/shard_map/pallas_call | solution.py:454
  116.1 7.3 shard_map.307
  158.9 3.1 multiply_reduce_fusion.1
  187.6 2.6 copy-done.24
  190.4 3.2 copy-done.36
  204.6 3.5 collective-permute-start.1
  215.9 3.0 collective-permute-start.2
  224.7 3.3 collective-permute-done.2
  228.0 4.3 collective-permute-start.3
  233.1 2.6 collective-permute-done.25
  238.1 3.3 collective-permute-done.3
  260.1 11.4 %collective-permute-done.33 = bf16[128,1408]{0,1:T(8,128)(2,1)} collective-permute-done((bf16[128,1408]{0,1:T(8,128)(2,1)}, bf16[128,1408]{0,1:T(8,128)(2,1)}, u32[]{:S(2)}, u32[]{:S(2)}) %collective-permute-start.33) | collective-permute-done | bytes 360480 | tf_op jit(solution)/shard_map/ppermute | solution.py:531
  275.1 6.4 shard_map.308
  286.0 4.1 convolution_convert_fusion.4
  290.5 10.5 %collective-permute-done.11 = bf16[128,2816]{1,0:T(8,128)(2,1)S(1)} collective-permute-done((bf16[128,2816]{1,0:T(8,128)(2,1)}, bf16[128,2816]{1,0:T(8,128)(2,1)S(1)}, u32[]{:S(2)}, u32[]{:S(2)}) %collective-permute-start.11) | collective-permute-done | bytes 720928 | tf_op jit(solution)/shard_map/ppermute | solution.py:530
  303.0 7.0 collective-permute-done.35
  320.2 8.1 collective-permute-done.36
  333.5 13.3 %collective-permute-done.13 = bf16[128,2816]{1,0:T(8,128)(2,1)S(1)} collective-permute-done((bf16[128,2816]{1,0:T(8,128)(2,1)S(1)}, bf16[128,2816]{1,0:T(8,128)(2,1)S(1)}, u32[]{:S(2)}, u32[]{:S(2)}) %collective-permute-start.13) | collective-permute-done | bytes 720928 | tf_op jit(solution)/shard_map/ppermute | solution.py:530
  349.2 8.5 fusion.78
  357.7 8.3 collective-permute-done.14
  373.8 3.5 collective-permute-done.15
  396.5 12.4 %fusion.2 = f32[1024,1408]{1,0:T(8,128)} fusion(bf16[1024,2048]{1,0:T(8,128)(2,1)S(1)} %bitcast.315, bf16[2048,2816]{1,0:T(8,128)(2,1)} %constant_dynamic-update-slice_fusion.23), kind=kOutput, calls=%fused_computation.38 | convolution fusion | flops 5905580032 | bytes 15728640 | tf_op jit(solution)/shard_map/dot_general | solution.py:23
  409.0 14.7 %multiply_convert_fusion.1 = (bf16[1024,1408]{1,0:T(8,128)(2,1)}, bf16[1024,1408]{1,0:T(8,128)(2,1)}, bf16[1024,1408]{1,0:T(8,128)(2,1)}) fusion(f32[1024,1408]{1,0:T(8,128)S(1)} %bitcast.373, f32[1024,1408]{1,0:T(8,128)} %fusion.2, bf16[1024,2048]{1,0:T(8,128)(2,1)S(1)} %bitcast.316, bf16[2048,2816]{1,0:T(8,128)(2,1)} %constant_dynamic-update-slice_fusion.23), kind=kOutput, calls=%fused_computation.44 | convolution fusion | flops 5928648704 | bytes 30146560 | tf_op jit(solution)/shard_map/dot_general | solution.py:23
  423.7 9.4 %convolution_convert_fusion.1 = bf16[2048,1408]{1,0:T(8,128)(2,1)S(1)} fusion(bf16[1024,2048]{1,0:T(8,128)(2,1)} %dynamic-slice_dynamic-update-slice_fusion.16, bf16[1024,1408]{1,0:T(8,128)(2,1)} %get-tuple-element.157), kind=kOutput, calls=%fused_computation.35 | convolution fusion | flops 5908463616 | bytes 12845056 | tf_op jit(solution)/shard_map/dot_general | solution.py:23
  435.2 18.2 %convolution_convert_fusion.2 = bf16[1024,2048]{1,0:T(8,128)(2,1)} fusion(bf16[2048,2816]{1,0:T(8,128)(2,1)} %constant_dynamic-update-slice_fusion.23, bf16[1024,1408]{1,0:T(8,128)(2,1)} %get-tuple-element.158, bf16[1024,1408]{1,0:T(8,128)(2,1)} %get-tuple-element.156), kind=kOutput, calls=%fused_computation.56 | convolution fusion | flops 11824791552 | bytes 21495808 | tf_op jit(solution)/shard_map/dot_general | solution.py:23
  453.4 18.5 %convolution_convert_fusion = bf16[2048,2816]{1,0:T(8,128)(2,1)} fusion(bf16[1024,2048]{1,0:T(8,128)(2,1)} %bitcast.317, bf16[1024,1408]{1,0:T(8,128)(2,1)} %get-tuple-element.158, bf16[1024,1408]{1,0:T(8,128)(2,1)} %get-tuple-element.156), kind=kOutput, calls=%fused_computation.30 | convolution fusion | flops 11828461568 | bytes 21495808 | tf_op jit(solution)/shard_map/dot_general | solution.py:23
  474.2 9.3 %convolution_convert_fusion.3 = bf16[1024,2048]{1,0:T(8,128)(2,1)S(1)} fusion(bf16[1024,1408]{1,0:T(8,128)(2,1)S(1)} %copy-done.70, bf16[2048,1408]{0,1:T(8,128)(2,1)} %copy-done.62), kind=kOutput, calls=%fused_computation.57 | convolution fusion | flops 5907677184 | bytes 12845056 | tf_op jit(solution)/shard_map/dot_general | solution.py:23
  489.0 6.8 collective-permute-done.100
  498.7 12.5 %collective-permute-done.84 = bf16[128,2816]{1,0:T(8,128)(2,1)S(1)} collective-permute-done((bf16[128,2816]{1,0:T(8,128)(2,1)S(1)}, bf16[128,2816]{1,0:T(8,128)(2,1)S(1)}, u32[]{:S(2)}, u32[]{:S(2)}) %collective-permute-start.84) | collective-permute-done | bytes 720928 | tf_op jit(solution)/shard_map/ppermute | solution.py:549
  514.5 4.4 collective-permute-done.101
  521.9 12.5 %collective-permute-done.85 = bf16[128,2816]{1,0:T(8,128)(2,1)S(1)} collective-permute-done((bf16[128,2816]{1,0:T(8,128)(2,1)S(1)}, bf16[128,2816]{1,0:T(8,128)(2,1)S(1)}, u32[]{:S(2)}, u32[]{:S(2)}) %collective-permute-start.85) | collective-permute-done | bytes 720928 | tf_op jit(solution)/shard_map/ppermute | solution.py:549
  537.7 4.4 collective-permute-done.102
  554.4 9.4 %collective-permute-done.103 = bf16[128,1408]{1,0:T(8,128)(2,1)S(1)} collective-permute-done((bf16[128,1408]{1,0:T(8,128)(2,1)}, bf16[128,1408]{1,0:T(8,128)(2,1)S(1)}, u32[]{:S(2)}, u32[]{:S(2)}) %collective-permute-start.103) | collective-permute-done | bytes 360480 | tf_op jit(solution)/shard_map/ppermute | solution.py:549
  571.2 5.7 collective-permute-done.104
  580.5 9.4 %collective-permute-done.87 = bf16[128,2816]{1,0:T(8,128)(2,1)} collective-permute-done((bf16[128,2816]{1,0:T(8,128)(2,1)}, bf16[128,2816]{1,0:T(8,128)(2,1)}, u32[]{:S(2)}, u32[]{:S(2)}) %collective-permute-start.87) | collective-permute-done | bytes 720928 | tf_op jit(solution)/shard_map/ppermute | solution.py:549
  595.1 2.6 fusion.23
  597.8 3.8 convert_bitcast_fusion
  612.6 15.1 %collective-permute-done.43 = bf16[1,256,2048]{2,1,0:T(8,128)(2,1)S(1)} collective-permute-done((bf16[1,256,2048]{2,1,0:T(8,128)(2,1)S(1)}, bf16[1,256,2048]{2,1,0:T(8,128)(2,1)S(1)}, u32[]{:S(2)}, u32[]{:S(2)}) %collective-permute-start.43) | collective-permute-done | bytes 1048608 | tf_op jit(solution)/shard_map/ppermute | solution.py:584
  632.0 13.1 %collective-permute-done.39 = bf16[1,256,2048]{2,1,0:T(8,128)(2,1)S(1)} collective-permute-done((bf16[1,256,2048]{2,1,0:T(8,128)(2,1)S(1)}, bf16[1,256,2048]{2,1,0:T(8,128)(2,1)S(1)}, u32[]{:S(2)}, u32[]{:S(2)}) %collective-permute-start.39) | collective-permute-done | bytes 1048608 | tf_op jit(solution)/shard_map/ppermute | solution.py:584
  645.7 2.7 collective-permute-done.90
  654.2 5.3 fusion.21.grad_ref
  659.5 5.7 shard_map.309
  675.6 3.5 collective-permute-done.77
  682.2 6.2 collective-permute-done.78
  689.6 4.6 collective-permute-done.46
  695.5 4.3 collective-permute-done.79
  700.1 5.5 collective-permute-done.47
  707.1 4.1 collective-permute-done.80
  712.0 5.0 collective-permute-done.48
  725.6 10.3 %shard_map.310 = (bf16[2,512,256]{2,1,0:T(8,128)(2,1)S(1)}, bf16[2,512,512]{2,1,0:T(8,128)(2,1)S(1)}, bf16[2,512,256]{2,1,0:T(8,128)(2,1)S(1)}, f32[2,512,16]{2,...) custom-call(bf16[2,512,256]{2,1,0:T(8,128)(2,1)S(1)} %bitcast.263, bf16[2,512,768]{2,1,0:T(8,128)(2,1)} %bitcast.257, ...), custom_call_target="tpu_custom_call" | custom-call | flops 1744830464 | bytes 17998848 | tf_op jit(solution)/shard_map/pallas_call | solution.py:218
  738.7 12.2 %fusion = f32[1024,2048]{1,0:T(8,128)} fusion(bf16[2048,2064]{1,0:T(8,128)(2,1)} %bitcast.356, bf16[1024,512]{1,0:T(8,128)(2,1)} %bitcast.277, bf16[1024,256]{1,0:T(8,128)(2,1)} %bitcast.268, bf16[1024,256]{1,0:T(8,128)(2,1)} %bitcast.270, bf16[1024,512]{1,0:T(8,128)(2,1)S(1)} %bitcast.266), kind=kOutput, calls=%fused_computation.36 | convolution fusion | flops 6455033856 | bytes 17825792 | tf_op jit(solution)/shard_map/dot_general | solution.py:23
  751.0 3.2 concatenate.145
  754.2 9.2 %multiply_reduce_fusion = (f32[2048]{0:T(1024)S(1)}, bf16[1024,2048]{1,0:T(8,128)(2,1)}) fusion(f32[1024,2048]{1,0:T(8,128)} %dynamic-slice_dynamic-update-slice_fusion, f32[1024,2048]{1,0:T(8,128)} %fusion, bf16[1024,16]{1,0:T(8,128)(2,1)S(1)} %bitcast.336, bf16[2048,2064]{1,0:T(8,128)(2,1)} %bitcast.357), kind=kOutput, calls=%fused_computation.32 | convolution fusion | flops 75495424 | bytes 21536768 | tf_op jit(solution)/shard_map/dot_general | solution.py:23
  763.8 8.4 add_convert_fusion
  789.0 2.8 collective-permute-done.62
  796.6 5.4 collective-permute-done.56
  808.5 5.4 collective-permute-done.57
  816.1 3.4 collective-permute-done.73
  820.4 7.6 collective-permute-done.51
  834.0 6.7 collective-permute-done.59
  843.0 8.4 collective-permute-done.52
  858.5 4.4 collective-permute-done.76
  866.4 2.7 collective-permute-done.69
  (615 shorter events, 308.3 us)
Async XLA Ops:
  127.0 75.7 %collective-permute-start = (bf16[2,258,256]{2,1,0:T(8,128)(2,1)}, bf16[2,258,256]{2,1,0:T(8,128)(2,1)S(1)}, u32[]{:S(2)}, u32[]{:S(2)}) collective-permute-start(bf16[2,258,256]{2,1,0:T(8,128)(2,1)} %pad_maximum_fusion.13), channel_id=1, source_target_pairs={{0,4},{4,0},{8,12},{12,8},{16,20},{20,16},{24,28},{28,24},{1,5},{5... | collective-permute-start | bytes 792584 | tf_op jit(solution)/shard_map/ppermute | solution.py:612
  131.8 115.7 %collective-permute-start.9 = (bf16[128,2816]{1,0:T(8,128)(2,1)}, bf16[128,2816]{1,0:T(8,128)(2,1)}, u32[]{:S(2)}, u32[]{:S(2)}) collective-permute-start(bf16[128,2816]{1,0:T(8,128)(2,1)} %get-tuple-element.54), channel_id=1, source_target_pairs={{0,8},{8,16},{16,24},{24,28},{28,20},{20,12},{12,4},{4,0},{1,9},{9... | collective-permute-start | bytes 2162696 | tf_op jit(solution)/shard_map/ppermute | solution.py:530
  132.7 117.3 %collective-permute-start.16 = (bf16[128,2816]{1,0:T(8,128)(2,1)}, bf16[128,2816]{1,0:T(8,128)(2,1)}, u32[]{:S(2)}, u32[]{:S(2)}) collective-permute-start(bf16[128,2816]{1,0:T(8,128)(2,1)} %get-tuple-element.55), channel_id=1, source_target_pairs={{0,4},{8,0},{16,8},{24,16},{28,24},{20,28},{12,20},{4,12},{1,5},{9... | collective-permute-start | bytes 2162696 | tf_op jit(solution)/shard_map/ppermute | solution.py:531
  134.7 77.4 %collective-permute-start.23 = (bf16[128,1408]{0,1:T(8,128)(2,1)}, bf16[128,1408]{0,1:T(8,128)(2,1)}, u32[]{:S(2)}, u32[]{:S(2)}) collective-permute-start(bf16[128,1408]{0,1:T(8,128)(2,1)} %get-tuple-element.56), channel_id=1, source_target_pairs={{0,8},{8,16},{16,24},{24,28},{28,20},{20,12},{12,4},{4,0},{1,9},{9... | collective-permute-start | bytes 1081352 | tf_op jit(solution)/shard_map/ppermute | solution.py:530
  135.7 77.1 %collective-permute-start.30 = (bf16[128,1408]{0,1:T(8,128)(2,1)}, bf16[128,1408]{0,1:T(8,128)(2,1)}, u32[]{:S(2)}, u32[]{:S(2)}) collective-permute-start(bf16[128,1408]{0,1:T(8,128)(2,1)} %get-tuple-element.57), channel_id=1, source_target_pairs={{0,4},{8,0},{16,8},{24,16},{28,24},{20,28},{12,20},{4,12},{1,5},{9... | collective-permute-start | bytes 1081352 | tf_op jit(solution)/shard_map/ppermute | solution.py:531
  224.7 25.3 %collective-permute-start.32 = (bf16[128,1408]{0,1:T(8,128)(2,1)}, bf16[128,1408]{0,1:T(8,128)(2,1)}, u32[]{:S(2)}, u32[]{:S(2)}) collective-permute-start(bf16[128,1408]{0,1:T(8,128)(2,1)} %collective-permute-done.31), channel_id=1, source_target_pairs={{0,4},{8,0},{16,8},{24,16},{28,24},{20,28},{12,20},{4,12},{1,5},{9... | collective-permute-start | bytes 1081352 | tf_op jit(solution)/shard_map/ppermute | solution.py:531
  235.7 16.3 %collective-permute-start.26 = (bf16[128,1408]{0,1:T(8,128)(2,1)S(1)}, bf16[128,1408]{0,1:T(8,128)(2,1)}, u32[]{:S(2)}, u32[]{:S(2)}) collective-permute-start(bf16[128,1408]{0,1:T(8,128)(2,1)S(1)} %collective-permute-done.25), channel_id=1, source_target_pairs={{0,8},{8,16},{16,24},{24,28},{28,20},{20,12},{12,4},{4,0},{1,9},{9... | collective-permute-start | bytes 1081352 | tf_op jit(solution)/shard_map/ppermute | solution.py:530
  243.5 15.1 %collective-permute-start.4 = (bf16[2,256,256]{2,1,0:T(8,128)(2,1)}, bf16[2,256,256]{2,1,0:T(8,128)(2,1)}, u32[]{:S(2)}, u32[]{:S(2)}) collective-permute-start(bf16[2,256,256]{2,1,0:T(8,128)(2,1)} %select_convert_fusion.2), channel_id=1, source_target_pairs={{0,4},{4,0},{8,12},{12,8},{16,20},{20,16},{24,28},{28,24},{1,5},{5... | collective-permute-start | bytes 786440 | tf_op jit(solution)/shard_map/ppermute | solution.py:627
  247.5 34.0 %collective-permute-start.10 = (bf16[128,2816]{1,0:T(8,128)(2,1)}, bf16[128,2816]{1,0:T(8,128)(2,1)}, u32[]{:S(2)}, u32[]{:S(2)}) collective-permute-start(bf16[128,2816]{1,0:T(8,128)(2,1)} %collective-permute-done.9), channel_id=1, source_target_pairs={{0,8},{8,16},{16,24},{24,28},{28,20},{20,12},{12,4},{4,0},{1,9},{9... | collective-permute-start | bytes 2162696 | tf_op jit(solution)/shard_map/ppermute | solution.py:530
  250.0 33.0 %collective-permute-start.17 = (bf16[128,2816]{1,0:T(8,128)(2,1)}, bf16[128,2816]{1,0:T(8,128)(2,1)}, u32[]{:S(2)}, u32[]{:S(2)}) collective-permute-start(bf16[128,2816]{1,0:T(8,128)(2,1)} %collective-permute-done.16), channel_id=1, source_target_pairs={{0,4},{8,0},{16,8},{24,16},{28,24},{20,28},{12,20},{4,12},{1,5},{9... | collective-permute-start | bytes 2162696 | tf_op jit(solution)/shard_map/ppermute | solution.py:531
  250.0 21.5 %collective-permute-start.33 = (bf16[128,1408]{0,1:T(8,128)(2,1)}, bf16[128,1408]{0,1:T(8,128)(2,1)}, u32[]{:S(2)}, u32[]{:S(2)}) collective-permute-start(bf16[128,1408]{0,1:T(8,128)(2,1)} %collective-permute-done.32), channel_id=1, source_target_pairs={{0,4},{8,0},{16,8},{24,16},{28,24},{20,28},{12,20},{4,12},{1,5},{9... | collective-permute-start | bytes 1081352 | tf_op jit(solution)/shard_map/ppermute | solution.py:531
  252.1 21.9 %collective-permute-start.27 = (bf16[128,1408]{0,1:T(8,128)(2,1)}, bf16[128,1408]{0,1:T(8,128)(2,1)}, u32[]{:S(2)}, u32[]{:S(2)}) collective-permute-start(bf16[128,1408]{0,1:T(8,128)(2,1)} %collective-permute-done.26), channel_id=1, source_target_pairs={{0,8},{8,16},{16,24},{24,28},{28,20},{20,12},{12,4},{4,0},{1,9},{9... | collective-permute-start | bytes 1081352 | tf_op jit(solution)/shard_map/ppermute | solution.py:530
  281.5 19.4 %collective-permute-start.11 = (bf16[128,2816]{1,0:T(8,128)(2,1)}, bf16[128,2816]{1,0:T(8,128)(2,1)S(1)}, u32[]{:S(2)}, u32[]{:S(2)}) collective-permute-start(bf16[128,2816]{1,0:T(8,128)(2,1)} %collective-permute-done.10), channel_id=1, source_target_pairs={{0,8},{8,16},{16,24},{24,28},{28,20},{20,12},{12,4},{4,0},{1,9},{9... | collective-permute-start | bytes 2162696 | tf_op jit(solution)/shard_map/ppermute | solution.py:530
  283.0 19.3 %collective-permute-start.18 = (bf16[128,2816]{1,0:T(8,128)(2,1)}, bf16[128,2816]{1,0:T(8,128)(2,1)S(1)}, u32[]{:S(2)}, u32[]{:S(2)}) collective-permute-start(bf16[128,2816]{1,0:T(8,128)(2,1)} %collective-permute-done.17), channel_id=1, source_target_pairs={{0,4},{8,0},{16,8},{24,16},{28,24},{20,28},{12,20},{4,12},{1,5},{9... | collective-permute-start | bytes 2162696 | tf_op jit(solution)/shard_map/ppermute | solution.py:531
  283.6 26.4 %collective-permute-start.35 = (bf16[128,1408]{0,1:T(8,128)(2,1)S(1)}, bf16[128,1408]{0,1:T(8,128)(2,1)S(1)}, u32[]{:S(2)}, u32[]{:S(2)}) collective-permute-start(bf16[128,1408]{0,1:T(8,128)(2,1)S(1)} %collective-permute-done.34), channel_id=1, source_target_pairs={{0,4},{8,0},{16,8},{24,16},{28,24},{20,28},{12,20},{4,12},{1,5},{9... | collective-permute-start | bytes 1081352 | tf_op jit(solution)/shard_map/ppermute | solution.py:531
  285.5 25.1 %collective-permute-start.29 = (bf16[128,1408]{0,1:T(8,128)(2,1)S(1)}, bf16[128,1408]{0,1:T(8,128)(2,1)S(1)}, u32[]{:S(2)}, u32[]{:S(2)}) collective-permute-start(bf16[128,1408]{0,1:T(8,128)(2,1)S(1)} %collective-permute-done.28), channel_id=1, source_target_pairs={{0,8},{8,16},{16,24},{24,28},{28,20},{20,12},{12,4},{4,0},{1,9},{9... | collective-permute-start | bytes 1081352 | tf_op jit(solution)/shard_map/ppermute | solution.py:530
  290.4 40.6 %collective-permute-start.5 = (bf16[2,256,2048]{2,1,0:T(8,128)(2,1)S(1)}, bf16[2,256,2048]{2,1,0:T(8,128)(2,1)S(1)}, u32[]{:S(2)}, u32[]{:S(2)}) collective-permute-start(bf16[2,256,2048]{2,1,0:T(8,128)(2,1)S(1)} %dynamic-slice_bitcast_fusion.3), channel_id=1, source_target_pairs={{0,1},{1,0},{2,3},{3,2},{4,5},{5,4},{6,7},{7,6},{8,9},{9,8},{10,11... | collective-permute-start | bytes 6291464 | tf_op jit(solution)/shard_map/ppermute | solution.py:572
  300.9 27.4 %collective-permute-start.12 = (bf16[128,2816]{1,0:T(8,128)(2,1)S(1)}, bf16[128,2816]{1,0:T(8,128)(2,1)S(1)}, u32[]{:S(2)}, u32[]{:S(2)}) collective-permute-start(bf16[128,2816]{1,0:T(8,128)(2,1)S(1)} %collective-permute-done.11), channel_id=1, source_target_pairs={{0,8},{8,16},{16,24},{24,28},{28,20},{20,12},{12,4},{4,0},{1,9},{9... | collective-permute-start | bytes 2162696 | tf_op jit(solution)/shard_map/ppermute | solution.py:530
  302.3 27.0 %collective-permute-start.19 = (bf16[128,2816]{1,0:T(8,128)(2,1)S(1)}, bf16[128,2816]{1,0:T(8,128)(2,1)S(1)}, u32[]{:S(2)}, u32[]{:S(2)}) collective-permute-start(bf16[128,2816]{1,0:T(8,128)(2,1)S(1)} %collective-permute-done.18), channel_id=1, source_target_pairs={{0,4},{8,0},{16,8},{24,16},{28,24},{20,28},{12,20},{4,12},{1,5},{9... | collective-permute-start | bytes 2162696 | tf_op jit(solution)/shard_map/ppermute | solution.py:531
  310.0 18.2 %collective-permute-start.36 = (bf16[128,1408]{0,1:T(8,128)(2,1)S(1)}, bf16[128,1408]{0,1:T(8,128)(2,1)S(1)}, u32[]{:S(2)}, u32[]{:S(2)}) collective-permute-start(bf16[128,1408]{0,1:T(8,128)(2,1)S(1)} %collective-permute-done.35), channel_id=1, source_target_pairs={{0,4},{8,0},{16,8},{24,16},{28,24},{20,28},{12,20},{4,12},{1,5},{9... | collective-permute-start | bytes 1081352 | tf_op jit(solution)/shard_map/ppermute | solution.py:531
  328.4 18.4 %collective-permute-start.13 = (bf16[128,2816]{1,0:T(8,128)(2,1)S(1)}, bf16[128,2816]{1,0:T(8,128)(2,1)S(1)}, u32[]{:S(2)}, u32[]{:S(2)}) collective-permute-start(bf16[128,2816]{1,0:T(8,128)(2,1)S(1)} %collective-permute-done.12), channel_id=1, source_target_pairs={{0,8},{8,16},{16,24},{24,28},{28,20},{20,12},{12,4},{4,0},{1,9},{9... | collective-permute-start | bytes 2162696 | tf_op jit(solution)/shard_map/ppermute | solution.py:530
  329.3 18.0 %collective-permute-start.20 = (bf16[128,2816]{1,0:T(8,128)(2,1)S(1)}, bf16[128,2816]{1,0:T(8,128)(2,1)S(1)}, u32[]{:S(2)}, u32[]{:S(2)}) collective-permute-start(bf16[128,2816]{1,0:T(8,128)(2,1)S(1)} %collective-permute-done.19), channel_id=1, source_target_pairs={{0,4},{8,0},{16,8},{24,16},{28,24},{20,28},{12,20},{4,12},{1,5},{9... | collective-permute-start | bytes 2162696 | tf_op jit(solution)/shard_map/ppermute | solution.py:531
  331.9 36.2 %collective-permute-start.6 = (bf16[1,256,2048]{2,1,0:T(8,128)(2,1)S(1)}, bf16[1,256,2048]{2,1,0:T(8,128)(2,1)S(1)}, u32[]{:S(2)}, u32[]{:S(2)}) collective-permute-start(bf16[1,256,2048]{2,1,0:T(8,128)(2,1)S(1)} %dynamic-slice_convert_fusion.3), channel_id=1, source_target_pairs={{0,2},{1,3},{2,0},{3,1},{4,6},{5,7},{6,4},{7,5},{8,10},{9,11},{10,... | collective-permute-start | bytes 3145736 | tf_op jit(solution)/shard_map/ppermute | solution.py:572
  346.8 19.1 %collective-permute-start.14 = (bf16[128,2816]{1,0:T(8,128)(2,1)S(1)}, bf16[128,2816]{1,0:T(8,128)(2,1)S(1)}, u32[]{:S(2)}, u32[]{:S(2)}) collective-permute-start(bf16[128,2816]{1,0:T(8,128)(2,1)S(1)} %collective-permute-done.13), channel_id=1, source_target_pairs={{0,8},{8,16},{16,24},{24,28},{28,20},{20,12},{12,4},{4,0},{1,9},{9... | collective-permute-start | bytes 2162696 | tf_op jit(solution)/shard_map/ppermute | solution.py:530
  347.2 19.0 %collective-permute-start.21 = (bf16[128,2816]{1,0:T(8,128)(2,1)S(1)}, bf16[128,2816]{1,0:T(8,128)(2,1)S(1)}, u32[]{:S(2)}, u32[]{:S(2)}) collective-permute-start(bf16[128,2816]{1,0:T(8,128)(2,1)S(1)} %collective-permute-done.20), channel_id=1, source_target_pairs={{0,4},{8,0},{16,8},{24,16},{28,24},{20,28},{12,20},{4,12},{1,5},{9... | collective-permute-start | bytes 2162696 | tf_op jit(solution)/shard_map/ppermute | solution.py:531
  366.2 28.2 %collective-permute-start.22 = (bf16[128,2816]{1,0:T(8,128)(2,1)S(1)}, bf16[128,2816]{1,0:T(8,128)(2,1)S(1)}, u32[]{:S(2)}, u32[]{:S(2)}) collective-permute-start(bf16[128,2816]{1,0:T(8,128)(2,1)S(1)} %collective-permute-done.21), channel_id=1, source_target_pairs={{0,4},{8,0},{16,8},{24,16},{28,24},{20,28},{12,20},{4,12},{1,5},{9... | collective-permute-start | bytes 2162696 | tf_op jit(solution)/shard_map/ppermute | solution.py:531
  371.7 15.4 %collective-permute-start.7 = (bf16[1,256,2048]{2,1,0:T(8,128)(2,1)S(1)}, bf16[1,256,2048]{2,1,0:T(8,128)(2,1)S(1)}, u32[]{:S(2)}, u32[]{:S(2)}) collective-permute-start(bf16[1,256,2048]{2,1,0:T(8,128)(2,1)S(1)} %multiply_convert_fusion.3), channel_id=1, source_target_pairs={{0,2},{1,3},{2,0},{3,1},{4,6},{5,7},{6,4},{7,5},{8,10},{9,11},{10,... | collective-permute-start | bytes 3145736 | tf_op jit(solution)/shard_map/ppermute | solution.py:584
  433.1 38.7 %collective-permute-start.105 = (bf16[128,1408]{1,0:T(8,128)(2,1)S(1)}, bf16[128,1408]{1,0:T(8,128)(2,1)S(1)}, u32[]{:S(2)}, u32[]{:S(2)}) collective-permute-start(bf16[128,1408]{1,0:T(8,128)(2,1)S(1)} %get-tuple-element.176), channel_id=1, source_target_pairs={{0,4},{8,0},{16,8},{24,16},{28,24},{20,28},{12,20},{4,12},{1,5},{9... | collective-permute-start | bytes 1081352 | tf_op jit(solution)/shard_map/ppermute | solution.py:550
  435.2 36.7 %collective-permute-start.98 = (bf16[128,1408]{1,0:T(8,128)(2,1)S(1)}, bf16[128,1408]{1,0:T(8,128)(2,1)S(1)}, u32[]{:S(2)}, u32[]{:S(2)}) collective-permute-start(bf16[128,1408]{1,0:T(8,128)(2,1)S(1)} %get-tuple-element.175), channel_id=1, source_target_pairs={{0,8},{8,16},{16,24},{24,28},{28,20},{20,12},{12,4},{4,0},{1,9},{9... | collective-permute-start | bytes 1081352 | tf_op jit(solution)/shard_map/ppermute | solution.py:549
  486.5 24.6 %collective-permute-start.84 = (bf16[128,2816]{1,0:T(8,128)(2,1)S(1)}, bf16[128,2816]{1,0:T(8,128)(2,1)S(1)}, u32[]{:S(2)}, u32[]{:S(2)}) collective-permute-start(bf16[128,2816]{1,0:T(8,128)(2,1)S(1)} %get-tuple-element.155), channel_id=1, source_target_pairs={{0,8},{8,16},{16,24},{24,28},{28,20},{20,12},{12,4},{4,0},{1,9},{9... | collective-permute-start | bytes 2162696 | tf_op jit(solution)/shard_map/ppermute | solution.py:549
  487.3 24.6 %collective-permute-start.91 = (bf16[128,2816]{1,0:T(8,128)(2,1)S(1)}, bf16[128,2816]{1,0:T(8,128)(2,1)S(1)}, u32[]{:S(2)}, u32[]{:S(2)}) collective-permute-start(bf16[128,2816]{1,0:T(8,128)(2,1)S(1)} %get-tuple-element.154), channel_id=1, source_target_pairs={{0,4},{8,0},{16,8},{24,16},{28,24},{20,28},{12,20},{4,12},{1,5},{9... | collective-permute-start | bytes 2162696 | tf_op jit(solution)/shard_map/ppermute | solution.py:550
  488.9 56.3 %collective-permute-start.41 = (bf16[2,256,2048]{2,1,0:T(8,128)(2,1)S(1)}, bf16[2,256,2048]{2,1,0:T(8,128)(2,1)S(1)}, u32[]{:S(2)}, u32[]{:S(2)}) collective-permute-start(bf16[2,256,2048]{2,1,0:T(8,128)(2,1)S(1)} %dynamic-slice_bitcast_fusion.1), channel_id=1, source_target_pairs={{0,1},{1,0},{2,3},{3,2},{4,5},{5,4},{6,7},{7,6},{8,9},{9,8},{10,11... | collective-permute-start | bytes 6291464 | tf_op jit(solution)/shard_map/ppermute | solution.py:572
  496.6 22.3 %collective-permute-start.101 = (bf16[128,1408]{1,0:T(8,128)(2,1)S(1)}, bf16[128,1408]{1,0:T(8,128)(2,1)S(1)}, u32[]{:S(2)}, u32[]{:S(2)}) collective-permute-start(bf16[128,1408]{1,0:T(8,128)(2,1)S(1)} %get-tuple-element.169), channel_id=1, source_target_pairs={{0,8},{8,16},{16,24},{24,28},{28,20},{20,12},{12,4},{4,0},{1,9},{9... | collective-permute-start | bytes 1081352 | tf_op jit(solution)/shard_map/ppermute | solution.py:549
  498.7 20.9 %collective-permute-start.108 = (bf16[128,1408]{1,0:T(8,128)(2,1)S(1)}, bf16[128,1408]{1,0:T(8,128)(2,1)S(1)}, u32[]{:S(2)}, u32[]{:S(2)}) collective-permute-start(bf16[128,1408]{1,0:T(8,128)(2,1)S(1)} %get-tuple-element.170), channel_id=1, source_target_pairs={{0,4},{8,0},{16,8},{24,16},{28,24},{20,28},{12,20},{4,12},{1,5},{9... | collective-permute-start | bytes 1081352 | tf_op jit(solution)/shard_map/ppermute | solution.py:550
  512.2 22.2 %collective-permute-start.85 = (bf16[128,2816]{1,0:T(8,128)(2,1)S(1)}, bf16[128,2816]{1,0:T(8,128)(2,1)S(1)}, u32[]{:S(2)}, u32[]{:S(2)}) collective-permute-start(bf16[128,2816]{1,0:T(8,128)(2,1)S(1)} %get-tuple-element.153), channel_id=1, source_target_pairs={{0,8},{8,16},{16,24},{24,28},{28,20},{20,12},{12,4},{4,0},{1,9},{9... | collective-permute-start | bytes 2162696 | tf_op jit(solution)/shard_map/ppermute | solution.py:549
  514.3 22.0 %collective-permute-start.92 = (bf16[128,2816]{1,0:T(8,128)(2,1)S(1)}, bf16[128,2816]{1,0:T(8,128)(2,1)S(1)}, u32[]{:S(2)}, u32[]{:S(2)}) collective-permute-start(bf16[128,2816]{1,0:T(8,128)(2,1)S(1)} %get-tuple-element.152), channel_id=1, source_target_pairs={{0,4},{8,0},{16,8},{24,16},{28,24},{20,28},{12,20},{4,12},{1,5},{9... | collective-permute-start | bytes 2162696 | tf_op jit(solution)/shard_map/ppermute | solution.py:550
  518.9 30.3 %collective-permute-start.37 = (bf16[2,256,2048]{2,1,0:T(8,128)(2,1)S(1)}, bf16[2,256,2048]{2,1,0:T(8,128)(2,1)}, u32[]{:S(2)}, u32[]{:S(2)}) collective-permute-start(bf16[2,256,2048]{2,1,0:T(8,128)(2,1)S(1)} %dynamic-slice_bitcast_fusion.2), channel_id=1, source_target_pairs={{0,1},{1,0},{2,3},{3,2},{4,5},{5,4},{6,7},{7,6},{8,9},{9,8},{10,11... | collective-permute-start | bytes 6291464 | tf_op jit(solution)/shard_map/ppermute | solution.py:572
  519.8 22.3 %collective-permute-start.102 = (bf16[128,1408]{1,0:T(8,128)(2,1)S(1)}, bf16[128,1408]{1,0:T(8,128)(2,1)S(1)}, u32[]{:S(2)}, u32[]{:S(2)}) collective-permute-start(bf16[128,1408]{1,0:T(8,128)(2,1)S(1)} %get-tuple-element.167), channel_id=1, source_target_pairs={{0,8},{8,16},{16,24},{24,28},{28,20},{20,12},{12,4},{4,0},{1,9},{9... | collective-permute-start | bytes 1081352 | tf_op jit(solution)/shard_map/ppermute | solution.py:549
  537.6 29.1 %collective-permute-start.86 = (bf16[128,2816]{1,0:T(8,128)(2,1)}, bf16[128,2816]{1,0:T(8,128)(2,1)S(1)}, u32[]{:S(2)}, u32[]{:S(2)}) collective-permute-start(bf16[128,2816]{1,0:T(8,128)(2,1)} %get-tuple-element.151), channel_id=1, source_target_pairs={{0,8},{8,16},{16,24},{24,28},{28,20},{20,12},{12,4},{4,0},{1,9},{9... | collective-permute-start | bytes 2162696 | tf_op jit(solution)/shard_map/ppermute | solution.py:549
  542.1 25.5 %collective-permute-start.93 = (bf16[128,2816]{1,0:T(8,128)(2,1)S(1)}, bf16[128,2816]{1,0:T(8,128)(2,1)}, u32[]{:S(2)}, u32[]{:S(2)}) collective-permute-start(bf16[128,2816]{1,0:T(8,128)(2,1)S(1)} %get-tuple-element.150), channel_id=1, source_target_pairs={{0,4},{8,0},{16,8},{24,16},{28,24},{20,28},{12,20},{4,12},{1,5},{9... | collective-permute-start | bytes 2162696 | tf_op jit(solution)/shard_map/ppermute | solution.py:550
  545.1 18.7 %collective-permute-start.103 = (bf16[128,1408]{1,0:T(8,128)(2,1)}, bf16[128,1408]{1,0:T(8,128)(2,1)S(1)}, u32[]{:S(2)}, u32[]{:S(2)}) collective-permute-start(bf16[128,1408]{1,0:T(8,128)(2,1)} %get-tuple-element.165), channel_id=1, source_target_pairs={{0,8},{8,16},{16,24},{24,28},{28,20},{20,12},{12,4},{4,0},{1,9},{9... | collective-permute-start | bytes 1081352 | tf_op jit(solution)/shard_map/ppermute | solution.py:549
  545.2 20.1 %collective-permute-start.110 = (bf16[128,1408]{1,0:T(8,128)(2,1)}, bf16[128,1408]{1,0:T(8,128)(2,1)S(1)}, u32[]{:S(2)}, u32[]{:S(2)}) collective-permute-start(bf16[128,1408]{1,0:T(8,128)(2,1)} %get-tuple-element.166), channel_id=1, source_target_pairs={{0,4},{8,0},{16,8},{24,16},{28,24},{20,28},{12,20},{4,12},{1,5},{9... | collective-permute-start | bytes 1081352 | tf_op jit(solution)/shard_map/ppermute | solution.py:550
  549.3 45.8 %collective-permute-start.42 = (bf16[1,256,2048]{2,1,0:T(8,128)(2,1)}, bf16[1,256,2048]{2,1,0:T(8,128)(2,1)}, u32[]{:S(2)}, u32[]{:S(2)}) collective-permute-start(bf16[1,256,2048]{2,1,0:T(8,128)(2,1)} %dynamic-slice_convert_fusion.1), channel_id=1, source_target_pairs={{0,2},{1,3},{2,0},{3,1},{4,6},{5,7},{6,4},{7,5},{8,10},{9,11},{10,... | collective-permute-start | bytes 3145736 | tf_op jit(solution)/shard_map/ppermute | solution.py:572
  563.8 38.4 %collective-permute-start.38 = (bf16[1,256,2048]{2,1,0:T(8,128)(2,1)}, bf16[1,256,2048]{2,1,0:T(8,128)(2,1)}, u32[]{:S(2)}, u32[]{:S(2)}) collective-permute-start(bf16[1,256,2048]{2,1,0:T(8,128)(2,1)} %dynamic-slice_convert_fusion.2), channel_id=1, source_target_pairs={{0,2},{1,3},{2,0},{3,1},{4,6},{5,7},{6,4},{7,5},{8,10},{9,11},{10,... | collective-permute-start | bytes 3145736 | tf_op jit(solution)/shard_map/ppermute | solution.py:572
  570.2 19.7 %collective-permute-start.87 = (bf16[128,2816]{1,0:T(8,128)(2,1)}, bf16[128,2816]{1,0:T(8,128)(2,1)}, u32[]{:S(2)}, u32[]{:S(2)}) collective-permute-start(bf16[128,2816]{1,0:T(8,128)(2,1)} %get-tuple-element.149), channel_id=1, source_target_pairs={{0,8},{8,16},{16,24},{24,28},{28,20},{20,12},{12,4},{4,0},{1,9},{9... | collective-permute-start | bytes 2162696 | tf_op jit(solution)/shard_map/ppermute | solution.py:549
  593.0 14.7 %collective-permute-start.88 = (bf16[128,2816]{1,0:T(8,128)(2,1)S(1)}, bf16[128,2816]{1,0:T(8,128)(2,1)S(1)}, u32[]{:S(2)}, u32[]{:S(2)}) collective-permute-start(bf16[128,2816]{1,0:T(8,128)(2,1)S(1)} %get-tuple-element.147), channel_id=1, source_target_pairs={{0,8},{8,16},{16,24},{24,28},{28,20},{20,12},{12,4},{4,0},{1,9},{9... | collective-permute-start | bytes 2162696 | tf_op jit(solution)/shard_map/ppermute | solution.py:549
  601.6 26.1 %collective-permute-start.43 = (bf16[1,256,2048]{2,1,0:T(8,128)(2,1)S(1)}, bf16[1,256,2048]{2,1,0:T(8,128)(2,1)S(1)}, u32[]{:S(2)}, u32[]{:S(2)}) collective-permute-start(bf16[1,256,2048]{2,1,0:T(8,128)(2,1)S(1)} %get-tuple-element.130), channel_id=1, source_target_pairs={{0,2},{1,3},{2,0},{3,1},{4,6},{5,7},{6,4},{7,5},{8,10},{9,11},{10,... | collective-permute-start | bytes 3145736 | tf_op jit(solution)/shard_map/ppermute | solution.py:584
  605.2 39.9 %collective-permute-start.39 = (bf16[1,256,2048]{2,1,0:T(8,128)(2,1)S(1)}, bf16[1,256,2048]{2,1,0:T(8,128)(2,1)S(1)}, u32[]{:S(2)}, u32[]{:S(2)}) collective-permute-start(bf16[1,256,2048]{2,1,0:T(8,128)(2,1)S(1)} %add_convert_fusion.1), channel_id=1, source_target_pairs={{0,2},{1,3},{2,0},{3,1},{4,6},{5,7},{6,4},{7,5},{8,10},{9,11},{10,... | collective-permute-start | bytes 3145736 | tf_op jit(solution)/shard_map/ppermute | solution.py:584
  610.5 17.6 %collective-permute-start.89 = (bf16[128,2816]{1,0:T(8,128)(2,1)S(1)}, bf16[128,2816]{1,0:T(8,128)(2,1)S(1)}, u32[]{:S(2)}, u32[]{:S(2)}) collective-permute-start(bf16[128,2816]{1,0:T(8,128)(2,1)S(1)} %get-tuple-element.145), channel_id=1, source_target_pairs={{0,8},{8,16},{16,24},{24,28},{28,20},{20,12},{12,4},{4,0},{1,9},{9... | collective-permute-start | bytes 2162696 | tf_op jit(solution)/shard_map/ppermute | solution.py:549
  612.0 16.1 %collective-permute-start.96 = (bf16[128,2816]{1,0:T(8,128)(2,1)S(1)}, bf16[128,2816]{1,0:T(8,128)(2,1)S(1)}, u32[]{:S(2)}, u32[]{:S(2)}) collective-permute-start(bf16[128,2816]{1,0:T(8,128)(2,1)S(1)} %get-tuple-element.144), channel_id=1, source_target_pairs={{0,4},{8,0},{16,8},{24,16},{28,24},{20,28},{12,20},{4,12},{1,5},{9... | collective-permute-start | bytes 2162696 | tf_op jit(solution)/shard_map/ppermute | solution.py:550
  628.0 25.2 %collective-permute-start.44 = (bf16[2,256,2048]{2,1,0:T(8,128)(2,1)S(1)}, bf16[2,256,2048]{2,1,0:T(8,128)(2,1)S(1)}, u32[]{:S(2)}, u32[]{:S(2)}) collective-permute-start(bf16[2,256,2048]{2,1,0:T(8,128)(2,1)S(1)} %maximum_bitcast_fusion.2), channel_id=1, source_target_pairs={{0,1},{1,0},{2,3},{3,2},{4,5},{5,4},{6,7},{7,6},{8,9},{9,8},{10,11... | collective-permute-start | bytes 6291464 | tf_op jit(solution)/shard_map/ppermute | solution.py:584
  629.8 18.6 %collective-permute-start.90 = (bf16[128,2816]{1,0:T(8,128)(2,1)S(1)}, bf16[128,2816]{1,0:T(8,128)(2,1)S(1)}, u32[]{:S(2)}, u32[]{:S(2)}) collective-permute-start(bf16[128,2816]{1,0:T(8,128)(2,1)S(1)} %get-tuple-element.143), channel_id=1, source_target_pairs={{0,8},{8,16},{16,24},{24,28},{28,20},{20,12},{12,4},{4,0},{1,9},{9... | collective-permute-start | bytes 2162696 | tf_op jit(solution)/shard_map/ppermute | solution.py:549
  631.4 18.4 %collective-permute-start.97 = (bf16[128,2816]{1,0:T(8,128)(2,1)S(1)}, bf16[128,2816]{1,0:T(8,128)(2,1)S(1)}, u32[]{:S(2)}, u32[]{:S(2)}) collective-permute-start(bf16[128,2816]{1,0:T(8,128)(2,1)S(1)} %get-tuple-element.142), channel_id=1, source_target_pairs={{0,4},{8,0},{16,8},{24,16},{28,24},{20,28},{12,20},{4,12},{1,5},{9... | collective-permute-start | bytes 2162696 | tf_op jit(solution)/shard_map/ppermute | solution.py:550
  645.6 28.1 %collective-permute-start.40 = (bf16[2,256,2048]{2,1,0:T(8,128)(2,1)S(1)}, bf16[2,256,2048]{2,1,0:T(8,128)(2,1)}, u32[]{:S(2)}, u32[]{:S(2)}) collective-permute-start(bf16[2,256,2048]{2,1,0:T(8,128)(2,1)S(1)} %maximum_bitcast_fusion.1), channel_id=1, source_target_pairs={{0,1},{1,0},{2,3},{3,2},{4,5},{5,4},{6,7},{7,6},{8,9},{9,8},{10,11... | collective-permute-start | bytes 6291464 | tf_op jit(solution)/shard_map/ppermute | solution.py:584
  665.3 15.4 %collective-permute-start.45 = (bf16[2,258,256]{2,1,0:T(8,128)(2,1)S(1)}, bf16[2,258,256]{2,1,0:T(8,128)(2,1)S(1)}, u32[]{:S(2)}, u32[]{:S(2)}) collective-permute-start(bf16[2,258,256]{2,1,0:T(8,128)(2,1)S(1)} %pad_maximum_fusion.12), channel_id=1, source_target_pairs={{0,4},{4,0},{8,12},{12,8},{16,20},{20,16},{24,28},{28,24},{1,5},{5... | collective-permute-start | bytes 792584 | tf_op jit(solution)/shard_map/ppermute | solution.py:612
  673.3 110.5 %collective-permute-start.70 = (bf16[128,1024]{0,1:T(8,128)(2,1)}, bf16[128,1024]{0,1:T(8,128)(2,1)}, u32[]{:S(2)}, u32[]{:S(2)}) collective-permute-start(bf16[128,1024]{0,1:T(8,128)(2,1)} %get-tuple-element.196), channel_id=1, source_target_pairs={{0,8},{8,16},{16,24},{24,28},{28,20},{20,12},{12,4},{4,0},{1,9},{9... | collective-permute-start | bytes 786440 | tf_op jit(solution)/shard_map/ppermute | solution.py:549
  723.2 51.5 %collective-permute-start.82 = (bf16[128,1024]{0,1:T(8,128)(2,1)}, bf16[128,1024]{0,1:T(8,128)(2,1)}, u32[]{:S(2)}, u32[]{:S(2)}) collective-permute-start(bf16[128,1024]{0,1:T(8,128)(2,1)} %add_convert_fusion.39), channel_id=1, source_target_pairs={{0,4},{8,0},{16,8},{24,16},{28,24},{20,28},{12,20},{4,12},{1,5},{9... | collective-permute-start | bytes 786440 | tf_op jit(solution)/shard_map/ppermute | solution.py:550
  774.6 29.6 %collective-permute-start.50 = (bf16[2,256,2048]{2,1,0:T(8,128)(2,1)S(1)}, bf16[2,256,2048]{2,1,0:T(8,128)(2,1)S(1)}, u32[]{:S(2)}, u32[]{:S(2)}) collective-permute-start(bf16[2,256,2048]{2,1,0:T(8,128)(2,1)S(1)} %dynamic-slice_bitcast_fusion), channel_id=1, source_target_pairs={{0,1},{1,0},{2,3},{3,2},{4,5},{5,4},{6,7},{7,6},{8,9},{9,8},{10,11... | collective-permute-start | bytes 6291464 | tf_op jit(solution)/shard_map/ppermute | solution.py:572
  805.2 22.9 %collective-permute-start.51 = (bf16[1,256,2048]{2,1,0:T(8,128)(2,1)S(1)}, bf16[1,256,2048]{2,1,0:T(8,128)(2,1)S(1)}, u32[]{:S(2)}, u32[]{:S(2)}) collective-permute-start(bf16[1,256,2048]{2,1,0:T(8,128)(2,1)S(1)} %dynamic-slice_convert_fusion), channel_id=1, source_target_pairs={{0,2},{1,3},{2,0},{3,1},{4,6},{5,7},{6,4},{7,5},{8,10},{9,11},{10,... | collective-permute-start | bytes 3145736 | tf_op jit(solution)/shard_map/ppermute | solution.py:572
  814.0 15.9 %collective-permute-start.58 = (bf16[128,1152]{1,0:T(8,128)(2,1)S(1)}, bf16[128,1152]{1,0:T(8,128)(2,1)S(1)}, u32[]{:S(2)}, u32[]{:S(2)}) collective-permute-start(bf16[128,1152]{1,0:T(8,128)(2,1)S(1)} %get-tuple-element.183), channel_id=1, source_target_pairs={{0,8},{8,16},{16,24},{24,28},{28,20},{20,12},{12,4},{4,0},{1,9},{9... | collective-permute-start | bytes 884744 | tf_op jit(solution)/shard_map/ppermute | solution.py:549
  814.9 15.1 %collective-permute-start.65 = (bf16[128,1152]{1,0:T(8,128)(2,1)S(1)}, bf16[128,1152]{1,0:T(8,128)(2,1)S(1)}, u32[]{:S(2)}, u32[]{:S(2)}) collective-permute-start(bf16[128,1152]{1,0:T(8,128)(2,1)S(1)} %get-tuple-element.184), channel_id=1, source_target_pairs={{0,4},{8,0},{16,8},{24,16},{28,24},{20,28},{12,20},{4,12},{1,5},{9... | collective-permute-start | bytes 884744 | tf_op jit(solution)/shard_map/ppermute | solution.py:550
  829.4 22.0 %collective-permute-start.52 = (bf16[1,256,2048]{2,1,0:T(8,128)(2,1)S(1)}, bf16[1,256,2048]{2,1,0:T(8,128)(2,1)S(1)}, u32[]{:S(2)}, u32[]{:S(2)}) collective-permute-start(bf16[1,256,2048]{2,1,0:T(8,128)(2,1)S(1)} %fusion.27), channel_id=1, source_target_pairs={{0,2},{1,3},{2,0},{3,1},{4,6},{5,7},{6,4},{7,5},{8,10},{9,11},{10,... | collective-permute-start | bytes 3145736 | tf_op jit(solution)/shard_map/ppermute | solution.py:584
  833.8 20.2 %collective-permute-start.75 = (bf16[128,1024]{0,1:T(8,128)(2,1)S(1)}, bf16[128,1024]{0,1:T(8,128)(2,1)S(1)}, u32[]{:S(2)}, u32[]{:S(2)}) collective-permute-start(bf16[128,1024]{0,1:T(8,128)(2,1)S(1)} %add_convert_fusion.45), channel_id=1, source_target_pairs={{0,8},{8,16},{16,24},{24,28},{28,20},{20,12},{12,4},{4,0},{1,9},{9... | collective-permute-start | bytes 786440 | tf_op jit(solution)/shard_map/ppermute | solution.py:549
  853.1 18.2 %collective-permute-start.53 = (bf16[2,256,2048]{2,1,0:T(8,128)(2,1)}, bf16[2,256,2048]{2,1,0:T(8,128)(2,1)}, u32[]{:S(2)}, u32[]{:S(2)}) collective-permute-start(bf16[2,256,2048]{2,1,0:T(8,128)(2,1)} %maximum_bitcast_fusion.3), channel_id=1, source_target_pairs={{0,1},{1,0},{2,3},{3,2},{4,5},{5,4},{6,7},{7,6},{8,9},{9,8},{10,11... | collective-permute-start | bytes 6291464 | tf_op jit(solution)/shard_map/ppermute | solution.py:584
  (126 other events, 1696.0 us)

commit v4 on v3

--- a/solution.py
+++ b/solution.py
@@ -15,7 +15,7 @@
 NN = (((1,), (0,)), ((), ()))
 NT = (((1,), (1,)), ((), ()))
 TN = (((0,), (0,)), ((), ()))
-VMEM_BYTES = 48 * 1024 * 1024
+VMEM_BYTES = 56 * 1024 * 1024
 MESH = pl.DeviceIdType.MESH
 
 
@@ -53,17 +53,9 @@
     return (rows >= columns) & (mark_column == mark_row)
 
 
-def state_kernel(
-    value_ref, key_ref, low_ref, up_ref, bias_ref, mark_ref,
-    run_ref, slope_ref, state_ref, total_ref, state, total,
+def state_chunk(
+    value_ref, key_ref, low_ref, up_ref, bias_ref, mark_ref, run_ref, slope_ref, state, total
 ):
-    step = pl.program_id(0)
-
-    @pl.when(step == 0)
-    def _():
-        state[...] = jnp.zeros_like(state)
-        total[...] = jnp.ones_like(total)
-
     lower = triangle(True)
     for b in range(value_ref.shape[0]):
         raw = product(low_ref[b], up_ref[...], NN, HIGH) + bias_ref[...]
@@ -81,22 +73,32 @@
         state[b] = state[b] * keep + product(value_ref[b], tail, TN)
         total[b] = total[b] * keep
 
+
+def state_kernel(
+    value_ref, key_ref, low_ref, up_ref, bias_ref, mark_ref,
+    run_ref, slope_ref, state_ref, total_ref, state, total,
+):
+    step = pl.program_id(0)
+
+    @pl.when(step == 0)
+    def _():
+        state[...] = jnp.zeros_like(state)
+        total[...] = jnp.ones_like(total)
+
+    state_chunk(
+        value_ref, key_ref, low_ref, up_ref, bias_ref, mark_ref, run_ref, slope_ref, state, total
+    )
+
     @pl.when(step == pl.num_programs(0) - 1)
     def _():
         state_ref[...] = narrow(state[...])
         total_ref[...] = total[...]
 
 
-def mixer_kernel(
-    query_ref, value_ref, key_ref, run_ref, mark_ref, row_ref, first_ref, gate_ref, gain_ref,
+def mixer_chunk(
+    query_ref, value_ref, key_ref, run_ref, mark_ref, row_ref, gate_ref, gain_ref,
     heads_ref, mixed_ref, states_ref, state,
 ):
-    step = pl.program_id(0)
-
-    @pl.when(step == 0)
-    def _():
-        state[...] = wide(first_ref[...])
-
     for b in range(value_ref.shape[0]):
         run, mark = run_ref[b], mark_ref[b]
         middle, last = run[CHUNK // 2 - 1 : CHUNK // 2], run[CHUNK - 1 :]
@@ -120,17 +122,24 @@
         heads_ref[b] = narrow(mixed * root_scale(mixed) * gain_ref[...] * active)
 
 
-def head_back_kernel(
+def mixer_kernel(
+    query_ref, value_ref, key_ref, run_ref, mark_ref, row_ref, first_ref, gate_ref, gain_ref,
+    heads_ref, mixed_ref, states_ref, state,
+):
+    @pl.when(pl.program_id(0) == 0)
+    def _():
+        state[...] = wide(first_ref[...])
+
+    mixer_chunk(
+        query_ref, value_ref, key_ref, run_ref, mark_ref, row_ref, gate_ref, gain_ref,
+        heads_ref, mixed_ref, states_ref, state,
+    )
+
+
+def head_back_chunk(
     grad_ref, gate_ref, mixed_ref, gain_ref, query_ref, run_ref, mark_ref,
-    gate_grad_ref, mixed_grad_ref, gain_grad_ref, state_ref, state,
+    gate_grad_ref, mixed_grad_ref, gain_grad_ref, state,
 ):
-    step = pl.program_id(0)
-
-    @pl.when(step == 0)
-    def _():
-        state[...] = jnp.zeros_like(state)
-        gain_grad_ref[...] = jnp.zeros_like(gain_grad_ref)
-
     gain = gain_ref[...]
     for b in range(grad_ref.shape[0]):
         mixed, gate, grad = mixed_ref[b], gate_ref[b], wide(grad_ref[b])
@@ -150,24 +159,33 @@
         keep = jnp.where(mark[CHUNK - 1 :] == 0.0, jnp.exp(last), 0.0)
         state[b] = state[b] * keep + product(mixed_grad, opened, TN)
 
+
+def head_back_kernel(
+    grad_ref, gate_ref, mixed_ref, gain_ref, query_ref, run_ref, mark_ref,
+    gate_grad_ref, mixed_grad_ref, gain_grad_ref, state_ref, state,
+):
+    step = pl.program_id(0)
+
+    @pl.when(step == 0)
+    def _():
+        state[...] = jnp.zeros_like(state)
+        gain_grad_ref[...] = jnp.zeros_like(gain_grad_ref)
+
+    head_back_chunk(
+        grad_ref, gate_ref, mixed_ref, gain_ref, query_ref, run_ref, mark_ref,
+        gate_grad_ref, mixed_grad_ref, gain_grad_ref, state,
+    )
+
     @pl.when(step == pl.num_programs(0) - 1)
     def _():
         state_ref[...] = narrow(state[...])
 
 
-def mixer_back_kernel(
+def mixer_back_chunk(
     query_ref, value_ref, key_ref, run_ref, slope_ref, mark_ref, row_ref, grad_ref,
-    start_ref, end_ref, last_ref, low_ref, up_ref,
+    start_ref, end_ref, low_ref, up_ref,
     query_grad_ref, value_grad_ref, key_grad_ref, low_grad_ref, up_grad_ref, bias_grad_ref, state,
 ):
-    step = pl.program_id(0)
-
-    @pl.when(step == 0)
-    def _():
-        state[...] = wide(last_ref[...])
-        up_grad_ref[...] = jnp.zeros_like(up_grad_ref)
-        bias_grad_ref[...] = jnp.zeros_like(bias_grad_ref)
-
     upper = triangle(False)
     for b in range(value_ref.shape[0]):
         run, mark = run_ref[b], mark_ref[b]
@@ -193,9 +211,29 @@
         query_grad_ref[b] = narrow(query_grad * DK ** (-0.5))
         key_grad_ref[b] = narrow(key_grad)
         value_grad_ref[b] = narrow(value_grad)
-        low_grad_ref[b] = product(raw_grad, up_ref[...], NT, HIGH)
+        low_grad = narrow(product(raw_grad, up_ref[...], NT, HIGH))
+        low_grad_ref[b, :, : low_grad.shape[1]] = low_grad
         up_grad_ref[...] += product(low_ref[b], raw_grad, TN, HIGH)
         bias_grad_ref[...] += jnp.sum(raw_grad, axis=0, keepdims=True)
+
+
+def mixer_back_kernel(
+    query_ref, value_ref, key_ref, run_ref, slope_ref, mark_ref, row_ref, grad_ref,
+    start_ref, end_ref, last_ref, low_ref, up_ref,
+    query_grad_ref, value_grad_ref, key_grad_ref, low_grad_ref, up_grad_ref, bias_grad_ref, state,
+):
+    @pl.when(pl.program_id(0) == 0)
+    def _():
+        state[...] = wide(last_ref[...])
+        up_grad_ref[...] = jnp.zeros_like(up_grad_ref)
+        bias_grad_ref[...] = jnp.zeros_like(bias_grad_ref)
+
+    mixer_back_chunk(
+        query_ref, value_ref, key_ref, run_ref, slope_ref, mark_ref, row_ref, grad_ref,
+        start_ref, end_ref, low_ref, up_ref,
+        query_grad_ref, value_grad_ref, key_grad_ref, low_grad_ref, up_grad_ref, bias_grad_ref,
+        state,
+    )
 
 
 def along(batch, width, last=0, reverse=0):
@@ -305,7 +343,7 @@
         [along(batch, DK, 0, steps), along(batch, DV, 0, steps), along(batch, DK, 0, steps),
          along(batch, rank, 0, steps), still(rank, DK), still(1, DK)],
         [shape_of(BF16, batch, block, DK), shape_of(BF16, batch, block, DV),
-         shape_of(BF16, batch, block, DK), shape_of(F32, batch, block, rank),
+         shape_of(BF16, batch, block, DK), shape_of(BF16, batch, block, rank),
          shape_of(F32, rank, DK), shape_of(F32, 1, DK)],
         [pltpu.VMEM((batch, DV, DK), F32)],
         (query, value_key, value_key, run, slope, mark, row, grad, states, states, later, low, up),
@@ -336,141 +374,1204 @@
 
 
 def enter_kernel(
-    order, input_ref, block_ref, small_ref,
-    normed_ref, weight_ref, vk_ref, query_ref, gate_ref, low_ref, smalls_ref,
-    total, low_total, send, receive, small_send, small_receive,
+    order, input_ref, block_ref, out_block_ref, small_ref, rise_ref,
+    normed_ref, weight_ref, out_ref, vk_ref, query_ref, gate_ref, low_ref,
+    gains_ref, head_gain_ref, bias_ref, up_ref,
+    smalls_ref, rises_ref, total, small_send, small_receive, rise_send, rise_receive, *scratch,
 ):
     count = len(order)
     share, half = block_ref.shape[0], block_ref.shape[0] // 2
     rows, tile = input_ref.shape[0], 256
-    wide_cols = total.shape[1]
-    low_start = block_ref.shape[1] - low_ref.shape[1]
     mine = lax.axis_index("seq")
-    right, left = block_at(order, 1), block_at(order, -1)
+    ring = BlockRing(order, block_ref, weight_ref, *scratch[:3])
+    out_ring = BlockRing(order, out_block_ref, out_ref, *scratch[3:])
     greet("seq", count)
 
-    def hop(step, side):
-        part = pl.ds(side * half, half)
-        if step == 1:
-            source = block_ref.at[part]
-        else:
-            source = weight_ref.at[(count - step + 1) if side == 0 else step - 1, part]
-        return pltpu.make_async_remote_copy(
-            src_ref=source,
-            dst_ref=weight_ref.at[(count - step) if side == 0 else step, part],
-            send_sem=send.at[step - 1, side],
-            recv_sem=receive.at[step - 1, side],
-            device_id={"seq": right if side == 0 else left},
-            device_id_type=MESH,
-        )
-
-    def small_hop(d):
-        return pltpu.make_async_remote_copy(
-            src_ref=small_ref,
-            dst_ref=smalls_ref.at[mine],
-            send_sem=small_send.at[d - 1],
-            recv_sem=small_receive.at[d - 1],
-            device_id={"seq": lax.rem(mine + d, count)},
-            device_id_type=MESH,
-        )
-
-    smalls = [small_hop(d) for d in range(1, count)]
+    def spread(source, target, send, receive):
+        return [
+            pltpu.make_async_remote_copy(
+                src_ref=source,
+                dst_ref=target.at[mine],
+                send_sem=send.at[d - 1],
+                recv_sem=receive.at[d - 1],
+                device_id={"seq": lax.rem(mine + d, count)},
+                device_id_type=MESH,
+            )
+            for d in range(1, count)
+        ]
+
+    smalls = spread(small_ref, smalls_ref, small_send, small_receive)
+    smalls += spread(rise_ref, rises_ref, rise_send, rise_receive)
     for copy in smalls:
         copy.start()
-    hops = {(step, side): hop(step, side) for step in range(1, count) for side in range(2)}
-    hops[1, 0].start()
-    hops[1, 1].start()
+    ring.start()
+    out_ring.start()
     smalls_ref[mine] = small_ref[...]
-    weight_ref[0] = block_ref[...]
+    rises_ref[mine] = rise_ref[...]
 
     scales = []
     for t in range(rows // tile):
         field = wide(input_ref[t * tile : (t + 1) * tile])
         scales.append(root_scale(field))
 
-    def gain_of(slot):
-        owner = block_at(order, slot)
-        return owner, wide(smalls_ref[owner])[:, :share]
-
     def multiply(first, second, begin):
         sides = []
         for slot, side in (first, second):
-            owner, gain = gain_of(slot)
-            sides.append((slot, side, owner, gain[:, side * half : (side + 1) * half]))
+            start = slot * share + side * half
+            sides.append((slot, side, gains_ref[0:1, start : start + half]))
         for t in range(rows // tile):
             here = slice(t * tile, (t + 1) * tile)
             parts, blocks = [], []
-            for slot, side, owner, gain in sides:
-                start = pl.multiple_of(owner * share + side * half, half)
+            for slot, side, gain in sides:
+                start = pl.multiple_of(block_at(order, slot) * share + side * half, half)
                 field = wide(input_ref[here, pl.ds(start, half)])
                 part = narrow(field * scales[t] * gain)
                 column = slot * share + side * half
                 normed_ref[here, column : column + half] = part
                 parts.append(part)
-                blocks.append(weight_ref[slot, side * half : (side + 1) * half, :])
-            left_side = jnp.concatenate(parts, axis=1)
-            right_side = jnp.concatenate(blocks, axis=0)
-            added = product(left_side, right_side[:, :wide_cols], NN)
-            low_added = product(left_side, right_side[:, low_start:], NN)
+                source = block_ref if slot == 0 else weight_ref.at[slot]
+                blocks.append(source[side * half : (side + 1) * half])
+            added = product(jnp.concatenate(parts, axis=1), jnp.concatenate(blocks, axis=0), NN)
             if begin:
                 total[here] = added
-                low_total[here] = low_added
             else:
                 total[here] += added
-                low_total[here] += low_added
 
     for copy in smalls:
         copy.wait_recv()
+    head_share, bias_share = DV // count, DK // count
+    for j in range(count):
+        near = wide(smalls_ref[block_at(order, j)])
+        gains_ref[0:1, j * share : (j + 1) * share] = near[:, :share]
+        gains_ref[1:2, j * share : (j + 1) * share] = near[:, share : 2 * share]
+        block = wide(smalls_ref[j])
+        at = 2 * share
+        head_gain_ref[:, j * head_share : (j + 1) * head_share] = block[:, at : at + head_share]
+        at += head_share
+        bias_ref[:, j * bias_share : (j + 1) * bias_share] = block[:, at : at + bias_share]
+        up_ref[:, j * bias_share : (j + 1) * bias_share] = wide(rises_ref[j])
     multiply((0, 0), (0, 1), True)
     for step in range(1, count):
-        for side in range(2):
-            hops[step, side].wait_recv()
-            if step + 1 < count:
-                hops[step + 1, side].start()
+        ring.advance()
+        out_ring.advance()
         multiply((count - step, 0), (step, 1), False)
-    vk_cols, query_cols = vk_ref.shape[1], query_ref.shape[1]
+    vk_cols, query_cols, gate_cols = vk_ref.shape[1], query_ref.shape[1], gate_ref.shape[1]
     vk_ref[...] = narrow(total[:, :vk_cols])
     query_ref[...] = narrow(total[:, vk_cols : vk_cols + query_cols])
-    gate_ref[...] = total[:, vk_cols + query_cols :]
-    low_ref[...] = low_total[...]
-    for copy in smalls + list(hops.values()):
+    low_from = vk_cols + query_cols + gate_cols
+    gate_ref[...] = total[:, vk_cols + query_cols : low_from]
+    low_ref[...] = total[:, low_from : low_from + low_ref.shape[1]]
+    for copy in smalls:
         copy.wait_send()
-
-
-def enter(inputs, block, small, rank):
+    ring.finish()
+    out_ring.finish()
+
+
+def enter(inputs, block, out_block, small, rise):
     count = lax.axis_size("seq")
     rows, width = inputs.shape
-    cols = DV + DK + DK + DV
-    out_shape = [
-        shape_of(BF16, rows, width),
-        shape_of(BF16, count, *block.shape),
-        shape_of(BF16, rows, DV + DK),
-        shape_of(BF16, rows, DK),
-        shape_of(F32, rows, DV),
-        shape_of(F32, rows, rank),
-        shape_of(BF16, count, *small.shape),
+    rank, cols = rise.shape[0], block.shape[1]
+    dma = [pltpu.SemaphoreType.DMA((count - 1,))] * 4
+    return remote_call(
+        functools.partial(enter_kernel, ring_order(count)),
+        0,
+        [NEAR] * 5,
+        [NEAR] * 11,
+        [
+            shape_of(BF16, rows, width),
+            shape_of(BF16, count, *block.shape),
+            shape_of(BF16, count, *out_block.shape),
+            shape_of(BF16, rows, DV + DK),
+            shape_of(BF16, rows, DK),
+            shape_of(F32, rows, DV),
+            shape_of(F32, rows, rank),
+            shape_of(F32, 2, width),
+            shape_of(F32, 1, DV),
+            shape_of(F32, 1, DK),
+            shape_of(F32, rank, DK),
+        ],
+        [
+            pltpu.VMEM((count, *small.shape), BF16),
+            pltpu.VMEM((count, *rise.shape), BF16),
+            pltpu.VMEM((rows, cols), F32),
+        ]
+        + dma
+        + ring_semaphores(count)
+        + ring_semaphores(count),
+        (inputs, block, out_block, small, rise),
+        2 * rows * width * cols,
+    )
+
+
+class BlockRing:
+    def __init__(self, order, block_ref, whole_ref, send, receive, local):
+        self.count = count = len(order)
+        half = block_ref.shape[0] // 2
+        aims = (block_at(order, 1), block_at(order, -1))
+        self.local = pltpu.make_async_copy(block_ref, whole_ref.at[0], local)
+        self.hops = {}
+        for step in range(1, count):
+            for side in range(2):
+                part = pl.ds(side * half, half)
+                held = (count - step + 1) if side == 0 else step - 1
+                lands = (count - step) if side == 0 else step
+                self.hops[step, side] = pltpu.make_async_remote_copy(
+                    src_ref=(block_ref if step == 1 else whole_ref.at[held]).at[part],
+                    dst_ref=whole_ref.at[lands, part],
+                    send_sem=send.at[step - 1, side],
+                    recv_sem=receive.at[step - 1, side],
+                    device_id={"seq": aims[side]},
+                    device_id_type=MESH,
+                )
+        self.step = 1
+
+    def start(self):
+        self.local.start()
+        for side in range(2):
+            self.hops[1, side].start()
+
+    def advance(self):
+        if self.step < self.count:
+            for side in range(2):
+                self.hops[self.step, side].wait_recv()
+                if self.step + 1 < self.count:
+                    self.hops[self.step + 1, side].start()
+            self.step += 1
+
+    def finish(self):
+        while self.step < self.count:
+            self.advance()
+        for copy in self.hops.values():
+            copy.wait_send()
+        self.local.wait()
+
+
+def ring_semaphores(count):
+    return [
+        pltpu.SemaphoreType.DMA((count - 1, 2)),
+        pltpu.SemaphoreType.DMA((count - 1, 2)),
+        pltpu.SemaphoreType.DMA,
     ]
-    steps = count - 1
+
+
+class Handover:
+    def __init__(self, count, later, state, decay, scratch):
+        (self.decays, self.sent, self.got, self.chain, decay_send, decay_receive, send, receive) = scratch
+        self.count, self.later, self.state, self.decay = count, later, state, decay
+        self.mine = mine = lax.axis_index("seq")
+        self.inner = lax.rem(mine, 2)
+        self.pairs = count // 2
+        self.pair = mine // 2
+        self.place = self.pairs - 1 - self.pair if later else self.pair
+        beside = mine + 1 - 2 * self.inner
+        self.beside = beside
+        self.ahead = (self.inner == 0) != later
+        self.half = state.shape[1] // 2
+        onward = mine - 2 if later else mine + 2
+        self.decay_copies = [
+            pltpu.make_async_remote_copy(
+                src_ref=decay,
+                dst_ref=self.decays.at[mine],
+                send_sem=decay_send.at[d - 1],
+                recv_sem=decay_receive.at[d - 1],
+                device_id={"seq": lax.rem(mine + d, count)},
+                device_id_type=MESH,
+            )
+            for d in range(1, count)
+        ]
+        self.swaps = [
+            pltpu.make_async_remote_copy(
+                src_ref=self.sent.at[i],
+                dst_ref=self.got.at[i],
+                send_sem=send.at[i],
+                recv_sem=receive.at[i],
+                device_id={"seq": beside},
+                device_id_type=MESH,
+            )
+            for i in range(2)
+        ]
+        self.links = [
+            pltpu.make_async_remote_copy(
+                src_ref=self.chain.at[r],
+                dst_ref=self.chain.at[r + 1],
+                send_sem=send.at[2 + r],
+                recv_sem=receive.at[2 + r],
+                device_id={"seq": onward},
+                device_id_type=MESH,
+            )
+            for r in range(self.pairs - 1)
+        ]
+
+    def clear(self):
+        self.chain[...] = jnp.zeros_like(self.chain)
+
+    def rows(self, own):
+        part = self.inner if own else 1 - self.inner
+        return pl.ds(pl.multiple_of(part * self.half, self.half), self.half)
+
+    def begin(self):
+        self.decays[self.mine] = self.decay[...]
+        for copy in self.decay_copies:
+            copy.start()
+        for b in range(self.state.shape[0]):
+            self.sent[0, b] = narrow(self.state[b, self.rows(False)])
+        self.swaps[0].start()
+
+    def firsts(self, b):
+        kept, other = self.state[b, self.rows(True)], wide(self.got[0, b])
+        decay, other_decay = self.decays[self.mine, b], self.decays[self.beside, b]
+        return (
+            jnp.where(self.ahead, kept, other),
+            jnp.where(self.ahead, other, kept),
+            jnp.where(self.ahead, decay, other_decay),
+            jnp.where(self.ahead, other_decay, decay),
+        )
+
+    def send(self, r):
+        @pl.when((self.place >= r) & (self.place + 1 < self.pairs))
+        def _():
+            self.links[r].start()
+
+    def join(self):
+        self.swaps[0].wait_recv()
+        for copy in self.decay_copies:
+            copy.wait_recv()
+        for b in range(self.state.shape[0]):
+            first, second, _, decay = self.firsts(b)
+            self.chain[0, b] = narrow(decay * first + second)
+        self.send(0)
+
+    def hop(self, r):
+        @pl.when(self.place >= r)
+        def _():
+            self.links[r - 1].wait_recv()
+
+        if r < self.pairs - 1:
+            self.send(r)
+
+    def finish(self):
+        own = []
+        for b in range(self.state.shape[0]):
+            before = wide(self.chain[1, b])
+            reach = None
+            for r in range(2, self.pairs):
+                far = self.pair + r - 1 if self.later else self.pair - r + 1
+                far = jnp.minimum(jnp.maximum(far, 0), self.pairs - 1)
+                both = self.decays[2 * far, b] * self.decays[2 * far + 1, b]
+                reach = both if reach is None else reach * both
+                before = before + reach * wide(self.chain[r, b])
+            first, _, decay, _ = self.firsts(b)
+            after = decay * before + first
+            self.sent[1, b] = narrow(jnp.where(self.ahead, after, before))
+            own.append(jnp.where(self.ahead, before, after))
+        self.swaps[1].start()
+        for b in range(self.state.shape[0]):
+            self.state[b, self.rows(True)] = own[b]
+        self.swaps[1].wait_recv()
+        for b in range(self.state.shape[0]):
+            self.state[b, self.rows(False)] = wide(self.got[1, b])
+        for copy in self.decay_copies + self.swaps:
+            copy.wait_send()
+        for r in range(self.pairs - 1):
+
+            @pl.when((self.place >= r) & (self.place + 1 < self.pairs))
+            def _(r=r):
+                self.links[r].wait_send()
+
+
+def handover_scratch(count, batch):
+    half = (batch, DV // 2, DK)
+    return [
+        pltpu.VMEM((count, batch, 1, DK), F32),
+        pltpu.VMEM((2, *half), BF16),
+        pltpu.VMEM((2, *half), BF16),
+        pltpu.VMEM((count // 2, *half), BF16),
+        pltpu.SemaphoreType.DMA((count - 1,)),
+        pltpu.SemaphoreType.DMA((count - 1,)),
+        pltpu.SemaphoreType.DMA((count // 2 + 1,)),
+        pltpu.SemaphoreType.DMA((count // 2 + 1,)),
+    ]
+
+
+PIECES = 4
+
+
+class Rows:
+    def __init__(self, part, out, scratch):
+        self.got, self.across, self.far, send, receive = scratch
+        self.part, self.out = part, out
+        head = lax.axis_index("head")
+        core, chip = lax.rem(head, 2), head // 2
+        self.share = part.shape[0] // 4
+        self.size = self.share // PIECES
+        beside, facing = 2 * chip + 1 - core, 2 * (1 - chip) + core
+        self.own, self.facing = head, facing
+        corner = 2 * (1 - chip) + 1 - core
+
+        def copy(kind, p, source, target, aim):
+            return pltpu.make_async_remote_copy(
+                src_ref=source,
+                dst_ref=target,
+                send_sem=send.at[kind, p],
+                recv_sem=receive.at[kind, p],
+                device_id={"head": aim},
+                device_id_type=MESH,
+            )
+
+        self.copies = {}
+        for p in range(PIECES):
+            here = self.piece(p)
+            mine = out.at[self.rows(head, p)]
+            met = out.at[self.rows(facing, p)]
+            self.copies[0, p] = copy(0, p, part.at[self.rows(corner, p)], self.got.at[0, here], beside)
+            self.copies[1, p] = copy(1, p, part.at[self.rows(beside, p)], self.got.at[1, here], beside)
+            self.copies[2, p] = copy(2, p, self.across.at[here], self.far.at[here], facing)
+            self.copies[3, p] = copy(3, p, mine, mine, facing)
+            self.copies[4, p] = copy(4, p, mine, mine, beside)
+            self.copies[5, p] = copy(5, p, met, met, beside)
+
+    def piece(self, p):
+        return pl.ds(p * self.size, self.size)
+
+    def rows(self, owner, p):
+        return pl.ds(pl.multiple_of(owner * self.share + p * self.size, self.size), self.size)
+
+    def start(self, p):
+        self.copies[0, p].start()
+        self.copies[1, p].start()
+
+    def cross(self, p):
+        self.copies[0, p].wait_recv()
+        here = self.piece(p)
+        self.across[here] = narrow(wide(self.part[self.rows(self.facing, p)]) + wide(self.got[0, here]))
+        self.copies[2, p].start()
+
+    def turn(self, p, middle):
+        self.copies[1, p].wait_recv()
+        self.copies[2, p].wait_recv()
+        here = self.piece(p)
+        total = wide(self.part[self.rows(self.own, p)]) + wide(self.got[1, here])
+        self.out[self.rows(self.own, p)] = middle(here, total + wide(self.far[here]))
+        self.copies[3, p].start()
+        self.copies[4, p].start()
+
+    def relay(self, p):
+        self.copies[3, p].wait_recv()
+        self.copies[5, p].start()
+
+    def finish(self):
+        for p in range(PIECES):
+            self.copies[4, p].wait_recv()
+            self.copies[5, p].wait_recv()
+        for copy in self.copies.values():
+            copy.wait_send()
+
+
+def rows_scratch(share, width):
+    return [
+        pltpu.VMEM((2, share, width), BF16),
+        pltpu.VMEM((share, width), BF16),
+        pltpu.VMEM((share, width), BF16),
+        pltpu.SemaphoreType.DMA((6, PIECES)),
+        pltpu.SemaphoreType.DMA((6, PIECES)),
+    ]
+
+
+def greet_all(count, heads):
+    barrier = pltpu.get_barrier_semaphore()
+    for axis, size in (("seq", count), ("head", heads)):
+        mine = lax.axis_index(axis)
+        for d in range(1, size):
+            pl.semaphore_signal(
+                barrier, inc=1, device_id={axis: lax.rem(mine + d, size)}, device_id_type=MESH
+            )
+    pl.semaphore_wait(barrier, count + heads - 2)
+
+
+def chunk_at(i):
+    return pl.ds(pl.multiple_of(i * CHUNK, CHUNK), CHUNK)
+
+
+def token_phase_kernel(
+    order, vk_ref, query_ref, gate_ref, low_ref, up_ref, bias_ref, starts_ref, gain_ref,
+    out_ref, block_ref,
+    run_ref, slope_ref, total_ref, mixed_ref, heads_ref, states_ref, part_ref, whole_ref,
+    state, ring_send, ring_receive, ring_local, mark_ref, row_ref, *scratch,
+):
+    count = len(order)
+    ring = BlockRing(order, block_ref, whole_ref, ring_send, ring_receive, ring_local)
+    hand = Handover(count, False, state, total_ref, scratch)
+    hand.clear()
+    greet("seq", count)
+    ring.start()
+    fill_marks(starts_ref, mark_ref, row_ref)
+    state[...] = jnp.zeros_like(state)
+    total_ref[...] = jnp.ones_like(total_ref)
+    chunks = run_ref.shape[1] // CHUNK
+
+    @pl.loop(0, chunks)
+    def _(i):
+        at = chunk_at(i)
+        state_chunk(
+            vk_ref.at[:, at, pl.ds(0, DV)], vk_ref.at[:, at, pl.ds(DV, DK)], low_ref.at[:, at],
+            up_ref, bias_ref, mark_ref.at[:, at], run_ref.at[:, at], slope_ref.at[:, at],
+            state, total_ref,
+        )
+
+    hand.begin()
+    ring.advance()
+    hand.join()
+    ring.advance()
+    for r in range(1, count // 2):
+        hand.hop(r)
+        if r % 2 == 0:
+            ring.advance()
+    hand.finish()
+    ring.advance()
+
+    @pl.loop(0, chunks)
+    def _(i):
+        at = chunk_at(i)
+        mixer_chunk(
+            query_ref.at[:, at], vk_ref.at[:, at, pl.ds(0, DV)], vk_ref.at[:, at, pl.ds(DV, DK)],
+            run_ref.at[:, at], mark_ref.at[:, at], row_ref.at[pl.ds(i, 1)], gate_ref.at[:, at],
+            gain_ref, heads_ref.at[:, at], mixed_ref.at[:, at], states_ref.at[pl.ds(2 * i, 2)],
+            state,
+        )
+
+    ring.advance()
+    batch, block, _ = heads_ref.shape
+    tile = 256
+    for b in range(batch):
+        for t in range(block // tile):
+            field = heads_ref[b, t * tile : (t + 1) * tile]
+            start = b * block + t * tile
+            part_ref[start : start + tile] = narrow(product(field, out_ref[...], NT))
+        ring.advance()
+    ring.finish()
+
+
+def remote_call(kernel, number, in_specs, out_specs, out_shape, scratch, operands, flops):
+    moved = sum(a.size * a.dtype.itemsize for a in operands)
+    moved += sum(s.size * s.dtype.itemsize for s in out_shape)
     return pl.pallas_call(
-        functools.partial(enter_kernel, ring_order(count)),
-        in_specs=[pl.BlockSpec(memory_space=pltpu.VMEM)] * 3,
-        out_specs=[pl.BlockSpec(memory_space=pltpu.VMEM)] * 7,
+        kernel,
+        in_specs=in_specs,
+        out_specs=out_specs,
         out_shape=out_shape,
-        scratch_shapes=[
-            pltpu.VMEM((rows, cols), F32),
-            pltpu.VMEM((rows, rank), F32),
-            pltpu.SemaphoreType.DMA((steps, 2)),
-            pltpu.SemaphoreType.DMA((steps, 2)),
-            pltpu.SemaphoreType.DMA((steps,)),
-            pltpu.SemaphoreType.DMA((steps,)),
+        scratch_shapes=scratch,
+        cost_estimate=pl.CostEstimate(flops=flops, bytes_accessed=moved, transcendentals=0),
+        compiler_params=pltpu.CompilerParams(
+            collective_id=number, has_side_effects=True, vmem_limit_bytes=VMEM_BYTES
+        ),
+    )(*operands)
+
+
+NEAR = pl.BlockSpec(memory_space=pltpu.VMEM)
+AWAY = pl.BlockSpec(memory_space=pl.ANY)
+
+
+def token_phase(value_key, query, gates, low, up, bias, starts, gain, out_t, block):
+    count = lax.axis_size("seq")
+    batch, length, _ = low.shape
+    chunks, width = length // CHUNK, out_t.shape[0]
+    return remote_call(
+        functools.partial(token_phase_kernel, ring_order(count)),
+        1,
+        [NEAR] * 9 + [AWAY],
+        [NEAR] * 7 + [AWAY],
+        [
+            shape_of(F32, batch, length, DK),
+            shape_of(F32, batch, length, DK),
+            shape_of(F32, batch, 1, DK),
+            shape_of(F32, batch, length, DV),
+            shape_of(BF16, batch, length, DV),
+            shape_of(BF16, 2 * chunks, batch, DV, DK),
+            shape_of(BF16, batch * length, width),
+            shape_of(BF16, count, *block.shape),
         ],
-        cost_estimate=pl.CostEstimate(
-            flops=2 * rows * width * cols, bytes_accessed=400_000_000, transcendentals=0
-        ),
-        compiler_params=pltpu.CompilerParams(
-            collective_id=0, has_side_effects=True, vmem_limit_bytes=VMEM_BYTES
-        ),
-    )(inputs, block, small)
+        [pltpu.VMEM((batch, DV, DK), F32)]
+        + ring_semaphores(count)
+        + marks_scratch(batch, length)
+        + handover_scratch(count, batch),
+        (value_key, query, gates, low, up, bias, starts, gain, out_t, block),
+        2 * batch * length * DV * (2 * DK + width),
+    )
+
+
+def row_phase_kernel(
+    order, heads, part_ref, input_ref, gain_ref, block_ref,
+    resid_ref, normed_ref, whole_ref,
+    own, own_sems, ring_send, ring_receive, ring_local, *scratch,
+):
+    ring = BlockRing(order, block_ref, whole_ref, ring_send, ring_receive, ring_local)
+    rows = Rows(part_ref, normed_ref, scratch)
+    first = pl.multiple_of(rows.own * rows.share, rows.share)
+    copies = near_copies(order, input_ref, own, pl.ds(first, rows.share), own_sems)
+    for copy in copies:
+        copy.start()
+    greet_all(len(order), heads)
+    for p in range(PIECES):
+        rows.start(p)
+    ring.start()
+
+    def middle(here, total):
+        resid = wide(own[here]) + total
+        resid_ref[here] = resid
+        return narrow(resid * root_scale(resid) * gain_ref[1:2])
+
+    for p in range(PIECES):
+        rows.cross(p)
+    for copy in copies:
+        copy.wait()
+    ring.advance()
+    for p in range(PIECES):
+        rows.turn(p, middle)
+        if p % 2 == 0:
+            ring.advance()
+    ring.advance()
+    for p in range(PIECES):
+        rows.relay(p)
+        if p % 2 == 0:
+            ring.advance()
+    rows.finish()
+    ring.finish()
+
+
+def row_phase(part, inputs, gains, block):
+    count, heads = lax.axis_size("seq"), lax.axis_size("head")
+    rows, width = part.shape
+    return remote_call(
+        functools.partial(row_phase_kernel, ring_order(count), heads),
+        2,
+        [NEAR, AWAY, NEAR, AWAY],
+        [NEAR] * 2 + [AWAY],
+        [
+            shape_of(F32, rows // heads, width),
+            shape_of(BF16, rows, width),
+            shape_of(BF16, count, *block.shape),
+        ],
+        [pltpu.VMEM((rows // heads, width), BF16), pltpu.SemaphoreType.DMA((count,))]
+        + ring_semaphores(count)
+        + rows_scratch(rows // heads, width),
+        (part, inputs, gains, block),
+        16 * rows * width,
+    )
+
+
+def near_copies(order, source, target, rows, semaphores):
+    share = source.shape[1] // len(order)
+    return [
+        pltpu.make_async_copy(
+            source.at[rows, pl.ds(pl.multiple_of(block_at(order, r) * share, share), share)],
+            target.at[:, pl.ds(r * share, share)],
+            semaphores.at[r],
+        )
+        for r in range(len(order))
+    ]
+
+
+def home_copies(order, source, target, semaphores):
+    share = source.shape[1] // len(order)
+    return [
+        pltpu.make_async_copy(
+            source.at[:, pl.ds(r * share, share)],
+            target.at[:, pl.ds(pl.multiple_of(block_at(order, r) * share, share), share)],
+            semaphores.at[r],
+        )
+        for r in range(len(order))
+    ]
+
+
+def fill_marks(starts_ref, mark_ref, row_ref):
+    batch, length, _ = mark_ref.shape
+    chunks = length // CHUNK
+    starts = starts_ref[...].astype(F32)
+    across = product(starts, triangle(False), NN, HIGH)
+    down = product(triangle(True), starts, NT, HIGH)
+    for b in range(batch):
+        for i in range(chunks):
+            n = b * chunks + i
+            mark_ref[b, i * CHUNK : (i + 1) * CHUNK] = down[:, n : n + 1]
+            row_ref[i, b] = across[n : n + 1]
+
+
+def marks_scratch(batch, length):
+    return [
+        pltpu.VMEM((batch, length, 1), F32),
+        pltpu.VMEM((length // CHUNK, batch, 1, CHUNK), F32),
+    ]
+
+
+class SumRing:
+    def __init__(self, order, items, out_ref, scratch):
+        lefts = []
+        for left, _, _ in items:
+            if not any(left is other for other in lefts):
+                lefts.append(left)
+        buffers, rest = scratch[: len(lefts)], scratch[len(lefts) :]
+        self.sent, self.got, load, send, receive = rest
+        self.order, self.items, self.out = order, items, out_ref
+        self.count = count = len(order)
+        self.half = half = out_ref.shape[0] // 2
+        self.buffers = {id(left): buffer for left, buffer in zip(lefts, buffers)}
+        homes = {id(left): home for left, _, home in items}
+        aims = (block_at(order, 1), block_at(order, -1))
+        self.loads, self.hops = {}, {}
+        for k in range(count):
+            for side in range(2):
+                slot = (count - 1 - k) if side == 0 else (k + 1) % count
+                for n, (left, buffer) in enumerate(zip(lefts, buffers)):
+                    block = block_at(order, slot) if homes[id(left)] else slot
+                    column = pl.multiple_of(block * 2 * half + side * half, half)
+                    self.loads[k, side, n] = pltpu.make_async_copy(
+                        left.at[:, pl.ds(column, half)],
+                        buffer.at[k % 2, side],
+                        load.at[k % 2, side, n],
+                    )
+                if k < count - 1:
+                    self.hops[k, side] = pltpu.make_async_remote_copy(
+                        src_ref=self.sent.at[k % 2, side],
+                        dst_ref=self.got.at[k, side],
+                        send_sem=send.at[k, side],
+                        recv_sem=receive.at[k, side],
+                        device_id={"seq": aims[side]},
+                        device_id_type=MESH,
+                    )
+        self.number = len(lefts)
+        self.k = 0
+
+    def load(self, k):
+        if k < self.count:
+            for side in range(2):
+                for n in range(self.number):
+                    self.loads[k, side, n].start()
+
+    def prepare(self):
+        self.load(0)
+        self.load(1)
+
+    def advance(self):
+        k, last = self.k, self.count - 1
+        if k > last:
+            return
+        for side in range(2):
+            for n in range(self.number):
+                self.loads[k, side, n].wait()
+            products = [
+                product(self.buffers[id(left)][k % 2, side], right[...], TN)
+                for left, right, _ in self.items
+            ]
+            if k > 0:
+                self.hops[k - 1, side].wait_recv()
+            if 2 <= k < last:
+                self.hops[k - 2, side].wait_send()
+            column = 0
+            for value in products:
+                columns = slice(column, column + value.shape[1])
+                column += value.shape[1]
+                if k > 0:
+                    value = value + wide(self.got[k - 1, side, :, columns])
+                if k < last:
+                    self.sent[k % 2, side, :, columns] = narrow(value)
+                else:
+                    self.out[side * self.half : (side + 1) * self.half, columns] = value
+            if k < last:
+                self.hops[k, side].start()
+        self.load(k + 2)
+        self.k += 1
+
+    def finish(self):
+        while self.k < self.count:
+            self.advance()
+        for k in (self.count - 3, self.count - 2):
+            for side in range(2):
+                self.hops[k, side].wait_send()
+
+
+def sum_scratch(count, rows, lefts, half, columns):
+    return [pltpu.VMEM((2, 2, rows, half), BF16)] * lefts + [
+        pltpu.VMEM((2, 2, half, columns), BF16),
+        pltpu.VMEM((count - 1, 2, half, columns), BF16),
+        pltpu.SemaphoreType.DMA((2, 2, lefts)),
+        pltpu.SemaphoreType.DMA((count - 1, 2)),
+        pltpu.SemaphoreType.DMA((count - 1, 2)),
+    ]
+
+
+def unit_phase_kernel(
+    order, normed_ref, gate_ref, up_ref, grad_ref, block_ref,
+    act_ref, gate_grad_ref, up_grad_ref, whole_ref,
+    pre_gate, pre_up, act_grad, tiles, tile_sems, ring_send, ring_receive, ring_local,
+):
+    count = len(order)
+    ring = BlockRing(order, block_ref, whole_ref, ring_send, ring_receive, ring_local)
+    greet("seq", count)
+    ring.start()
+    rows = normed_ref.shape[0]
+    tile = 128
+    share, half = block_ref.shape[0], block_ref.shape[0] // 2
+
+    def written(kind, target, i):
+        return pltpu.make_async_copy(
+            tiles.at[kind], target.at[pl.ds(i * tile, tile)], tile_sems.at[kind]
+        )
+
+    def forward(begin, end):
+        @pl.loop(begin, end)
+        def _(i):
+            here = pl.ds(pl.multiple_of(i * tile, tile), tile)
+            field = normed_ref[here]
+            gate = product(field, gate_ref[...], NN)
+            up = product(field, up_ref[...], NN)
+            pre_gate[here] = gate
+            pre_up[here] = up
+
+            @pl.when(i > 0)
+            def _():
+                written(0, act_ref, i - 1).wait()
+
+            tiles[0] = narrow(gate * jax.nn.sigmoid(gate) * up)
+            written(0, act_ref, i).start()
+
+    def multiply(parts, begin):
+        @pl.loop(0, rows // 256)
+        def _(t):
+            here = pl.ds(pl.multiple_of(t * 256, 256), 256)
+            lefts, rights = [], []
+            for slot, side in parts:
+                start = pl.multiple_of(block_at(order, slot) * share + side * half, half)
+                lefts.append(grad_ref[here, pl.ds(start, half)])
+                source = block_ref if slot == 0 else whole_ref.at[slot]
+                rights.append(source[side * half : (side + 1) * half])
+            added = product(jnp.concatenate(lefts, axis=1), jnp.concatenate(rights, axis=0), NN)
+            if begin:
+                act_grad[here] = added
+            else:
+                act_grad[here] += added
+
+    steps = rows // tile
+    arrived = []
+    done = 0
+    for step in range(1, count):
+        goal = min(steps, (step * steps + count - 3) // (count - 2))
+        if goal > done:
+            forward(done, goal)
+            done = goal
+        ring.advance()
+        arrived += [(count - step, 0), (step, 1)]
+        if step == 1:
+            multiply([(0, 0), (0, 1)] + arrived, True)
+            arrived = []
+        elif len(arrived) == 4:
+            multiply(arrived, False)
+            arrived = []
+    if arrived:
+        multiply(arrived, False)
+    written(0, act_ref, steps - 1).wait()
+
+    @pl.loop(0, steps)
+    def _(i):
+        here = pl.ds(pl.multiple_of(i * tile, tile), tile)
+        gate, up, grad = pre_gate[here], pre_up[here], act_grad[here]
+        sigma = jax.nn.sigmoid(gate)
+
+        @pl.when(i > 0)
+        def _():
+            written(0, gate_grad_ref, i - 1).wait()
+            written(1, up_grad_ref, i - 1).wait()
+
+        tiles[0] = narrow(grad * up * sigma * (1.0 + gate * (1.0 - sigma)))
+        tiles[1] = narrow(grad * gate * sigma)
+        written(0, gate_grad_ref, i).start()
+        written(1, up_grad_ref, i).start()
+
+    written(0, gate_grad_ref, steps - 1).wait()
+    written(1, up_grad_ref, steps - 1).wait()
+    ring.finish()
+
+
+def unit_phase(normed_two, fgate, fup, grad_rows, block):
+    count = lax.axis_size("seq")
+    rows, width = normed_two.shape
+    hidden = block.shape[1]
+    flat = shape_of(BF16, rows, hidden)
+    return remote_call(
+        functools.partial(unit_phase_kernel, ring_order(count)),
+        3,
+        [NEAR] * 5,
+        [AWAY] * 3 + [NEAR],
+        [flat, flat, flat, shape_of(BF16, count, *block.shape)],
+        [pltpu.VMEM((rows, hidden), F32)] * 3
+        + [pltpu.VMEM((2, 128, hidden), BF16), pltpu.SemaphoreType.DMA((2,))]
+        + ring_semaphores(count),
+        (normed_two, fgate, fup, grad_rows, block),
+        6 * rows * width * hidden,
+    )
+
+
+def resid_phase_kernel(
+    order, heads, part_ref, resid_ref, grad_ref, gain_ref, out_ref, act_ref, normed_ref, up_grad_ref,
+    resid_grad_ref, attn_grad_ref, heads_grad_ref, gain_grad_ref, sums_ref,
+    own, own_sems, *scratch,
+):
+    count = len(order)
+    rows = Rows(part_ref, attn_grad_ref, scratch[:5])
+    ring = SumRing(
+        order, [(grad_ref, act_ref, True), (normed_ref, up_grad_ref, False)], sums_ref, scratch[5:]
+    )
+    first = pl.multiple_of(rows.own * rows.share, rows.share)
+    copies = near_copies(order, grad_ref, own, pl.ds(first, rows.share), own_sems)
+    for copy in copies:
+        copy.start()
+    ring.prepare()
+    greet_all(count, heads)
+    for p in range(PIECES):
+        rows.start(p)
+    ring.advance()
+    gain_grad_ref[...] = jnp.zeros_like(gain_grad_ref)
+
+    def middle(here, total):
+        resid = resid_ref[here]
+        scale = root_scale(resid)
+        unit = resid * scale
+        gain_grad_ref[...] += jnp.sum(total * unit, axis=0, keepdims=True)
+        grad = wide(own[here]) + norm_back(total * gain_ref[1:2], unit, scale)
+        resid_grad_ref[here] = grad
+        return narrow(grad)
+
+    for p in range(PIECES):
+        rows.cross(p)
+    for copy in copies:
+        copy.wait()
+    rows.turn(0, middle)
+    ring.advance()
+    for p in range(1, PIECES):
+        rows.turn(p, middle)
+    ring.advance()
+    for p in range(PIECES):
+        rows.relay(p)
+        if p == 2:
+            ring.advance()
+    rows.finish()
+    for t in range(4):
+        at = pl.ds(t * rows.share, rows.share)
+        heads_grad_ref[at] = product(attn_grad_ref[at], out_ref[...], NN)
+    ring.finish()
+
+
+def resid_phase(part, resid, grad_rows, gains, out_t, act, normed_two, d_up):
+    count, heads = lax.axis_size("seq"), lax.axis_size("head")
+    rows, width = part.shape
+    share, hidden = width // count, act.shape[1]
+    quarter = rows // heads
+    return remote_call(
+        functools.partial(resid_phase_kernel, ring_order(count), heads),
+        4,
+        [NEAR, NEAR, AWAY, NEAR, NEAR, NEAR, AWAY, NEAR],
+        [NEAR] * 5,
+        [
+            shape_of(F32, quarter, width),
+            shape_of(BF16, rows, width),
+            shape_of(F32, rows, DV),
+            shape_of(F32, 1, width),
+            shape_of(F32, share, 2 * hidden),
+        ],
+        [pltpu.VMEM((quarter, width), BF16), pltpu.SemaphoreType.DMA((count,))]
+        + rows_scratch(quarter, width)
+        + sum_scratch(count, rows, 2, share // 2, 2 * hidden),
+        (part, resid, grad_rows, gains, out_t, act, normed_two, d_up),
+        2 * rows * width * (2 * hidden + DV),
+    )
+
+
+def back_phase_kernel(
+    order, heads, part_ref, resid_ref, heads_grad_ref, gate_ref, mixed_ref, gain_ref, query_ref,
+    vk_ref, run_ref, slope_ref, states_ref, low_ref, up_ref, starts_ref, total_ref,
+    normed_ref, act_grad_ref,
+    packed_ref, up_grad_ref, bias_grad_ref, gain_grad_ref, layer_ref, sums_ref,
+    state, mixed_grad, layer, layer_sems, mark_ref, row_ref, *scratch,
+):
+    count = len(order)
+    rows = Rows(part_ref, layer, scratch[:5])
+    hand = Handover(count, True, state, total_ref, scratch[5:13])
+    ring = SumRing(order, [(normed_ref, act_grad_ref, False)], sums_ref, scratch[13:])
+    hand.clear()
+    ring.prepare()
+    greet_all(count, heads)
+    for p in range(PIECES):
+        rows.start(p)
+    ring.advance()
+    batch, length, _ = run_ref.shape
+    chunks = length // CHUNK
+    gates_from, low_from = DV + 2 * DK, 2 * DV + 2 * DK
+    fill_marks(starts_ref, mark_ref, row_ref)
+    state[...] = jnp.zeros_like(state)
+    for ref in (gain_grad_ref, up_grad_ref, bias_grad_ref):
+        ref[...] = jnp.zeros_like(ref)
+    packed_ref[:, :, low_from:] = jnp.zeros(packed_ref.shape[:2] + (packed_ref.shape[2] - low_from,), BF16)
+
+    @pl.loop(0, chunks)
+    def _(i):
+        at = chunk_at(chunks - 1 - i)
+        head_back_chunk(
+            heads_grad_ref.at[:, at], gate_ref.at[:, at], mixed_ref.at[:, at], gain_ref,
+            query_ref.at[:, at], run_ref.at[:, at], mark_ref.at[:, at],
+            packed_ref.at[:, at, pl.ds(gates_from, DV)], mixed_grad.at[:, at], gain_grad_ref, state,
+        )
+
+    def middle(here, total):
+        return narrow(resid_ref[here] + total)
+
+    hand.begin()
+    for p in range(PIECES):
+        rows.cross(p)
+    ring.advance()
+    hand.join()
+    rows.turn(0, middle)
+    ring.advance()
+    for r in range(1, count // 2):
+        hand.hop(r)
+        if r < PIECES:
+            rows.turn(r, middle)
+    ring.advance()
+    hand.finish()
+    for r in range(count // 2, PIECES):
+        rows.turn(r, middle)
+    rows.relay(0)
+    rows.relay(1)
+    ring.advance()
+
+    def back(begin, end):
+        @pl.loop(begin, end)
+        def _(i):
+            n = chunks - 1 - i
+            at = chunk_at(n)
+            mixer_back_chunk(
+                query_ref.at[:, at], vk_ref.at[:, at, pl.ds(0, DV)],
+                vk_ref.at[:, at, pl.ds(DV, DK)], run_ref.at[:, at], slope_ref.at[:, at],
+                mark_ref.at[:, at], row_ref.at[pl.ds(n, 1)], mixed_grad.at[:, at],
+                states_ref.at[pl.ds(2 * n, 1)], states_ref.at[pl.ds(2 * n + 1, 1)],
+                low_ref.at[:, at], up_ref,
+                packed_ref.at[:, at, pl.ds(DV + DK, DK)], packed_ref.at[:, at, pl.ds(0, DV)],
+                packed_ref.at[:, at, pl.ds(DV, DK)], packed_ref.at[:, at, pl.ds(low_from, 128)],
+                up_grad_ref, bias_grad_ref, state,
+            )
+
+    back(0, chunks // 2)
+    rows.relay(2)
+    ring.advance()
+    back(chunks // 2, chunks)
+    rows.relay(3)
+    rows.finish()
+    copies = home_copies(order, layer, layer_ref, layer_sems)
+    for copy in copies:
+        copy.start()
+    ring.finish()
+    for copy in copies:
+        copy.wait()
+
+
+def back_phase(
+    part, resid, d_heads, gates, mixed, gain, query, vk, run, slope, states, low, up, starts, total,
+    normed_two, d_gate, packed_cols,
+):
+    count, heads = lax.axis_size("seq"), lax.axis_size("head")
+    rows, width = part.shape
+    batch, length, rank = low.shape
+    share, hidden, quarter = width // count, d_gate.shape[1], rows // heads
+    return remote_call(
+        functools.partial(back_phase_kernel, ring_order(count), heads),
+        5,
+        [NEAR] * 15 + [AWAY, NEAR],
+        [NEAR] * 4 + [AWAY, NEAR],
+        [
+            shape_of(BF16, batch, length, packed_cols),
+            shape_of(F32, rank, DK),
+            shape_of(F32, 1, DK),
+            shape_of(F32, 1, DV),
+            shape_of(BF16, rows, width),
+            shape_of(F32, share, hidden),
+        ],
+        [
+            pltpu.VMEM((batch, DV, DK), F32),
+            pltpu.VMEM((batch, length, DV), BF16),
+            pltpu.VMEM((rows, width), BF16),
+            pltpu.SemaphoreType.DMA((count,)),
+        ]
+        + marks_scratch(batch, length)
+        + rows_scratch(quarter, width)
+        + handover_scratch(count, batch)
+        + sum_scratch(count, rows, 1, share // 2, hidden),
+        (part, resid, d_heads, gates, mixed, gain, query, vk, run, slope, states, low, up, starts,
+         total, normed_two, d_gate),
+        2 * rows * width * hidden,
+    )
+
+
+SMALL = 24
+
+
+def last_phase_kernel(
+    order, heads, part_ref, input_ref, resid_grad_ref, gain_ref, normed_ref, packed_ref, attn_ref,
+    heads_ref, ffn_gain_ref, head_gain_ref, bias_ref, up_ref,
+    input_grad_ref, sums_ref, small_ref, tail_ref,
+    own, own_sems, grads, grad_sems, gain_grad, stage, stage_got, shared, shared_got, tail_got,
+    seq_send, seq_receive, head_send, head_receive, *scratch,
+):
+    count = len(order)
+    rows = Rows(part_ref, grads, scratch[:5])
+    ring = SumRing(
+        order, [(normed_ref, packed_ref, False), (attn_ref, heads_ref, False)], sums_ref, scratch[5:]
+    )
+    first = pl.multiple_of(rows.own * rows.share, rows.share)
+    copies = near_copies(order, input_ref, own, pl.ds(first, rows.share), own_sems)
+    for copy in copies:
+        copy.start()
+    ring.prepare()
+    greet_all(count, heads)
+    for p in range(PIECES):
+        rows.start(p)
+    ring.advance()
+    gain_grad[...] = jnp.zeros_like(gain_grad)
+
+    def middle(here, total):
+        field = wide(own[here])
+        scale = root_scale(field)
+        unit = field * scale
+        gain_grad[...] += jnp.sum(total * unit, axis=0, keepdims=True)
+        return narrow(resid_grad_ref[here] + norm_back(total * gain_ref[0:1], unit, scale))
+
+    for p in range(PIECES):
+        rows.cross(p)
+    for copy in copies:
+        copy.wait()
+    ring.advance()
+    for p in range(PIECES):
+        rows.turn(p, middle)
+        if p == 2:
+            ring.advance()
+
+    mine, head = lax.axis_index("seq"), lax.axis_index("head")
+    share = sums_ref.shape[0]
+    stage[...] = jnp.zeros_like(stage)
+    pieces = [ref.shape[1] // count for ref in (head_gain_ref, bias_ref, up_ref)]
+    for j in range(count):
+        stage[j, 0:1, : pieces[0]] = head_gain_ref[:, j * pieces[0] : (j + 1) * pieces[0]]
+        stage[j, 1:2, : pieces[1]] = bias_ref[:, j * pieces[1] : (j + 1) * pieces[1]]
+        stage[j, 8:, : pieces[2]] = up_ref[:, j * pieces[2] : (j + 1) * pieces[2]]
+        owner = block_at(order, j)
+        for n, ref in ((2, gain_grad), (4, ffn_gain_ref)):
+            for t in range(share // 128):
+                start = j * share + t * 128
+                stage[owner, n + t : n + t + 1, :] = ref[:, start : start + 128]
+    stage_hops = []
+    for d in range(1, count):
+        aim = lax.rem(mine + d, count)
+        stage_hops.append(
+            pltpu.make_async_remote_copy(
+                src_ref=stage.at[aim],
+                dst_ref=stage_got.at[d - 1],
+                send_sem=seq_send.at[d - 1],
+                recv_sem=seq_receive.at[d - 1],
+                device_id={"seq": aim},
+                device_id_type=MESH,
+            )
+        )
+    for hop in stage_hops:
+        hop.start()
+
+    def head_hops(kind, source, target):
+        return [
+            pltpu.make_async_remote_copy(
+                src_ref=source,
+                dst_ref=target.at[d - 1],
+                send_sem=head_send.at[kind, d - 1],
+                recv_sem=head_receive.at[kind, d - 1],
+                device_id={"head": lax.rem(head + d, heads)},
+                device_id_type=MESH,
+            )
+            for d in range(1, heads)
+        ]
+
+    rows.relay(0)
+    rows.relay(1)
+    ring.advance()
+    rows.relay(2)
+    rows.relay(3)
+    for hop in stage_hops:
+        hop.wait_recv()
+    total = stage[mine]
+    for d in range(count - 1):
+        total = total + stage_got[d]
+    small_ref[...] = total
+    shared[...] = total[:8]
+    shared_hops = head_hops(0, shared, shared_got)
+    for hop in shared_hops:
+        hop.start()
+    ring.advance()
+    rows.finish()
+    backs = home_copies(order, grads, input_grad_ref, grad_sems)
+    for copy in backs:
+        copy.start()
+    for hop in shared_hops:
+        hop.wait_recv()
+    small_ref[0:8] = shared[...] + (shared_got[0] + shared_got[1] + shared_got[2])
+    small_ref[1:2] = shared[1:2]
+    ring.finish()
+    low_from = 2 * DV + 2 * DK
+    tail_ref[...] = sums_ref[:, low_from : low_from + 128]
+    tail_hops = head_hops(1, tail_ref, tail_got)
+    for hop in tail_hops:
+        hop.start()
+    for hop in tail_hops:
+        hop.wait_recv()
+    for hop in stage_hops + shared_hops + tail_hops:
+        hop.wait_send()
+    tail_ref[...] = tail_ref[...] + (tail_got[0] + tail_got[1] + tail_got[2])
+    for copy in backs:
+        copy.wait()
+
+
+def last_phase(
+    part, inputs, d_resid, gains, normed, packed, d_attn, heads_out, ffn_gain, head_gain, bias, up
+):
+    count, heads = lax.axis_size("seq"), lax.axis_size("head")
+    rows, width = part.shape
+    share, quarter = width // count, rows // heads
+    columns = packed.shape[1] + heads_out.shape[1]
+    return remote_call(
+        functools.partial(last_phase_kernel, ring_order(count), heads),
+        6,
+        [NEAR, AWAY, NEAR, NEAR, AWAY, NEAR, AWAY, NEAR, NEAR, NEAR, NEAR, NEAR],
+        [AWAY, NEAR, NEAR, NEAR],
+        [
+            shape_of(BF16, rows, width),
+            shape_of(F32, share, columns),
+            shape_of(F32, SMALL, 128),
+            shape_of(F32, share, 128),
+        ],
+        [
+            pltpu.VMEM((quarter, width), BF16),
+            pltpu.SemaphoreType.DMA((count,)),
+            pltpu.VMEM((rows, width), BF16),
+            pltpu.SemaphoreType.DMA((count,)),
+            pltpu.VMEM((1, width), F32),
+            pltpu.VMEM((count, SMALL, 128), F32),
+            pltpu.VMEM((count - 1, SMALL, 128), F32),
+            pltpu.VMEM((8, 128), F32),
+            pltpu.VMEM((heads - 1, 8, 128), F32),
+            pltpu.VMEM((heads - 1, share, 128), F32),
+            pltpu.SemaphoreType.DMA((count - 1,)),
+            pltpu.SemaphoreType.DMA((count - 1,)),
+            pltpu.SemaphoreType.DMA((2, heads - 1)),
+            pltpu.SemaphoreType.DMA((2, heads - 1)),
+        ]
+        + rows_scratch(quarter, width)
+        + sum_scratch(count, rows, 2, share // 2, columns),
+        (part, inputs, d_resid, gains, normed, packed, d_attn, heads_out, ffn_gain, head_gain, bias, up),
+        2 * rows * width * columns,
+    )
 
 
 def matmul(left, right):
@@ -638,7 +1739,7 @@
     return jnp.swapaxes(shaped, -1, -2)
 
 
-def shards(
+def plain_layer(
     layer_in,
     seg_starts,
     attn_gain,
@@ -672,18 +1773,13 @@
         [value_weight, key_weight, query_weight, gate_weight, out_weight.T, decay_down], axis=1
     )
     inputs = layer_in.reshape(rows, width)
-    if share % 256 == 0:
-        normed, weights, value_key, query, gates, low, small = enter(inputs, shard, small, rank)
-        weights = weights.reshape(width, -1)
-        mark = low[:8]
-    else:
-        weights, mark = ring.gather(shard)
-        small = lax.all_gather(small, "seq")
-        gain = wide(small[:, 0, :share]).reshape(width)
-        normed = ring.near(narrow(wide(inputs) * root_scale(wide(inputs)) * gain), 1)
-        projected = matmul(normed, weights)
-        value_key, query = narrow(projected[:, : DV + DK]), narrow(projected[:, DV + DK : DV + 2 * DK])
-        gates, low = projected[:, DV + 2 * DK : 2 * DV + 2 * DK], projected[:, -rank:]
+    weights, mark = ring.gather(shard)
+    small = lax.all_gather(small, "seq")
+    gain = wide(small[:, 0, :share]).reshape(width)
+    normed = ring.near(narrow(wide(inputs) * root_scale(wide(inputs)) * gain), 1)
+    projected = matmul(normed, weights)
+    value_key, query = narrow(projected[:, : DV + DK]), narrow(projected[:, DV + DK : DV + 2 * DK])
+    gates, low = projected[:, DV + 2 * DK : 2 * DV + 2 * DK], projected[:, -rank:]
     third, mark = ring.gather(jnp.concatenate([ffn_gate, ffn_up], axis=1), mark)
     fdown_t, mark = ring.gather(ffn_down.T, mark)
     projections = weights[:, : 2 * DV + 2 * DK]
@@ -813,6 +1909,95 @@
         grad_third[:, hidden:],
         grad_fdown.T,
     )
+
+
+def fused_layer(
+    layer_in,
+    seg_starts,
+    attn_gain,
+    query_weight,
+    key_weight,
+    value_weight,
+    gate_weight,
+    decay_down,
+    decay_up,
+    decay_bias,
+    head_gain,
+    out_weight,
+    ffn_gain,
+    ffn_gate,
+    ffn_up,
+    ffn_down,
+    out_grad,
+):
+    count = lax.axis_size("seq")
+    batch, block, width = layer_in.shape
+    rows = batch * block
+    rank, share = decay_down.shape[1], attn_gain.shape[0]
+    hidden = ffn_gate.shape[1]
+    used = 2 * DV + 2 * DK
+    inputs, grad_rows = layer_in.reshape(rows, width), out_grad.reshape(rows, width)
+    starts = seg_starts.reshape(-1, CHUNK)
+    small = jnp.concatenate([attn_gain, ffn_gain, head_gain, decay_bias])
+    small = jnp.pad(small, (0, -small.size % 128))[None]
+    down = jnp.pad(decay_down, ((0, 0), (0, -rank % 128)))
+    shard = jnp.concatenate([value_weight, key_weight, query_weight, gate_weight, down], axis=1)
+
+    def tokens(field):
+        return field.reshape(batch, block, field.shape[-1])
+
+    normed, weights, out_t, value_key, query, gates, low, gains, gain_head, bias, up = enter(
+        inputs, shard, out_weight.T, small, decay_up
+    )
+    value_key, query, gates, low = map(tokens, (value_key, query, gates, low))
+    weights, out_t = weights.reshape(width, -1), out_t.reshape(width, DV)
+    run, slope, total, mixed, heads, states, part, fgate = token_phase(
+        value_key, query, gates, low, up, bias, starts, gain_head, out_t, ffn_gate
+    )
+    resid, normed_two, fup = row_phase(part, inputs, gains, ffn_up)
+    fgate, fup = fgate.reshape(width, hidden), fup.reshape(width, hidden)
+    act, d_gate, d_up, fdown_t = unit_phase(normed_two, fgate, fup, grad_rows, ffn_down.T)
+    fdown_t = fdown_t.reshape(width, hidden)
+    ffn_part = narrow(matmul_nt(act, fdown_t))
+    part = narrow(matmul_nt(d_gate, fgate) + matmul_nt(d_up, fup))
+    d_resid, d_attn, d_heads, grad_gain_two, grad_first = resid_phase(
+        part, resid, grad_rows, gains, out_t, act, normed_two, d_up
+    )
+    packed, grad_up, grad_bias, grad_gain_head, layer_out, grad_fgate = back_phase(
+        ffn_part, resid, tokens(d_heads), gates, mixed, gain_head, query, value_key, run, slope,
+        states, low, up, starts, total, normed_two, d_gate, shard.shape[1],
+    )
+    packed = packed.reshape(rows, -1)
+    part = narrow(matmul_nt(packed, weights))
+    input_grad, grad_last, small, tail = last_phase(
+        part, inputs, d_resid, gains, normed, packed, d_attn, heads.reshape(rows, DV),
+        grad_gain_two, grad_gain_head, grad_bias, grad_up,
+    )
+    lines = share // 128
+    return (
+        layer_out.reshape(batch, block, width),
+        input_grad.reshape(batch, block, width),
+        small[2 : 2 + lines].reshape(share),
+        grad_last[:, DV + DK : DV + 2 * DK],
+        grad_last[:, DV : DV + DK],
+        grad_last[:, :DV],
+        grad_last[:, DV + 2 * DK : used],
+        tail[:, :rank],
+        small[8:, : decay_up.shape[1]],
+        small[1, : decay_bias.size],
+        small[0, : head_gain.size],
+        grad_last[:, shard.shape[1] :].T,
+        small[4 : 4 + lines].reshape(share),
+        grad_fgate,
+        grad_first[:, hidden:],
+        grad_first[:, :hidden].T,
+    )
+
+
+def shards(layer_in, seg_starts, attn_gain, *rest):
+    fits = attn_gain.shape[0] == 256 and lax.axis_size("head") == 4
+    layer = fused_layer if fits and rest[4].shape[1] == 16 else plain_layer
+    return layer(layer_in, seg_starts, attn_gain, *rest)
 
 
 def solution(mesh):

time: 889 us -> 779 us (0.88)
  Pallas kernels: 131 us -> 692 us
  waiting for transfers between devices: 263 us -> 0 us
  starting transfers between devices: 116 us -> 0 us
  local copies, waits for them, and re-layouts: 133 us -> 36.4 us
  matrix products: 135 us -> 39.3 us
  other arithmetic: 70.1 us -> 0.78 us
  between operations: 28.7 us -> 1.1 us
    pallas_call x5 -> x7, Pallas kernels: 131 us -> 692 us  [remote_call(): pl.pallas_call(kernel, in_specs=in_specs, out_specs=out_specs, out_shape=...]
    ppermute x112 -> x0, waiting for transfers between devices: 263 us -> none  [the longest x28 98.4 us: scatter(): up = lax.ppermute(up, self.axis, self.right)]
    ppermute x112 -> x0, starting transfers between devices: 116 us -> none  [the longest x28 34.1 us: scatter(): down = lax.ppermute(down, self.axis, self.left)]
    dot_general x14 -> x4, matrix products: 135 us -> 39.3 us  [product(): lax.dot_general(left, right, dims, precision=precision, preferred_element...]
    unnamed x250 -> x33, local copies, waits for them, and re-layouts: 98.9 us -> 22.1 us
    convert_element_type x41 -> x0, other arithmetic: 25.6 us -> none  [the longest x39 25.5 us: narrow(): return field.astype(jnp.bfloat16)]
    concatenate x16 -> x1, local copies, waits for them, and re-layouts: 17.3 us -> 0.03 us  [fused_layer(): jnp.concatenate([value_weight, key_weight, query_weight, gate_weight, dow...]
    add x11 -> x0, other arithmetic: 9.51 us -> none  [the longest x4 4.7 us: head_scatter(): held = wide(kept) + wide(got)]
  transfers between devices with their start and end apart: 112 -> 0, of which waited for: 52 -> 0; matrix products, arithmetic and copies ran while one was open for 30% -> 0% of each run, Pallas kernels for 3% -> 0%
where the time goes in v4:
time: 779 us; the launch traced here: 770 us
  Pallas kernels  692 us (89%)
  matrix products  39.3 us (5%)
  local copies, waits for them, and re-layouts  36.4 us (5%)
    pallas_call x7, Pallas kernels, remote_call(): pl.pallas_call(kernel, in_specs=in_specs, out_specs=out_specs, out_shape=...  692 us
    dot_general x4, matrix products, product(): lax.dot_general(left, right, dims, precision=precision, preferred_element...  39.3 us
    unnamed x33, local copies, waits for them, and re-layouts  22.1 us

profile of v4, /device:TPU:0, one launch (start us, length us, event | category | flops | bytes accessed | tf_op | source)
XLA Modules:
  0.0 769.7 jit_solution(8468619346552590213)
XLA Ops:
  0.6 0.8 fusion.6
  1.4 0.6 broadcast_in_dim.3.small_ref
  2.0 1.3 reshape.94.starts_ref
  3.3 0.8 copy.33
  4.1 1.8 copy.34
  5.9 2.2 copy.35
  8.2 1.0 constant_dynamic-update-slice_fusion.3
  9.1 0.9 constant_dynamic-update-slice_fusion.2
  10.0 0.9 constant_dynamic-update-slice_fusion.1
  11.0 1.0 constant_dynamic-update-slice_fusion
  12.0 0.0 copy-start.3
  12.0 0.9 copy-done.3
  12.9 102.3 %shard_map.288 = (bf16[1024,2048]{1,0:T(8,128)(2,1)}, bf16[8,256,1664]{2,1,0:T(8,128)(2,1)}, bf16[8,256,512]{2,1,0:T(8,128)(2,1)}, bf16[1024,768]{1,0:T(8,128)(2...) custom-call(bf16[1024,2048]{1,0:T(8,128)(2,1)} %bitcast.39, ...), custom_call_target="tpu_custom_call" | custom-call | flops 6979321856 | bytes 22713600 | tf_op jit(solution)/shard_map/pallas_call | solution.py:857
  115.2 91.2 %shard_map.289 = (f32[2,512,256]{2,1,0:T(8,128)}, f32[2,512,256]{2,1,0:T(8,128)}, f32[2,1,256]{2,1,0:T(1,128)}, f32[2,512,512]{2,1,0:T(8,128)}, bf16[2,512,512]{...) custom-call(bf16[2,512,768]{2,1,0:T(8,128)(2,1)} %bitcast.47, ...), custom_call_target="tpu_custom_call" | custom-call | flops 2684354560 | bytes 26502144 | tf_op jit(solution)/shard_map/pallas_call | solution.py:857
  206.4 0.0 slice-start.4
  206.4 70.2 %shard_map.290 = (f32[256,2048]{1,0:T(8,128)}, bf16[1024,2048]{1,0:T(8,128)(2,1)}, bf16[8,256,1408]{2,1,0:T(8,128)(2,1)}) custom-call(bf16[1024,2048]{1,0:T(8,128)(2,1)} %get-tuple-element.65.part_ref, bf16[1024,2048]{1,0:T(8,128)(2,1)} %bitcast.40, f32[2,2048]{1,0:T(2,128)} %get-tuple-element.66.gain_ref, bf16[256,1408]{1,0:T(8,128)(2,1)} %block_ref.3), custom_call_target="tpu_custom_call" | custom-call | flops 33554432 | bytes 21184512 | tf_op jit(solution)/shard_map/pallas_call | solution.py:857
  276.6 0.0 slice-start.5
  276.6 82.9 %shard_map.291 = (bf16[1024,1408]{1,0:T(8,128)(2,1)}, bf16[1024,1408]{1,0:T(8,128)(2,1)}, bf16[1024,1408]{1,0:T(8,128)(2,1)}, bf16[8,256,1408]{2,1,0:T(8,128)(2,1)}) custom-call(bf16[1024,2048]{1,0:T(8,128)(2,1)} %get-tuple-element.67.normed_ref, bf16[2048,1408]{1,0:T(8,128)(2,1)} %bitcast.67, bf16[2048,1408]{1,0:T(8,128)(2,1)} %bitcast.56, ...), custom_call_target="tpu_custom_call" | custom-call | flops 17716740096 | bytes 35061760 | tf_op jit(solution)/shard_map/pallas_call | solution.py:857
  359.5 0.0 copy-start.1
  359.5 0.0 slice-start
  359.5 11.1 %convolution_convert_fusion.1.part_ref = bf16[1024,2048]{1,0:T(8,128)(2,1)} fusion(bf16[1024,1408]{1,0:T(8,128)(2,1)} %get-tuple-element.70.act_ref, bf16[2048,1408]{1,0:T(8,128)(2,1)} %bitcast.71), kind=kOutput, calls=%fused_computation.2 | convolution fusion | flops 5907677184 | bytes 12845056 | tf_op jit(solution)/shard_map/dot_general | solution.py:23
  370.6 0.0 slice-done.4
  370.6 0.0 slice-done.5
  370.6 0.0 copy-done.1
  370.6 0.0 slice-start.1
  370.6 6.7 fusion.8
  377.3 0.0 slice-done
  377.3 0.0 slice-done.1
  377.3 0.0 slice-start.2
  377.3 10.6 %add_convert_fusion.part_ref = bf16[1024,2048]{1,0:T(8,128)(2,1)} fusion(f32[1024,2048]{1,0:T(8,128)S(1)} %fusion.8, bf16[1024,1408]{1,0:T(8,128)(2,1)} %get-tuple-element.74.up_grad_ref, bf16[2048,1408]{1,0:T(8,128)(2,1)S(1)} %bitcast.59), kind=kOutput, calls=%fused_computation | convolution fusion | flops 5909774336 | bytes 21233664 | tf_op jit(solution)/shard_map/dot_general | solution.py:23
  388.0 0.0 slice-start.3
  388.0 133.2 %shard_map.292 = (f32[256,2048]{1,0:T(8,128)}, bf16[1024,2048]{1,0:T(8,128)(2,1)}, f32[1024,512]{1,0:T(8,128)}, f32[1,2048]{1,0:T(1,128)}, f32[256,2816]{1,0:T(8,128)}) custom-call(bf16[1024,2048]{1,0:T(8,128)(2,1)} %add_convert_fusion.part_ref, f32[256,2048]{1,0:T(8,128)} %get-tuple-element.72.resid_ref, bf16[1024,2048]{1,0:T(8,128)(2,1)} %bitcast.61, ...), custom_call_target="tpu_custom_call" | custom-call | flops 13958643712 | bytes 33841152 | tf_op jit(solution)/shard_map/pallas_call | solution.py:857
  521.2 104.1 %shard_map.293 = (bf16[2,512,1664]{2,1,0:T(8,128)(2,1)}, f32[16,256]{1,0:T(8,128)}, f32[1,256]{1,0:T(1,128)}, f32[1,512]{1,0:T(1,128)}, bf16[1024,2048]{1,0:T(8,128)(2,1)}, /*index=5*/f32[256,1408]{1,0:T(8,128)}) custom-call(bf16[1024,2048]{1,0:T(8,128)(2,1)} %convolution_convert_fusion.1.part_ref, f32[256,2048]{1,0:T(8,128)} %get-tuple-element.72.resid_ref, ...), custom_call_target="tpu_custom_call" | custom-call | flops 5905580032 | bytes 37202944 | tf_op jit(solution)/shard_map/pallas_call | solution.py:857
  625.3 0.0 slice-done.2
  625.3 0.0 slice-done.3
  625.3 10.9 %convolution_convert_fusion.part_ref = bf16[1024,2048]{1,0:T(8,128)(2,1)} fusion(bf16[1024,1664]{1,0:T(8,128)(2,1)} %bitcast.62, bf16[2048,1664]{1,0:T(8,128)(2,1)S(1)} %bitcast.66), kind=kOutput, calls=%fused_computation.1 | convolution fusion | flops 6981419008 | bytes 14417920 | tf_op jit(solution)/shard_map/dot_general | solution.py:23
  636.3 108.3 %shard_map.294 = (bf16[1024,2048]{1,0:T(8,128)(2,1)}, f32[256,2176]{1,0:T(8,128)}, f32[24,128]{1,0:T(8,128)}, f32[256,128]{1,0:T(8,128)}) custom-call(bf16[1024,2048]{1,0:T(8,128)(2,1)} %convolution_convert_fusion.part_ref, bf16[1024,2048]{1,0:T(8,128)(2,1)} %bitcast.41, f32[256,2048]{1,0:T(8,128)} %get-tuple-element.84.resid_grad_ref, ...), custom_call_target="tpu_custom_call" | custom-call | flops 9126805504 | bytes 29940736 | tf_op jit(solution)/shard_map/pallas_call | solution.py:857
  744.6 1.6 copy.36
  746.1 1.2 slice_bitcast_fusion.4
  747.3 1.2 slice_bitcast_fusion.5
  748.5 1.3 slice_bitcast_fusion.2
  749.8 1.3 slice.45
  751.1 1.9 fusion.7
  753.0 2.4 slice_bitcast_fusion.1
  755.4 1.0 copy.37
  756.4 3.1 slice_bitcast_fusion
  759.5 1.5 copy.38
  761.0 0.0 copy-start
  761.0 4.9 copy.46
  766.0 0.0 copy-done
  766.0 0.0 copy-start.2
  766.0 2.0 copy.47
  768.0 0.4 copy-done.2
  768.4 1.1 copy.48
  (4 shorter events, 0.0 us)
Async XLA Ops:
  12.0 0.9 copy-start.3
  206.4 164.2 %slice-start.4 = ((s8[5767168]{0:T(1024)(128)(4,1)}), s8[4194304]{0:T(1024)(128)(4,1)S(1)}, s32[]{:S(2)}) async-start(s8[5767168]{0:T(1024)(128)(4,1)} %bitcast.68), calls=%async_computation.4 | async-start | bytes 8388608
  276.6 94.0 %slice-start.5 = ((s8[5767168]{0:T(1024)(128)(4,1)}), s8[1572864]{0:T(1024)(128)(4,1)S(1)}, s32[]{:S(2)}) async-start(s8[5767168]{0:T(1024)(128)(4,1)} %bitcast.68), calls=%async_computation.5 | async-start | bytes 3145728
  359.5 11.1 %copy-start.1 = (bf16[1024,1408]{1,0:T(8,128)(2,1)S(1)}, bf16[1024,1408]{1,0:T(8,128)(2,1)}, u32[]{:S(2)}) copy-start(bf16[1024,1408]{1,0:T(8,128)(2,1)} %get-tuple-element.73.act_grad_ref) | copy-start | bytes 8650756
  359.5 17.8 %slice-start = ((s8[5767168]{0:T(1024)(128)(4,1)}), s8[4194304]{0:T(1024)(128)(4,1)S(1)}, s32[]{:S(2)}) async-start(s8[5767168]{0:T(1024)(128)(4,1)} %bitcast.57), calls=%async_computation | async-start | bytes 8388608
  370.6 6.7 slice-start.1
  377.3 248.0 %slice-start.2 = ((s8[6815744]{0:T(1024)(128)(4,1)}), s8[4194304]{0:T(1024)(128)(4,1)S(1)}, s32[]{:S(2)}) async-start(s8[6815744]{0:T(1024)(128)(4,1)} %bitcast.64), calls=%async_computation.2 | async-start | bytes 8388608
  388.0 237.4 %slice-start.3 = ((s8[6815744]{0:T(1024)(128)(4,1)}), s8[2621440]{0:T(1024)(128)(4,1)S(1)}, s32[]{:S(2)}) async-start(s8[6815744]{0:T(1024)(128)(4,1)} %bitcast.64), calls=%async_computation.3 | async-start | bytes 5242880
  761.0 4.9 copy-start
  766.0 2.4 copy-start.2

commit v5 on v4

--- a/solution.py
+++ b/solution.py
@@ -15,7 +15,7 @@
 NN = (((1,), (0,)), ((), ()))
 NT = (((1,), (1,)), ((), ()))
 TN = (((0,), (0,)), ((), ()))
-VMEM_BYTES = 56 * 1024 * 1024
+VMEM_BYTES = 60 * 1024 * 1024
 MESH = pl.DeviceIdType.MESH
 
 
@@ -374,7 +374,7 @@
 
 
 def enter_kernel(
-    order, input_ref, block_ref, out_block_ref, small_ref, rise_ref,
+    order, ready, input_ref, block_ref, out_block_ref, small_ref, rise_ref,
     normed_ref, weight_ref, out_ref, vk_ref, query_ref, gate_ref, low_ref,
     gains_ref, head_gain_ref, bias_ref, up_ref,
     smalls_ref, rises_ref, total, small_send, small_receive, rise_send, rise_receive, *scratch,
@@ -408,6 +408,7 @@
     out_ring.start()
     smalls_ref[mine] = small_ref[...]
     rises_ref[mine] = rise_ref[...]
+    ready()
 
     scales = []
     for t in range(rows // tile):
@@ -475,7 +476,7 @@
     return remote_call(
         functools.partial(enter_kernel, ring_order(count)),
         0,
-        [NEAR] * 5,
+        [LOAD, NEAR, NEAR, NEAR, NEAR],
         [NEAR] * 11,
         [
             shape_of(BF16, rows, width),
@@ -503,39 +504,46 @@
     )
 
 
+PARTS = 2
+
+
 class BlockRing:
     def __init__(self, order, block_ref, whole_ref, send, receive, local):
         self.count = count = len(order)
         half = block_ref.shape[0] // 2
+        size = half // PARTS
         aims = (block_at(order, 1), block_at(order, -1))
         self.local = pltpu.make_async_copy(block_ref, whole_ref.at[0], local)
         self.hops = {}
         for step in range(1, count):
             for side in range(2):
-                part = pl.ds(side * half, half)
                 held = (count - step + 1) if side == 0 else step - 1
                 lands = (count - step) if side == 0 else step
-                self.hops[step, side] = pltpu.make_async_remote_copy(
-                    src_ref=(block_ref if step == 1 else whole_ref.at[held]).at[part],
-                    dst_ref=whole_ref.at[lands, part],
-                    send_sem=send.at[step - 1, side],
-                    recv_sem=receive.at[step - 1, side],
-                    device_id={"seq": aims[side]},
-                    device_id_type=MESH,
-                )
+                for n in range(PARTS):
+                    part = pl.ds(side * half + n * size, size)
+                    self.hops[step, n, side] = pltpu.make_async_remote_copy(
+                        src_ref=(block_ref if step == 1 else whole_ref.at[held]).at[part],
+                        dst_ref=whole_ref.at[lands, part],
+                        send_sem=send.at[step - 1, side, n],
+                        recv_sem=receive.at[step - 1, side, n],
+                        device_id={"seq": aims[side]},
+                        device_id_type=MESH,
+                    )
         self.step = 1
 
     def start(self):
+        for n in range(PARTS):
+            for side in range(2):
+                self.hops[1, n, side].start()
         self.local.start()
-        for side in range(2):
-            self.hops[1, side].start()
 
     def advance(self):
         if self.step < self.count:
-            for side in range(2):
-                self.hops[self.step, side].wait_recv()
-                if self.step + 1 < self.count:
-                    self.hops[self.step + 1, side].start()
+            for n in range(PARTS):
+                for side in range(2):
+                    self.hops[self.step, n, side].wait_recv()
+                    if self.step + 1 < self.count:
+                        self.hops[self.step + 1, n, side].start()
             self.step += 1
 
     def finish(self):
@@ -548,8 +556,8 @@
 
 def ring_semaphores(count):
     return [
-        pltpu.SemaphoreType.DMA((count - 1, 2)),
-        pltpu.SemaphoreType.DMA((count - 1, 2)),
+        pltpu.SemaphoreType.DMA((count - 1, 2, PARTS)),
+        pltpu.SemaphoreType.DMA((count - 1, 2, PARTS)),
         pltpu.SemaphoreType.DMA,
     ]
 
@@ -579,26 +587,33 @@
             )
             for d in range(1, count)
         ]
+        self.batch = state.shape[0]
         self.swaps = [
-            pltpu.make_async_remote_copy(
-                src_ref=self.sent.at[i],
-                dst_ref=self.got.at[i],
-                send_sem=send.at[i],
-                recv_sem=receive.at[i],
-                device_id={"seq": beside},
-                device_id_type=MESH,
-            )
+            [
+                pltpu.make_async_remote_copy(
+                    src_ref=self.sent.at[i, b],
+                    dst_ref=self.got.at[i, b],
+                    send_sem=send.at[i, b],
+                    recv_sem=receive.at[i, b],
+                    device_id={"seq": beside},
+                    device_id_type=MESH,
+                )
+                for b in range(self.batch)
+            ]
             for i in range(2)
         ]
         self.links = [
-            pltpu.make_async_remote_copy(
-                src_ref=self.chain.at[r],
-                dst_ref=self.chain.at[r + 1],
-                send_sem=send.at[2 + r],
-                recv_sem=receive.at[2 + r],
-                device_id={"seq": onward},
-                device_id_type=MESH,
-            )
+            [
+                pltpu.make_async_remote_copy(
+                    src_ref=self.chain.at[r, b],
+                    dst_ref=self.chain.at[r + 1, b],
+                    send_sem=send.at[2 + r, b],
+                    recv_sem=receive.at[2 + r, b],
+                    device_id={"seq": onward},
+                    device_id_type=MESH,
+                )
+                for b in range(self.batch)
+            ]
             for r in range(self.pairs - 1)
         ]
 
@@ -613,9 +628,9 @@
         self.decays[self.mine] = self.decay[...]
         for copy in self.decay_copies:
             copy.start()
-        for b in range(self.state.shape[0]):
+        for b in range(self.batch):
             self.sent[0, b] = narrow(self.state[b, self.rows(False)])
-        self.swaps[0].start()
+            self.swaps[0][b].start()
 
     def firsts(self, b):
         kept, other = self.state[b, self.rows(True)], wide(self.got[0, b])
@@ -627,31 +642,36 @@
             jnp.where(self.ahead, other_decay, decay),
         )
 
-    def send(self, r):
-        @pl.when((self.place >= r) & (self.place + 1 < self.pairs))
-        def _():
-            self.links[r].start()
+    def sends(self, r):
+        return (self.place >= r) & (self.place + 1 < self.pairs)
 
     def join(self):
-        self.swaps[0].wait_recv()
         for copy in self.decay_copies:
             copy.wait_recv()
-        for b in range(self.state.shape[0]):
+        for b in range(self.batch):
+            self.swaps[0][b].wait_recv()
             first, second, _, decay = self.firsts(b)
             self.chain[0, b] = narrow(decay * first + second)
-        self.send(0)
+
+            @pl.when(self.sends(0))
+            def _(b=b):
+                self.links[0][b].start()
 
     def hop(self, r):
-        @pl.when(self.place >= r)
-        def _():
-            self.links[r - 1].wait_recv()
-
-        if r < self.pairs - 1:
-            self.send(r)
-
-    def finish(self):
-        own = []
-        for b in range(self.state.shape[0]):
+        for b in range(self.batch):
+
+            @pl.when(self.place >= r)
+            def _(b=b):
+                self.links[r - 1][b].wait_recv()
+
+            if r < self.pairs - 1:
+
+                @pl.when(self.sends(r))
+                def _(b=b):
+                    self.links[r][b].start()
+
+    def close(self):
+        for b in range(self.batch):
             before = wide(self.chain[1, b])
             reach = None
             for r in range(2, self.pairs):
@@ -663,20 +683,21 @@
             first, _, decay, _ = self.firsts(b)
             after = decay * before + first
             self.sent[1, b] = narrow(jnp.where(self.ahead, after, before))
-            own.append(jnp.where(self.ahead, before, after))
-        self.swaps[1].start()
-        for b in range(self.state.shape[0]):
-            self.state[b, self.rows(True)] = own[b]
-        self.swaps[1].wait_recv()
-        for b in range(self.state.shape[0]):
+            self.swaps[1][b].start()
+            self.state[b, self.rows(True)] = jnp.where(self.ahead, before, after)
+
+    def finish(self):
+        for b in range(self.batch):
+            self.swaps[1][b].wait_recv()
             self.state[b, self.rows(False)] = wide(self.got[1, b])
-        for copy in self.decay_copies + self.swaps:
+        for copy in self.decay_copies + self.swaps[0] + self.swaps[1]:
             copy.wait_send()
         for r in range(self.pairs - 1):
 
-            @pl.when((self.place >= r) & (self.place + 1 < self.pairs))
+            @pl.when(self.sends(r))
             def _(r=r):
-                self.links[r].wait_send()
+                for b in range(self.batch):
+                    self.links[r][b].wait_send()
 
 
 def handover_scratch(count, batch):
@@ -688,8 +709,8 @@
         pltpu.VMEM((count // 2, *half), BF16),
         pltpu.SemaphoreType.DMA((count - 1,)),
         pltpu.SemaphoreType.DMA((count - 1,)),
-        pltpu.SemaphoreType.DMA((count // 2 + 1,)),
-        pltpu.SemaphoreType.DMA((count // 2 + 1,)),
+        pltpu.SemaphoreType.DMA((count // 2 + 1, batch)),
+        pltpu.SemaphoreType.DMA((count // 2 + 1, batch)),
     ]
 
 
@@ -793,21 +814,27 @@
 
 
 def token_phase_kernel(
-    order, vk_ref, query_ref, gate_ref, low_ref, up_ref, bias_ref, starts_ref, gain_ref,
-    out_ref, block_ref,
-    run_ref, slope_ref, total_ref, mixed_ref, heads_ref, states_ref, part_ref, whole_ref,
-    state, ring_send, ring_receive, ring_local, mark_ref, row_ref, *scratch,
+    order, early, ready, vk_ref, query_ref, gate_ref, low_ref, up_ref, bias_ref, starts_ref, gain_ref,
+    out_ref, block_ref, down_ref,
+    run_ref, slope_ref, total_ref, mixed_ref, heads_ref, states_ref, part_ref, whole_ref, down_whole,
+    state, ring_send, ring_receive, ring_local, down_send, down_receive, down_local,
+    mark_ref, row_ref, *scratch,
 ):
     count = len(order)
     ring = BlockRing(order, block_ref, whole_ref, ring_send, ring_receive, ring_local)
     hand = Handover(count, False, state, total_ref, scratch)
+    down_ring = BlockRing(
+        order, down_ref.at[:, pl.ds(0, early)], down_whole, down_send, down_receive, down_local
+    )
     hand.clear()
     greet("seq", count)
+    ready(9)
     ring.start()
     fill_marks(starts_ref, mark_ref, row_ref)
     state[...] = jnp.zeros_like(state)
     total_ref[...] = jnp.ones_like(total_ref)
     chunks = run_ref.shape[1] // CHUNK
+    ready(0, 3)
 
     @pl.loop(0, chunks)
     def _(i):
@@ -824,22 +851,30 @@
     ring.advance()
     for r in range(1, count // 2):
         hand.hop(r)
-        if r % 2 == 0:
-            ring.advance()
+        ring.advance()
+    hand.close()
+    ready()
+    ring.advance()
+    down_ring.start()
     hand.finish()
-    ring.advance()
-
-    @pl.loop(0, chunks)
-    def _(i):
-        at = chunk_at(i)
-        mixer_chunk(
-            query_ref.at[:, at], vk_ref.at[:, at, pl.ds(0, DV)], vk_ref.at[:, at, pl.ds(DV, DK)],
-            run_ref.at[:, at], mark_ref.at[:, at], row_ref.at[pl.ds(i, 1)], gate_ref.at[:, at],
-            gain_ref, heads_ref.at[:, at], mixed_ref.at[:, at], states_ref.at[pl.ds(2 * i, 2)],
-            state,
-        )
-
-    ring.advance()
+    ring.finish()
+    down_ring.advance()
+
+    def mixer(begin, end):
+        @pl.loop(begin, end)
+        def _(i):
+            at = chunk_at(i)
+            mixer_chunk(
+                query_ref.at[:, at], vk_ref.at[:, at, pl.ds(0, DV)],
+                vk_ref.at[:, at, pl.ds(DV, DK)], run_ref.at[:, at], mark_ref.at[:, at],
+                row_ref.at[pl.ds(i, 1)], gate_ref.at[:, at], gain_ref, heads_ref.at[:, at],
+                mixed_ref.at[:, at], states_ref.at[pl.ds(2 * i, 2)], state,
+            )
+
+    mixer(0, chunks // 2)
+    down_ring.advance()
+    mixer(chunks // 2, chunks)
+    down_ring.advance()
     batch, block, _ = heads_ref.shape
     tile = 256
     for b in range(batch):
@@ -847,16 +882,36 @@
             field = heads_ref[b, t * tile : (t + 1) * tile]
             start = b * block + t * tile
             part_ref[start : start + tile] = narrow(product(field, out_ref[...], NT))
-        ring.advance()
-    ring.finish()
+        down_ring.advance()
+    down_ring.finish()
 
 
 def remote_call(kernel, number, in_specs, out_specs, out_shape, scratch, operands, flops):
     moved = sum(a.size * a.dtype.itemsize for a in operands)
     moved += sum(s.size * s.dtype.itemsize for s in out_shape)
+    loads = [i for i, spec in enumerate(in_specs) if spec is LOAD]
+    scratch = list(scratch)
+    scratch += [pltpu.VMEM(operands[i].shape, operands[i].dtype) for i in loads]
+    scratch += [pltpu.SemaphoreType.DMA((max(len(loads), 1),))]
+
+    def body(*refs):
+        refs = list(refs)
+        refs, buffers, arrivals = refs[: -1 - len(loads)], refs[-1 - len(loads) : -1], refs[-1]
+        waits = {}
+        for n, (i, buffer) in enumerate(zip(loads, buffers)):
+            waits[i] = pltpu.make_async_copy(refs[i], buffer, arrivals.at[n])
+            waits[i].start()
+            refs[i] = buffer
+
+        def ready(*positions):
+            for i in positions or list(waits):
+                waits.pop(i).wait()
+
+        kernel(ready, *refs)
+
     return pl.pallas_call(
-        kernel,
-        in_specs=in_specs,
+        body,
+        in_specs=[AWAY if spec is LOAD else spec for spec in in_specs],
         out_specs=out_specs,
         out_shape=out_shape,
         scratch_shapes=scratch,
@@ -867,19 +922,20 @@
     )(*operands)
 
 
+LOAD = None
 NEAR = pl.BlockSpec(memory_space=pltpu.VMEM)
 AWAY = pl.BlockSpec(memory_space=pl.ANY)
 
 
-def token_phase(value_key, query, gates, low, up, bias, starts, gain, out_t, block):
+def token_phase(value_key, query, gates, low, up, bias, starts, gain, out_t, block, down, early):
     count = lax.axis_size("seq")
     batch, length, _ = low.shape
     chunks, width = length // CHUNK, out_t.shape[0]
     return remote_call(
-        functools.partial(token_phase_kernel, ring_order(count)),
+        functools.partial(token_phase_kernel, ring_order(count), early),
         1,
-        [NEAR] * 9 + [AWAY],
-        [NEAR] * 7 + [AWAY],
+        [LOAD, LOAD, LOAD, LOAD, NEAR, NEAR, NEAR, NEAR, LOAD, LOAD, LOAD],
+        [NEAR] * 7 + [AWAY] * 2,
         [
             shape_of(F32, batch, length, DK),
             shape_of(F32, batch, length, DK),
@@ -889,18 +945,20 @@
             shape_of(BF16, 2 * chunks, batch, DV, DK),
             shape_of(BF16, batch * length, width),
             shape_of(BF16, count, *block.shape),
+            shape_of(BF16, count, down.shape[0], early),
         ],
         [pltpu.VMEM((batch, DV, DK), F32)]
         + ring_semaphores(count)
+        + ring_semaphores(count)
         + marks_scratch(batch, length)
         + handover_scratch(count, batch),
-        (value_key, query, gates, low, up, bias, starts, gain, out_t, block),
+        (value_key, query, gates, low, up, bias, starts, gain, out_t, block, down),
         2 * batch * length * DV * (2 * DK + width),
     )
 
 
 def row_phase_kernel(
-    order, heads, part_ref, input_ref, gain_ref, block_ref,
+    order, heads, ready, part_ref, input_ref, gain_ref, block_ref,
     resid_ref, normed_ref, whole_ref,
     own, own_sems, ring_send, ring_receive, ring_local, *scratch,
 ):
@@ -911,9 +969,11 @@
     for copy in copies:
         copy.start()
     greet_all(len(order), heads)
+    ready(3)
+    ring.start()
+    ready()
     for p in range(PIECES):
         rows.start(p)
-    ring.start()
 
     def middle(here, total):
         resid = wide(own[here]) + total
@@ -944,7 +1004,7 @@
     return remote_call(
         functools.partial(row_phase_kernel, ring_order(count), heads),
         2,
-        [NEAR, AWAY, NEAR, AWAY],
+        [LOAD, AWAY, NEAR, LOAD],
         [NEAR] * 2 + [AWAY],
         [
             shape_of(F32, rows // heads, width),
@@ -1001,6 +1061,17 @@
         pltpu.VMEM((batch, length, 1), F32),
         pltpu.VMEM((length // CHUNK, batch, 1, CHUNK), F32),
     ]
+
+
+def split_columns(widths):
+    pieces, begin = [], 0
+    for item, columns in enumerate(widths):
+        number = -(-columns // 1024)
+        size = -(-columns // (128 * number)) * 128
+        for start in range(0, columns, size):
+            pieces.append((item, start, min(size, columns - start), begin + start))
+        begin += columns
+    return pieces
 
 
 class SumRing:
@@ -1015,6 +1086,7 @@
         self.count = count = len(order)
         self.half = half = out_ref.shape[0] // 2
         self.buffers = {id(left): buffer for left, buffer in zip(lefts, buffers)}
+        self.pieces = split_columns([right.shape[1] for _, right, _ in items])
         homes = {id(left): home for left, _, home in items}
         aims = (block_at(order, 1), block_at(order, -1))
         self.loads, self.hops = {}, {}
@@ -1029,12 +1101,14 @@
                         buffer.at[k % 2, side],
                         load.at[k % 2, side, n],
                     )
-                if k < count - 1:
-                    self.hops[k, side] = pltpu.make_async_remote_copy(
-                        src_ref=self.sent.at[k % 2, side],
-                        dst_ref=self.got.at[k, side],
-                        send_sem=send.at[k, side],
-                        recv_sem=receive.at[k, side],
+                if k == count - 1:
+                    continue
+                for n, (_, _, size, begin) in enumerate(self.pieces):
+                    self.hops[k, side, n] = pltpu.make_async_remote_copy(
+                        src_ref=self.sent.at[k % 2, side, :, pl.ds(begin, size)],
+                        dst_ref=self.got.at[k, side, :, pl.ds(begin, size)],
+                        send_sem=send.at[k, side, n],
+                        recv_sem=receive.at[k, side, n],
                         device_id={"seq": aims[side]},
                         device_id_type=MESH,
                     )
@@ -1058,26 +1132,22 @@
         for side in range(2):
             for n in range(self.number):
                 self.loads[k, side, n].wait()
-            products = [
-                product(self.buffers[id(left)][k % 2, side], right[...], TN)
-                for left, right, _ in self.items
-            ]
-            if k > 0:
-                self.hops[k - 1, side].wait_recv()
-            if 2 <= k < last:
-                self.hops[k - 2, side].wait_send()
-            column = 0
-            for value in products:
-                columns = slice(column, column + value.shape[1])
-                column += value.shape[1]
+        for n, (item, start, size, begin) in enumerate(self.pieces):
+            left, right, _ = self.items[item]
+            columns = slice(begin, begin + size)
+            for side in range(2):
+                buffer = self.buffers[id(left)]
+                value = product(buffer[k % 2, side], right[:, start : start + size], TN)
                 if k > 0:
+                    self.hops[k - 1, side, n].wait_recv()
                     value = value + wide(self.got[k - 1, side, :, columns])
                 if k < last:
+                    if k >= 2:
+                        self.hops[k - 2, side, n].wait_send()
                     self.sent[k % 2, side, :, columns] = narrow(value)
+                    self.hops[k, side, n].start()
                 else:
                     self.out[side * self.half : (side + 1) * self.half, columns] = value
-            if k < last:
-                self.hops[k, side].start()
         self.load(k + 2)
         self.k += 1
 
@@ -1085,113 +1155,96 @@
         while self.k < self.count:
             self.advance()
         for k in (self.count - 3, self.count - 2):
-            for side in range(2):
-                self.hops[k, side].wait_send()
-
-
-def sum_scratch(count, rows, lefts, half, columns):
+            for n in range(len(self.pieces)):
+                for side in range(2):
+                    self.hops[k, side, n].wait_send()
+
+
+def sum_scratch(count, rows, lefts, half, widths):
+    columns, pieces = sum(widths), len(split_columns(widths))
     return [pltpu.VMEM((2, 2, rows, half), BF16)] * lefts + [
         pltpu.VMEM((2, 2, half, columns), BF16),
         pltpu.VMEM((count - 1, 2, half, columns), BF16),
         pltpu.SemaphoreType.DMA((2, 2, lefts)),
-        pltpu.SemaphoreType.DMA((count - 1, 2)),
-        pltpu.SemaphoreType.DMA((count - 1, 2)),
+        pltpu.SemaphoreType.DMA((count - 1, 2, pieces)),
+        pltpu.SemaphoreType.DMA((count - 1, 2, pieces)),
     ]
 
 
 def unit_phase_kernel(
-    order, normed_ref, gate_ref, up_ref, grad_ref, block_ref,
+    order, ready, normed_ref, gate_ref, up_ref, grad_ref, block_ref, early_ref,
     act_ref, gate_grad_ref, up_grad_ref, whole_ref,
-    pre_gate, pre_up, act_grad, tiles, tile_sems, ring_send, ring_receive, ring_local,
+    pre_gate, pre_up, act_grad, tiles, tile_sems, early_sem, ring_send, ring_receive, ring_local,
 ):
     count = len(order)
-    ring = BlockRing(order, block_ref, whole_ref, ring_send, ring_receive, ring_local)
+    early = early_ref.shape[2]
+    late = block_ref.shape[1] - early
+    ring = BlockRing(
+        order, block_ref.at[:, pl.ds(early, late)], whole_ref.at[:, :, pl.ds(early, late)],
+        ring_send, ring_receive, ring_local,
+    )
+    placed = pltpu.make_async_copy(early_ref, whole_ref.at[:, :, pl.ds(0, early)], early_sem)
     greet("seq", count)
     ring.start()
-    rows = normed_ref.shape[0]
-    tile = 128
-    share, half = block_ref.shape[0], block_ref.shape[0] // 2
+    rows, width = normed_ref.shape
+    tile = 256
+    share = block_ref.shape[0]
 
     def written(kind, target, i):
         return pltpu.make_async_copy(
             tiles.at[kind], target.at[pl.ds(i * tile, tile)], tile_sems.at[kind]
         )
 
-    def forward(begin, end):
-        @pl.loop(begin, end)
-        def _(i):
-            here = pl.ds(pl.multiple_of(i * tile, tile), tile)
-            field = normed_ref[here]
-            gate = product(field, gate_ref[...], NN)
-            up = product(field, up_ref[...], NN)
-            pre_gate[here] = gate
-            pre_up[here] = up
-
-            @pl.when(i > 0)
-            def _():
-                written(0, act_ref, i - 1).wait()
-
-            tiles[0] = narrow(gate * jax.nn.sigmoid(gate) * up)
-            written(0, act_ref, i).start()
-
-    def multiply(parts, begin):
-        @pl.loop(0, rows // 256)
-        def _(t):
-            here = pl.ds(pl.multiple_of(t * 256, 256), 256)
-            lefts, rights = [], []
-            for slot, side in parts:
-                start = pl.multiple_of(block_at(order, slot) * share + side * half, half)
-                lefts.append(grad_ref[here, pl.ds(start, half)])
-                source = block_ref if slot == 0 else whole_ref.at[slot]
-                rights.append(source[side * half : (side + 1) * half])
-            added = product(jnp.concatenate(lefts, axis=1), jnp.concatenate(rights, axis=0), NN)
-            if begin:
-                act_grad[here] = added
-            else:
-                act_grad[here] += added
-
+    ready(0, 1, 2)
+    placed.start()
     steps = rows // tile
-    arrived = []
-    done = 0
-    for step in range(1, count):
-        goal = min(steps, (step * steps + count - 3) // (count - 2))
-        if goal > done:
-            forward(done, goal)
-            done = goal
+    for i in range(steps):
+        here = pl.ds(i * tile, tile)
+        field = normed_ref[here]
+        gate = product(field, gate_ref[...], NN)
+        pre_gate[here] = gate
+        up = product(field, up_ref[...], NN)
+        pre_up[here] = up
+        if i > 0:
+            written(0, act_ref, i - 1).wait()
+        tiles[0] = narrow(gate * jax.nn.sigmoid(gate) * up)
+        written(0, act_ref, i).start()
         ring.advance()
-        arrived += [(count - step, 0), (step, 1)]
-        if step == 1:
-            multiply([(0, 0), (0, 1)] + arrived, True)
-            arrived = []
-        elif len(arrived) == 4:
-            multiply(arrived, False)
-            arrived = []
-    if arrived:
-        multiply(arrived, False)
+    ready()
+    placed.wait()
+
+    def against(here, columns):
+        parts = [
+            grad_ref[here, pl.ds(pl.multiple_of(block_at(order, r) * share, share), share)]
+            for r in range(count)
+        ]
+        right = whole_ref[:, :, columns].reshape(width, -1)
+        return product(jnp.concatenate(parts, axis=1), right, NN)
+
+    for i in range(steps):
+        act_grad[i * tile : (i + 1) * tile] = against(pl.ds(i * tile, tile), slice(0, early))
+        if i % 2:
+            ring.advance()
     written(0, act_ref, steps - 1).wait()
-
-    @pl.loop(0, steps)
-    def _(i):
-        here = pl.ds(pl.multiple_of(i * tile, tile), tile)
-        gate, up, grad = pre_gate[here], pre_up[here], act_grad[here]
-        sigma = jax.nn.sigmoid(gate)
-
-        @pl.when(i > 0)
-        def _():
-            written(0, gate_grad_ref, i - 1).wait()
-            written(1, up_grad_ref, i - 1).wait()
-
-        tiles[0] = narrow(grad * up * sigma * (1.0 + gate * (1.0 - sigma)))
-        tiles[1] = narrow(grad * gate * sigma)
-        written(0, gate_grad_ref, i).start()
-        written(1, up_grad_ref, i).start()
-
-    written(0, gate_grad_ref, steps - 1).wait()
-    written(1, up_grad_ref, steps - 1).wait()
     ring.finish()
-
-
-def unit_phase(normed_two, fgate, fup, grad_rows, block):
+    for i in range(steps):
+        here = pl.ds(i * tile, tile)
+        ends = against(here, slice(early, early + late))
+        for kind, target in ((0, gate_grad_ref), (1, up_grad_ref)):
+            if i > 0:
+                written(kind, target, i - 1).wait()
+        for columns, grad in ((slice(0, early), act_grad[here]), (slice(early, early + late), ends)):
+            gate, up = pre_gate[here, columns], pre_up[here, columns]
+            sigma = jax.nn.sigmoid(gate)
+            tiles[0, :, columns] = narrow(grad * up * sigma * (1.0 + gate * (1.0 - sigma)))
+            tiles[1, :, columns] = narrow(grad * gate * sigma)
+        for kind, target in ((0, gate_grad_ref), (1, up_grad_ref)):
+            written(kind, target, i).start()
+    for kind, target in ((0, gate_grad_ref), (1, up_grad_ref)):
+        written(kind, target, steps - 1).wait()
+
+
+def unit_phase(normed_two, fgate, fup, grad_rows, block, early):
     count = lax.axis_size("seq")
     rows, width = normed_two.shape
     hidden = block.shape[1]
@@ -1199,37 +1252,68 @@
     return remote_call(
         functools.partial(unit_phase_kernel, ring_order(count)),
         3,
-        [NEAR] * 5,
+        [LOAD] * 4 + [AWAY, AWAY],
         [AWAY] * 3 + [NEAR],
         [flat, flat, flat, shape_of(BF16, count, *block.shape)],
-        [pltpu.VMEM((rows, hidden), F32)] * 3
-        + [pltpu.VMEM((2, 128, hidden), BF16), pltpu.SemaphoreType.DMA((2,))]
+        [
+            pltpu.VMEM((rows, hidden), F32),
+            pltpu.VMEM((rows, hidden), F32),
+            pltpu.VMEM((rows, early.shape[2]), F32),
+            pltpu.VMEM((2, 256, hidden), BF16),
+            pltpu.SemaphoreType.DMA((2,)),
+            pltpu.SemaphoreType.DMA,
+        ]
         + ring_semaphores(count),
-        (normed_two, fgate, fup, grad_rows, block),
+        (normed_two, fgate, fup, grad_rows, block, early),
         6 * rows * width * hidden,
     )
 
 
 def resid_phase_kernel(
-    order, heads, part_ref, resid_ref, grad_ref, gain_ref, out_ref, act_ref, normed_ref, up_grad_ref,
-    resid_grad_ref, attn_grad_ref, heads_grad_ref, gain_grad_ref, sums_ref,
-    own, own_sems, *scratch,
+    order, heads, ready, part_ref, resid_ref, grad_ref, gain_ref, out_ref, act_ref, normed_ref,
+    up_grad_ref, gate_ref, mixed_ref, head_gain_ref, query_ref, run_ref, starts_ref, total_ref, ffn_ref,
+    resid_grad_ref, attn_grad_ref, gates_grad_ref, mixed_grad_ref, state_ref, gain_grad_ref,
+    head_gain_grad_ref, layer_ref, sums_ref,
+    own, own_sems, wholes, whole_sems, ffn_sem, pair, pair_sems, heads_grad, state, mark_ref, row_ref,
+    *scratch,
 ):
     count = len(order)
-    rows = Rows(part_ref, attn_grad_ref, scratch[:5])
+    rows = Rows(part_ref, wholes, scratch[:5])
+    hand = Handover(count, True, state, total_ref, scratch[5:13])
     ring = SumRing(
-        order, [(grad_ref, act_ref, True), (normed_ref, up_grad_ref, False)], sums_ref, scratch[5:]
+        order, [(grad_ref, act_ref, True), (normed_ref, up_grad_ref, False)], sums_ref, scratch[13:]
     )
     first = pl.multiple_of(rows.own * rows.share, rows.share)
     copies = near_copies(order, grad_ref, own, pl.ds(first, rows.share), own_sems)
+    ring.prepare()
     for copy in copies:
         copy.start()
-    ring.prepare()
+    batch, length, _ = run_ref.shape
+    chunks = length // CHUNK
+    pairs = [
+        [
+            pltpu.make_async_copy(
+                field.at[:, pl.ds((chunks - 1 - i) * CHUNK, CHUNK)],
+                pair.at[i % 2, kind],
+                pair_sems.at[i % 2, kind],
+            )
+            for kind, field in enumerate((gate_ref, mixed_ref))
+        ]
+        for i in range(chunks)
+    ]
+    hand.clear()
     greet_all(count, heads)
+    ready(0)
     for p in range(PIECES):
         rows.start(p)
+    ready(5, 7)
     ring.advance()
+    for copy in pairs[0] + pairs[1]:
+        copy.start()
     gain_grad_ref[...] = jnp.zeros_like(gain_grad_ref)
+    head_gain_grad_ref[...] = jnp.zeros_like(head_gain_grad_ref)
+    state[...] = jnp.zeros_like(state)
+    fill_marks(starts_ref, mark_ref, row_ref)
 
     def middle(here, total):
         resid = resid_ref[here]
@@ -1240,10 +1324,14 @@
         resid_grad_ref[here] = grad
         return narrow(grad)
 
+    def layer(here, total):
+        return narrow(resid_ref[here] + total)
+
     for p in range(PIECES):
         rows.cross(p)
     for copy in copies:
         copy.wait()
+    ready()
     rows.turn(0, middle)
     ring.advance()
     for p in range(1, PIECES):
@@ -1254,93 +1342,130 @@
         if p == 2:
             ring.advance()
     rows.finish()
-    for t in range(4):
-        at = pl.ds(t * rows.share, rows.share)
-        heads_grad_ref[at] = product(attn_grad_ref[at], out_ref[...], NN)
+    kept = pltpu.make_async_copy(wholes, attn_grad_ref, whole_sems.at[0])
+    kept.start()
+    following = pltpu.make_async_copy(ffn_ref, part_ref, ffn_sem)
+    following.start()
+
+    for i in range(chunks):
+        at = pl.ds((chunks - 1 - i) * CHUNK, CHUNK)
+        for copy in pairs[i]:
+            copy.wait()
+        for b in range(batch):
+            here = pl.ds(b * length + (chunks - 1 - i) * CHUNK, CHUNK)
+            heads_grad[b] = product(wholes[here], out_ref[...], NN)
+        head_back_chunk(
+            heads_grad, pair.at[i % 2, 0], pair.at[i % 2, 1], head_gain_ref,
+            query_ref.at[:, at], run_ref.at[:, at], mark_ref.at[:, at],
+            gates_grad_ref.at[:, at], mixed_grad_ref.at[:, at], head_gain_grad_ref, state,
+        )
+        if i + 2 < chunks:
+            for copy in pairs[i + 2]:
+                copy.start()
+
+    hand.begin()
+    kept.wait()
+    following.wait()
+    for p in range(PIECES):
+        rows.start(p)
+    ring.advance()
+    hand.join()
+    for p in range(PIECES):
+        rows.cross(p)
+    for r in range(1, count // 2):
+        hand.hop(r)
+        if r < PIECES:
+            rows.turn(r - 1, layer)
+        if r == 2:
+            ring.advance()
+    for r in range(count // 2 - 1, PIECES):
+        rows.turn(r, layer)
+    hand.close()
+    ring.advance()
+    hand.finish()
+    state_ref[...] = narrow(state[...])
+    for p in range(PIECES):
+        rows.relay(p)
+        if p == 2:
+            ring.advance()
+    rows.finish()
+    backs = home_copies(order, wholes, layer_ref, whole_sems)
+    for copy in backs:
+        copy.start()
     ring.finish()
-
-
-def resid_phase(part, resid, grad_rows, gains, out_t, act, normed_two, d_up):
+    for copy in backs:
+        copy.wait()
+
+
+def resid_phase(
+    part, resid, grad_rows, gains, out_t, act, normed_two, d_up, gates, mixed, head_gain, query, run,
+    starts, total, ffn_part,
+):
     count, heads = lax.axis_size("seq"), lax.axis_size("head")
     rows, width = part.shape
+    batch, length, _ = run.shape
     share, hidden = width // count, act.shape[1]
     quarter = rows // heads
     return remote_call(
         functools.partial(resid_phase_kernel, ring_order(count), heads),
         4,
-        [NEAR, NEAR, AWAY, NEAR, NEAR, NEAR, AWAY, NEAR],
-        [NEAR] * 5,
+        [LOAD, LOAD, AWAY, NEAR, LOAD, LOAD, AWAY, LOAD, AWAY, AWAY, NEAR, LOAD, LOAD, NEAR, NEAR, AWAY],
+        [NEAR, AWAY, NEAR, NEAR, NEAR, NEAR, NEAR, AWAY, NEAR],
         [
             shape_of(F32, quarter, width),
             shape_of(BF16, rows, width),
-            shape_of(F32, rows, DV),
+            shape_of(BF16, batch, length, DV),
+            shape_of(BF16, batch, length, DV),
+            shape_of(BF16, batch, DV, DK),
             shape_of(F32, 1, width),
+            shape_of(F32, 1, DV),
+            shape_of(BF16, rows, width),
             shape_of(F32, share, 2 * hidden),
         ],
-        [pltpu.VMEM((quarter, width), BF16), pltpu.SemaphoreType.DMA((count,))]
+        [
+            pltpu.VMEM((quarter, width), BF16),
+            pltpu.SemaphoreType.DMA((count,)),
+            pltpu.VMEM((rows, width), BF16),
+            pltpu.SemaphoreType.DMA((count,)),
+            pltpu.SemaphoreType.DMA,
+            pltpu.VMEM((2, 2, batch, CHUNK, DV), F32),
+            pltpu.SemaphoreType.DMA((2, 2)),
+            pltpu.VMEM((batch, CHUNK, DV), F32),
+            pltpu.VMEM((batch, DV, DK), F32),
+        ]
+        + marks_scratch(batch, length)
         + rows_scratch(quarter, width)
-        + sum_scratch(count, rows, 2, share // 2, 2 * hidden),
-        (part, resid, grad_rows, gains, out_t, act, normed_two, d_up),
+        + handover_scratch(count, batch)
+        + sum_scratch(count, rows, 2, share // 2, [hidden, hidden]),
+        (part, resid, grad_rows, gains, out_t, act, normed_two, d_up, gates, mixed, head_gain, query,
+         run, starts, total, ffn_part),
         2 * rows * width * (2 * hidden + DV),
     )
 
 
 def back_phase_kernel(
-    order, heads, part_ref, resid_ref, heads_grad_ref, gate_ref, mixed_ref, gain_ref, query_ref,
-    vk_ref, run_ref, slope_ref, states_ref, low_ref, up_ref, starts_ref, total_ref,
-    normed_ref, act_grad_ref,
-    packed_ref, up_grad_ref, bias_grad_ref, gain_grad_ref, layer_ref, sums_ref,
-    state, mixed_grad, layer, layer_sems, mark_ref, row_ref, *scratch,
+    order, ready, query_ref, vk_ref, run_ref, slope_ref, states_ref, low_ref, up_ref, starts_ref,
+    mixed_grad_ref, later_ref, gates_grad_ref, normed_ref, act_grad_ref, weight_ref,
+    packed_ref, up_grad_ref, bias_grad_ref, part_ref, sums_ref,
+    state, mark_ref, row_ref, *scratch,
 ):
     count = len(order)
-    rows = Rows(part_ref, layer, scratch[:5])
-    hand = Handover(count, True, state, total_ref, scratch[5:13])
-    ring = SumRing(order, [(normed_ref, act_grad_ref, False)], sums_ref, scratch[13:])
-    hand.clear()
+    ring = SumRing(order, [(normed_ref, act_grad_ref, False)], sums_ref, scratch)
     ring.prepare()
-    greet_all(count, heads)
-    for p in range(PIECES):
-        rows.start(p)
+    greet("seq", count)
+    ready(12)
     ring.advance()
     batch, length, _ = run_ref.shape
     chunks = length // CHUNK
     gates_from, low_from = DV + 2 * DK, 2 * DV + 2 * DK
     fill_marks(starts_ref, mark_ref, row_ref)
-    state[...] = jnp.zeros_like(state)
-    for ref in (gain_grad_ref, up_grad_ref, bias_grad_ref):
+    for ref in (up_grad_ref, bias_grad_ref):
         ref[...] = jnp.zeros_like(ref)
-    packed_ref[:, :, low_from:] = jnp.zeros(packed_ref.shape[:2] + (packed_ref.shape[2] - low_from,), BF16)
-
-    @pl.loop(0, chunks)
-    def _(i):
-        at = chunk_at(chunks - 1 - i)
-        head_back_chunk(
-            heads_grad_ref.at[:, at], gate_ref.at[:, at], mixed_ref.at[:, at], gain_ref,
-            query_ref.at[:, at], run_ref.at[:, at], mark_ref.at[:, at],
-            packed_ref.at[:, at, pl.ds(gates_from, DV)], mixed_grad.at[:, at], gain_grad_ref, state,
-        )
-
-    def middle(here, total):
-        return narrow(resid_ref[here] + total)
-
-    hand.begin()
-    for p in range(PIECES):
-        rows.cross(p)
-    ring.advance()
-    hand.join()
-    rows.turn(0, middle)
-    ring.advance()
-    for r in range(1, count // 2):
-        hand.hop(r)
-        if r < PIECES:
-            rows.turn(r, middle)
-    ring.advance()
-    hand.finish()
-    for r in range(count // 2, PIECES):
-        rows.turn(r, middle)
-    rows.relay(0)
-    rows.relay(1)
-    ring.advance()
+    spare = packed_ref.shape[2] - low_from
+    packed_ref[:, :, low_from:] = jnp.zeros((batch, length, spare), BF16)
+    ready(0, 1, 2, 3, 4, 5, 8, 9, 10)
+    state[...] = wide(later_ref[...])
+    packed_ref[:, :, gates_from:low_from] = gates_grad_ref[...]
 
     def back(begin, end):
         @pl.loop(begin, end)
@@ -1350,7 +1475,7 @@
             mixer_back_chunk(
                 query_ref.at[:, at], vk_ref.at[:, at, pl.ds(0, DV)],
                 vk_ref.at[:, at, pl.ds(DV, DK)], run_ref.at[:, at], slope_ref.at[:, at],
-                mark_ref.at[:, at], row_ref.at[pl.ds(n, 1)], mixed_grad.at[:, at],
+                mark_ref.at[:, at], row_ref.at[pl.ds(n, 1)], mixed_grad_ref.at[:, at],
                 states_ref.at[pl.ds(2 * n, 1)], states_ref.at[pl.ds(2 * n + 1, 1)],
                 low_ref.at[:, at], up_ref,
                 packed_ref.at[:, at, pl.ds(DV + DK, DK)], packed_ref.at[:, at, pl.ds(0, DV)],
@@ -1359,52 +1484,44 @@
             )
 
     back(0, chunks // 2)
-    rows.relay(2)
     ring.advance()
     back(chunks // 2, chunks)
-    rows.relay(3)
-    rows.finish()
-    copies = home_copies(order, layer, layer_ref, layer_sems)
-    for copy in copies:
-        copy.start()
+    ring.advance()
+    ready()
+    tile = 256
+    for b in range(batch):
+        for t in range(length // tile):
+            field = packed_ref[b, t * tile : (t + 1) * tile]
+            start = b * length + t * tile
+            part_ref[start : start + tile] = narrow(product(field, weight_ref[...], NT))
+        ring.advance()
     ring.finish()
-    for copy in copies:
-        copy.wait()
 
 
 def back_phase(
-    part, resid, d_heads, gates, mixed, gain, query, vk, run, slope, states, low, up, starts, total,
-    normed_two, d_gate, packed_cols,
+    query, vk, run, slope, states, low, up, starts, d_mixed, later, d_gates, normed_two, d_gate, weights
 ):
-    count, heads = lax.axis_size("seq"), lax.axis_size("head")
-    rows, width = part.shape
+    count = lax.axis_size("seq")
     batch, length, rank = low.shape
-    share, hidden, quarter = width // count, d_gate.shape[1], rows // heads
+    width, packed_cols = weights.shape
+    share, hidden, rows = width // count, d_gate.shape[1], d_gate.shape[0]
     return remote_call(
-        functools.partial(back_phase_kernel, ring_order(count), heads),
+        functools.partial(back_phase_kernel, ring_order(count)),
         5,
-        [NEAR] * 15 + [AWAY, NEAR],
-        [NEAR] * 4 + [AWAY, NEAR],
+        [LOAD] * 6 + [NEAR, NEAR, LOAD, LOAD, LOAD, AWAY, LOAD, LOAD],
+        [NEAR] * 5,
         [
             shape_of(BF16, batch, length, packed_cols),
             shape_of(F32, rank, DK),
             shape_of(F32, 1, DK),
-            shape_of(F32, 1, DV),
             shape_of(BF16, rows, width),
             shape_of(F32, share, hidden),
         ],
-        [
-            pltpu.VMEM((batch, DV, DK), F32),
-            pltpu.VMEM((batch, length, DV), BF16),
-            pltpu.VMEM((rows, width), BF16),
-            pltpu.SemaphoreType.DMA((count,)),
-        ]
+        [pltpu.VMEM((batch, DV, DK), F32)]
         + marks_scratch(batch, length)
-        + rows_scratch(quarter, width)
-        + handover_scratch(count, batch)
-        + sum_scratch(count, rows, 1, share // 2, hidden),
-        (part, resid, d_heads, gates, mixed, gain, query, vk, run, slope, states, low, up, starts,
-         total, normed_two, d_gate),
+        + sum_scratch(count, rows, 1, share // 2, [hidden]),
+        (query, vk, run, slope, states, low, up, starts, d_mixed, later, d_gates, normed_two, d_gate,
+         weights),
         2 * rows * width * hidden,
     )
 
@@ -1413,7 +1530,7 @@
 
 
 def last_phase_kernel(
-    order, heads, part_ref, input_ref, resid_grad_ref, gain_ref, normed_ref, packed_ref, attn_ref,
+    order, heads, ready, part_ref, input_ref, resid_grad_ref, gain_ref, normed_ref, packed_ref, attn_ref,
     heads_ref, ffn_gain_ref, head_gain_ref, bias_ref, up_ref,
     input_grad_ref, sums_ref, small_ref, tail_ref,
     own, own_sems, grads, grad_sems, gain_grad, stage, stage_got, shared, shared_got, tail_got,
@@ -1430,9 +1547,12 @@
         copy.start()
     ring.prepare()
     greet_all(count, heads)
+    ready(0)
     for p in range(PIECES):
         rows.start(p)
+    ready(5, 7)
     ring.advance()
+    ready()
     gain_grad[...] = jnp.zeros_like(gain_grad)
 
     def middle(here, total):
@@ -1543,7 +1663,7 @@
     return remote_call(
         functools.partial(last_phase_kernel, ring_order(count), heads),
         6,
-        [NEAR, AWAY, NEAR, NEAR, AWAY, NEAR, AWAY, NEAR, NEAR, NEAR, NEAR, NEAR],
+        [LOAD, AWAY, LOAD, NEAR, AWAY, LOAD, AWAY, LOAD, NEAR, NEAR, NEAR, NEAR],
         [AWAY, NEAR, NEAR, NEAR],
         [
             shape_of(BF16, rows, width),
@@ -1568,10 +1688,67 @@
             pltpu.SemaphoreType.DMA((2, heads - 1)),
         ]
         + rows_scratch(quarter, width)
-        + sum_scratch(count, rows, 2, share // 2, columns),
+        + sum_scratch(count, rows, 2, share // 2, [packed.shape[1], DV]),
         (part, inputs, d_resid, gains, normed, packed, d_attn, heads_out, ffn_gain, head_gain, bias, up),
         2 * rows * width * columns,
     )
+
+
+def leave_kernel(
+    layer_ref, input_ref, first_ref, gate_ref, last_ref,
+    layer_out, input_out, query_out, key_out, value_out, gates_out, attn_out, ffn_gate_out,
+    ffn_up_out, ffn_down_out,
+):
+    hidden = gate_ref.shape[1]
+    used = last_ref.shape[1] - DV
+    layer_out[...] = layer_ref[...]
+    input_out[...] = input_ref[...]
+    ffn_gate_out[...] = gate_ref[...]
+    ffn_up_out[...] = first_ref[:, hidden:]
+    ffn_down_out[...] = first_ref[:, :hidden].T
+    value_out[...] = last_ref[:, :DV]
+    key_out[...] = last_ref[:, DV : DV + DK]
+    query_out[...] = last_ref[:, DV + DK : DV + 2 * DK]
+    gates_out[...] = last_ref[:, DV + 2 * DK : 2 * DV + 2 * DK]
+    attn_out[...] = last_ref[:, used:].T
+
+
+def leave(layer, input_grad, first, gate, last):
+    share, hidden = gate.shape
+    steps = share // 128
+
+    def by_rows(field):
+        return pl.BlockSpec((field.shape[0] // steps, field.shape[1]), lambda i: (i, 0))
+
+    out_shape = [
+        shape_of(BF16, *layer.shape),
+        shape_of(BF16, *layer.shape),
+        shape_of(F32, share, DK),
+        shape_of(F32, share, DK),
+        shape_of(F32, share, DV),
+        shape_of(F32, share, DV),
+        shape_of(F32, DV, share),
+        shape_of(F32, share, hidden),
+        shape_of(F32, share, hidden),
+        shape_of(F32, hidden, share),
+    ]
+    specs = [by_rows(shape) for shape in out_shape]
+    for n in (6, 9):
+        specs[n] = pl.BlockSpec((out_shape[n].shape[0], 128), lambda i: (0, i))
+    operands = (layer, input_grad, first, gate, last)
+    return pl.pallas_call(
+        leave_kernel,
+        grid=(steps,),
+        in_specs=[by_rows(field) for field in operands],
+        out_specs=specs,
+        out_shape=out_shape,
+        compiler_params=pltpu.CompilerParams(
+            dimension_semantics=("arbitrary",), vmem_limit_bytes=VMEM_BYTES
+        ),
+    )(*operands)
+
+
+EARLY = 384
 
 
 def matmul(left, right):
@@ -1951,46 +2128,49 @@
     )
     value_key, query, gates, low = map(tokens, (value_key, query, gates, low))
     weights, out_t = weights.reshape(width, -1), out_t.reshape(width, DV)
-    run, slope, total, mixed, heads, states, part, fgate = token_phase(
-        value_key, query, gates, low, up, bias, starts, gain_head, out_t, ffn_gate
+    down_block = ffn_down.T
+    run, slope, total, mixed, heads, states, part, fgate, fdown = token_phase(
+        value_key, query, gates, low, up, bias, starts, gain_head, out_t, ffn_gate, down_block, EARLY
     )
     resid, normed_two, fup = row_phase(part, inputs, gains, ffn_up)
     fgate, fup = fgate.reshape(width, hidden), fup.reshape(width, hidden)
-    act, d_gate, d_up, fdown_t = unit_phase(normed_two, fgate, fup, grad_rows, ffn_down.T)
+    act, d_gate, d_up, fdown_t = unit_phase(normed_two, fgate, fup, grad_rows, down_block, fdown)
     fdown_t = fdown_t.reshape(width, hidden)
     ffn_part = narrow(matmul_nt(act, fdown_t))
     part = narrow(matmul_nt(d_gate, fgate) + matmul_nt(d_up, fup))
-    d_resid, d_attn, d_heads, grad_gain_two, grad_first = resid_phase(
-        part, resid, grad_rows, gains, out_t, act, normed_two, d_up
-    )
-    packed, grad_up, grad_bias, grad_gain_head, layer_out, grad_fgate = back_phase(
-        ffn_part, resid, tokens(d_heads), gates, mixed, gain_head, query, value_key, run, slope,
-        states, low, up, starts, total, normed_two, d_gate, shard.shape[1],
+    (
+        d_resid, d_attn, d_gates, d_mixed, state_back, grad_gain_two, grad_gain_head, layer_out, grad_first
+    ) = resid_phase(
+        part, resid, grad_rows, gains, out_t, act, normed_two, d_up, gates, mixed, gain_head, query,
+        run, starts, total, ffn_part,
+    )
+    packed, grad_up, grad_bias, part, grad_fgate = back_phase(
+        query, value_key, run, slope, states, low, up, starts, d_mixed, state_back, d_gates,
+        normed_two, d_gate, weights,
     )
     packed = packed.reshape(rows, -1)
-    part = narrow(matmul_nt(packed, weights))
     input_grad, grad_last, small, tail = last_phase(
         part, inputs, d_resid, gains, normed, packed, d_attn, heads.reshape(rows, DV),
         grad_gain_two, grad_gain_head, grad_bias, grad_up,
     )
     lines = share // 128
+    results = leave(layer_out, input_grad, grad_first, grad_fgate, grad_last)
+    layer_out, input_grad, grad_query, grad_key, grad_value, grad_gate, grad_out = results[:7]
     return (
         layer_out.reshape(batch, block, width),
         input_grad.reshape(batch, block, width),
         small[2 : 2 + lines].reshape(share),
-        grad_last[:, DV + DK : DV + 2 * DK],
-        grad_last[:, DV : DV + DK],
-        grad_last[:, :DV],
-        grad_last[:, DV + 2 * DK : used],
+        grad_query,
+        grad_key,
+        grad_value,
+        grad_gate,
         tail[:, :rank],
         small[8:, : decay_up.shape[1]],
         small[1, : decay_bias.size],
         small[0, : head_gain.size],
-        grad_last[:, shard.shape[1] :].T,
+        grad_out,
         small[4 : 4 + lines].reshape(share),
-        grad_fgate,
-        grad_first[:, hidden:],
-        grad_first[:, :hidden].T,
+        *results[7:],
     )
 
 

time: 779 us -> 712 us (0.914)
  Pallas kernels: 692 us -> 660 us
  local copies, waits for them, and re-layouts: 36.4 us -> 14.3 us
  matrix products: 39.3 us -> 26.4 us
    pallas_call x7 -> x8, Pallas kernels: 692 us -> 660 us  [the longest x7 649 us: remote_call(): pl.pallas_call(body, in_specs=[AWAY if spec is LOAD else spec for spec in...]
    dot_general x4 -> x3, matrix products: 39.3 us -> 26.4 us  [product(): lax.dot_general(left, right, dims, precision=precision, preferred_element...]
    unnamed x33 -> x22, local copies, waits for them, and re-layouts: 22.1 us -> 10.2 us
where the time goes in v5:
time: 712 us; the launch traced here: 702 us
  Pallas kernels  660 us (93%)
  matrix products  26.4 us (4%)
  local copies, waits for them, and re-layouts  14.3 us (2%)
    pallas_call x7, Pallas kernels, remote_call(): pl.pallas_call(body, in_specs=[AWAY if spec is LOAD else spec for spec in...  649 us
    dot_general x3, matrix products, product(): lax.dot_general(left, right, dims, precision=precision, preferred_element...  26.4 us

profile of v5, /device:TPU:0, one launch (start us, length us, event | category | flops | bytes accessed | tf_op | source)
XLA Modules:
  0.0 702.5 jit_solution(2336262365872673998)
XLA Ops:
  0.6 0.8 fusion.6
  1.4 0.6 broadcast_in_dim.3.refs_3_
  2.0 1.3 reshape.91.refs_6_.refs_13_.refs_7_
  3.3 0.8 copy.33
  4.1 1.8 copy.34
  5.9 2.2 copy.35
  8.2 1.0 constant_dynamic-update-slice_fusion.3
  9.1 0.9 constant_dynamic-update-slice_fusion.2
  10.0 0.9 constant_dynamic-update-slice_fusion.1
  11.0 1.0 constant_dynamic-update-slice_fusion
  12.0 0.0 copy-start.2
  12.0 0.9 copy-done.2
  12.9 101.8 %shard_map.288 = (bf16[1024,2048]{1,0:T(8,128)(2,1)}, bf16[8,256,1664]{2,1,0:T(8,128)(2,1)}, bf16[8,256,512]{2,1,0:T(8,128)(2,1)}, bf16[1024,768]{1,0:T(8,128)(2...) custom-call(bf16[1024,2048]{1,0:T(8,128)(2,1)} %bitcast.33, ...), custom_call_target="tpu_custom_call" | custom-call | flops 6979321856 | bytes 22713600 | tf_op jit(solution)/shard_map/pallas_call | solution.py:912
  114.7 111.8 %shard_map.289 = (f32[2,512,256]{2,1,0:T(8,128)}, f32[2,512,256]{2,1,0:T(8,128)}, f32[2,1,256]{2,1,0:T(1,128)}, f32[2,512,512]{2,1,0:T(8,128)}, bf16[2,512,512]{...) custom-call(bf16[2,512,768]{2,1,0:T(8,128)(2,1)} %bitcast.36, ...), custom_call_target="tpu_custom_call" | custom-call | flops 2684354560 | bytes 28795904 | tf_op jit(solution)/shard_map/pallas_call | solution.py:912
  226.4 61.1 %shard_map.290 = (f32[256,2048]{1,0:T(8,128)}, bf16[1024,2048]{1,0:T(8,128)(2,1)}, bf16[8,256,1408]{2,1,0:T(8,128)(2,1)}) custom-call(bf16[1024,2048]{1,0:T(8,128)(2,1)} %get-tuple-element.79.refs_0_, bf16[1024,2048]{1,0:T(8,128)(2,1)} %bitcast.34, f32[2,2048]{1,0:T(2,128)} %get-tuple-element.80.refs_2_.refs_3_, bf16[256,1408]{1,0:T(8,128)(2,1)} %refs_3_.1), custom_call_target="tpu_custom_call" | custom-call | flops 33554432 | bytes 21184512 | tf_op jit(solution)/shard_map/pallas_call | solution.py:912
  287.5 61.0 %shard_map.291 = (bf16[1024,1408]{1,0:T(8,128)(2,1)}, bf16[1024,1408]{1,0:T(8,128)(2,1)}, bf16[1024,1408]{1,0:T(8,128)(2,1)}, bf16[8,256,1408]{2,1,0:T(8,128)(2,1)}) custom-call(bf16[1024,2048]{1,0:T(8,128)(2,1)} %get-tuple-element.81.refs_0_.refs_6_.refs_11_, bf16[2048,1408]{1,0:T(8,128)(2,1)} %bitcast.54, bf16[2048,1408]{1,0:T(8,128)(2,1)} %bitcast.47, ...), custom_call_target="tpu_custom_call" | custom-call | flops 17716740096 | bytes 36634624 | tf_op jit(solution)/shard_map/pallas_call | solution.py:912
  348.5 0.0 copy-start
  348.5 0.0 copy-start.5
  348.5 11.1 %convolution_convert_fusion.refs_15_ = bf16[1024,2048]{1,0:T(8,128)(2,1)} fusion(bf16[1024,1408]{1,0:T(8,128)(2,1)} %get-tuple-element.88.refs_5_, bf16[2048,1408]{1,0:T(8,128)(2,1)} %bitcast.56), kind=kOutput, calls=%fused_computation.1 | convolution fusion | flops 5907677184 | bytes 12845056 | tf_op jit(solution)/shard_map/dot_general | solution.py:23
  359.6 0.0 copy-done
  359.6 0.0 copy-done.5
  359.6 0.0 copy-start.4
  359.6 0.0 copy-start.6
  359.6 6.7 fusion.7
  366.3 0.0 copy-done.4
  366.3 0.0 copy-done.6
  366.3 8.6 %add_convert_fusion.refs_0_ = bf16[1024,2048]{1,0:T(8,128)(2,1)} fusion(f32[1024,2048]{1,0:T(8,128)S(1)} %fusion.7, bf16[1024,1408]{1,0:T(8,128)(2,1)S(1)} %copy-done.6, bf16[2048,1408]{1,0:T(8,128)(2,1)S(1)} %bitcast.48), kind=kOutput, calls=%fused_computation | convolution fusion | flops 5909774336 | bytes 21233664 | tf_op jit(solution)/shard_map/dot_general | solution.py:23
  375.0 143.6 %shard_map.292 = (f32[256,2048]{1,0:T(8,128)}, bf16[1024,2048]{1,0:T(8,128)(2,1)}, bf16[2,512,512]{2,1,0:T(8,128)(2,1)}, bf16[2,512,512]{2,1,0:T(8,128)(2,1)}, b...) custom-call(bf16[1024,2048]{1,0:T(8,128)(2,1)} %add_convert_fusion.r, ...), custom_call_target="tpu_custom_call" | custom-call | flops 13958643712 | bytes 48531456 | tf_op jit(solution)/shard_map/pallas_call | solution.py:912
  518.6 67.9 %shard_map.293 = (bf16[2,512,1664]{2,1,0:T(8,128)(2,1)}, f32[16,256]{1,0:T(8,128)}, f32[1,256]{1,0:T(1,128)}, bf16[1024,2048]{1,0:T(8,128)(2,1)}, f32[256,1408]{1,0:T(8,128)}) custom-call(bf16[2,512,256]{2,1,0:T(8,128)(2,1)} %bitcast.42, bf16[2,512,768]{2,1,0:T(8,128)(2,1)} %bitcast.37, f32[2,512,256]{2,1,0:T(8,128)} %get-tuple-element.90.refs_12_.refs_2_, ...), custom_call_target="tpu_custom_call" | custom-call | flops 5905580032 | bytes 34051072 | tf_op jit(solution)/shard_map/pallas_call | solution.py:912
  586.5 102.1 %shard_map.294 = (bf16[1024,2048]{1,0:T(8,128)(2,1)}, f32[256,2176]{1,0:T(8,128)}, f32[24,128]{1,0:T(8,128)}, f32[256,128]{1,0:T(8,128)}) custom-call(bf16[1024,2048]{1,0:T(8,128)(2,1)} %get-tuple-element.100.refs_0_, bf16[1024,2048]{1,0:T(8,128)(2,1)} %bitcast.35, f32[256,2048]{1,0:T(8,128)} %get-tuple-element.101.refs_2_, ...), custom_call_target="tpu_custom_call" | custom-call | flops 9126805504 | bytes 29940736 | tf_op jit(solution)/shard_map/pallas_call | solution.py:912
  688.6 0.0 copy-start.3
  688.6 0.0 copy-start.1
  688.7 10.7 %shard_map.295 = (bf16[1024,2048]{1,0:T(8,128)(2,1)}, bf16[1024,2048]{1,0:T(8,128)(2,1)}, f32[256,256]{1,0:T(8,128)}, f32[256,256]{1,0:T(8,128)}, f32[256,512]{1...) custom-call(bf16[1024,2048]{1,0:T(8,128)(2,1)} %get-tuple-element.93, ...), custom_call_target="tpu_custom_call" | custom-call | tf_op jit(solution)/shard_map/pallas_call | solution.py:1739
  699.4 0.0 copy-done.3
  699.4 0.5 slice_bitcast_fusion.2
  699.9 0.5 slice_bitcast_fusion.3
  700.4 0.6 slice_bitcast_fusion
  701.0 0.6 slice.20
  701.6 0.0 copy-done.1
  701.6 0.7 copy.36
  (1 shorter events, 0.0 us)
Async XLA Ops:
  12.0 0.9 copy-start.2
  348.5 11.1 %copy-start = (bf16[1024,1408]{1,0:T(8,128)(2,1)S(1)}, bf16[1024,1408]{1,0:T(8,128)(2,1)}, u32[]{:S(2)}) copy-start(bf16[1024,1408]{1,0:T(8,128)(2,1)} %get-tuple-element.85.refs_12_) | copy-start | bytes 8650756
  348.5 11.1 %copy-start.5 = (bf16[8,256,1408]{2,1,0:T(8,128)(2,1)S(1)}, bf16[8,256,1408]{2,1,0:T(8,128)(2,1)}, u32[]{:S(2)}) copy-start(bf16[8,256,1408]{2,1,0:T(8,128)(2,1)} %get-tuple-element.82) | copy-start | bytes 17301508
  359.6 6.7 copy-start.4
  359.6 6.7 copy-start.6
  688.6 10.7 %copy-start.3 = (f32[24,128]{1,0:T(8,128)S(1)}, f32[24,128]{1,0:T(8,128)}, u32[]{:S(2)}) copy-start(f32[24,128]{1,0:T(8,128)} %get-tuple-element.116) | copy-start | bytes 36868
  688.6 12.9 %copy-start.1 = (f32[256,128]{1,0:T(8,128)S(1)}, f32[256,128]{1,0:T(8,128)}, u32[]{:S(2)}) copy-start(f32[256,128]{1,0:T(8,128)} %get-tuple-element.121) | copy-start | bytes 393220

commit v6 on v5

--- a/solution.py
+++ b/solution.py
@@ -374,18 +374,33 @@
 
 
 def enter_kernel(
-    order, ready, input_ref, block_ref, out_block_ref, small_ref, rise_ref,
-    normed_ref, weight_ref, out_ref, vk_ref, query_ref, gate_ref, low_ref,
+    order, ready, input_ref, value_ref, key_ref, query_weight_ref, gate_weight_ref, down_ref,
+    out_block_ref, ffn_down_ref, small_ref, rise_ref,
+    normed_out, weight_out, out_out, turned_ref, downs_ref, vk_ref, query_ref, gate_ref, low_ref,
     gains_ref, head_gain_ref, bias_ref, up_ref,
-    smalls_ref, rises_ref, total, small_send, small_receive, rise_send, rise_receive, *scratch,
+    normed_ref, weight_ref, out_ref, down_t, smalls_ref, rises_ref, total, low_total,
+    places, keeps, small_send, small_receive, rise_send, rise_receive, down_send, down_receive,
+    ring_send, ring_receive, out_send, out_receive,
 ):
     count = len(order)
-    share, half = block_ref.shape[0], block_ref.shape[0] // 2
+    share, half = down_ref.shape[0], down_ref.shape[0] // 2
     rows, tile = input_ref.shape[0], 256
     mine = lax.axis_index("seq")
-    ring = BlockRing(order, block_ref, weight_ref, *scratch[:3])
-    out_ring = BlockRing(order, out_block_ref, out_ref, *scratch[3:])
+    placed, column = [], 0
+    for n, ref in enumerate((value_ref, key_ref, query_weight_ref, gate_weight_ref)):
+        target = weight_ref.at[0, :, pl.ds(column, ref.shape[1])]
+        placed.append(pltpu.make_async_copy(ref, target, places.at[n]))
+        placed[-1].start()
+        column += ref.shape[1]
+    ring = BlockRing(order, weight_ref.at[0], weight_ref, ring_send, ring_receive, None)
+    out_ring = BlockRing(order, out_ref.at[0], out_ref, out_send, out_receive, None)
+    down_t[...] = down_ref[...].T
+    out_ref[0] = out_block_ref[...].T
     greet("seq", count)
+    for copy in placed:
+        copy.wait()
+    ring.start()
+    out_ring.start()
 
     def spread(source, target, send, receive):
         return [
@@ -402,13 +417,27 @@
 
     smalls = spread(small_ref, smalls_ref, small_send, small_receive)
     smalls += spread(rise_ref, rises_ref, rise_send, rise_receive)
+    smalls += spread(down_t, downs_ref, down_send, down_receive)
     for copy in smalls:
         copy.start()
-    ring.start()
-    out_ring.start()
     smalls_ref[mine] = small_ref[...]
     rises_ref[mine] = rise_ref[...]
+    downs_ref[mine] = down_t[...]
+    turned_ref[...] = ffn_down_ref[...].T
     ready()
+    kept = []
+
+    def keep(slot, side):
+        part = pl.ds(side * half, half)
+        column = pl.ds(slot * share + side * half, half)
+        pairs = (
+            (weight_ref.at[slot, part], weight_out.at[slot, part]),
+            (out_ref.at[slot, part], out_out.at[slot, part]),
+            (normed_ref.at[:, column], normed_out.at[:, column]),
+        )
+        for n, (source, target) in enumerate(pairs):
+            kept.append(pltpu.make_async_copy(source, target, keeps.at[slot, side, n]))
+            kept[-1].start()
 
     scales = []
     for t in range(rows // tile):
@@ -422,21 +451,28 @@
             sides.append((slot, side, gains_ref[0:1, start : start + half]))
         for t in range(rows // tile):
             here = slice(t * tile, (t + 1) * tile)
-            parts, blocks = [], []
+            parts, blocks, downs = [], [], []
             for slot, side, gain in sides:
-                start = pl.multiple_of(block_at(order, slot) * share + side * half, half)
+                owner = block_at(order, slot)
+                start = pl.multiple_of(owner * share + side * half, half)
                 field = wide(input_ref[here, pl.ds(start, half)])
                 part = narrow(field * scales[t] * gain)
                 column = slot * share + side * half
                 normed_ref[here, column : column + half] = part
                 parts.append(part)
-                source = block_ref if slot == 0 else weight_ref.at[slot]
-                blocks.append(source[side * half : (side + 1) * half])
-            added = product(jnp.concatenate(parts, axis=1), jnp.concatenate(blocks, axis=0), NN)
+                blocks.append(weight_ref[slot, side * half : (side + 1) * half])
+                downs.append(downs_ref[owner][:, side * half : (side + 1) * half])
+            left = jnp.concatenate(parts, axis=1)
+            added = product(left, jnp.concatenate(blocks, axis=0), NN)
+            low_added = product(left, jnp.concatenate(downs, axis=1), NT)
             if begin:
                 total[here] = added
+                low_total[here] = low_added
             else:
                 total[here] += added
+                low_total[here] += low_added
+        for slot, side in (first, second):
+            keep(slot, side)
 
     for copy in smalls:
         copy.wait_recv()
@@ -456,32 +492,37 @@
         ring.advance()
         out_ring.advance()
         multiply((count - step, 0), (step, 1), False)
-    vk_cols, query_cols, gate_cols = vk_ref.shape[1], query_ref.shape[1], gate_ref.shape[1]
+    vk_cols, query_cols = vk_ref.shape[1], query_ref.shape[1]
     vk_ref[...] = narrow(total[:, :vk_cols])
     query_ref[...] = narrow(total[:, vk_cols : vk_cols + query_cols])
-    low_from = vk_cols + query_cols + gate_cols
-    gate_ref[...] = total[:, vk_cols + query_cols : low_from]
-    low_ref[...] = total[:, low_from : low_from + low_ref.shape[1]]
+    gate_ref[...] = total[:, vk_cols + query_cols :]
+    low_ref[...] = low_total[...]
     for copy in smalls:
         copy.wait_send()
     ring.finish()
     out_ring.finish()
-
-
-def enter(inputs, block, out_block, small, rise):
+    for copy in kept:
+        copy.wait()
+
+
+def enter(inputs, value, key, query, gate, down, out_block, ffn_down, small, rise):
     count = lax.axis_size("seq")
     rows, width = inputs.shape
-    rank, cols = rise.shape[0], block.shape[1]
-    dma = [pltpu.SemaphoreType.DMA((count - 1,))] * 4
+    share, rank = down.shape
+    cols = 2 * DV + 2 * DK
+    dma = [pltpu.SemaphoreType.DMA((count - 1,))] * 6
+    whole, outs = (count, share, cols), (count, share, DV)
     return remote_call(
         functools.partial(enter_kernel, ring_order(count)),
         0,
-        [LOAD, NEAR, NEAR, NEAR, NEAR],
-        [NEAR] * 11,
+        [LOAD] + [AWAY] * 4 + [NEAR] * 5,
+        [AWAY] * 3 + [NEAR] * 10,
         [
             shape_of(BF16, rows, width),
-            shape_of(BF16, count, *block.shape),
-            shape_of(BF16, count, *out_block.shape),
+            shape_of(BF16, *whole),
+            shape_of(BF16, *outs),
+            shape_of(BF16, share, ffn_down.shape[0]),
+            shape_of(BF16, count, rank, share),
             shape_of(BF16, rows, DV + DK),
             shape_of(BF16, rows, DK),
             shape_of(F32, rows, DV),
@@ -492,14 +533,21 @@
             shape_of(F32, rank, DK),
         ],
         [
+            pltpu.VMEM((rows, width), BF16),
+            pltpu.VMEM(whole, BF16),
+            pltpu.VMEM(outs, BF16),
+            pltpu.VMEM((rank, share), BF16),
             pltpu.VMEM((count, *small.shape), BF16),
             pltpu.VMEM((count, *rise.shape), BF16),
             pltpu.VMEM((rows, cols), F32),
+            pltpu.VMEM((rows, rank), F32),
+            pltpu.SemaphoreType.DMA((4,)),
+            pltpu.SemaphoreType.DMA((count, 2, 3)),
         ]
         + dma
-        + ring_semaphores(count)
-        + ring_semaphores(count),
-        (inputs, block, out_block, small, rise),
+        + ring_semaphores(count)[:2]
+        + ring_semaphores(count)[:2],
+        (inputs, value, key, query, gate, down, out_block, ffn_down, small, rise),
         2 * rows * width * cols,
     )
 
@@ -513,7 +561,9 @@
         half = block_ref.shape[0] // 2
         size = half // PARTS
         aims = (block_at(order, 1), block_at(order, -1))
-        self.local = pltpu.make_async_copy(block_ref, whole_ref.at[0], local)
+        self.local = None
+        if local is not None:
+            self.local = pltpu.make_async_copy(block_ref, whole_ref.at[0], local)
         self.hops = {}
         for step in range(1, count):
             for side in range(2):
@@ -535,7 +585,8 @@
         for n in range(PARTS):
             for side in range(2):
                 self.hops[1, n, side].start()
-        self.local.start()
+        if self.local is not None:
+            self.local.start()
 
     def advance(self):
         if self.step < self.count:
@@ -551,7 +602,8 @@
             self.advance()
         for copy in self.hops.values():
             copy.wait_send()
-        self.local.wait()
+        if self.local is not None:
+            self.local.wait()
 
 
 def ring_semaphores(count):
@@ -846,6 +898,7 @@
         )
 
     hand.begin()
+    ready.save(0, 1)
     ring.advance()
     hand.join()
     ring.advance()
@@ -874,6 +927,7 @@
     mixer(0, chunks // 2)
     down_ring.advance()
     mixer(chunks // 2, chunks)
+    ready.save(3, 4, 5)
     down_ring.advance()
     batch, block, _ = heads_ref.shape
     tile = 256
@@ -890,13 +944,23 @@
     moved = sum(a.size * a.dtype.itemsize for a in operands)
     moved += sum(s.size * s.dtype.itemsize for s in out_shape)
     loads = [i for i, spec in enumerate(in_specs) if spec is LOAD]
+    saves = [i for i, spec in enumerate(out_specs) if spec is SAVE]
     scratch = list(scratch)
+    scratch += [pltpu.VMEM(out_shape[i].shape, out_shape[i].dtype) for i in saves]
     scratch += [pltpu.VMEM(operands[i].shape, operands[i].dtype) for i in loads]
     scratch += [pltpu.SemaphoreType.DMA((max(len(loads), 1),))]
+    scratch += [pltpu.SemaphoreType.DMA((max(len(saves), 1),))]
 
     def body(*refs):
         refs = list(refs)
-        refs, buffers, arrivals = refs[: -1 - len(loads)], refs[-1 - len(loads) : -1], refs[-1]
+        arrivals, departures = refs[-2:]
+        refs = refs[:-2]
+        refs, buffers = refs[: len(refs) - len(loads)], refs[len(refs) - len(loads) :]
+        refs, results = refs[: len(refs) - len(saves)], refs[len(refs) - len(saves) :]
+        pending, started = {}, []
+        for n, (i, buffer) in enumerate(zip(saves, results)):
+            pending[i] = pltpu.make_async_copy(buffer, refs[len(in_specs) + i], departures.at[n])
+            refs[len(in_specs) + i] = buffer
         waits = {}
         for n, (i, buffer) in enumerate(zip(loads, buffers)):
             waits[i] = pltpu.make_async_copy(refs[i], buffer, arrivals.at[n])
@@ -907,12 +971,21 @@
             for i in positions or list(waits):
                 waits.pop(i).wait()
 
+        def save(*positions):
+            for i in positions:
+                started.append(pending.pop(i))
+                started[-1].start()
+
+        ready.save = save
         kernel(ready, *refs)
+        save(*list(pending))
+        for copy in started:
+            copy.wait()
 
     return pl.pallas_call(
         body,
         in_specs=[AWAY if spec is LOAD else spec for spec in in_specs],
-        out_specs=out_specs,
+        out_specs=[AWAY if spec is SAVE else spec for spec in out_specs],
         out_shape=out_shape,
         scratch_shapes=scratch,
         cost_estimate=pl.CostEstimate(flops=flops, bytes_accessed=moved, transcendentals=0),
@@ -922,7 +995,7 @@
     )(*operands)
 
 
-LOAD = None
+LOAD, SAVE = "load", "save"
 NEAR = pl.BlockSpec(memory_space=pltpu.VMEM)
 AWAY = pl.BlockSpec(memory_space=pl.ANY)
 
@@ -935,7 +1008,7 @@
         functools.partial(token_phase_kernel, ring_order(count), early),
         1,
         [LOAD, LOAD, LOAD, LOAD, NEAR, NEAR, NEAR, NEAR, LOAD, LOAD, LOAD],
-        [NEAR] * 7 + [AWAY] * 2,
+        [SAVE, SAVE, NEAR, SAVE, SAVE, SAVE, NEAR] + [AWAY] * 2,
         [
             shape_of(F32, batch, length, DK),
             shape_of(F32, batch, length, DK),
@@ -1173,8 +1246,8 @@
 
 def unit_phase_kernel(
     order, ready, normed_ref, gate_ref, up_ref, grad_ref, block_ref, early_ref,
-    act_ref, gate_grad_ref, up_grad_ref, whole_ref,
-    pre_gate, pre_up, act_grad, tiles, tile_sems, early_sem, ring_send, ring_receive, ring_local,
+    act_ref, gate_grad_ref, up_grad_ref, ffn_ref, part_ref,
+    whole_ref, pre_gate, pre_up, act_grad, tiles, tile_sems, early_sem, ring_send, ring_receive, ring_local,
 ):
     count = len(order)
     early = early_ref.shape[2]
@@ -1205,11 +1278,9 @@
         pre_gate[here] = gate
         up = product(field, up_ref[...], NN)
         pre_up[here] = up
-        if i > 0:
-            written(0, act_ref, i - 1).wait()
-        tiles[0] = narrow(gate * jax.nn.sigmoid(gate) * up)
-        written(0, act_ref, i).start()
+        act_ref[here] = narrow(gate * jax.nn.sigmoid(gate) * up)
         ring.advance()
+    ready.save(0)
     ready()
     placed.wait()
 
@@ -1225,7 +1296,6 @@
         act_grad[i * tile : (i + 1) * tile] = against(pl.ds(i * tile, tile), slice(0, early))
         if i % 2:
             ring.advance()
-    written(0, act_ref, steps - 1).wait()
     ring.finish()
     for i in range(steps):
         here = pl.ds(i * tile, tile)
@@ -1240,6 +1310,9 @@
             tiles[1, :, columns] = narrow(grad * gate * sigma)
         for kind, target in ((0, gate_grad_ref), (1, up_grad_ref)):
             written(kind, target, i).start()
+        part = product(tiles[0], gate_ref[...], NT) + product(tiles[1], up_ref[...], NT)
+        part_ref[here] = narrow(part)
+        ffn_ref[here] = narrow(product(act_ref[here], whole_ref[...].reshape(width, -1), NT))
     for kind, target in ((0, gate_grad_ref), (1, up_grad_ref)):
         written(kind, target, steps - 1).wait()
 
@@ -1253,9 +1326,10 @@
         functools.partial(unit_phase_kernel, ring_order(count)),
         3,
         [LOAD] * 4 + [AWAY, AWAY],
-        [AWAY] * 3 + [NEAR],
-        [flat, flat, flat, shape_of(BF16, count, *block.shape)],
+        [SAVE, AWAY, AWAY, SAVE, SAVE],
+        [flat, flat, flat, shape_of(BF16, rows, width), shape_of(BF16, rows, width)],
         [
+            pltpu.VMEM((count, *block.shape), BF16),
             pltpu.VMEM((rows, hidden), F32),
             pltpu.VMEM((rows, hidden), F32),
             pltpu.VMEM((rows, early.shape[2]), F32),
@@ -1342,6 +1416,7 @@
         if p == 2:
             ring.advance()
     rows.finish()
+    ready.save(0)
     kept = pltpu.make_async_copy(wholes, attn_grad_ref, whole_sems.at[0])
     kept.start()
     following = pltpu.make_async_copy(ffn_ref, part_ref, ffn_sem)
@@ -1364,6 +1439,7 @@
                 copy.start()
 
     hand.begin()
+    ready.save(2, 3)
     kept.wait()
     following.wait()
     for p in range(PIECES):
@@ -1410,7 +1486,7 @@
         functools.partial(resid_phase_kernel, ring_order(count), heads),
         4,
         [LOAD, LOAD, AWAY, NEAR, LOAD, LOAD, AWAY, LOAD, AWAY, AWAY, NEAR, LOAD, LOAD, NEAR, NEAR, AWAY],
-        [NEAR, AWAY, NEAR, NEAR, NEAR, NEAR, NEAR, AWAY, NEAR],
+        [SAVE, AWAY, SAVE, SAVE, NEAR, NEAR, NEAR, AWAY, NEAR],
         [
             shape_of(F32, quarter, width),
             shape_of(BF16, rows, width),
@@ -1445,7 +1521,7 @@
 
 def back_phase_kernel(
     order, ready, query_ref, vk_ref, run_ref, slope_ref, states_ref, low_ref, up_ref, starts_ref,
-    mixed_grad_ref, later_ref, gates_grad_ref, normed_ref, act_grad_ref, weight_ref,
+    mixed_grad_ref, later_ref, gates_grad_ref, normed_ref, act_grad_ref, weight_ref, down_ref,
     packed_ref, up_grad_ref, bias_grad_ref, part_ref, sums_ref,
     state, mark_ref, row_ref, *scratch,
 ):
@@ -1486,30 +1562,36 @@
     back(0, chunks // 2)
     ring.advance()
     back(chunks // 2, chunks)
+    ready.save(0)
     ring.advance()
     ready()
-    tile = 256
+    tile, rank = 256, low_ref.shape[2]
+    down = [down_ref[block_at(order, r)] for r in range(count)]
+    down = jnp.concatenate(down, axis=1)
     for b in range(batch):
         for t in range(length // tile):
-            field = packed_ref[b, t * tile : (t + 1) * tile]
+            field = packed_ref[b, t * tile : (t + 1) * tile, :low_from]
+            low = packed_ref[b, t * tile : (t + 1) * tile, low_from : low_from + rank]
             start = b * length + t * tile
-            part_ref[start : start + tile] = narrow(product(field, weight_ref[...], NT))
+            total = product(field, weight_ref[...], NT) + product(low, down, NN)
+            part_ref[start : start + tile] = narrow(total)
         ring.advance()
     ring.finish()
 
 
 def back_phase(
-    query, vk, run, slope, states, low, up, starts, d_mixed, later, d_gates, normed_two, d_gate, weights
+    query, vk, run, slope, states, low, up, starts, d_mixed, later, d_gates, normed_two, d_gate, weights,
+    down,
 ):
     count = lax.axis_size("seq")
     batch, length, rank = low.shape
-    width, packed_cols = weights.shape
+    width, packed_cols = weights.shape[0], weights.shape[1] + 128
     share, hidden, rows = width // count, d_gate.shape[1], d_gate.shape[0]
     return remote_call(
         functools.partial(back_phase_kernel, ring_order(count)),
         5,
-        [LOAD] * 6 + [NEAR, NEAR, LOAD, LOAD, LOAD, AWAY, LOAD, LOAD],
-        [NEAR] * 5,
+        [LOAD] * 6 + [NEAR, NEAR, LOAD, LOAD, LOAD, AWAY, LOAD, LOAD, NEAR],
+        [SAVE] + [NEAR] * 4,
         [
             shape_of(BF16, batch, length, packed_cols),
             shape_of(F32, rank, DK),
@@ -1521,7 +1603,7 @@
         + marks_scratch(batch, length)
         + sum_scratch(count, rows, 1, share // 2, [hidden]),
         (query, vk, run, slope, states, low, up, starts, d_mixed, later, d_gates, normed_two, d_gate,
-         weights),
+         weights, down),
         2 * rows * width * hidden,
     )
 
@@ -2117,27 +2199,24 @@
     starts = seg_starts.reshape(-1, CHUNK)
     small = jnp.concatenate([attn_gain, ffn_gain, head_gain, decay_bias])
     small = jnp.pad(small, (0, -small.size % 128))[None]
-    down = jnp.pad(decay_down, ((0, 0), (0, -rank % 128)))
-    shard = jnp.concatenate([value_weight, key_weight, query_weight, gate_weight, down], axis=1)
 
     def tokens(field):
         return field.reshape(batch, block, field.shape[-1])
 
-    normed, weights, out_t, value_key, query, gates, low, gains, gain_head, bias, up = enter(
-        inputs, shard, out_weight.T, small, decay_up
+    (
+        normed, weights, out_t, down_block, down, value_key, query, gates, low, gains, gain_head, bias, up
+    ) = enter(
+        inputs, value_weight, key_weight, query_weight, gate_weight, decay_down, out_weight, ffn_down,
+        small, decay_up,
     )
     value_key, query, gates, low = map(tokens, (value_key, query, gates, low))
     weights, out_t = weights.reshape(width, -1), out_t.reshape(width, DV)
-    down_block = ffn_down.T
     run, slope, total, mixed, heads, states, part, fgate, fdown = token_phase(
         value_key, query, gates, low, up, bias, starts, gain_head, out_t, ffn_gate, down_block, EARLY
     )
     resid, normed_two, fup = row_phase(part, inputs, gains, ffn_up)
     fgate, fup = fgate.reshape(width, hidden), fup.reshape(width, hidden)
-    act, d_gate, d_up, fdown_t = unit_phase(normed_two, fgate, fup, grad_rows, down_block, fdown)
-    fdown_t = fdown_t.reshape(width, hidden)
-    ffn_part = narrow(matmul_nt(act, fdown_t))
-    part = narrow(matmul_nt(d_gate, fgate) + matmul_nt(d_up, fup))
+    act, d_gate, d_up, ffn_part, part = unit_phase(normed_two, fgate, fup, grad_rows, down_block, fdown)
     (
         d_resid, d_attn, d_gates, d_mixed, state_back, grad_gain_two, grad_gain_head, layer_out, grad_first
     ) = resid_phase(
@@ -2146,7 +2225,7 @@
     )
     packed, grad_up, grad_bias, part, grad_fgate = back_phase(
         query, value_key, run, slope, states, low, up, starts, d_mixed, state_back, d_gates,
-        normed_two, d_gate, weights,
+        normed_two, d_gate, weights, down,
     )
     packed = packed.reshape(rows, -1)
     input_grad, grad_last, small, tail = last_phase(

time: 712 us -> 682 us (0.958)
  matrix products: 26.4 us -> 0 us
  local copies, waits for them, and re-layouts: 14.3 us -> 6.17 us
    dot_general x3 -> x0, matrix products: 26.4 us -> none  [product(): lax.dot_general(left, right, dims, precision=precision, preferred_element...]
    unnamed x22 -> x6, local copies, waits for them, and re-layouts: 10.2 us -> 2.11 us
where the time goes in v6:
time: 682 us; the launch traced here: 673 us
  Pallas kernels  665 us (98%)
    pallas_call x7, Pallas kernels, remote_call(): pl.pallas_call(body, in_specs=[AWAY if spec is LOAD else spec for spec in...  654 us

profile of v6, /device:TPU:0, one launch (start us, length us, event | category | flops | bytes accessed | tf_op | source)
XLA Modules:
  0.0 672.8 jit_solution(9036494941924692615)
XLA Ops:
  0.6 0.8 fusion.6
  1.4 0.6 broadcast_in_dim.3.refs_8_
  2.0 1.3 reshape.88.refs_6_.refs_13_.refs_7_
  3.3 1.4 copy.33.refs_5_
  4.7 98.2 %shard_map.288 = (bf16[1024,2048]{1,0:T(8,128)(2,1)}, bf16[8,256,1536]{2,1,0:T(8,128)(2,1)}, bf16[8,256,512]{2,1,0:T(8,128)(2,1)}, bf16[256,1408]{1,0:T(8,128)(2...) custom-call(bf16[1024,2048]{1,0:T(8,128)(2,1)} %bitcast.24, ...), custom_call_target="tpu_custom_call" | custom-call | flops 6442450944 | bytes 23639296 | tf_op jit(solution)/shard_map/pallas_call | solution.py:985
  102.9 107.4 %shard_map.289 = (f32[2,512,256]{2,1,0:T(8,128)}, f32[2,512,256]{2,1,0:T(8,128)}, f32[2,1,256]{2,1,0:T(1,128)}, f32[2,512,512]{2,1,0:T(8,128)}, bf16[2,512,512]{...) custom-call(bf16[2,512,768]{2,1,0:T(8,128)(2,1)} %bitcast.27, ...), custom_call_target="tpu_custom_call" | custom-call | flops 2684354560 | bytes 28795904 | tf_op jit(solution)/shard_map/pallas_call | solution.py:985
  210.3 62.0 %shard_map.290 = (f32[256,2048]{1,0:T(8,128)}, bf16[1024,2048]{1,0:T(8,128)(2,1)}, bf16[8,256,1408]{2,1,0:T(8,128)(2,1)}) custom-call(bf16[1024,2048]{1,0:T(8,128)(2,1)} %get-tuple-element.83.refs_0_, bf16[1024,2048]{1,0:T(8,128)(2,1)} %bitcast.25, f32[2,2048]{1,0:T(2,128)} %get-tuple-element.84.refs_2_.refs_3_, bf16[256,1408]{1,0:T(8,128)(2,1)} %refs_3_.3), custom_call_target="tpu_custom_call" | custom-call | flops 33554432 | bytes 21184512 | tf_op jit(solution)/shard_map/pallas_call | solution.py:985
  272.3 74.1 %shard_map.291 = (bf16[1024,1408]{1,0:T(8,128)(2,1)}, bf16[1024,1408]{1,0:T(8,128)(2,1)}, bf16[1024,1408]{1,0:T(8,128)(2,1)}, bf16[1024,2048]{1,0:T(8,128)(2,1)}, bf16[1024,2048]{1,0:T(8,128)(2,1)}) custom-call(bf16[1024,2048]{1,0:T(8,128)(2,1)} %get-tuple-element.85.refs_0_.refs_6_.refs_11_, bf16[2048,1408]{1,0:T(8,128)(2,1)} %bitcast.41, ...), custom_call_target="tpu_custom_call" | custom-call | flops 17716740096 | bytes 39256064 | tf_op jit(solution)/shard_map/pallas_call | solution.py:985
  346.4 143.3 %shard_map.292 = (f32[256,2048]{1,0:T(8,128)}, bf16[1024,2048]{1,0:T(8,128)(2,1)}, bf16[2,512,512]{2,1,0:T(8,128)(2,1)}, bf16[2,512,512]{2,1,0:T(8,128)(2,1)}, b...) custom-call(bf16[1024,2048]{1,0:T(8,128)(2,1)} %get-tuple-element.89, ...), custom_call_target="tpu_custom_call" | custom-call | flops 13958643712 | bytes 48531456 | tf_op jit(solution)/shard_map/pallas_call | solution.py:985
  489.8 67.0 %shard_map.293 = (bf16[2,512,1664]{2,1,0:T(8,128)(2,1)}, f32[16,256]{1,0:T(8,128)}, f32[1,256]{1,0:T(1,128)}, bf16[1024,2048]{1,0:T(8,128)(2,1)}, f32[256,1408]{1,0:T(8,128)}) custom-call(bf16[2,512,256]{2,1,0:T(8,128)(2,1)} %bitcast.31, bf16[2,512,768]{2,1,0:T(8,128)(2,1)} %bitcast.28, f32[2,512,256]{2,1,0:T(8,128)} %get-tuple-element.94.refs_12_.refs_2_, ...), custom_call_target="tpu_custom_call" | custom-call | flops 5905580032 | bytes 33592320 | tf_op jit(solution)/shard_map/pallas_call | solution.py:985
  556.8 102.1 %shard_map.294 = (bf16[1024,2048]{1,0:T(8,128)(2,1)}, f32[256,2176]{1,0:T(8,128)}, f32[24,128]{1,0:T(8,128)}, f32[256,128]{1,0:T(8,128)}) custom-call(bf16[1024,2048]{1,0:T(8,128)(2,1)} %get-tuple-element.106.refs_0_, bf16[1024,2048]{1,0:T(8,128)(2,1)} %bitcast.26, f32[256,2048]{1,0:T(8,128)} %get-tuple-element.107.refs_2_, ...), custom_call_target="tpu_custom_call" | custom-call | flops 9126805504 | bytes 29940736 | tf_op jit(solution)/shard_map/pallas_call | solution.py:985
  659.0 0.0 copy-start.1
  659.0 0.0 copy-start
  659.0 10.7 %shard_map.295 = (bf16[1024,2048]{1,0:T(8,128)(2,1)}, bf16[1024,2048]{1,0:T(8,128)(2,1)}, f32[256,256]{1,0:T(8,128)}, f32[256,256]{1,0:T(8,128)}, f32[256,512]{1...) custom-call(bf16[1024,2048]{1,0:T(8,128)(2,1)} %get-tuple-element.97, ...), custom_call_target="tpu_custom_call" | custom-call | tf_op jit(solution)/shard_map/pallas_call | solution.py:1821
  669.7 0.0 copy-done.1
  669.7 0.5 slice_bitcast_fusion.2
  670.2 0.5 slice_bitcast_fusion.3
  670.8 0.6 slice_bitcast_fusion
  671.3 0.6 slice.20
  671.9 0.0 copy-done
  671.9 0.7 copy.34
Async XLA Ops:
  659.0 10.7 %copy-start.1 = (f32[24,128]{1,0:T(8,128)S(1)}, f32[24,128]{1,0:T(8,128)}, u32[]{:S(2)}) copy-start(f32[24,128]{1,0:T(8,128)} %get-tuple-element.122) | copy-start | bytes 36868
  659.0 12.9 %copy-start = (f32[256,128]{1,0:T(8,128)S(1)}, f32[256,128]{1,0:T(8,128)}, u32[]{:S(2)}) copy-start(f32[256,128]{1,0:T(8,128)} %get-tuple-element.127) | copy-start | bytes 393220

commit v7 on v6

--- a/solution.py
+++ b/solution.py
@@ -902,13 +902,17 @@
     ring.advance()
     hand.join()
     ring.advance()
+    ready(10)
+    down_ring.start()
     for r in range(1, count // 2):
         hand.hop(r)
         ring.advance()
+        if r > 1:
+            down_ring.advance()
     hand.close()
     ready()
     ring.advance()
-    down_ring.start()
+    down_ring.advance()
     hand.finish()
     ring.finish()
     down_ring.advance()
@@ -1148,7 +1152,8 @@
 
 
 class SumRing:
-    def __init__(self, order, items, out_ref, scratch):
+    def __init__(self, order, items, out_ref, scratch, visit=None):
+        self.visit, self.arrived = visit, 0
         lefts = []
         for left, _, _ in items:
             if not any(left is other for other in lefts):
@@ -1198,13 +1203,22 @@
         self.load(0)
         self.load(1)
 
+    def arrive(self, k):
+        if k < self.arrived:
+            return
+        self.arrived = k + 1
+        for side in range(2):
+            for n in range(self.number):
+                self.loads[k, side, n].wait()
+            if self.visit is not None:
+                slot = (self.count - 1 - k) if side == 0 else (k + 1) % self.count
+                self.visit(slot, side, self.buffers[id(self.items[0][0])][k % 2, side])
+
     def advance(self):
         k, last = self.k, self.count - 1
         if k > last:
             return
-        for side in range(2):
-            for n in range(self.number):
-                self.loads[k, side, n].wait()
+        self.arrive(k)
         for n, (item, start, size, begin) in enumerate(self.pieces):
             left, right, _ = self.items[item]
             columns = slice(begin, begin + size)
@@ -1522,7 +1536,7 @@
 def back_phase_kernel(
     order, ready, query_ref, vk_ref, run_ref, slope_ref, states_ref, low_ref, up_ref, starts_ref,
     mixed_grad_ref, later_ref, gates_grad_ref, normed_ref, act_grad_ref, weight_ref, down_ref,
-    packed_ref, up_grad_ref, bias_grad_ref, part_ref, sums_ref,
+    packed_ref, low_grad_ref, up_grad_ref, bias_grad_ref, part_ref, sums_ref,
     state, mark_ref, row_ref, *scratch,
 ):
     count = len(order)
@@ -1537,8 +1551,6 @@
     fill_marks(starts_ref, mark_ref, row_ref)
     for ref in (up_grad_ref, bias_grad_ref):
         ref[...] = jnp.zeros_like(ref)
-    spare = packed_ref.shape[2] - low_from
-    packed_ref[:, :, low_from:] = jnp.zeros((batch, length, spare), BF16)
     ready(0, 1, 2, 3, 4, 5, 8, 9, 10)
     state[...] = wide(later_ref[...])
     packed_ref[:, :, gates_from:low_from] = gates_grad_ref[...]
@@ -1555,7 +1567,7 @@
                 states_ref.at[pl.ds(2 * n, 1)], states_ref.at[pl.ds(2 * n + 1, 1)],
                 low_ref.at[:, at], up_ref,
                 packed_ref.at[:, at, pl.ds(DV + DK, DK)], packed_ref.at[:, at, pl.ds(0, DV)],
-                packed_ref.at[:, at, pl.ds(DV, DK)], packed_ref.at[:, at, pl.ds(low_from, 128)],
+                packed_ref.at[:, at, pl.ds(DV, DK)], low_grad_ref.at[:, at],
                 up_grad_ref, bias_grad_ref, state,
             )
 
@@ -1565,13 +1577,13 @@
     ready.save(0)
     ring.advance()
     ready()
-    tile, rank = 256, low_ref.shape[2]
+    tile = 256
     down = [down_ref[block_at(order, r)] for r in range(count)]
     down = jnp.concatenate(down, axis=1)
     for b in range(batch):
         for t in range(length // tile):
-            field = packed_ref[b, t * tile : (t + 1) * tile, :low_from]
-            low = packed_ref[b, t * tile : (t + 1) * tile, low_from : low_from + rank]
+            field = packed_ref[b, t * tile : (t + 1) * tile]
+            low = low_grad_ref[b, t * tile : (t + 1) * tile]
             start = b * length + t * tile
             total = product(field, weight_ref[...], NT) + product(low, down, NN)
             part_ref[start : start + tile] = narrow(total)
@@ -1585,15 +1597,16 @@
 ):
     count = lax.axis_size("seq")
     batch, length, rank = low.shape
-    width, packed_cols = weights.shape[0], weights.shape[1] + 128
+    width, packed_cols = weights.shape
     share, hidden, rows = width // count, d_gate.shape[1], d_gate.shape[0]
     return remote_call(
         functools.partial(back_phase_kernel, ring_order(count)),
         5,
         [LOAD] * 6 + [NEAR, NEAR, LOAD, LOAD, LOAD, AWAY, LOAD, LOAD, NEAR],
-        [SAVE] + [NEAR] * 4,
+        [SAVE] + [NEAR] * 5,
         [
             shape_of(BF16, batch, length, packed_cols),
+            shape_of(BF16, batch, length, rank),
             shape_of(F32, rank, DK),
             shape_of(F32, 1, DK),
             shape_of(BF16, rows, width),
@@ -1613,16 +1626,21 @@
 
 def last_phase_kernel(
     order, heads, ready, part_ref, input_ref, resid_grad_ref, gain_ref, normed_ref, packed_ref, attn_ref,
-    heads_ref, ffn_gain_ref, head_gain_ref, bias_ref, up_ref,
+    heads_ref, ffn_gain_ref, head_gain_ref, bias_ref, up_ref, low_ref,
     input_grad_ref, sums_ref, small_ref, tail_ref,
-    own, own_sems, grads, grad_sems, gain_grad, stage, stage_got, shared, shared_got, tail_got,
+    own, own_sems, grads, grad_sems, gain_grad, stage, stage_got, downs, downs_got, shared, shared_got,
     seq_send, seq_receive, head_send, head_receive, *scratch,
 ):
     count = len(order)
     rows = Rows(part_ref, grads, scratch[:5])
-    ring = SumRing(
-        order, [(normed_ref, packed_ref, False), (attn_ref, heads_ref, False)], sums_ref, scratch[5:]
-    )
+    rank = low_ref.shape[1]
+
+    def visit(slot, side, columns):
+        block = narrow(product(low_ref[...], columns, TN))
+        downs[block_at(order, slot), side * rank : (side + 1) * rank] = block
+
+    items = [(normed_ref, packed_ref, False), (attn_ref, heads_ref, False)]
+    ring = SumRing(order, items, sums_ref, scratch[5:], visit)
     first = pl.multiple_of(rows.own * rows.share, rows.share)
     copies = near_copies(order, input_ref, own, pl.ds(first, rows.share), own_sems)
     for copy in copies:
@@ -1651,7 +1669,7 @@
     ring.advance()
     for p in range(PIECES):
         rows.turn(p, middle)
-        if p == 2:
+        if p == 1:
             ring.advance()
 
     mine, head = lax.axis_index("seq"), lax.axis_index("head")
@@ -1667,91 +1685,94 @@
             for t in range(share // 128):
                 start = j * share + t * 128
                 stage[owner, n + t : n + t + 1, :] = ref[:, start : start + 128]
-    stage_hops = []
-    for d in range(1, count):
-        aim = lax.rem(mine + d, count)
-        stage_hops.append(
-            pltpu.make_async_remote_copy(
-                src_ref=stage.at[aim],
-                dst_ref=stage_got.at[d - 1],
-                send_sem=seq_send.at[d - 1],
-                recv_sem=seq_receive.at[d - 1],
-                device_id={"seq": aim},
-                device_id_type=MESH,
+
+    def spread(kind, source, target):
+        hops = []
+        for d in range(1, count):
+            aim = lax.rem(mine + d, count)
+            hops.append(
+                pltpu.make_async_remote_copy(
+                    src_ref=source.at[aim],
+                    dst_ref=target.at[d - 1],
+                    send_sem=seq_send.at[kind, d - 1],
+                    recv_sem=seq_receive.at[kind, d - 1],
+                    device_id={"seq": aim},
+                    device_id_type=MESH,
+                )
             )
-        )
-    for hop in stage_hops:
-        hop.start()
-
-    def head_hops(kind, source, target):
-        return [
-            pltpu.make_async_remote_copy(
-                src_ref=source,
-                dst_ref=target.at[d - 1],
-                send_sem=head_send.at[kind, d - 1],
-                recv_sem=head_receive.at[kind, d - 1],
-                device_id={"head": lax.rem(head + d, heads)},
-                device_id_type=MESH,
-            )
-            for d in range(1, heads)
-        ]
-
+            hops[-1].start()
+        return hops
+
+    stage_hops = spread(0, stage, stage_got)
+
+    ring.advance()
     rows.relay(0)
     rows.relay(1)
     ring.advance()
     rows.relay(2)
     rows.relay(3)
-    for hop in stage_hops:
-        hop.wait_recv()
-    total = stage[mine]
-    for d in range(count - 1):
-        total = total + stage_got[d]
-    small_ref[...] = total
-    shared[...] = total[:8]
-    shared_hops = head_hops(0, shared, shared_got)
-    for hop in shared_hops:
-        hop.start()
     ring.advance()
     rows.finish()
     backs = home_copies(order, grads, input_grad_ref, grad_sems)
     for copy in backs:
         copy.start()
+    while ring.k < count - 1:
+        ring.advance()
+    ring.arrive(count - 1)
+    down_hops = spread(1, downs, downs_got)
+    for hop in stage_hops + down_hops:
+        hop.wait_recv()
+    total, down = stage[mine], wide(downs[mine])
+    for d in range(count - 1):
+        total = total + stage_got[d]
+        down = down + wide(downs_got[d])
+    small_ref[...] = total
+    shared[0:8] = total[:8]
+    shared[8:] = down
+    shared_hops = [
+        pltpu.make_async_remote_copy(
+            src_ref=shared,
+            dst_ref=shared_got.at[d - 1],
+            send_sem=head_send.at[d - 1],
+            recv_sem=head_receive.at[d - 1],
+            device_id={"head": lax.rem(head + d, heads)},
+            device_id_type=MESH,
+        )
+        for d in range(1, heads)
+    ]
+    for hop in shared_hops:
+        hop.start()
     for hop in shared_hops:
         hop.wait_recv()
-    small_ref[0:8] = shared[...] + (shared_got[0] + shared_got[1] + shared_got[2])
-    small_ref[1:2] = shared[1:2]
+    total = shared[...] + (shared_got[0] + shared_got[1] + shared_got[2])
+    small_ref[0:1] = total[0:1]
+    small_ref[2:8] = total[2:8]
+    tail_ref[...] = total[8:]
     ring.finish()
-    low_from = 2 * DV + 2 * DK
-    tail_ref[...] = sums_ref[:, low_from : low_from + 128]
-    tail_hops = head_hops(1, tail_ref, tail_got)
-    for hop in tail_hops:
-        hop.start()
-    for hop in tail_hops:
-        hop.wait_recv()
-    for hop in stage_hops + shared_hops + tail_hops:
+    for hop in stage_hops + down_hops + shared_hops:
         hop.wait_send()
-    tail_ref[...] = tail_ref[...] + (tail_got[0] + tail_got[1] + tail_got[2])
     for copy in backs:
         copy.wait()
 
 
 def last_phase(
-    part, inputs, d_resid, gains, normed, packed, d_attn, heads_out, ffn_gain, head_gain, bias, up
+    part, inputs, d_resid, gains, normed, packed, d_attn, heads_out, ffn_gain, head_gain, bias, up,
+    low,
 ):
     count, heads = lax.axis_size("seq"), lax.axis_size("head")
     rows, width = part.shape
     share, quarter = width // count, rows // heads
-    columns = packed.shape[1] + heads_out.shape[1]
+    columns, rank = packed.shape[1] + heads_out.shape[1], low.shape[1]
     return remote_call(
         functools.partial(last_phase_kernel, ring_order(count), heads),
         6,
-        [LOAD, AWAY, LOAD, NEAR, AWAY, LOAD, AWAY, LOAD, NEAR, NEAR, NEAR, NEAR],
+        [LOAD, AWAY, LOAD, NEAR, AWAY, LOAD, AWAY, LOAD, NEAR, NEAR, NEAR, NEAR, NEAR],
         [AWAY, NEAR, NEAR, NEAR],
         [
             shape_of(BF16, rows, width),
             shape_of(F32, share, columns),
             shape_of(F32, SMALL, 128),
-            shape_of(F32, share, 128),
+            shape_of(F32, 2 * rank, 128),
         ],
         [
             pltpu.VMEM((quarter, width), BF16),
@@ -1761,17 +1782,19 @@
             pltpu.VMEM((1, width), F32),
             pltpu.VMEM((count, SMALL, 128), F32),
             pltpu.VMEM((count - 1, SMALL, 128), F32),
-            pltpu.VMEM((8, 128), F32),
-            pltpu.VMEM((heads - 1, 8, 128), F32),
-            pltpu.VMEM((heads - 1, share, 128), F32),
-            pltpu.SemaphoreType.DMA((count - 1,)),
-            pltpu.SemaphoreType.DMA((count - 1,)),
-            pltpu.SemaphoreType.DMA((2, heads - 1)),
-            pltpu.SemaphoreType.DMA((2, heads - 1)),
+            pltpu.VMEM((count, 2 * rank, 128), BF16),
+            pltpu.VMEM((count - 1, 2 * rank, 128), BF16),
+            pltpu.VMEM((8 + 2 * rank, 128), F32),
+            pltpu.VMEM((heads - 1, 8 + 2 * rank, 128), F32),
+            pltpu.SemaphoreType.DMA((2, count - 1)),
+            pltpu.SemaphoreType.DMA((2, count - 1)),
+            pltpu.SemaphoreType.DMA((heads - 1,)),
+            pltpu.SemaphoreType.DMA((heads - 1,)),
         ]
         + rows_scratch(quarter, width)
         + sum_scratch(count, rows, 2, share // 2, [packed.shape[1], DV]),
-        (part, inputs, d_resid, gains, normed, packed, d_attn, heads_out, ffn_gain, head_gain, bias, up),
+        (part, inputs, d_resid, gains, normed, packed, d_attn, heads_out, ffn_gain, head_gain, bias, up,
+         low),
         2 * rows * width * columns,
     )
 
@@ -2223,14 +2246,14 @@
         part, resid, grad_rows, gains, out_t, act, normed_two, d_up, gates, mixed, gain_head, query,
         run, starts, total, ffn_part,
     )
-    packed, grad_up, grad_bias, part, grad_fgate = back_phase(
+    packed, d_low, grad_up, grad_bias, part, grad_fgate = back_phase(
         query, value_key, run, slope, states, low, up, starts, d_mixed, state_back, d_gates,
         normed_two, d_gate, weights, down,
     )
     packed = packed.reshape(rows, -1)
     input_grad, grad_last, small, tail = last_phase(
         part, inputs, d_resid, gains, normed, packed, d_attn, heads.reshape(rows, DV),
-        grad_gain_two, grad_gain_head, grad_bias, grad_up,
+        grad_gain_two, grad_gain_head, grad_bias, grad_up, d_low.reshape(rows, rank),
     )
     lines = share // 128
     results = leave(layer_out, input_grad, grad_first, grad_fgate, grad_last)
@@ -2243,7 +2266,7 @@
         grad_key,
         grad_value,
         grad_gate,
-        tail[:, :rank],
+        jnp.swapaxes(tail.reshape(2, rank, share // 2), 1, 2).reshape(share, rank),
         small[8:, : decay_up.shape[1]],
         small[1, : decay_bias.size],
         small[0, : head_gain.size],

time: 682 us -> 674 us (0.988)
  Pallas kernels: 665 us -> 658 us
    pallas_call x7, Pallas kernels: 654 us -> 647 us  [remote_call(): pl.pallas_call(body, in_specs=[AWAY if spec is LOAD else spec for spec in...]
where the time goes in v7:
time: 674 us; the launch traced here: 665 us
  Pallas kernels  658 us (98%)
    pallas_call x7, Pallas kernels, remote_call(): pl.pallas_call(body, in_specs=[AWAY if spec is LOAD else spec for spec in...  647 us

profile of v7, /device:TPU:0, one launch (start us, length us, event | category | flops | bytes accessed | tf_op | source)
XLA Modules:
  0.0 665.4 jit_solution(17327056935648791166)
XLA Ops:
  0.6 0.8 fusion.6
  1.4 0.6 broadcast_in_dim.3.refs_8_
  2.0 1.3 reshape.97.refs_6_.refs_13_.refs_7_
  3.3 1.4 copy.33.refs_5_
  4.7 98.3 %shard_map.288 = (bf16[1024,2048]{1,0:T(8,128)(2,1)}, bf16[8,256,1536]{2,1,0:T(8,128)(2,1)}, bf16[8,256,512]{2,1,0:T(8,128)(2,1)}, bf16[256,1408]{1,0:T(8,128)(2...) custom-call(bf16[1024,2048]{1,0:T(8,128)(2,1)} %bitcast.31, ...), custom_call_target="tpu_custom_call" | custom-call | flops 6442450944 | bytes 23639296 | tf_op jit(solution)/shard_map/pallas_call | solution.py:989
  103.0 102.1 %shard_map.289 = (f32[2,512,256]{2,1,0:T(8,128)}, f32[2,512,256]{2,1,0:T(8,128)}, f32[2,1,256]{2,1,0:T(1,128)}, f32[2,512,512]{2,1,0:T(8,128)}, bf16[2,512,512]{...) custom-call(bf16[2,512,768]{2,1,0:T(8,128)(2,1)} %bitcast.34, ...), custom_call_target="tpu_custom_call" | custom-call | flops 2684354560 | bytes 28795904 | tf_op jit(solution)/shard_map/pallas_call | solution.py:989
  205.1 62.4 %shard_map.290 = (f32[256,2048]{1,0:T(8,128)}, bf16[1024,2048]{1,0:T(8,128)(2,1)}, bf16[8,256,1408]{2,1,0:T(8,128)(2,1)}) custom-call(bf16[1024,2048]{1,0:T(8,128)(2,1)} %get-tuple-element.84.refs_0_, bf16[1024,2048]{1,0:T(8,128)(2,1)} %bitcast.32, f32[2,2048]{1,0:T(2,128)} %get-tuple-element.85.refs_2_.refs_3_, bf16[256,1408]{1,0:T(8,128)(2,1)} %refs_3_.3), custom_call_target="tpu_custom_call" | custom-call | flops 33554432 | bytes 21184512 | tf_op jit(solution)/shard_map/pallas_call | solution.py:989
  267.5 73.3 %shard_map.291 = (bf16[1024,1408]{1,0:T(8,128)(2,1)}, bf16[1024,1408]{1,0:T(8,128)(2,1)}, bf16[1024,1408]{1,0:T(8,128)(2,1)}, bf16[1024,2048]{1,0:T(8,128)(2,1)}, bf16[1024,2048]{1,0:T(8,128)(2,1)}) custom-call(bf16[1024,2048]{1,0:T(8,128)(2,1)} %get-tuple-element.86.refs_0_.refs_6_.refs_11_, bf16[2048,1408]{1,0:T(8,128)(2,1)} %bitcast.50, ...), custom_call_target="tpu_custom_call" | custom-call | flops 17716740096 | bytes 39256064 | tf_op jit(solution)/shard_map/pallas_call | solution.py:989
  340.8 142.2 %shard_map.292 = (f32[256,2048]{1,0:T(8,128)}, bf16[1024,2048]{1,0:T(8,128)(2,1)}, bf16[2,512,512]{2,1,0:T(8,128)(2,1)}, bf16[2,512,512]{2,1,0:T(8,128)(2,1)}, b...) custom-call(bf16[1024,2048]{1,0:T(8,128)(2,1)} %get-tuple-element.90, ...), custom_call_target="tpu_custom_call" | custom-call | flops 13958643712 | bytes 48531456 | tf_op jit(solution)/shard_map/pallas_call | solution.py:989
  483.0 69.0 %shard_map.293 = (bf16[2,512,1536]{2,1,0:T(8,128)(2,1)}, bf16[2,512,16]{2,1,0:T(8,128)(2,1)}, f32[16,256]{1,0:T(8,128)}, f32[1,256]{1,0:T(1,128)}, bf16[1024,2048]{1,0:T(8,128)(2,1)}, /*index=5*/f32[256,1408]{1,0:T(8,128)}) custom-call(bf16[2,512,256]{2,1,0:T(8,128)(2,1)} %bitcast.38, bf16[2,512,768]{2,1,0:T(8,128)(2,1)} %bitcast.35, ...), custom_call_target="tpu_custom_call" | custom-call | flops 5905580032 | bytes 33362944 | tf_op jit(solution)/shard_map/pallas_call | solution.py:989
  552.0 99.7 %shard_map.294 = (bf16[1024,2048]{1,0:T(8,128)(2,1)}, f32[256,2048]{1,0:T(8,128)}, f32[24,128]{1,0:T(8,128)}, f32[32,128]{1,0:T(8,128)}) custom-call(bf16[1024,2048]{1,0:T(8,128)(2,1)} %get-tuple-element.107.refs_0_, bf16[1024,2048]{1,0:T(8,128)(2,1)} %bitcast.33, f32[256,2048]{1,0:T(8,128)} %get-tuple-element.108.refs_2_, ...), custom_call_target="tpu_custom_call" | custom-call | flops 8589934592 | bytes 29465600 | tf_op jit(solution)/shard_map/pallas_call | solution.py:989
  651.7 0.0 copy-start.1
  651.7 0.0 copy-start
  651.8 10.6 %shard_map.295 = (bf16[1024,2048]{1,0:T(8,128)(2,1)}, bf16[1024,2048]{1,0:T(8,128)(2,1)}, f32[256,256]{1,0:T(8,128)}, f32[256,256]{1,0:T(8,128)}, f32[256,512]{1...) custom-call(bf16[1024,2048]{1,0:T(8,128)(2,1)} %get-tuple-element.98, ...), custom_call_target="tpu_custom_call" | custom-call | tf_op jit(solution)/shard_map/pallas_call | solution.py:1844
  662.4 0.0 copy-done.1
  662.4 0.5 slice_bitcast_fusion.2
  662.9 0.5 slice_bitcast_fusion.3
  663.4 0.6 slice_bitcast_fusion
  664.0 0.6 slice.16
  664.6 0.0 copy-done
  664.6 0.6 copy.37
Async XLA Ops:
  651.7 10.6 %copy-start.1 = (f32[24,128]{1,0:T(8,128)S(1)}, f32[24,128]{1,0:T(8,128)}, u32[]{:S(2)}) copy-start(f32[24,128]{1,0:T(8,128)} %get-tuple-element.124) | copy-start | bytes 36868
  651.7 12.8 %copy-start = (f32[32,128]{1,0:T(8,128)S(1)}, f32[32,128]{1,0:T(8,128)}, u32[]{:S(2)}) copy-start(f32[32,128]{1,0:T(8,128)} %get-tuple-element.129) | copy-start | bytes 49156
